TPU v7x, 128 devices: a whole 4x4x4 slice. The times are simulated.
128 devices in a mesh: row: 16 (over y_lo, z, core), col: 8 (over x, y_hi).
Axes of the slice: x: 4, y: 4 (y_hi: 2, y_lo: 2; y = y_hi * 2 + y_lo), z: 4, core: 2. Of those that a mesh axis runs over, the one named last changes fastest.
Arguments:
- covariance: float32 [1, 8192, 8192], P(None, 'row', 'col'), may hold values from -120 to 120, as said below
- latitude_offset: int32 [1, 1, 8192], replicated, may hold values from -2 to 2
- longitude_offset: int32 [1, 1, 8192], replicated, may hold values from -3 to 3
- upwind: int32 [1, 1, 8192], replicated, may hold values from 0 to 3
- courant: float32 [1, 1, 8192], replicated, may hold values from 0.05 to 0.45
- longitude_diffusion: float32 [1, 8192], replicated, may hold values from 0.01 to 0.08
- latitude_diffusion: float32 [1, 8192], replicated, may hold values from 0.01 to 0.08
Outputs:
- forecast_cov: float32 [1, 8192, 8192], P(None, 'row', 'col')
Inputs may be any that keep to these rules, and one draw needn't show every extreme that they name: `covariance`: each level's matrix is symmetric up to rounding.
All inputs are finite; a program needn't handle non-finite values.
Results may differ from a plain program's by a relative error of at most 0.0003.
Values sent between devices are 32-bit elements; how exact they have to be, the bound alone decides.
No kernel may reach another device: no remote copies, remote signals or barrier semaphores. Data moves between devices by JAX's collectives and lax.ppermute only.
A program may use at most 128 MiB of HBM per device.

v0:
```python
import functools

import jax
import jax.numpy as jnp
from jax import lax
from jax.experimental import pallas as pl
from jax.experimental.pallas import tpu as pltpu
from jax.sharding import PartitionSpec as P


NLAT = 64
NLON = 128
HALO = 4
SPAN = 10 * NLON
PAIR = 2 * NLON


def split(x):
    high = x.astype(jnp.bfloat16)
    low = (x - high.astype(jnp.float32)).astype(jnp.bfloat16)
    return high, low


def dot3(a_high, a_low, b_high, b_low):
    dot = functools.partial(jnp.dot, preferred_element_type=jnp.float32)
    return dot(a_high, b_high) + (dot(a_high, b_low) + dot(a_low, b_high))


def band_kernel(
    transposed, place, lat_off, lon_off, upwind, courant, lon_diff, lat_diff,
    high, low, depart_lat, depart_lon, near_lat, near_lon,
):
    shape = (NLAT, NLON)
    lat = lax.broadcasted_iota(jnp.int32, shape, 0)
    lon = lax.broadcasted_iota(jnp.int32, shape, 1)
    up = upwind[...]
    one = jnp.ones(shape, jnp.int32)
    zero = jnp.zeros(shape, jnp.int32)
    d_lat = jnp.clip(lat + lat_off[...], 0, NLAT - 1)
    d_lon = (lon + lon_off[...]) & (NLON - 1)
    depart_lat[...] = d_lat
    depart_lon[...] = d_lon
    near_lat[...] = jnp.clip(
        d_lat + jnp.where(up == 2, one, zero) - jnp.where(up == 3, one, zero), 0, NLAT - 1
    )
    near_lon[...] = (
        d_lon + jnp.where(up == 0, one, zero) - jnp.where(up == 1, one, zero)
    ) & (NLON - 1)

    sub = lax.broadcasted_iota(jnp.int32, (NLON, NLON), 0)

    def advect_block(y, in_lat):
        row = pl.ds(y, 1)
        w = courant[row, :]
        none = jnp.zeros_like(w)
        keep = jnp.where(depart_lat[row, :] == in_lat, 1.0 - w, none)
        take = jnp.where(near_lat[row, :] == in_lat, w, none)
        empty = jnp.zeros((NLON, NLON), jnp.float32)
        return jnp.where(sub == depart_lon[row, :], keep, empty) + jnp.where(
            sub == near_lon[row, :], take, empty
        )

    def model_block(y, in_lat):
        lx = lon_diff[pl.ds(y, 1), :]
        ly = lat_diff[pl.ds(y, 1), :]
        here = advect_block(y, in_lat)
        north = advect_block(jnp.minimum(y + 1, NLAT - 1), in_lat)
        south = advect_block(jnp.maximum(y - 1, 0), in_lat)
        beside = pltpu.roll(here, 1, 1) + pltpu.roll(here, NLON - 1, 1)
        return here + lx * (beside - 2.0 * here) + ly * (north + south - 2.0 * here)

    first = place[0]
    for pair in range(high.shape[0]):

        def step(t, carry, pair=pair):
            for half in range(2):
                y = first + 2 * pair + half
                value = model_block(y, first + 2 * pair - HALO + t)
                if transposed:
                    value = value.T
                h, l = split(value)
                rows = pl.ds(pl.multiple_of(t * NLON, NLON), NLON)
                cols = pl.ds(half * NLON, NLON)
                at = (pair, cols, rows) if transposed else (pair, rows, cols)
                high[at] = h
                low[at] = l
            return carry

        lax.fori_loop(0, SPAN // NLON, step, 0)


VMEM_SPEC = pl.BlockSpec(memory_space=pltpu.VMEM)


def held(x):
    return pltpu.with_memory_space_constraint(x, pltpu.VMEM)


def build_bands(place, fields, pairs, transposed):
    shape = (pairs, PAIR, SPAN) if transposed else (pairs, SPAN, PAIR)
    band = pltpu.VMEM(shape, jnp.bfloat16)
    return pl.pallas_call(
        functools.partial(band_kernel, transposed),
        out_shape=(band, band),
        in_specs=[pl.BlockSpec(memory_space=pltpu.SMEM)] + [VMEM_SPEC] * 6,
        out_specs=(VMEM_SPEC,) * 2,
        scratch_shapes=[pltpu.VMEM((NLAT, NLON), jnp.int32)] * 4,
        compiler_params=pltpu.CompilerParams(vmem_limit_bytes=24 << 20),
        name="row_bands" if transposed else "col_bands",
    )(place, *fields)


def rows_kernel(north, own, south, band_high, band_low, left, right, high, low):
    at = 0
    for ref in (north, own, south):
        h, l = split(ref[...])
        high[at : at + ref.shape[0], :] = h
        low[at : at + ref.shape[0], :] = l
        at += ref.shape[0]
    width = left.shape[1]
    for pair in range(left.shape[0] // PAIR):
        at = pair * PAIR
        value = dot3(
            band_high[pair], band_low[pair], high[at : at + SPAN, :], low[at : at + SPAN, :]
        )
        left[at : at + PAIR, :] = value[:, :width]
        right[at : at + PAIR, :] = value[:, width:]


def apply_rows(north, own, south, bands):
    rows, width = own.shape
    ext = pltpu.VMEM((3 * rows, width), jnp.bfloat16)
    half = pltpu.VMEM((rows, width // 2), jnp.float32)
    args = [held(a) for a in (north, own, south, *bands)]
    return pl.pallas_call(
        rows_kernel,
        out_shape=(half, half),
        in_specs=[VMEM_SPEC] * 5,
        out_specs=(VMEM_SPEC,) * 2,
        scratch_shapes=[ext, ext],
        compiler_params=pltpu.CompilerParams(vmem_limit_bytes=16 << 20),
        name="rows",
    )(*args)


def cols_kernel(*refs):
    parts = refs[:-5]
    band_high, band_low, out, high, low = refs[-5:]
    at = 0
    for ref in parts:
        h, l = split(ref[...])
        high[:, at : at + ref.shape[1]] = h
        low[:, at : at + ref.shape[1]] = l
        at += ref.shape[1]
    for pair in range(out.shape[1] // PAIR):
        begin = (pair - 1) * PAIR
        skip = max(0, -begin)
        stop = min(at, begin + SPAN)
        ext = slice(begin + skip, stop)
        band = slice(skip, stop - begin)
        out[:, pair * PAIR : (pair + 1) * PAIR] = dot3(
            high[:, ext], low[:, ext], band_high[pair, band], band_low[pair, band]
        )


def apply_cols(parts, bands, width):
    rows = parts[0].shape[0]
    ext = pltpu.VMEM((rows, sum(p.shape[1] for p in parts)), jnp.bfloat16)
    args = [held(a) for a in (*parts, *bands)]
    return pl.pallas_call(
        cols_kernel,
        out_shape=jax.ShapeDtypeStruct((rows, width), jnp.float32),
        in_specs=[VMEM_SPEC] * len(args),
        out_specs=VMEM_SPEC,
        scratch_shapes=[ext, ext],
        compiler_params=pltpu.CompilerParams(vmem_limit_bytes=32 << 20),
        name="cols",
    )(*args)


def tail_kernel(west, east, band_high, band_low, part, out):
    last = band_high.shape[0] - 1

    def add(ref, pair, rows):
        h, l = split(ref[...])
        out[...] = part[...] + dot3(h, l, band_high[pair, rows], band_low[pair, rows])

    @pl.when(pl.program_id(0) == 0)
    def _():
        add(west, 0, slice(0, west.shape[1]))

    @pl.when(pl.program_id(0) == 1)
    def _():
        add(east, last, slice(SPAN - east.shape[1], SPAN))


def apply_tail(west, east, bands, part):
    rows, width = part.shape
    block = pl.BlockSpec((rows, PAIR), lambda i: (0, i * (width // PAIR - 1)))
    args = [held(a) for a in (west, east, *bands)]
    return pl.pallas_call(
        tail_kernel,
        grid=(2,),
        out_shape=jax.ShapeDtypeStruct((rows, width), jnp.float32),
        in_specs=[VMEM_SPEC] * 4 + [block],
        out_specs=block,
        input_output_aliases={4: 0},
        compiler_params=pltpu.CompilerParams(vmem_limit_bytes=16 << 20),
        name="tail",
    )(*args, part)


def body(
    covariance, latitude_offset, longitude_offset, upwind, courant,
    longitude_diffusion, latitude_diffusion,
):
    own = covariance[0]
    rows, width = own.shape
    row_count, col_count = lax.axis_size("row"), lax.axis_size("col")
    forward = lambda n: [(i, i + 1) for i in range(n - 1)]
    backward = lambda n: [(i + 1, i) for i in range(n - 1)]

    def columns(first, stop):
        west = own[:, first * NLON : stop * NLON]
        east = own[:, width - stop * NLON : width - first * NLON]
        return jnp.concatenate([west, east], axis=1)

    def from_rows(x):
        return (
            lax.ppermute(x, "row", forward(row_count)),
            lax.ppermute(x, "row", backward(row_count)),
        )

    def from_cols(left, right):
        return (
            lax.ppermute(right, "col", forward(col_count)),
            lax.ppermute(left, "col", backward(col_count)),
        )

    fields = [
        a.reshape(NLAT, NLON)
        for a in (
            latitude_offset, longitude_offset, upwind, courant,
            longitude_diffusion, latitude_diffusion,
        )
    ]
    lat_row = (lax.axis_index("row") * (rows // NLON)).astype(jnp.int32).reshape(1)
    lat_col = (lax.axis_index("col") * (width // NLON)).astype(jnp.int32).reshape(1)

    own0, own1, own2 = columns(0, 1), columns(1, 2), columns(2, 4)
    north0, south0 = from_rows(own0)
    row_bands = build_bands(lat_row, fields, rows // PAIR, True)
    north1, south1 = from_rows(own1)
    left0, right0 = apply_rows(north0, own0, south0, row_bands)
    west0, east0 = from_cols(left0, right0)
    north2, south2 = from_rows(own2)
    left1, right1 = apply_rows(north1, own1, south1, row_bands)
    west1, east1 = from_cols(left1, right1)
    col_bands = build_bands(lat_col, fields, width // PAIR, False)
    left2, right2 = apply_rows(north2, own2, south2, row_bands)
    west2, east2 = from_cols(left2, right2)
    parts = [west1, west0, left0, left1, left2, right2, right1, right0, east0, east1]
    part = apply_cols(parts, col_bands, width)
    return apply_tail(west2, east2, col_bands, part)[None]


def solution(mesh):
    in_specs = (P(None, "row", "col"), P(), P(), P(), P(), P(), P())
    out_specs = P(None, "row", "col")
    return jax.shard_map(
        body, mesh=mesh, in_specs=in_specs, out_specs=out_specs, check_vma=False
    )
```

profile of v0, /device:TPU:15, one launch (start us, length us, event | category | flops | bytes accessed | tf_op | source)
XLA Modules:
  0.0 102.4 jit_solution(6580835708115265530)
XLA Ops:
  0.0 0.0 copy-start.12
  0.0 1.4 %concatenate.12.own = f32[512,512]{1,0:T(8,128)S(1)} slice(f32[512,1024]{1,0:T(8,128)} %bitcast.22), slice={[0:512], [256:768]} | slice | bytes 2097152 | tf_op jit(solution)/shard_map/concatenate | solution.py:226
  1.4 0.0 copy-start.4
  1.5 0.0 copy-start.5
  1.5 0.0 copy-start.6
  1.5 0.0 copy-start.7
  1.5 0.0 copy-start.8
  1.5 0.0 copy-start.10
  1.5 4.2 %collective-permute-start = (f32[512,512]{1,0:T(8,128)S(1)}, f32[512,512]{1,0:T(8,128)S(1)}, u32[]{:S(2)}, u32[]{:S(2)}) collective-permute-start(f32[512,512]{1,0:T(8,128)S(1)} %concatenate.12.own), channel_id=1, source_target_pairs={{0,8},{8,16},{16,24},{24,32},{32,40},{40,48},{48,56},{56,64},{64,7... | collective-permute-start | bytes 3145736 | tf_op jit(solution)/shard_map/ppermute | solution.py:230
  5.8 1.9 %collective-permute-start.1 = (f32[512,512]{1,0:T(8,128)S(1)}, f32[512,512]{1,0:T(8,128)}, u32[]{:S(2)}, u32[]{:S(2)}) collective-permute-start(f32[512,512]{1,0:T(8,128)S(1)} %concatenate.12.own), channel_id=1, source_target_pairs={{8,0},{16,8},{24,16},{32,24},{40,32},{48,40},{56,48},{64,56},{72,6... | collective-permute-start | bytes 3145736 | tf_op jit(solution)/shard_map/ppermute | solution.py:231
  7.7 0.0 copy-done.12
  7.7 0.1 fusion
  7.8 3.6 %collective-permute-start.7 = (f32[512,256]{1,0:T(8,128)S(1)}, f32[512,256]{1,0:T(8,128)S(1)}, u32[]{:S(2)}, u32[]{:S(2)}) collective-permute-start(f32[512,256]{1,0:T(8,128)S(1)} %pad_maximum_fusion.1.own), channel_id=1, source_target_pairs={{0,8},{8,16},{16,24},{24,32},{32,40},{40,48},{48,56},{56,64},{64,7... | collective-permute-start | bytes 1572872 | tf_op jit(solution)/shard_map/ppermute | solution.py:230
  11.5 2.5 %collective-permute-start.8 = (f32[512,256]{1,0:T(8,128)S(1)}, f32[512,256]{1,0:T(8,128)}, u32[]{:S(2)}, u32[]{:S(2)}) collective-permute-start(f32[512,256]{1,0:T(8,128)S(1)} %pad_maximum_fusion.1.own), channel_id=1, source_target_pairs={{8,0},{16,8},{24,16},{32,24},{40,32},{48,40},{56,48},{64,56},{72,6... | collective-permute-start | bytes 1572872 | tf_op jit(solution)/shard_map/ppermute | solution.py:231
  14.0 3.1 %collective-permute-start.4 = (f32[512,256]{1,0:T(8,128)S(1)}, f32[512,256]{1,0:T(8,128)}, u32[]{:S(2)}, u32[]{:S(2)}) collective-permute-start(f32[512,256]{1,0:T(8,128)S(1)} %pad_maximum_fusion.own), channel_id=1, source_target_pairs={{0,8},{8,16},{16,24},{24,32},{32,40},{40,48},{48,56},{56,64},{64,7... | collective-permute-start | bytes 1572872 | tf_op jit(solution)/shard_map/ppermute | solution.py:230
  17.1 6.0 %collective-permute-done.7.north = f32[512,256]{1,0:T(8,128)S(1)} collective-permute-done((f32[512,256]{1,0:T(8,128)S(1)}, f32[512,256]{1,0:T(8,128)S(1)}, u32[]{:S(2)}, u32[]{:S(2)}) %collective-permute-start.7) | collective-permute-done | bytes 524320 | tf_op jit(solution)/shard_map/ppermute | solution.py:230
  23.1 0.0 copy-start
  23.1 0.8 copy-done
  23.9 5.0 %collective-permute-start.5 = (f32[512,256]{1,0:T(8,128)S(1)}, f32[512,256]{1,0:T(8,128)}, u32[]{:S(2)}, u32[]{:S(2)}) collective-permute-start(f32[512,256]{1,0:T(8,128)S(1)} %pad_maximum_fusion.own), channel_id=1, source_target_pairs={{8,0},{16,8},{24,16},{32,24},{40,32},{48,40},{56,48},{64,56},{72,6... | collective-permute-start | bytes 1572872 | tf_op jit(solution)/shard_map/ppermute | solution.py:231
  28.9 0.0 copy-done.4
  28.9 0.0 copy-done.5
  28.9 0.0 copy-done.6
  28.9 0.0 copy-done.7
  28.9 0.0 copy-done.8
  28.9 0.0 copy-done.10
  28.9 4.6 %row_bands.1 = (bf16[2,256,1280]{2,1,0:T(8,128)(2,1)S(1)}, bf16[2,256,1280]{2,1,0:T(8,128)(2,1)S(1)}) custom-call(s32[1]{0:T(128)} %bitcast.1.place, s32[64,128]{1,0:T(8,128)S(1)} %bitcast.10, s32[64,128]{1,0:T(8,128)S(1)} %bitcast.12, s32[64,128]{1,0:T(8,128)S(1)} %bitcast.14, f32[64,128]{1,0:T(8,128)S(1)} %bitcast.16, f32[64,128]{1,0:T(8,128)S(1)} %bitcast.18, ...), custom_call_target="tpu_custom_call" | custom-call | tf_op jit(solution)/shard_map/row_bands/pallas_call | solution.py:102
  33.5 0.0 collective-permute-done.8.south
  33.5 0.0 copy-start.1
  33.5 1.0 %copy-done.1 = f32[512,256]{1,0:T(8,128)S(1)} copy-done((f32[512,256]{1,0:T(8,128)S(1)}, f32[512,256]{1,0:T(8,128)}, u32[]{:S(2)}) %copy-start.1) | copy-done | bytes 524312
  34.6 3.0 %rows.5 = (f32[512,128]{1,0:T(8,128)S(1)}, f32[512,128]{1,0:T(8,128)}) custom-call(f32[512,256]{1,0:T(8,128)S(1)} %copy-done.1, f32[512,256]{1,0:T(8,128)S(1)} %pad_maximum_fusion.1.own, f32[512,256]{1,0:T(8,128)} %collective-permute-done.8.south, bf16[2,256,1280]{2,1,0:T(8,128)(2,1)S(1)} %get-tuple-element.15.band_high, ...), custom_call_target="tpu_custom_call" | custom-call | tf_op jit(solution)/shard_map/rows/pallas_call | solution.py:135
  37.6 4.2 %collective-permute-start.10 = (f32[512,128]{1,0:T(8,128)S(1)}, f32[512,128]{1,0:T(8,128)S(1)}, u32[]{:S(2)}, u32[]{:S(2)}) collective-permute-start(f32[512,128]{1,0:T(8,128)S(1)} %get-tuple-element.23.refs_2_), channel_id=1, source_target_pairs={{1,0},{2,1},{3,2},{4,3},{5,4},{6,5},{7,6},{9,8},{10,9},{11,10},{12... | collective-permute-start | bytes 786440 | tf_op jit(solution)/shard_map/ppermute | solution.py:237
  41.7 0.0 collective-permute-done.north
  41.8 0.0 collective-permute-done.1.south
  41.8 4.3 %rows.3 = (f32[512,256]{1,0:T(8,128)S(1)}, f32[512,256]{1,0:T(8,128)}) custom-call(f32[512,512]{1,0:T(8,128)S(1)} %collective-permute-done.north, f32[512,512]{1,0:T(8,128)S(1)} %concatenate.12.own, f32[512,512]{1,0:T(8,128)} %collective-permute-done.1.south, bf16[2,256,1280]{2,1,0:T(8,128)(2,1)S(1)} %get-tuple-element.15.band_high, ...), custom_call_target="tpu_custom_call" | custom-call | tf_op jit(solution)/shard_map/rows/pallas_call | solution.py:135
  46.1 2.6 %collective-permute-start.2 = (f32[512,256]{1,0:T(8,128)}, f32[512,256]{1,0:T(8,128)S(1)}, u32[]{:S(2)}, u32[]{:S(2)}) collective-permute-start(f32[512,256]{1,0:T(8,128)} %get-tuple-element.17.refs_5_), channel_id=1, source_target_pairs={{0,1},{1,2},{2,3},{3,4},{4,5},{5,6},{6,7},{8,9},{9,10},{10,11},{11... | collective-permute-start | bytes 1572872 | tf_op jit(solution)/shard_map/ppermute | solution.py:236
  48.7 0.0 copy-start.9
  48.7 0.0 copy-start.11
  48.7 5.1 %collective-permute-start.3 = (f32[512,256]{1,0:T(8,128)S(1)}, f32[512,256]{1,0:T(8,128)S(1)}, u32[]{:S(2)}, u32[]{:S(2)}) collective-permute-start(f32[512,256]{1,0:T(8,128)S(1)} %get-tuple-element.18.refs_4_), channel_id=1, source_target_pairs={{1,0},{2,1},{3,2},{4,3},{5,4},{6,5},{7,6},{9,8},{10,9},{11,10},{12... | collective-permute-start | bytes 1572872 | tf_op jit(solution)/shard_map/ppermute | solution.py:237
  53.8 0.0 collective-permute-done.4.north
  53.8 0.0 collective-permute-done.5.south
  53.8 2.4 %rows.4 = (f32[512,128]{1,0:T(8,128)S(1)}, f32[512,128]{1,0:T(8,128)S(1)}) custom-call(f32[512,256]{1,0:T(8,128)} %collective-permute-done.4.north, f32[512,256]{1,0:T(8,128)S(1)} %pad_maximum_fusion.own, f32[512,256]{1,0:T(8,128)} %collective-permute-done.5.south, bf16[2,256,1280]{2,1,0:T(8,128)(2,1)S(1)} %get-tuple-element.15.band_high, ...), custom_call_target="tpu_custom_call" | custom-call | tf_op jit(solution)/shard_map/rows/pallas_call | solution.py:135
  56.2 2.0 %collective-permute-start.11 = (f32[512,128]{1,0:T(8,128)S(1)}, f32[512,128]{1,0:T(8,128)S(1)}, u32[]{:S(2)}, u32[]{:S(2)}) collective-permute-start(f32[512,128]{1,0:T(8,128)S(1)} %get-tuple-element.24.refs_3_), channel_id=1, source_target_pairs={{1,0},{2,1},{3,2},{4,3},{5,4},{6,5},{7,6},{9,8},{10,9},{11,10},{12... | collective-permute-start | bytes 786440 | tf_op jit(solution)/shard_map/ppermute | solution.py:237
  58.2 4.8 %collective-permute-start.6 = (f32[512,128]{1,0:T(8,128)S(1)}, f32[512,128]{1,0:T(8,128)S(1)}, u32[]{:S(2)}, u32[]{:S(2)}) collective-permute-start(f32[512,128]{1,0:T(8,128)S(1)} %get-tuple-element.21.refs_6_), channel_id=1, source_target_pairs={{0,1},{1,2},{2,3},{3,4},{4,5},{5,6},{6,7},{8,9},{9,10},{10,11},{11... | collective-permute-start | bytes 786440 | tf_op jit(solution)/shard_map/ppermute | solution.py:236
  63.1 0.0 collective-permute-done.10.refs_8_
  63.1 0.0 copy-start.2
  63.1 0.7 copy-done.2
  63.8 1.9 %collective-permute-start.9 = (f32[512,128]{1,0:T(8,128)}, f32[512,128]{1,0:T(8,128)S(1)}, u32[]{:S(2)}, u32[]{:S(2)}) collective-permute-start(f32[512,128]{1,0:T(8,128)} %get-tuple-element.22.refs_7_), channel_id=1, source_target_pairs={{0,1},{1,2},{2,3},{3,4},{4,5},{5,6},{6,7},{8,9},{9,10},{10,11},{11... | collective-permute-start | bytes 786440 | tf_op jit(solution)/shard_map/ppermute | solution.py:236
  65.7 0.0 copy-done.9
  65.7 0.0 copy-done.11
  65.7 6.8 %col_bands.1 = (bf16[4,1280,256]{2,1,0:T(8,128)(2,1)S(1)}, bf16[4,1280,256]{2,1,0:T(8,128)(2,1)S(1)}) custom-call(s32[1]{0:T(128)} %bitcast.8.place, s32[64,128]{1,0:T(8,128)S(1)} %bitcast.11, s32[64,128]{1,0:T(8,128)S(1)} %bitcast.13, s32[64,128]{1,0:T(8,128)S(1)} %bitcast.15, f32[64,128]{1,0:T(8,128)S(1)} %bitcast.17, f32[64,128]{1,0:T(8,128)S(1)} %bitcast.19, ...), custom_call_target="tpu_custom_call" | custom-call | tf_op jit(solution)/shard_map/col_bands/pallas_call | solution.py:102
  72.5 20.0 %collective-permute-done.11.refs_9_ = f32[512,128]{1,0:T(8,128)S(1)} collective-permute-done((f32[512,128]{1,0:T(8,128)S(1)}, f32[512,128]{1,0:T(8,128)S(1)}, u32[]{:S(2)}, u32[]{:S(2)}) %collective-permute-start.11) | collective-permute-done | bytes 262176 | tf_op jit(solution)/shard_map/ppermute | solution.py:237
  92.5 0.0 collective-permute-done.6.refs_0_
  92.5 0.0 collective-permute-done.9.refs_1_
  92.5 0.0 copy-start.3
  92.5 0.9 copy-done.3
  93.5 6.3 %cols.1.part = f32[512,1024]{1,0:T(8,128)} custom-call(f32[512,128]{1,0:T(8,128)S(1)} %collective-permute-done.6.refs_0_, f32[512,128]{1,0:T(8,128)S(1)} %collective-permute-done.9.refs_1_, f32[512,128]{1,0:T(8,128)S(1)} %get-tuple-element.23.refs_2_, f32[512,128]{1,0:T(8,128)S(1)} %get-tuple-element.24.refs_3_, f32[512,256]{1,0:T(8,128)S(1)} %get-tuple-element.18.refs_4_, ...), custom_call_target="tpu_custom_call" | custom-call | tf_op jit(solution)/shard_map/cols/pallas_call | solution.py:170
  99.7 0.0 collective-permute-done.2.west
  99.7 0.0 collective-permute-done.3.east
  99.7 2.6 %tail.1 = f32[512,1024]{1,0:T(8,128)} custom-call(f32[512,256]{1,0:T(8,128)S(1)} %collective-permute-done.2.west, f32[512,256]{1,0:T(8,128)S(1)} %collective-permute-done.3.east, bf16[4,1280,256]{2,1,0:T(8,128)(2,1)S(1)} %get-tuple-element.19.refs_10_.band_high, ...), custom_call_target="tpu_custom_call", output_to_operand_aliasing={{}: (4, {})} | custom-call | tf_op jit(solution)/shard_map/tail/pallas_call | solution.py:201
  (2 shorter events, 0.1 us)
Async XLA Ops:
  0.0 7.7 %copy-start.12 = (f32[1,512,1024]{2,1,0:T(8,128)S(1)}, f32[1,512,1024]{2,1,0:T(8,128)}, u32[]{:S(2)}) copy-start(f32[1,512,1024]{2,1,0:T(8,128)} %param.7) | copy-start | bytes 6291460
  1.4 27.4 %copy-start.4 = (s32[1,1,8192]{2,1,0:T(1,128)S(1)}, s32[1,1,8192]{2,1,0:T(1,128)}, u32[]{:S(2)}) copy-start(s32[1,1,8192]{2,1,0:T(1,128)} %param.8) | copy-start | bytes 98308
  1.5 27.4 %copy-start.5 = (s32[1,1,8192]{2,1,0:T(1,128)S(1)}, s32[1,1,8192]{2,1,0:T(1,128)}, u32[]{:S(2)}) copy-start(s32[1,1,8192]{2,1,0:T(1,128)} %param.9) | copy-start | bytes 98308
  1.5 27.4 %copy-start.6 = (s32[1,1,8192]{2,1,0:T(1,128)S(1)}, s32[1,1,8192]{2,1,0:T(1,128)}, u32[]{:S(2)}) copy-start(s32[1,1,8192]{2,1,0:T(1,128)} %param.10) | copy-start | bytes 98308
  1.5 27.4 %copy-start.7 = (f32[1,1,8192]{2,1,0:T(1,128)S(1)}, f32[1,1,8192]{2,1,0:T(1,128)}, u32[]{:S(2)}) copy-start(f32[1,1,8192]{2,1,0:T(1,128)} %param.11) | copy-start | bytes 98308
  1.5 27.4 %copy-start.8 = (f32[1,8192]{1,0:T(1,128)S(1)}, f32[1,8192]{1,0:T(1,128)}, u32[]{:S(2)}) copy-start(f32[1,8192]{1,0:T(1,128)} %param.12) | copy-start | bytes 98308
  1.5 27.4 %copy-start.10 = (f32[1,8192]{1,0:T(1,128)S(1)}, f32[1,8192]{1,0:T(1,128)}, u32[]{:S(2)}) copy-start(f32[1,8192]{1,0:T(1,128)} %param.13) | copy-start | bytes 98308
  1.5 40.2 %collective-permute-start = (f32[512,512]{1,0:T(8,128)S(1)}, f32[512,512]{1,0:T(8,128)S(1)}, u32[]{:S(2)}, u32[]{:S(2)}) collective-permute-start(f32[512,512]{1,0:T(8,128)S(1)} %concatenate.12.own), channel_id=1, source_target_pairs={{0,8},{8,16},{16,24},{24,32},{32,40},{40,48},{48,56},{56,64},{64,7... | collective-permute-start | bytes 3145736 | tf_op jit(solution)/shard_map/ppermute | solution.py:230
  5.8 36.0 %collective-permute-start.1 = (f32[512,512]{1,0:T(8,128)S(1)}, f32[512,512]{1,0:T(8,128)}, u32[]{:S(2)}, u32[]{:S(2)}) collective-permute-start(f32[512,512]{1,0:T(8,128)S(1)} %concatenate.12.own), channel_id=1, source_target_pairs={{8,0},{16,8},{24,16},{32,24},{40,32},{48,40},{56,48},{64,56},{72,6... | collective-permute-start | bytes 3145736 | tf_op jit(solution)/shard_map/ppermute | solution.py:231
  7.8 15.3 %collective-permute-start.7 = (f32[512,256]{1,0:T(8,128)S(1)}, f32[512,256]{1,0:T(8,128)S(1)}, u32[]{:S(2)}, u32[]{:S(2)}) collective-permute-start(f32[512,256]{1,0:T(8,128)S(1)} %pad_maximum_fusion.1.own), channel_id=1, source_target_pairs={{0,8},{8,16},{16,24},{24,32},{32,40},{40,48},{48,56},{56,64},{64,7... | collective-permute-start | bytes 1572872 | tf_op jit(solution)/shard_map/ppermute | solution.py:230
  11.5 22.0 %collective-permute-start.8 = (f32[512,256]{1,0:T(8,128)S(1)}, f32[512,256]{1,0:T(8,128)}, u32[]{:S(2)}, u32[]{:S(2)}) collective-permute-start(f32[512,256]{1,0:T(8,128)S(1)} %pad_maximum_fusion.1.own), channel_id=1, source_target_pairs={{8,0},{16,8},{24,16},{32,24},{40,32},{48,40},{56,48},{64,56},{72,6... | collective-permute-start | bytes 1572872 | tf_op jit(solution)/shard_map/ppermute | solution.py:231
  14.0 39.8 %collective-permute-start.4 = (f32[512,256]{1,0:T(8,128)S(1)}, f32[512,256]{1,0:T(8,128)}, u32[]{:S(2)}, u32[]{:S(2)}) collective-permute-start(f32[512,256]{1,0:T(8,128)S(1)} %pad_maximum_fusion.own), channel_id=1, source_target_pairs={{0,8},{8,16},{16,24},{24,32},{32,40},{40,48},{48,56},{56,64},{64,7... | collective-permute-start | bytes 1572872 | tf_op jit(solution)/shard_map/ppermute | solution.py:230
  23.1 0.8 copy-start
  23.9 29.9 %collective-permute-start.5 = (f32[512,256]{1,0:T(8,128)S(1)}, f32[512,256]{1,0:T(8,128)}, u32[]{:S(2)}, u32[]{:S(2)}) collective-permute-start(f32[512,256]{1,0:T(8,128)S(1)} %pad_maximum_fusion.own), channel_id=1, source_target_pairs={{8,0},{16,8},{24,16},{32,24},{40,32},{48,40},{56,48},{64,56},{72,6... | collective-permute-start | bytes 1572872 | tf_op jit(solution)/shard_map/ppermute | solution.py:231
  33.5 1.0 %copy-start.1 = (f32[512,256]{1,0:T(8,128)S(1)}, f32[512,256]{1,0:T(8,128)}, u32[]{:S(2)}) copy-start(f32[512,256]{1,0:T(8,128)} %copy-done) | copy-start | bytes 1572868
  37.6 25.5 %collective-permute-start.10 = (f32[512,128]{1,0:T(8,128)S(1)}, f32[512,128]{1,0:T(8,128)S(1)}, u32[]{:S(2)}, u32[]{:S(2)}) collective-permute-start(f32[512,128]{1,0:T(8,128)S(1)} %get-tuple-element.23.refs_2_), channel_id=1, source_target_pairs={{1,0},{2,1},{3,2},{4,3},{5,4},{6,5},{7,6},{9,8},{10,9},{11,10},{12... | collective-permute-start | bytes 786440 | tf_op jit(solution)/shard_map/ppermute | solution.py:237
  46.1 53.6 %collective-permute-start.2 = (f32[512,256]{1,0:T(8,128)}, f32[512,256]{1,0:T(8,128)S(1)}, u32[]{:S(2)}, u32[]{:S(2)}) collective-permute-start(f32[512,256]{1,0:T(8,128)} %get-tuple-element.17.refs_5_), channel_id=1, source_target_pairs={{0,1},{1,2},{2,3},{3,4},{4,5},{5,6},{6,7},{8,9},{9,10},{10,11},{11... | collective-permute-start | bytes 1572872 | tf_op jit(solution)/shard_map/ppermute | solution.py:236
  48.7 17.0 %copy-start.9 = (f32[1,8192]{1,0:T(1,128)S(1)}, f32[1,8192]{1,0:T(1,128)}, u32[]{:S(2)}) copy-start(f32[1,8192]{1,0:T(1,128)} %param.12) | copy-start | bytes 98308
  48.7 17.0 %copy-start.11 = (f32[1,8192]{1,0:T(1,128)S(1)}, f32[1,8192]{1,0:T(1,128)}, u32[]{:S(2)}) copy-start(f32[1,8192]{1,0:T(1,128)} %param.13) | copy-start | bytes 98308
  48.7 51.0 %collective-permute-start.3 = (f32[512,256]{1,0:T(8,128)S(1)}, f32[512,256]{1,0:T(8,128)S(1)}, u32[]{:S(2)}, u32[]{:S(2)}) collective-permute-start(f32[512,256]{1,0:T(8,128)S(1)} %get-tuple-element.18.refs_4_), channel_id=1, source_target_pairs={{1,0},{2,1},{3,2},{4,3},{5,4},{6,5},{7,6},{9,8},{10,9},{11,10},{12... | collective-permute-start | bytes 1572872 | tf_op jit(solution)/shard_map/ppermute | solution.py:237
  56.2 36.3 %collective-permute-start.11 = (f32[512,128]{1,0:T(8,128)S(1)}, f32[512,128]{1,0:T(8,128)S(1)}, u32[]{:S(2)}, u32[]{:S(2)}) collective-permute-start(f32[512,128]{1,0:T(8,128)S(1)} %get-tuple-element.24.refs_3_), channel_id=1, source_target_pairs={{1,0},{2,1},{3,2},{4,3},{5,4},{6,5},{7,6},{9,8},{10,9},{11,10},{12... | collective-permute-start | bytes 786440 | tf_op jit(solution)/shard_map/ppermute | solution.py:237
  58.2 34.3 %collective-permute-start.6 = (f32[512,128]{1,0:T(8,128)S(1)}, f32[512,128]{1,0:T(8,128)S(1)}, u32[]{:S(2)}, u32[]{:S(2)}) collective-permute-start(f32[512,128]{1,0:T(8,128)S(1)} %get-tuple-element.21.refs_6_), channel_id=1, source_target_pairs={{0,1},{1,2},{2,3},{3,4},{4,5},{5,6},{6,7},{8,9},{9,10},{10,11},{11... | collective-permute-start | bytes 786440 | tf_op jit(solution)/shard_map/ppermute | solution.py:236
  63.1 0.7 copy-start.2
  63.8 28.7 %collective-permute-start.9 = (f32[512,128]{1,0:T(8,128)}, f32[512,128]{1,0:T(8,128)S(1)}, u32[]{:S(2)}, u32[]{:S(2)}) collective-permute-start(f32[512,128]{1,0:T(8,128)} %get-tuple-element.22.refs_7_), channel_id=1, source_target_pairs={{0,1},{1,2},{2,3},{3,4},{4,5},{5,6},{6,7},{8,9},{9,10},{10,11},{11... | collective-permute-start | bytes 786440 | tf_op jit(solution)/shard_map/ppermute | solution.py:236
  92.5 1.0 copy-start.3
where the time goes:
time: 103 us; the launch traced here: 102 us
  starting transfers between devices  40.9 us (40%)
  Pallas kernels  29.9 us (29%)
  waiting for transfers between devices  26 us (25%)
  local copies, waits for them, and re-layouts  5.04 us (5%)
    ppermute x3, waiting for transfers between devices, from_cols(): lax.ppermute(left, 'col', backward(col_count))  20 us
    pallas_call x2, Pallas kernels, build_bands(): pl.pallas_call(functools.partial(band_kernel, transposed), out_shape=(ban...  11.3 us
    ppermute x3, starting transfers between devices, from_cols(): lax.ppermute(left, 'col', backward(col_count))  11.2 us
    ppermute x3, starting transfers between devices, from_rows(): lax.ppermute(x, 'row', forward(row_count))  10.9 us
    pallas_call x3, Pallas kernels, apply_rows(): pl.pallas_call(rows_kernel, out_shape=(half, half), in_specs=[VMEM_SPEC]...  9.74 us
    ppermute x3, starting transfers between devices, from_rows(): lax.ppermute(x, 'row', backward(row_count))  9.39 us
    ppermute x3, starting transfers between devices, from_cols(): lax.ppermute(right, 'col', forward(col_count))  9.32 us
    pallas_call x1, Pallas kernels, apply_cols(): pl.pallas_call(cols_kernel, out_shape=jax.ShapeDtypeStruct((rows, width),...  6.25 us
  transfers between devices with their start and end apart: 12, of which 2 were waited for; matrix products, arithmetic and copies ran while one was open for 0% of the time, Pallas kernels for 27%

commit v1 on v0

--- a/solution.py
+++ b/solution.py
@@ -110,37 +110,60 @@
     )(place, *fields)
 
 
-def rows_kernel(north, own, south, band_high, band_low, left, right, high, low):
-    at = 0
-    for ref in (north, own, south):
+def take_kernel(starts, source, *refs):
+    outs, sems = refs[:-1], refs[-1]
+    copies = [
+        pltpu.make_async_copy(source.at[:, pl.ds(at, out.shape[1])], out, sems.at[i])
+        for i, (at, out) in enumerate(zip(starts, outs))
+    ]
+    for copy in copies:
+        copy.start()
+    for copy in copies:
+        copy.wait()
+
+
+def take_columns(source, starts, width):
+    out = pltpu.VMEM((source.shape[0], width), jnp.float32)
+    return pl.pallas_call(
+        functools.partial(take_kernel, starts),
+        out_shape=(out,) * len(starts),
+        in_specs=[pl.BlockSpec(memory_space=pltpu.HBM)],
+        out_specs=(VMEM_SPEC,) * len(starts),
+        scratch_shapes=[pltpu.SemaphoreType.DMA((len(starts),))],
+        compiler_params=pltpu.CompilerParams(vmem_limit_bytes=8 << 20),
+        name="take",
+    )(pltpu.with_memory_space_constraint(source, pltpu.HBM))
+
+
+def rows_kernel(place, chip, own, cross, band_high, band_low, out, high, low):
+    rows = own.shape[0]
+    odd = (place[0] // HALO) & 1
+    to_chip = pl.multiple_of((1 - odd) * 2 * rows, rows)
+    to_cross = pl.multiple_of(odd * 2 * rows, rows)
+    for ref, at in ((own, rows), (chip, to_chip), (cross, to_cross)):
         h, l = split(ref[...])
-        high[at : at + ref.shape[0], :] = h
-        low[at : at + ref.shape[0], :] = l
-        at += ref.shape[0]
-    width = left.shape[1]
-    for pair in range(left.shape[0] // PAIR):
+        high[pl.ds(at, rows), :] = h
+        low[pl.ds(at, rows), :] = l
+    for pair in range(rows // PAIR):
         at = pair * PAIR
-        value = dot3(
+        out[at : at + PAIR, :] = dot3(
             band_high[pair], band_low[pair], high[at : at + SPAN, :], low[at : at + SPAN, :]
         )
-        left[at : at + PAIR, :] = value[:, :width]
-        right[at : at + PAIR, :] = value[:, width:]
-
-
-def apply_rows(north, own, south, bands):
+
+
+def apply_rows(place, chip, own, cross, bands):
     rows, width = own.shape
     ext = pltpu.VMEM((3 * rows, width), jnp.bfloat16)
-    half = pltpu.VMEM((rows, width // 2), jnp.float32)
-    args = [held(a) for a in (north, own, south, *bands)]
+    args = [held(a) for a in (chip, own, cross, *bands)]
     return pl.pallas_call(
         rows_kernel,
-        out_shape=(half, half),
-        in_specs=[VMEM_SPEC] * 5,
-        out_specs=(VMEM_SPEC,) * 2,
+        out_shape=pltpu.VMEM((rows, width), jnp.float32),
+        in_specs=[pl.BlockSpec(memory_space=pltpu.SMEM)] + [VMEM_SPEC] * 5,
+        out_specs=VMEM_SPEC,
         scratch_shapes=[ext, ext],
         compiler_params=pltpu.CompilerParams(vmem_limit_bytes=16 << 20),
         name="rows",
-    )(*args)
+    )(place, *args)
 
 
 def cols_kernel(*refs):
@@ -178,33 +201,23 @@
     )(*args)
 
 
-def tail_kernel(west, east, band_high, band_low, part, out):
-    last = band_high.shape[0] - 1
-
-    def add(ref, pair, rows):
-        h, l = split(ref[...])
-        out[...] = part[...] + dot3(h, l, band_high[pair, rows], band_low[pair, rows])
-
-    @pl.when(pl.program_id(0) == 0)
-    def _():
-        add(west, 0, slice(0, west.shape[1]))
-
-    @pl.when(pl.program_id(0) == 1)
-    def _():
-        add(east, last, slice(SPAN - east.shape[1], SPAN))
-
-
-def apply_tail(west, east, bands, part):
+def tail_kernel(west, band_high, band_low, part, out):
+    h, l = split(west[...])
+    band = slice(0, west.shape[1])
+    out[...] = part[...] + dot3(h, l, band_high[0, band], band_low[0, band])
+
+
+def apply_tail(west, bands, part):
     rows, width = part.shape
-    block = pl.BlockSpec((rows, PAIR), lambda i: (0, i * (width // PAIR - 1)))
-    args = [held(a) for a in (west, east, *bands)]
+    block = pl.BlockSpec((rows, PAIR), lambda i: (0, 0))
+    args = [held(a) for a in (west, *bands)]
     return pl.pallas_call(
         tail_kernel,
-        grid=(2,),
+        grid=(1,),
         out_shape=jax.ShapeDtypeStruct((rows, width), jnp.float32),
-        in_specs=[VMEM_SPEC] * 4 + [block],
+        in_specs=[VMEM_SPEC] * 3 + [block],
         out_specs=block,
-        input_output_aliases={4: 0},
+        input_output_aliases={3: 0},
         compiler_params=pltpu.CompilerParams(vmem_limit_bytes=16 << 20),
         name="tail",
     )(*args, part)
@@ -214,28 +227,16 @@
     covariance, latitude_offset, longitude_offset, upwind, courant,
     longitude_diffusion, latitude_diffusion,
 ):
-    own = covariance[0]
-    rows, width = own.shape
+    block = covariance[0]
+    rows, width = block.shape
     row_count, col_count = lax.axis_size("row"), lax.axis_size("col")
     forward = lambda n: [(i, i + 1) for i in range(n - 1)]
     backward = lambda n: [(i + 1, i) for i in range(n - 1)]
 
-    def columns(first, stop):
-        west = own[:, first * NLON : stop * NLON]
-        east = own[:, width - stop * NLON : width - first * NLON]
-        return jnp.concatenate([west, east], axis=1)
-
     def from_rows(x):
-        return (
-            lax.ppermute(x, "row", forward(row_count)),
-            lax.ppermute(x, "row", backward(row_count)),
-        )
-
-    def from_cols(left, right):
-        return (
-            lax.ppermute(right, "col", forward(col_count)),
-            lax.ppermute(left, "col", backward(col_count)),
-        )
+        chip = [(i, i ^ 1) for i in range(row_count)]
+        cross = [((i + 1 ^ 1) - 1, i) for i in range(1, row_count - 1)]
+        return lax.ppermute(x, "row", chip), lax.ppermute(x, "row", cross)
 
     fields = [
         a.reshape(NLAT, NLON)
@@ -247,26 +248,25 @@
     lat_row = (lax.axis_index("row") * (rows // NLON)).astype(jnp.int32).reshape(1)
     lat_col = (lax.axis_index("col") * (width // NLON)).astype(jnp.int32).reshape(1)
 
-    own0, own1, own2 = columns(0, 1), columns(1, 2), columns(2, 4)
-    north0, south0 = from_rows(own0)
+    starts = (0, width - PAIR, PAIR, width - 2 * PAIR)
+    own = list(take_columns(block, starts[:1], PAIR))
+    near = [from_rows(own[0])]
     row_bands = build_bands(lat_row, fields, rows // PAIR, True)
-    north1, south1 = from_rows(own1)
-    left0, right0 = apply_rows(north0, own0, south0, row_bands)
-    west0, east0 = from_cols(left0, right0)
-    north2, south2 = from_rows(own2)
-    left1, right1 = apply_rows(north1, own1, south1, row_bands)
-    west1, east1 = from_cols(left1, right1)
+    own += take_columns(block, starts[1:], PAIR)
+    near += [from_rows(own[k]) for k in range(1, 4)]
+    half, side = [], []
+    for k in range(4):
+        chip, cross = near[k]
+        half.append(apply_rows(lat_row, chip, own[k], cross, row_bands))
+        pairs = forward(col_count) if k % 2 else backward(col_count)
+        side.append(lax.ppermute(half[k], "col", pairs))
     col_bands = build_bands(lat_col, fields, width // PAIR, False)
-    left2, right2 = apply_rows(north2, own2, south2, row_bands)
-    west2, east2 = from_cols(left2, right2)
-    parts = [west1, west0, left0, left1, left2, right2, right1, right0, east0, east1]
+    parts = [side[1], half[0], half[2], half[3], half[1], side[0], side[2]]
     part = apply_cols(parts, col_bands, width)
-    return apply_tail(west2, east2, col_bands, part)[None]
+    return apply_tail(side[3], col_bands, part)[None]
 
 
 def solution(mesh):
     in_specs = (P(None, "row", "col"), P(), P(), P(), P(), P(), P())
     out_specs = P(None, "row", "col")
-    return jax.shard_map(
-        body, mesh=mesh, in_specs=in_specs, out_specs=out_specs, check_vma=False
-    )
+    return jax.shard_map(body, mesh=mesh, in_specs=in_specs, out_specs=out_specs, check_vma=False)

time: 103 us -> 89.8 us (0.87)
  the two profiles are of different devices: /device:TPU:15 before, /device:TPU:10 now
where the time goes in v1:
time: 89.8 us; the launch traced here: 89.1 us
  Pallas kernels  31.6 us (35%)
  starting transfers between devices  31.4 us (35%)
  waiting for transfers between devices  21.4 us (24%)
  local copies, waits for them, and re-layouts  4.48 us (5%)
    ppermute x4, waiting for transfers between devices, body(): side.append(lax.ppermute(half[k], 'col', pairs))  21.4 us
    ppermute x8, starting transfers between devices, from_rows(): return (lax.ppermute(x, 'row', chip), lax.ppermute(x, 'row', cross))  16.7 us
    ppermute x4, starting transfers between devices, body(): side.append(lax.ppermute(half[k], 'col', pairs))  14.7 us
    pallas_call x2, Pallas kernels, build_bands(): pl.pallas_call(functools.partial(band_kernel, transposed), out_shape=(ban...  11.3 us
    pallas_call x4, Pallas kernels, apply_rows(): pl.pallas_call(rows_kernel, out_shape=pltpu.VMEM((rows, width), jnp.float...  8.99 us
    pallas_call x1, Pallas kernels, apply_cols(): pl.pallas_call(cols_kernel, out_shape=jax.ShapeDtypeStruct((rows, width),...  6.54 us
    unnamed x24, local copies, waits for them, and re-layouts  4.48 us
    pallas_call x2, Pallas kernels, take_columns(): pl.pallas_call(functools.partial(take_kernel, starts), out_shape=(out,) *...  2.5 us
  transfers between devices with their start and end apart: 12, of which 2 were waited for; matrix products, arithmetic and copies ran while one was open for 0% of the time, Pallas kernels for 31%

profile of v1, /device:TPU:10, one launch (start us, length us, event | category | flops | bytes accessed | tf_op | source)
XLA Modules:
  0.0 89.1 jit_solution(16476410815493242665)
XLA Ops:
  0.0 0.0 copy-start.6
  0.0 0.0 copy-start.7
  0.0 0.0 copy-start.8
  0.0 0.0 copy-start.9
  0.0 0.0 copy-start.10
  0.0 0.0 copy-start.11
  0.0 1.4 %take.2 = (f32[512,256]{1,0:T(8,128)S(1)}, f32[512,256]{1,0:T(8,128)S(1)}, f32[512,256]{1,0:T(8,128)S(1)}) custom-call(f32[512,1024]{1,0:T(8,128)} %bitcast.22), custom_call_target="tpu_custom_call" | custom-call | tf_op jit(solution)/shard_map/take/pallas_call | solution.py:127
  1.5 0.1 collective-permute-start.8
  1.6 5.9 %collective-permute-start.9 = (f32[512,256]{1,0:T(8,128)S(1)}, f32[512,256]{1,0:T(8,128)S(1)}, u32[]{:S(2)}, u32[]{:S(2)}) collective-permute-start(f32[512,256]{1,0:T(8,128)S(1)} %get-tuple-element.18.own), channel_id=1, source_target_pairs={{16,8},{8,16},{32,24},{24,32},{48,40},{40,48},{64,56},{56,64},{80,... | collective-permute-start | bytes 1572872 | tf_op jit(solution)/shard_map/ppermute | solution.py:239
  7.5 0.1 collective-permute-start.3
  7.6 2.4 %collective-permute-start.4 = (f32[512,256]{1,0:T(8,128)S(1)}, f32[512,256]{1,0:T(8,128)}, u32[]{:S(2)}, u32[]{:S(2)}) collective-permute-start(f32[512,256]{1,0:T(8,128)S(1)} %get-tuple-element.17.own), channel_id=1, source_target_pairs={{16,8},{8,16},{32,24},{24,32},{48,40},{40,48},{64,56},{56,64},{80,... | collective-permute-start | bytes 1572872 | tf_op jit(solution)/shard_map/ppermute | solution.py:239
  10.0 1.1 %take.3.own = f32[512,256]{1,0:T(8,128)S(1)} custom-call(f32[512,1024]{1,0:T(8,128)} %bitcast.23), custom_call_target="tpu_custom_call" | custom-call | tf_op jit(solution)/shard_map/take/pallas_call | solution.py:127
  11.1 0.1 collective-permute-start.6
  11.2 0.0 collective-permute-done.8.chip
  11.2 0.0 copy-start.2
  11.2 0.8 copy-done.2
  12.0 5.3 %collective-permute-start.7 = (f32[512,256]{1,0:T(8,128)S(1)}, f32[512,256]{1,0:T(8,128)}, u32[]{:S(2)}, u32[]{:S(2)}) collective-permute-start(f32[512,256]{1,0:T(8,128)S(1)} %take.3.own), channel_id=1, source_target_pairs={{16,8},{8,16},{32,24},{24,32},{48,40},{40,48},{64,56},{56,64},{80,... | collective-permute-start | bytes 1572872 | tf_op jit(solution)/shard_map/ppermute | solution.py:239
  17.3 0.0 collective-permute-done.9.cross
  17.3 0.0 copy-start.4
  17.3 0.8 copy-done.4
  18.1 0.0 collective-permute-start
  18.1 0.0 collective-permute-done.3.chip
  18.1 0.0 copy-start
  18.1 0.8 copy-done
  18.9 2.8 %collective-permute-start.1 = (f32[512,256]{1,0:T(8,128)S(1)}, f32[512,256]{1,0:T(8,128)}, u32[]{:S(2)}, u32[]{:S(2)}) collective-permute-start(f32[512,256]{1,0:T(8,128)S(1)} %get-tuple-element.12.own), channel_id=1, source_target_pairs={{16,8},{8,16},{32,24},{24,32},{48,40},{40,48},{64,56},{56,64},{80,... | collective-permute-start | bytes 1572872 | tf_op jit(solution)/shard_map/ppermute | solution.py:239
  21.7 0.0 copy-done.6
  21.7 0.0 copy-done.7
  21.7 0.0 copy-done.8
  21.8 0.0 copy-done.9
  21.8 0.0 copy-done.10
  21.8 0.0 copy-done.11
  21.8 4.6 %row_bands.1 = (bf16[2,256,1280]{2,1,0:T(8,128)(2,1)S(1)}, bf16[2,256,1280]{2,1,0:T(8,128)(2,1)S(1)}) custom-call(s32[1]{0:T(128)} %bitcast.place, s32[64,128]{1,0:T(8,128)S(1)} %bitcast.10, s32[64,128]{1,0:T(8,128)S(1)} %bitcast.12, s32[64,128]{1,0:T(8,128)S(1)} %bitcast.14, f32[64,128]{1,0:T(8,128)S(1)} %bitcast.16, f32[64,128]{1,0:T(8,128)S(1)} %bitcast.18, ...), custom_call_target="tpu_custom_call" | custom-call | tf_op jit(solution)/shard_map/row_bands/pallas_call | solution.py:102
  26.3 0.0 copy-start.3
  26.4 1.0 %copy-done.3 = f32[512,256]{1,0:T(8,128)S(1)} copy-done((f32[512,256]{1,0:T(8,128)S(1)}, f32[512,256]{1,0:T(8,128)}, u32[]{:S(2)}) %copy-start.3) | copy-done | bytes 524312
  27.4 0.0 copy-start.5
  27.4 1.0 %copy-done.5 = f32[512,256]{1,0:T(8,128)S(1)} copy-done((f32[512,256]{1,0:T(8,128)S(1)}, f32[512,256]{1,0:T(8,128)}, u32[]{:S(2)}) %copy-start.5) | copy-done | bytes 524312
  28.4 0.0 copy-start.1
  28.4 1.4 %rows.7.refs_2_ = f32[512,256]{1,0:T(8,128)S(1)} custom-call(s32[1]{0:T(128)} %bitcast.place, f32[512,256]{1,0:T(8,128)S(1)} %copy-done.3, f32[512,256]{1,0:T(8,128)S(1)} %get-tuple-element.18.own, f32[512,256]{1,0:T(8,128)S(1)} %copy-done.5, bf16[2,256,1280]{2,1,0:T(8,128)(2,1)S(1)} %get-tuple-element.13.band_high, ...), custom_call_target="tpu_custom_call" | custom-call | tf_op jit(solution)/shard_map/rows/pallas_call | solution.py:158
  29.9 0.0 collective-permute-done.4.cross
  29.9 4.5 %collective-permute-start.11 = (f32[512,256]{1,0:T(8,128)S(1)}, f32[512,256]{1,0:T(8,128)}, u32[]{:S(2)}, u32[]{:S(2)}) collective-permute-start(f32[512,256]{1,0:T(8,128)S(1)} %rows.7.refs_2_), channel_id=1, source_target_pairs={{1,0},{2,1},{3,2},{4,3},{5,4},{6,5},{7,6},{9,8},{10,9},{11,10},{12... | collective-permute-start | bytes 1572872 | tf_op jit(solution)/shard_map/ppermute | solution.py:262
  34.4 0.0 copy-done.1
  34.4 2.5 %rows.5.refs_4_ = f32[512,256]{1,0:T(8,128)S(1)} custom-call(s32[1]{0:T(128)} %bitcast.place, f32[512,256]{1,0:T(8,128)S(1)} %copy-done.1, f32[512,256]{1,0:T(8,128)S(1)} %get-tuple-element.17.own, f32[512,256]{1,0:T(8,128)} %collective-permute-done.4.cross, bf16[2,256,1280]{2,1,0:T(8,128)(2,1)S(1)} %get-tuple-element.13.band_high, ...), custom_call_target="tpu_custom_call" | custom-call | tf_op jit(solution)/shard_map/rows/pallas_call | solution.py:158
  36.8 0.0 collective-permute-done.6.chip
  36.9 2.9 %collective-permute-start.5 = (f32[512,256]{1,0:T(8,128)S(1)}, f32[512,256]{1,0:T(8,128)}, u32[]{:S(2)}, u32[]{:S(2)}) collective-permute-start(f32[512,256]{1,0:T(8,128)S(1)} %rows.5.refs_4_), channel_id=1, source_target_pairs={{0,1},{1,2},{2,3},{3,4},{4,5},{5,6},{6,7},{8,9},{9,10},{10,11},{11... | collective-permute-start | bytes 1572872 | tf_op jit(solution)/shard_map/ppermute | solution.py:262
  39.7 0.0 collective-permute-done.7.cross
  39.8 2.5 %rows.6.refs_1_ = f32[512,256]{1,0:T(8,128)S(1)} custom-call(s32[1]{0:T(128)} %bitcast.place, f32[512,256]{1,0:T(8,128)S(1)} %collective-permute-done.6.chip, f32[512,256]{1,0:T(8,128)S(1)} %take.3.own, f32[512,256]{1,0:T(8,128)} %collective-permute-done.7.cross, bf16[2,256,1280]{2,1,0:T(8,128)(2,1)S(1)} %get-tuple-element.13.band_high, ...), custom_call_target="tpu_custom_call" | custom-call | tf_op jit(solution)/shard_map/rows/pallas_call | solution.py:158
  42.2 5.4 %collective-permute-start.10 = (f32[512,256]{1,0:T(8,128)S(1)}, f32[512,256]{1,0:T(8,128)S(1)}, u32[]{:S(2)}, u32[]{:S(2)}) collective-permute-start(f32[512,256]{1,0:T(8,128)S(1)} %rows.6.refs_1_), channel_id=1, source_target_pairs={{1,0},{2,1},{3,2},{4,3},{5,4},{6,5},{7,6},{9,8},{10,9},{11,10},{12... | collective-permute-start | bytes 1572872 | tf_op jit(solution)/shard_map/ppermute | solution.py:262
  47.6 0.0 collective-permute-done.chip
  47.6 0.0 collective-permute-done.1.cross
  47.6 2.6 %rows.4.refs_3_ = f32[512,256]{1,0:T(8,128)S(1)} custom-call(s32[1]{0:T(128)} %bitcast.place, f32[512,256]{1,0:T(8,128)} %collective-permute-done.chip, f32[512,256]{1,0:T(8,128)S(1)} %get-tuple-element.12.own, f32[512,256]{1,0:T(8,128)} %collective-permute-done.1.cross, bf16[2,256,1280]{2,1,0:T(8,128)(2,1)S(1)} %get-tuple-element.13.band_high, ...), custom_call_target="tpu_custom_call" | custom-call | tf_op jit(solution)/shard_map/rows/pallas_call | solution.py:158
  50.3 2.0 %collective-permute-start.2 = (f32[512,256]{1,0:T(8,128)S(1)}, f32[512,256]{1,0:T(8,128)S(1)}, u32[]{:S(2)}, u32[]{:S(2)}) collective-permute-start(f32[512,256]{1,0:T(8,128)S(1)} %rows.4.refs_3_), channel_id=1, source_target_pairs={{0,1},{1,2},{2,3},{3,4},{4,5},{5,6},{6,7},{8,9},{9,10},{10,11},{11... | collective-permute-start | bytes 1572872 | tf_op jit(solution)/shard_map/ppermute | solution.py:262
  52.2 6.8 %col_bands.1 = (bf16[4,1280,256]{2,1,0:T(8,128)(2,1)S(1)}, bf16[4,1280,256]{2,1,0:T(8,128)(2,1)S(1)}) custom-call(s32[1]{0:T(128)} %bitcast.8.place, s32[64,128]{1,0:T(8,128)S(1)} %bitcast.11, s32[64,128]{1,0:T(8,128)S(1)} %bitcast.13, s32[64,128]{1,0:T(8,128)S(1)} %bitcast.15, f32[64,128]{1,0:T(8,128)S(1)} %bitcast.17, f32[64,128]{1,0:T(8,128)S(1)} %bitcast.19, ...), custom_call_target="tpu_custom_call" | custom-call | tf_op jit(solution)/shard_map/col_bands/pallas_call | solution.py:102
  59.0 11.6 %collective-permute-done.11.refs_6_ = f32[512,256]{1,0:T(8,128)} collective-permute-done((f32[512,256]{1,0:T(8,128)S(1)}, f32[512,256]{1,0:T(8,128)}, u32[]{:S(2)}, u32[]{:S(2)}) %collective-permute-start.11) | collective-permute-done | bytes 524320 | tf_op jit(solution)/shard_map/ppermute | solution.py:262
  70.7 0.0 collective-permute-done.5.refs_0_
  70.7 9.7 %collective-permute-done.10.refs_5_ = f32[512,256]{1,0:T(8,128)S(1)} collective-permute-done((f32[512,256]{1,0:T(8,128)S(1)}, f32[512,256]{1,0:T(8,128)S(1)}, u32[]{:S(2)}, u32[]{:S(2)}) %collective-permute-start.10) | collective-permute-done | bytes 524320 | tf_op jit(solution)/shard_map/ppermute | solution.py:262
  80.4 6.5 %cols.1.part = f32[512,1024]{1,0:T(8,128)} custom-call(f32[512,256]{1,0:T(8,128)} %collective-permute-done.5.refs_0_, f32[512,256]{1,0:T(8,128)S(1)} %rows.6.refs_1_, f32[512,256]{1,0:T(8,128)S(1)} %rows.7.refs_2_, f32[512,256]{1,0:T(8,128)S(1)} %rows.4.refs_3_, f32[512,256]{1,0:T(8,128)S(1)} %rows.5.refs_4_, ...), custom_call_target="tpu_custom_call" | custom-call | tf_op jit(solution)/shard_map/cols/pallas_call | solution.py:193
  86.9 0.0 collective-permute-done.2.west
  86.9 2.2 %tail.1 = f32[512,1024]{1,0:T(8,128)} custom-call(f32[512,256]{1,0:T(8,128)S(1)} %collective-permute-done.2.west, bf16[4,1280,256]{2,1,0:T(8,128)(2,1)S(1)} %get-tuple-element.15.refs_7_.band_high, bf16[4,1280,256]{2,1,0:T(8,128)(2,1)S(1)} %get-tuple-element.16.refs_8_.band_low, f32[512,1024]{1,0:T(8,128)} %cols.1.part), custom_call_target="tpu_custom_call", output_to_operand_aliasing={{}: (3, {})} | custom-call | tf_op jit(solution)/shard_map/tail/pallas_call | solution.py:214
Async XLA Ops:
  0.0 21.7 %copy-start.6 = (s32[1,1,8192]{2,1,0:T(1,128)S(1)}, s32[1,1,8192]{2,1,0:T(1,128)}, u32[]{:S(2)}) copy-start(s32[1,1,8192]{2,1,0:T(1,128)} %param.8) | copy-start | bytes 98308
  0.0 21.7 %copy-start.7 = (s32[1,1,8192]{2,1,0:T(1,128)S(1)}, s32[1,1,8192]{2,1,0:T(1,128)}, u32[]{:S(2)}) copy-start(s32[1,1,8192]{2,1,0:T(1,128)} %param.9) | copy-start | bytes 98308
  0.0 21.7 %copy-start.8 = (s32[1,1,8192]{2,1,0:T(1,128)S(1)}, s32[1,1,8192]{2,1,0:T(1,128)}, u32[]{:S(2)}) copy-start(s32[1,1,8192]{2,1,0:T(1,128)} %param.10) | copy-start | bytes 98308
  0.0 21.7 %copy-start.9 = (f32[1,1,8192]{2,1,0:T(1,128)S(1)}, f32[1,1,8192]{2,1,0:T(1,128)}, u32[]{:S(2)}) copy-start(f32[1,1,8192]{2,1,0:T(1,128)} %param.11) | copy-start | bytes 98308
  0.0 21.7 %copy-start.10 = (f32[1,8192]{1,0:T(1,128)S(1)}, f32[1,8192]{1,0:T(1,128)}, u32[]{:S(2)}) copy-start(f32[1,8192]{1,0:T(1,128)} %param.12) | copy-start | bytes 98308
  0.0 21.7 %copy-start.11 = (f32[1,8192]{1,0:T(1,128)S(1)}, f32[1,8192]{1,0:T(1,128)}, u32[]{:S(2)}) copy-start(f32[1,8192]{1,0:T(1,128)} %param.13) | copy-start | bytes 98308
  1.5 9.7 %collective-permute-start.8 = (f32[512,256]{1,0:T(8,128)S(1)}, f32[512,256]{1,0:T(8,128)S(1)}, u32[]{:S(2)}, u32[]{:S(2)}) collective-permute-start(f32[512,256]{1,0:T(8,128)S(1)} %get-tuple-element.18.own), channel_id=1, source_target_pairs={{0,8},{8,0},{16,24},{24,16},{32,40},{40,32},{48,56},{56,48},{64,72... | collective-permute-start | bytes 1572872 | tf_op jit(solution)/shard_map/ppermute | solution.py:239
  1.6 15.7 %collective-permute-start.9 = (f32[512,256]{1,0:T(8,128)S(1)}, f32[512,256]{1,0:T(8,128)S(1)}, u32[]{:S(2)}, u32[]{:S(2)}) collective-permute-start(f32[512,256]{1,0:T(8,128)S(1)} %get-tuple-element.18.own), channel_id=1, source_target_pairs={{16,8},{8,16},{32,24},{24,32},{48,40},{40,48},{64,56},{56,64},{80,... | collective-permute-start | bytes 1572872 | tf_op jit(solution)/shard_map/ppermute | solution.py:239
  7.5 10.6 %collective-permute-start.3 = (f32[512,256]{1,0:T(8,128)S(1)}, f32[512,256]{1,0:T(8,128)S(1)}, u32[]{:S(2)}, u32[]{:S(2)}) collective-permute-start(f32[512,256]{1,0:T(8,128)S(1)} %get-tuple-element.17.own), channel_id=1, source_target_pairs={{0,8},{8,0},{16,24},{24,16},{32,40},{40,32},{48,56},{56,48},{64,72... | collective-permute-start | bytes 1572872 | tf_op jit(solution)/shard_map/ppermute | solution.py:239
  7.6 22.3 %collective-permute-start.4 = (f32[512,256]{1,0:T(8,128)S(1)}, f32[512,256]{1,0:T(8,128)}, u32[]{:S(2)}, u32[]{:S(2)}) collective-permute-start(f32[512,256]{1,0:T(8,128)S(1)} %get-tuple-element.17.own), channel_id=1, source_target_pairs={{16,8},{8,16},{32,24},{24,32},{48,40},{40,48},{64,56},{56,64},{80,... | collective-permute-start | bytes 1572872 | tf_op jit(solution)/shard_map/ppermute | solution.py:239
  11.1 25.8 %collective-permute-start.6 = (f32[512,256]{1,0:T(8,128)S(1)}, f32[512,256]{1,0:T(8,128)S(1)}, u32[]{:S(2)}, u32[]{:S(2)}) collective-permute-start(f32[512,256]{1,0:T(8,128)S(1)} %take.3.own), channel_id=1, source_target_pairs={{0,8},{8,0},{16,24},{24,16},{32,40},{40,32},{48,56},{56,48},{64,72... | collective-permute-start | bytes 1572872 | tf_op jit(solution)/shard_map/ppermute | solution.py:239
  11.2 0.8 copy-start.2
  12.0 27.8 %collective-permute-start.7 = (f32[512,256]{1,0:T(8,128)S(1)}, f32[512,256]{1,0:T(8,128)}, u32[]{:S(2)}, u32[]{:S(2)}) collective-permute-start(f32[512,256]{1,0:T(8,128)S(1)} %take.3.own), channel_id=1, source_target_pairs={{16,8},{8,16},{32,24},{24,32},{48,40},{40,48},{64,56},{56,64},{80,... | collective-permute-start | bytes 1572872 | tf_op jit(solution)/shard_map/ppermute | solution.py:239
  17.3 0.8 copy-start.4
  18.1 29.5 %collective-permute-start = (f32[512,256]{1,0:T(8,128)S(1)}, f32[512,256]{1,0:T(8,128)}, u32[]{:S(2)}, u32[]{:S(2)}) collective-permute-start(f32[512,256]{1,0:T(8,128)S(1)} %get-tuple-element.12.own), channel_id=1, source_target_pairs={{0,8},{8,0},{16,24},{24,16},{32,40},{40,32},{48,56},{56,48},{64,72... | collective-permute-start | bytes 1572872 | tf_op jit(solution)/shard_map/ppermute | solution.py:239
  18.1 0.8 copy-start
  18.9 28.8 %collective-permute-start.1 = (f32[512,256]{1,0:T(8,128)S(1)}, f32[512,256]{1,0:T(8,128)}, u32[]{:S(2)}, u32[]{:S(2)}) collective-permute-start(f32[512,256]{1,0:T(8,128)S(1)} %get-tuple-element.12.own), channel_id=1, source_target_pairs={{16,8},{8,16},{32,24},{24,32},{48,40},{40,48},{64,56},{56,64},{80,... | collective-permute-start | bytes 1572872 | tf_op jit(solution)/shard_map/ppermute | solution.py:239
  26.3 1.0 %copy-start.3 = (f32[512,256]{1,0:T(8,128)S(1)}, f32[512,256]{1,0:T(8,128)}, u32[]{:S(2)}) copy-start(f32[512,256]{1,0:T(8,128)} %copy-done.2) | copy-start | bytes 1572868
  27.4 1.0 %copy-start.5 = (f32[512,256]{1,0:T(8,128)S(1)}, f32[512,256]{1,0:T(8,128)}, u32[]{:S(2)}) copy-start(f32[512,256]{1,0:T(8,128)} %copy-done.4) | copy-start | bytes 1572868
  28.4 5.9 %copy-start.1 = (f32[512,256]{1,0:T(8,128)S(1)}, f32[512,256]{1,0:T(8,128)}, u32[]{:S(2)}) copy-start(f32[512,256]{1,0:T(8,128)} %copy-done) | copy-start | bytes 1572868
  29.9 40.8 %collective-permute-start.11 = (f32[512,256]{1,0:T(8,128)S(1)}, f32[512,256]{1,0:T(8,128)}, u32[]{:S(2)}, u32[]{:S(2)}) collective-permute-start(f32[512,256]{1,0:T(8,128)S(1)} %rows.7.refs_2_), channel_id=1, source_target_pairs={{1,0},{2,1},{3,2},{4,3},{5,4},{6,5},{7,6},{9,8},{10,9},{11,10},{12... | collective-permute-start | bytes 1572872 | tf_op jit(solution)/shard_map/ppermute | solution.py:262
  36.9 33.8 %collective-permute-start.5 = (f32[512,256]{1,0:T(8,128)S(1)}, f32[512,256]{1,0:T(8,128)}, u32[]{:S(2)}, u32[]{:S(2)}) collective-permute-start(f32[512,256]{1,0:T(8,128)S(1)} %rows.5.refs_4_), channel_id=1, source_target_pairs={{0,1},{1,2},{2,3},{3,4},{4,5},{5,6},{6,7},{8,9},{9,10},{10,11},{11... | collective-permute-start | bytes 1572872 | tf_op jit(solution)/shard_map/ppermute | solution.py:262
  42.2 38.2 %collective-permute-start.10 = (f32[512,256]{1,0:T(8,128)S(1)}, f32[512,256]{1,0:T(8,128)S(1)}, u32[]{:S(2)}, u32[]{:S(2)}) collective-permute-start(f32[512,256]{1,0:T(8,128)S(1)} %rows.6.refs_1_), channel_id=1, source_target_pairs={{1,0},{2,1},{3,2},{4,3},{5,4},{6,5},{7,6},{9,8},{10,9},{11,10},{12... | collective-permute-start | bytes 1572872 | tf_op jit(solution)/shard_map/ppermute | solution.py:262
  50.3 36.7 %collective-permute-start.2 = (f32[512,256]{1,0:T(8,128)S(1)}, f32[512,256]{1,0:T(8,128)S(1)}, u32[]{:S(2)}, u32[]{:S(2)}) collective-permute-start(f32[512,256]{1,0:T(8,128)S(1)} %rows.4.refs_3_), channel_id=1, source_target_pairs={{0,1},{1,2},{2,3},{3,4},{4,5},{5,6},{6,7},{8,9},{9,10},{10,11},{11... | collective-permute-start | bytes 1572872 | tf_op jit(solution)/shard_map/ppermute | solution.py:262

commit v2 on v1

--- a/solution.py
+++ b/solution.py
@@ -28,7 +28,7 @@
 
 def band_kernel(
     transposed, place, lat_off, lon_off, upwind, courant, lon_diff, lat_diff,
-    high, low, depart_lat, depart_lon, near_lat, near_lon,
+    high, low, depart_lat, depart_lon, near_lat, near_lon, hot,
 ):
     shape = (NLAT, NLON)
     lat = lax.broadcasted_iota(jnp.int32, shape, 0)
@@ -48,45 +48,64 @@
     ) & (NLON - 1)
 
     sub = lax.broadcasted_iota(jnp.int32, (NLON, NLON), 0)
-
-    def advect_block(y, in_lat):
-        row = pl.ds(y, 1)
-        w = courant[row, :]
-        none = jnp.zeros_like(w)
-        keep = jnp.where(depart_lat[row, :] == in_lat, 1.0 - w, none)
-        take = jnp.where(near_lat[row, :] == in_lat, w, none)
-        empty = jnp.zeros((NLON, NLON), jnp.float32)
-        return jnp.where(sub == depart_lon[row, :], keep, empty) + jnp.where(
-            sub == near_lon[row, :], take, empty
-        )
-
-    def model_block(y, in_lat):
+    first = place[0]
+    pairs = high.shape[0]
+
+    def put(pair, half, t, value):
+        if transposed:
+            value = value.T
+        h, l = split(value)
+        cells = pl.ds(t * NLON, NLON)
+        cols = pl.ds(half * NLON, NLON)
+        at = (pair, cols, cells) if transposed else (pair, cells, cols)
+        high[at] = h
+        low[at] = l
+
+    def fill(pair, half):
+        y = first + 2 * pair + half
         lx = lon_diff[pl.ds(y, 1), :]
         ly = lat_diff[pl.ds(y, 1), :]
-        here = advect_block(y, in_lat)
-        north = advect_block(jnp.minimum(y + 1, NLAT - 1), in_lat)
-        south = advect_block(jnp.maximum(y - 1, 0), in_lat)
-        beside = pltpu.roll(here, 1, 1) + pltpu.roll(here, NLON - 1, 1)
-        return here + lx * (beside - 2.0 * here) + ly * (north + south - 2.0 * here)
-
-    first = place[0]
-    for pair in range(high.shape[0]):
-
-        def step(t, carry, pair=pair):
-            for half in range(2):
-                y = first + 2 * pair + half
-                value = model_block(y, first + 2 * pair - HALO + t)
-                if transposed:
-                    value = value.T
-                h, l = split(value)
-                rows = pl.ds(pl.multiple_of(t * NLON, NLON), NLON)
-                cols = pl.ds(half * NLON, NLON)
-                at = (pair, cols, rows) if transposed else (pair, rows, cols)
-                high[at] = h
-                low[at] = l
-            return carry
-
-        lax.fori_loop(0, SPAN // NLON, step, 0)
+        core = 1.0 - 2.0 * lx - 2.0 * ly
+        none = jnp.zeros_like(lx)
+        reach = ((0, 0), (0, 1), (-1, 0))
+        rows = (y, jnp.minimum(y + 1, NLAT - 1), jnp.maximum(y - 1, 0))
+        rows = [pl.ds(r, 1) for r in rows]
+        for k, row in enumerate(rows):
+            on = jnp.ones((NLON, NLON), jnp.float32)
+            off = jnp.zeros((NLON, NLON), jnp.float32)
+            hot[2 * k] = jnp.where(sub == depart_lon[row, :], on, off)
+            hot[2 * k + 1] = jnp.where(sub == near_lon[row, :], on, off)
+        for t in range(2 * HALO + 1):
+            far = t - HALO
+            in_lat = y + far
+            value = None
+            for k, row in enumerate(rows):
+                w = courant[row, :]
+                below, above = reach[k]
+                scale = ly if k else jnp.ones_like(lx)
+                terms = []
+                if -2 + below <= far <= 2 + above:
+                    keep = jnp.where(depart_lat[row, :] == in_lat, scale * (1.0 - w), none)
+                    terms.append(keep * hot[2 * k])
+                if -3 + below <= far <= 3 + above:
+                    take = jnp.where(near_lat[row, :] == in_lat, scale * w, none)
+                    terms.append(take * hot[2 * k + 1])
+                if not terms:
+                    continue
+                total = sum(terms[1:], terms[0])
+                if k == 0:
+                    beside = pltpu.roll(total, 1, 1) + pltpu.roll(total, NLON - 1, 1)
+                    total = core * total + lx * beside
+                value = total if value is None else value + total
+            put(pair, half, t + half, value)
+        put(pair, half, 0 if half else 2 * HALO + 1, jnp.zeros((NLON, NLON), jnp.float32))
+
+    def step(pair, carry):
+        fill(pair, 0)
+        fill(pair, 1)
+        return carry
+
+    lax.fori_loop(0, pairs, step, 0)
 
 
 VMEM_SPEC = pl.BlockSpec(memory_space=pltpu.VMEM)
@@ -104,7 +123,8 @@
         out_shape=(band, band),
         in_specs=[pl.BlockSpec(memory_space=pltpu.SMEM)] + [VMEM_SPEC] * 6,
         out_specs=(VMEM_SPEC,) * 2,
-        scratch_shapes=[pltpu.VMEM((NLAT, NLON), jnp.int32)] * 4,
+        scratch_shapes=[pltpu.VMEM((NLAT, NLON), jnp.int32)] * 4
+        + [pltpu.VMEM((6, NLON, NLON), jnp.float32)],
         compiler_params=pltpu.CompilerParams(vmem_limit_bytes=24 << 20),
         name="row_bands" if transposed else "col_bands",
     )(place, *fields)
@@ -135,13 +155,14 @@
     )(pltpu.with_memory_space_constraint(source, pltpu.HBM))
 
 
-def rows_kernel(place, chip, own, cross, band_high, band_low, out, high, low):
+def rows_kernel(place, chip, own, *refs):
+    *cross, band_high, band_low, out, high, low = refs
     rows = own.shape[0]
     odd = (place[0] // HALO) & 1
     to_chip = pl.multiple_of((1 - odd) * 2 * rows, rows)
     to_cross = pl.multiple_of(odd * 2 * rows, rows)
-    for ref, at in ((own, rows), (chip, to_chip), (cross, to_cross)):
-        h, l = split(ref[...])
+    for parts, at in (((own,), rows), ((chip,), to_chip), (cross, to_cross)):
+        h, l = split(sum((ref[...] for ref in parts[1:]), parts[0][...]))
         high[pl.ds(at, rows), :] = h
         low[pl.ds(at, rows), :] = l
     for pair in range(rows // PAIR):
@@ -154,11 +175,11 @@
 def apply_rows(place, chip, own, cross, bands):
     rows, width = own.shape
     ext = pltpu.VMEM((3 * rows, width), jnp.bfloat16)
-    args = [held(a) for a in (chip, own, cross, *bands)]
+    args = [held(a) for a in (chip, own, *cross, *bands)]
     return pl.pallas_call(
         rows_kernel,
         out_shape=pltpu.VMEM((rows, width), jnp.float32),
-        in_specs=[pl.BlockSpec(memory_space=pltpu.SMEM)] + [VMEM_SPEC] * 5,
+        in_specs=[pl.BlockSpec(memory_space=pltpu.SMEM)] + [VMEM_SPEC] * len(args),
         out_specs=VMEM_SPEC,
         scratch_shapes=[ext, ext],
         compiler_params=pltpu.CompilerParams(vmem_limit_bytes=16 << 20),
@@ -233,10 +254,22 @@
     forward = lambda n: [(i, i + 1) for i in range(n - 1)]
     backward = lambda n: [(i + 1, i) for i in range(n - 1)]
 
-    def from_rows(x):
-        chip = [(i, i ^ 1) for i in range(row_count)]
-        cross = [((i + 1 ^ 1) - 1, i) for i in range(1, row_count - 1)]
-        return lax.ppermute(x, "row", chip), lax.ppermute(x, "row", cross)
+    def shift(x, axis, pairs):
+        return lax.ppermute(x, axis, pairs)
+
+    last = row_count - 1
+    middle = row_count // 2
+    chip_pairs = [(i, i ^ 1) for i in range(row_count)]
+    cross_pairs = [((i + 1 ^ 1) - 1, i) for i in range(1, last)]
+    middle_pairs = [(middle - 1, middle), (middle, middle - 1)]
+
+    def from_rows(k, x):
+        chip = shift(x, "row", chip_pairs)
+        if k < 3:
+            return chip, [shift(x, "row", cross_pairs)]
+        ways = [pair for pair in cross_pairs if pair not in middle_pairs]
+        cross = shift(x, "row", ways + [(middle - 1, 0), (middle, last)])
+        return chip, [cross, shift(cross, "row", [(0, middle), (last, middle - 1)])]
 
     fields = [
         a.reshape(NLAT, NLON)
@@ -249,17 +282,16 @@
     lat_col = (lax.axis_index("col") * (width // NLON)).astype(jnp.int32).reshape(1)
 
     starts = (0, width - PAIR, PAIR, width - 2 * PAIR)
-    own = list(take_columns(block, starts[:1], PAIR))
-    near = [from_rows(own[0])]
+    own = list(take_columns(block, starts[:2], PAIR))
+    own += take_columns(block, starts[2:], PAIR)
+    near = [from_rows(k, own[k]) for k in range(4)]
     row_bands = build_bands(lat_row, fields, rows // PAIR, True)
-    own += take_columns(block, starts[1:], PAIR)
-    near += [from_rows(own[k]) for k in range(1, 4)]
     half, side = [], []
     for k in range(4):
         chip, cross = near[k]
         half.append(apply_rows(lat_row, chip, own[k], cross, row_bands))
         pairs = forward(col_count) if k % 2 else backward(col_count)
-        side.append(lax.ppermute(half[k], "col", pairs))
+        side.append(shift(half[k], "col", pairs))
     col_bands = build_bands(lat_col, fields, width // PAIR, False)
     parts = [side[1], half[0], half[2], half[3], half[1], side[0], side[2]]
     part = apply_cols(parts, col_bands, width)

time: 89.8 us -> 95.9 us (1.068)
  the two profiles are of different devices: /device:TPU:10 before, /device:TPU:6 now
where the time goes in v2:
time: 95.9 us; the launch traced here: 95.3 us
  starting transfers between devices  40.7 us (42%)
  Pallas kernels  26.4 us (28%)
  waiting for transfers between devices  24.2 us (25%)
  local copies, waits for them, and re-layouts  3.7 us (4%)
    ppermute x13, starting transfers between devices, shift(): return lax.ppermute(x, axis, pairs)  40.7 us
    ppermute x13, waiting for transfers between devices, shift(): return lax.ppermute(x, axis, pairs)  24.2 us
    pallas_call x4, Pallas kernels, apply_rows(): pl.pallas_call(rows_kernel, out_shape=pltpu.VMEM((rows, width), jnp.float...  9.35 us
    pallas_call x1, Pallas kernels, apply_cols(): pl.pallas_call(cols_kernel, out_shape=jax.ShapeDtypeStruct((rows, width),...  6.54 us
    pallas_call x2, Pallas kernels, build_bands(): pl.pallas_call(functools.partial(band_kernel, transposed), out_shape=(ban...  5.03 us
    unnamed x20, local copies, waits for them, and re-layouts  3.7 us
    pallas_call x2, Pallas kernels, take_columns(): pl.pallas_call(functools.partial(take_kernel, starts), out_shape=(out,) *...  3.29 us
    pallas_call x1, Pallas kernels, apply_tail(): pl.pallas_call(tail_kernel, grid=(1,), out_shape=jax.ShapeDtypeStruct((ro...  2.22 us
  transfers between devices with their start and end apart: 13, of which 3 were waited for; matrix products, arithmetic and copies ran while one was open for 0% of the time, Pallas kernels for 23%

profile of v2, /device:TPU:6, one launch (start us, length us, event | category | flops | bytes accessed | tf_op | source)
XLA Modules:
  0.0 95.3 jit_solution(3066630538423912277)
XLA Ops:
  0.0 0.0 copy-start.4
  0.0 0.0 copy-start.5
  0.0 0.0 copy-start.6
  0.0 0.0 copy-start.7
  0.0 0.0 copy-start.8
  0.0 0.0 copy-start.9
  0.0 2.1 %take.2 = (f32[512,256]{1,0:T(8,128)S(1)}, f32[512,256]{1,0:T(8,128)}) custom-call(f32[512,1024]{1,0:T(8,128)} %bitcast.22), custom_call_target="tpu_custom_call" | custom-call | tf_op jit(solution)/shard_map/take/pallas_call | solution.py:147
  2.1 1.3 %collective-permute-start.1 = (f32[512,256]{1,0:T(8,128)}, f32[512,256]{1,0:T(8,128)}, u32[]{:S(2)}, u32[]{:S(2)}) collective-permute-start(f32[512,256]{1,0:T(8,128)} %get-tuple-element.13.own), channel_id=1, source_target_pairs={{16,8},{8,16},{32,24},{24,32},{48,40},{40,48},{80,72},{72,80},{96,... | collective-permute-start | bytes 1572872 | tf_op jit(solution)/shard_map/ppermute | solution.py:258
  3.4 1.2 %take.3 = (f32[512,256]{1,0:T(8,128)S(1)}, f32[512,256]{1,0:T(8,128)S(1)}) custom-call(f32[512,1024]{1,0:T(8,128)} %bitcast.23), custom_call_target="tpu_custom_call" | custom-call | tf_op jit(solution)/shard_map/take/pallas_call | solution.py:147
  4.6 2.7 %collective-permute-start.7 = (f32[512,256]{1,0:T(8,128)S(1)}, f32[512,256]{1,0:T(8,128)S(1)}, u32[]{:S(2)}, u32[]{:S(2)}) collective-permute-start(f32[512,256]{1,0:T(8,128)S(1)} %get-tuple-element.19.own), channel_id=1, source_target_pairs={{0,8},{8,0},{16,24},{24,16},{32,40},{40,32},{48,56},{56,48},{64,72... | collective-permute-start | bytes 1572872 | tf_op jit(solution)/shard_map/ppermute | solution.py:258
  7.4 0.7 collective-permute-start.8
  8.1 0.7 collective-permute-start.10
  8.8 4.6 %collective-permute-start.9 = (f32[512,256]{1,0:T(8,128)S(1)}, f32[512,256]{1,0:T(8,128)}, u32[]{:S(2)}, u32[]{:S(2)}) collective-permute-start(f32[512,256]{1,0:T(8,128)S(1)} %get-tuple-element.20.own), channel_id=1, source_target_pairs={{0,8},{8,0},{16,24},{24,16},{32,40},{40,32},{48,56},{56,48},{64,72... | collective-permute-start | bytes 1572872 | tf_op jit(solution)/shard_map/ppermute | solution.py:258
  13.3 0.8 collective-permute-done.1.refs_0_
  14.1 0.0 collective-permute-start.4
  14.1 0.0 collective-permute-done.7.chip
  14.1 0.0 copy-start
  14.2 0.8 copy-done
  14.9 1.5 %collective-permute-start.5 = (f32[512,256]{1,0:T(8,128)S(1)}, f32[512,256]{1,0:T(8,128)}, u32[]{:S(2)}, u32[]{:S(2)}) collective-permute-start(f32[512,256]{1,0:T(8,128)S(1)} %get-tuple-element.18.own), channel_id=1, source_target_pairs={{16,8},{8,16},{32,24},{24,32},{48,40},{40,48},{64,56},{56,64},{80,... | collective-permute-start | bytes 1572872 | tf_op jit(solution)/shard_map/ppermute | solution.py:258
  16.4 0.0 collective-permute-done.8.refs_0_
  16.4 0.0 copy-start.2
  16.4 0.8 copy-done.2
  17.2 2.3 %collective-permute-start = (f32[512,256]{1,0:T(8,128)}, f32[512,256]{1,0:T(8,128)}, u32[]{:S(2)}, u32[]{:S(2)}) collective-permute-start(f32[512,256]{1,0:T(8,128)} %get-tuple-element.13.own), channel_id=1, source_target_pairs={{0,8},{8,0},{16,24},{24,16},{32,40},{40,32},{48,56},{56,48},{64,72... | collective-permute-start | bytes 1572872 | tf_op jit(solution)/shard_map/ppermute | solution.py:258
  19.5 0.0 collective-permute-done.10.refs_0_
  19.5 12.6 %collective-permute-start.2 = (f32[512,256]{1,0:T(8,128)}, f32[512,256]{1,0:T(8,128)}, u32[]{:S(2)}, u32[]{:S(2)}) collective-permute-start(f32[512,256]{1,0:T(8,128)} %collective-permute-done.1.refs_0_), channel_id=1, source_target_pairs={{0,64},{120,56},{1,65},{121,57},{2,66},{122,58},{3,67},{123,59},{4... | collective-permute-start | bytes 1572872 | tf_op jit(solution)/shard_map/ppermute | solution.py:258
  32.2 0.0 copy-done.4
  32.2 0.0 copy-done.5
  32.2 0.0 copy-done.6
  32.2 0.0 copy-done.7
  32.2 0.0 copy-done.8
  32.2 0.0 copy-done.9
  32.2 1.9 %row_bands.1 = (bf16[2,256,1280]{2,1,0:T(8,128)(2,1)S(1)}, bf16[2,256,1280]{2,1,0:T(8,128)(2,1)S(1)}) custom-call(s32[1]{0:T(128)} %bitcast.place, s32[64,128]{1,0:T(8,128)S(1)} %bitcast.10, s32[64,128]{1,0:T(8,128)S(1)} %bitcast.12, s32[64,128]{1,0:T(8,128)S(1)} %bitcast.14, f32[64,128]{1,0:T(8,128)S(1)} %bitcast.16, f32[64,128]{1,0:T(8,128)S(1)} %bitcast.18, ...), custom_call_target="tpu_custom_call" | custom-call | tf_op jit(solution)/shard_map/row_bands/pallas_call | solution.py:121
  34.1 0.0 copy-start.1
  34.1 1.0 %copy-done.1 = f32[512,256]{1,0:T(8,128)S(1)} copy-done((f32[512,256]{1,0:T(8,128)S(1)}, f32[512,256]{1,0:T(8,128)}, u32[]{:S(2)}) %copy-start.1) | copy-done | bytes 524312
  35.2 0.0 copy-start.3
  35.2 1.0 %copy-done.3 = f32[512,256]{1,0:T(8,128)S(1)} copy-done((f32[512,256]{1,0:T(8,128)S(1)}, f32[512,256]{1,0:T(8,128)}, u32[]{:S(2)}) %copy-start.3) | copy-done | bytes 524312
  36.2 1.4 %rows.6.refs_1_ = f32[512,256]{1,0:T(8,128)S(1)} custom-call(s32[1]{0:T(128)} %bitcast.place, f32[512,256]{1,0:T(8,128)S(1)} %copy-done.1, f32[512,256]{1,0:T(8,128)S(1)} %get-tuple-element.19.own, f32[512,256]{1,0:T(8,128)S(1)} %copy-done.3, bf16[2,256,1280]{2,1,0:T(8,128)(2,1)S(1)} %get-tuple-element.14.refs_2_.refs_1_, ...), custom_call_target="tpu_custom_call" | custom-call | tf_op jit(solution)/shard_map/rows/pallas_call | solution.py:179
  37.6 0.0 collective-permute-done.9.chip
  37.7 5.1 %collective-permute-start.11 = (f32[512,256]{1,0:T(8,128)S(1)}, f32[512,256]{1,0:T(8,128)}, u32[]{:S(2)}, u32[]{:S(2)}) collective-permute-start(f32[512,256]{1,0:T(8,128)S(1)} %rows.6.refs_1_), channel_id=1, source_target_pairs={{1,0},{2,1},{3,2},{4,3},{5,4},{6,5},{7,6},{9,8},{10,9},{11,10},{12... | collective-permute-start | bytes 1572872 | tf_op jit(solution)/shard_map/ppermute | solution.py:258
  42.7 2.5 %rows.7.refs_2_ = f32[512,256]{1,0:T(8,128)S(1)} custom-call(s32[1]{0:T(128)} %bitcast.place, f32[512,256]{1,0:T(8,128)} %collective-permute-done.9.chip, f32[512,256]{1,0:T(8,128)S(1)} %get-tuple-element.20.own, f32[512,256]{1,0:T(8,128)S(1)} %collective-permute-done.10.refs_0_, bf16[2,256,1280]{2,1,0:T(8,128)(2,1)S(1)} %get-tuple-element.14.refs_2_.refs_1_, ...), custom_call_target="tpu_custom_call" | custom-call | tf_op jit(solution)/shard_map/rows/pallas_call | solution.py:179
  45.2 0.0 collective-permute-done.4.chip
  45.2 2.5 %collective-permute-start.12 = (f32[512,256]{1,0:T(8,128)S(1)}, f32[512,256]{1,0:T(8,128)S(1)}, u32[]{:S(2)}, u32[]{:S(2)}) collective-permute-start(f32[512,256]{1,0:T(8,128)S(1)} %rows.7.refs_2_), channel_id=1, source_target_pairs={{1,0},{2,1},{3,2},{4,3},{5,4},{6,5},{7,6},{9,8},{10,9},{11,10},{12... | collective-permute-start | bytes 1572872 | tf_op jit(solution)/shard_map/ppermute | solution.py:258
  47.8 0.0 collective-permute-done.5.refs_0_
  47.8 2.5 %rows.5.refs_4_ = f32[512,256]{1,0:T(8,128)S(1)} custom-call(s32[1]{0:T(128)} %bitcast.place, f32[512,256]{1,0:T(8,128)S(1)} %collective-permute-done.4.chip, f32[512,256]{1,0:T(8,128)S(1)} %get-tuple-element.18.own, f32[512,256]{1,0:T(8,128)} %collective-permute-done.5.refs_0_, bf16[2,256,1280]{2,1,0:T(8,128)(2,1)S(1)} %get-tuple-element.14.refs_2_.refs_1_, ...), custom_call_target="tpu_custom_call" | custom-call | tf_op jit(solution)/shard_map/rows/pallas_call | solution.py:179
  50.3 4.8 %collective-permute-start.6 = (f32[512,256]{1,0:T(8,128)S(1)}, f32[512,256]{1,0:T(8,128)}, u32[]{:S(2)}, u32[]{:S(2)}) collective-permute-start(f32[512,256]{1,0:T(8,128)S(1)} %rows.5.refs_4_), channel_id=1, source_target_pairs={{0,1},{1,2},{2,3},{3,4},{4,5},{5,6},{6,7},{8,9},{9,10},{10,11},{11... | collective-permute-start | bytes 1572872 | tf_op jit(solution)/shard_map/ppermute | solution.py:258
  55.1 0.0 collective-permute-done.chip
  55.1 0.0 collective-permute-done.2.refs_1_
  55.1 3.0 %rows.4.refs_3_ = f32[512,256]{1,0:T(8,128)S(1)} custom-call(s32[1]{0:T(128)} %bitcast.place, f32[512,256]{1,0:T(8,128)} %collective-permute-done.chip, f32[512,256]{1,0:T(8,128)} %get-tuple-element.13.own, f32[512,256]{1,0:T(8,128)} %collective-permute-done.1.refs_0_, f32[512,256]{1,0:T(8,128)} %collective-permute-done.2.refs_1_, ...), custom_call_target="tpu_custom_call" | custom-call | tf_op jit(solution)/shard_map/rows/pallas_call | solution.py:179
  58.1 1.9 %collective-permute-start.3 = (f32[512,256]{1,0:T(8,128)S(1)}, f32[512,256]{1,0:T(8,128)S(1)}, u32[]{:S(2)}, u32[]{:S(2)}) collective-permute-start(f32[512,256]{1,0:T(8,128)S(1)} %rows.4.refs_3_), channel_id=1, source_target_pairs={{0,1},{1,2},{2,3},{3,4},{4,5},{5,6},{6,7},{8,9},{9,10},{10,11},{11... | collective-permute-start | bytes 1572872 | tf_op jit(solution)/shard_map/ppermute | solution.py:258
  60.0 3.1 %col_bands.1 = (bf16[4,1280,256]{2,1,0:T(8,128)(2,1)S(1)}, bf16[4,1280,256]{2,1,0:T(8,128)(2,1)S(1)}) custom-call(s32[1]{0:T(128)} %bitcast.8.place, s32[64,128]{1,0:T(8,128)S(1)} %bitcast.11, s32[64,128]{1,0:T(8,128)S(1)} %bitcast.13, s32[64,128]{1,0:T(8,128)S(1)} %bitcast.15, f32[64,128]{1,0:T(8,128)S(1)} %bitcast.17, f32[64,128]{1,0:T(8,128)S(1)} %bitcast.19, ...), custom_call_target="tpu_custom_call" | custom-call | tf_op jit(solution)/shard_map/col_bands/pallas_call | solution.py:121
  63.1 16.5 %collective-permute-done.11.refs_5_ = f32[512,256]{1,0:T(8,128)} collective-permute-done((f32[512,256]{1,0:T(8,128)S(1)}, f32[512,256]{1,0:T(8,128)}, u32[]{:S(2)}, u32[]{:S(2)}) %collective-permute-start.11) | collective-permute-done | bytes 524320 | tf_op jit(solution)/shard_map/ppermute | solution.py:258
  79.6 6.9 %collective-permute-done.12.refs_6_ = f32[512,256]{1,0:T(8,128)S(1)} collective-permute-done((f32[512,256]{1,0:T(8,128)S(1)}, f32[512,256]{1,0:T(8,128)S(1)}, u32[]{:S(2)}, u32[]{:S(2)}) %collective-permute-start.12) | collective-permute-done | bytes 524320 | tf_op jit(solution)/shard_map/ppermute | solution.py:258
  86.5 0.0 collective-permute-done.6.refs_0_
  86.5 6.5 %cols.1.part = f32[512,1024]{1,0:T(8,128)} custom-call(f32[512,256]{1,0:T(8,128)} %collective-permute-done.6.refs_0_, f32[512,256]{1,0:T(8,128)S(1)} %rows.6.refs_1_, f32[512,256]{1,0:T(8,128)S(1)} %rows.7.refs_2_, f32[512,256]{1,0:T(8,128)S(1)} %rows.4.refs_3_, f32[512,256]{1,0:T(8,128)S(1)} %rows.5.refs_4_, f32[512,256]{1,0:T(8,128)} %collective-permute-done.11.refs_5_, ...), custom_call_target="tpu_custom_call" | custom-call | tf_op jit(solution)/shard_map/cols/pallas_call | solution.py:214
  93.1 0.0 collective-permute-done.3.west
  93.1 2.2 %tail.1 = f32[512,1024]{1,0:T(8,128)} custom-call(f32[512,256]{1,0:T(8,128)S(1)} %collective-permute-done.3.west, bf16[4,1280,256]{2,1,0:T(8,128)(2,1)S(1)} %get-tuple-element.16.refs_7_.band_high, bf16[4,1280,256]{2,1,0:T(8,128)(2,1)S(1)} %get-tuple-element.17.refs_8_.band_low, f32[512,1024]{1,0:T(8,128)} %cols.1.part), custom_call_target="tpu_custom_call", output_to_operand_aliasing={{}: (3, {})} | custom-call | tf_op jit(solution)/shard_map/tail/pallas_call | solution.py:235
Async XLA Ops:
  0.0 32.2 %copy-start.4 = (s32[1,1,8192]{2,1,0:T(1,128)S(1)}, s32[1,1,8192]{2,1,0:T(1,128)}, u32[]{:S(2)}) copy-start(s32[1,1,8192]{2,1,0:T(1,128)} %param.8) | copy-start | bytes 98308
  0.0 32.2 %copy-start.5 = (s32[1,1,8192]{2,1,0:T(1,128)S(1)}, s32[1,1,8192]{2,1,0:T(1,128)}, u32[]{:S(2)}) copy-start(s32[1,1,8192]{2,1,0:T(1,128)} %param.9) | copy-start | bytes 98308
  0.0 32.2 %copy-start.6 = (s32[1,1,8192]{2,1,0:T(1,128)S(1)}, s32[1,1,8192]{2,1,0:T(1,128)}, u32[]{:S(2)}) copy-start(s32[1,1,8192]{2,1,0:T(1,128)} %param.10) | copy-start | bytes 98308
  0.0 32.2 %copy-start.7 = (f32[1,1,8192]{2,1,0:T(1,128)S(1)}, f32[1,1,8192]{2,1,0:T(1,128)}, u32[]{:S(2)}) copy-start(f32[1,1,8192]{2,1,0:T(1,128)} %param.11) | copy-start | bytes 98308
  0.0 32.1 %copy-start.8 = (f32[1,8192]{1,0:T(1,128)S(1)}, f32[1,8192]{1,0:T(1,128)}, u32[]{:S(2)}) copy-start(f32[1,8192]{1,0:T(1,128)} %param.12) | copy-start | bytes 98308
  0.0 32.1 %copy-start.9 = (f32[1,8192]{1,0:T(1,128)S(1)}, f32[1,8192]{1,0:T(1,128)}, u32[]{:S(2)}) copy-start(f32[1,8192]{1,0:T(1,128)} %param.13) | copy-start | bytes 98308
  2.1 12.0 %collective-permute-start.1 = (f32[512,256]{1,0:T(8,128)}, f32[512,256]{1,0:T(8,128)}, u32[]{:S(2)}, u32[]{:S(2)}) collective-permute-start(f32[512,256]{1,0:T(8,128)} %get-tuple-element.13.own), channel_id=1, source_target_pairs={{16,8},{8,16},{32,24},{24,32},{48,40},{40,48},{80,72},{72,80},{96,... | collective-permute-start | bytes 1572872 | tf_op jit(solution)/shard_map/ppermute | solution.py:258
  4.6 9.5 %collective-permute-start.7 = (f32[512,256]{1,0:T(8,128)S(1)}, f32[512,256]{1,0:T(8,128)S(1)}, u32[]{:S(2)}, u32[]{:S(2)}) collective-permute-start(f32[512,256]{1,0:T(8,128)S(1)} %get-tuple-element.19.own), channel_id=1, source_target_pairs={{0,8},{8,0},{16,24},{24,16},{32,40},{40,32},{48,56},{56,48},{64,72... | collective-permute-start | bytes 1572872 | tf_op jit(solution)/shard_map/ppermute | solution.py:258
  7.4 9.0 %collective-permute-start.8 = (f32[512,256]{1,0:T(8,128)S(1)}, f32[512,256]{1,0:T(8,128)S(1)}, u32[]{:S(2)}, u32[]{:S(2)}) collective-permute-start(f32[512,256]{1,0:T(8,128)S(1)} %get-tuple-element.19.own), channel_id=1, source_target_pairs={{16,8},{8,16},{32,24},{24,32},{48,40},{40,48},{64,56},{56,64},{80,... | collective-permute-start | bytes 1572872 | tf_op jit(solution)/shard_map/ppermute | solution.py:258
  8.1 11.5 %collective-permute-start.10 = (f32[512,256]{1,0:T(8,128)S(1)}, f32[512,256]{1,0:T(8,128)S(1)}, u32[]{:S(2)}, u32[]{:S(2)}) collective-permute-start(f32[512,256]{1,0:T(8,128)S(1)} %get-tuple-element.20.own), channel_id=1, source_target_pairs={{16,8},{8,16},{32,24},{24,32},{48,40},{40,48},{64,56},{56,64},{80,... | collective-permute-start | bytes 1572872 | tf_op jit(solution)/shard_map/ppermute | solution.py:258
  8.8 28.9 %collective-permute-start.9 = (f32[512,256]{1,0:T(8,128)S(1)}, f32[512,256]{1,0:T(8,128)}, u32[]{:S(2)}, u32[]{:S(2)}) collective-permute-start(f32[512,256]{1,0:T(8,128)S(1)} %get-tuple-element.20.own), channel_id=1, source_target_pairs={{0,8},{8,0},{16,24},{24,16},{32,40},{40,32},{48,56},{56,48},{64,72... | collective-permute-start | bytes 1572872 | tf_op jit(solution)/shard_map/ppermute | solution.py:258
  14.1 31.1 %collective-permute-start.4 = (f32[512,256]{1,0:T(8,128)S(1)}, f32[512,256]{1,0:T(8,128)S(1)}, u32[]{:S(2)}, u32[]{:S(2)}) collective-permute-start(f32[512,256]{1,0:T(8,128)S(1)} %get-tuple-element.18.own), channel_id=1, source_target_pairs={{0,8},{8,0},{16,24},{24,16},{32,40},{40,32},{48,56},{56,48},{64,72... | collective-permute-start | bytes 1572872 | tf_op jit(solution)/shard_map/ppermute | solution.py:258
  14.1 0.8 copy-start
  14.9 32.8 %collective-permute-start.5 = (f32[512,256]{1,0:T(8,128)S(1)}, f32[512,256]{1,0:T(8,128)}, u32[]{:S(2)}, u32[]{:S(2)}) collective-permute-start(f32[512,256]{1,0:T(8,128)S(1)} %get-tuple-element.18.own), channel_id=1, source_target_pairs={{16,8},{8,16},{32,24},{24,32},{48,40},{40,48},{64,56},{56,64},{80,... | collective-permute-start | bytes 1572872 | tf_op jit(solution)/shard_map/ppermute | solution.py:258
  16.4 0.8 copy-start.2
  17.2 37.9 %collective-permute-start = (f32[512,256]{1,0:T(8,128)}, f32[512,256]{1,0:T(8,128)}, u32[]{:S(2)}, u32[]{:S(2)}) collective-permute-start(f32[512,256]{1,0:T(8,128)} %get-tuple-element.13.own), channel_id=1, source_target_pairs={{0,8},{8,0},{16,24},{24,16},{32,40},{40,32},{48,56},{56,48},{64,72... | collective-permute-start | bytes 1572872 | tf_op jit(solution)/shard_map/ppermute | solution.py:258
  19.5 35.6 %collective-permute-start.2 = (f32[512,256]{1,0:T(8,128)}, f32[512,256]{1,0:T(8,128)}, u32[]{:S(2)}, u32[]{:S(2)}) collective-permute-start(f32[512,256]{1,0:T(8,128)} %collective-permute-done.1.refs_0_), channel_id=1, source_target_pairs={{0,64},{120,56},{1,65},{121,57},{2,66},{122,58},{3,67},{123,59},{4... | collective-permute-start | bytes 1572872 | tf_op jit(solution)/shard_map/ppermute | solution.py:258
  34.1 1.0 %copy-start.1 = (f32[512,256]{1,0:T(8,128)S(1)}, f32[512,256]{1,0:T(8,128)}, u32[]{:S(2)}) copy-start(f32[512,256]{1,0:T(8,128)} %copy-done) | copy-start | bytes 1572868
  35.2 1.0 %copy-start.3 = (f32[512,256]{1,0:T(8,128)S(1)}, f32[512,256]{1,0:T(8,128)}, u32[]{:S(2)}) copy-start(f32[512,256]{1,0:T(8,128)} %copy-done.2) | copy-start | bytes 1572868
  37.7 42.0 %collective-permute-start.11 = (f32[512,256]{1,0:T(8,128)S(1)}, f32[512,256]{1,0:T(8,128)}, u32[]{:S(2)}, u32[]{:S(2)}) collective-permute-start(f32[512,256]{1,0:T(8,128)S(1)} %rows.6.refs_1_), channel_id=1, source_target_pairs={{1,0},{2,1},{3,2},{4,3},{5,4},{6,5},{7,6},{9,8},{10,9},{11,10},{12... | collective-permute-start | bytes 1572872 | tf_op jit(solution)/shard_map/ppermute | solution.py:258
  45.2 41.3 %collective-permute-start.12 = (f32[512,256]{1,0:T(8,128)S(1)}, f32[512,256]{1,0:T(8,128)S(1)}, u32[]{:S(2)}, u32[]{:S(2)}) collective-permute-start(f32[512,256]{1,0:T(8,128)S(1)} %rows.7.refs_2_), channel_id=1, source_target_pairs={{1,0},{2,1},{3,2},{4,3},{5,4},{6,5},{7,6},{9,8},{10,9},{11,10},{12... | collective-permute-start | bytes 1572872 | tf_op jit(solution)/shard_map/ppermute | solution.py:258
  50.3 36.3 %collective-permute-start.6 = (f32[512,256]{1,0:T(8,128)S(1)}, f32[512,256]{1,0:T(8,128)}, u32[]{:S(2)}, u32[]{:S(2)}) collective-permute-start(f32[512,256]{1,0:T(8,128)S(1)} %rows.5.refs_4_), channel_id=1, source_target_pairs={{0,1},{1,2},{2,3},{3,4},{4,5},{5,6},{6,7},{8,9},{9,10},{10,11},{11... | collective-permute-start | bytes 1572872 | tf_op jit(solution)/shard_map/ppermute | solution.py:258
  58.1 35.0 %collective-permute-start.3 = (f32[512,256]{1,0:T(8,128)S(1)}, f32[512,256]{1,0:T(8,128)S(1)}, u32[]{:S(2)}, u32[]{:S(2)}) collective-permute-start(f32[512,256]{1,0:T(8,128)S(1)} %rows.4.refs_3_), channel_id=1, source_target_pairs={{0,1},{1,2},{2,3},{3,4},{4,5},{5,6},{6,7},{8,9},{9,10},{10,11},{11... | collective-permute-start | bytes 1572872 | tf_op jit(solution)/shard_map/ppermute | solution.py:258

commit v3 on v2

--- a/solution.py
+++ b/solution.py
@@ -143,28 +143,45 @@
 
 
 def take_columns(source, starts, width):
-    out = pltpu.VMEM((source.shape[0], width), jnp.float32)
+    hbm = pl.BlockSpec(memory_space=pltpu.HBM)
+    out = jax.ShapeDtypeStruct((source.shape[0], width), jnp.float32)
     return pl.pallas_call(
         functools.partial(take_kernel, starts),
         out_shape=(out,) * len(starts),
-        in_specs=[pl.BlockSpec(memory_space=pltpu.HBM)],
-        out_specs=(VMEM_SPEC,) * len(starts),
+        in_specs=[hbm],
+        out_specs=(hbm,) * len(starts),
         scratch_shapes=[pltpu.SemaphoreType.DMA((len(starts),))],
         compiler_params=pltpu.CompilerParams(vmem_limit_bytes=8 << 20),
         name="take",
-    )(pltpu.with_memory_space_constraint(source, pltpu.HBM))
-
-
-def rows_kernel(place, chip, own, *refs):
-    *cross, band_high, band_low, out, high, low = refs
-    rows = own.shape[0]
+    )(in_hbm(source))
+
+
+def rows_kernel(start, place, own, chip, *refs):
+    *cross, band_high, band_low, out, high, low, landed, sems = refs
+    rows, width = out.shape
+    sources = [ref.at[:, pl.ds(start, width)] for ref in (own, chip)] + list(cross)
+    copies = [
+        pltpu.make_async_copy(source, landed.at[i], sems.at[i])
+        for i, source in enumerate(sources)
+    ]
+    for copy in copies:
+        copy.start()
     odd = (place[0] // HALO) & 1
     to_chip = pl.multiple_of((1 - odd) * 2 * rows, rows)
     to_cross = pl.multiple_of(odd * 2 * rows, rows)
-    for parts, at in (((own,), rows), ((chip,), to_chip), (cross, to_cross)):
-        h, l = split(sum((ref[...] for ref in parts[1:]), parts[0][...]))
+
+    def put(value, at):
+        h, l = split(value)
         high[pl.ds(at, rows), :] = h
         low[pl.ds(at, rows), :] = l
+
+    copies[0].wait()
+    put(landed[0], rows)
+    copies[1].wait()
+    put(landed[1], to_chip)
+    for copy in copies[2:]:
+        copy.wait()
+    put(sum((landed[i] for i in range(3, len(copies))), landed[2]), to_cross)
     for pair in range(rows // PAIR):
         at = pair * PAIR
         out[at : at + PAIR, :] = dot3(
@@ -172,19 +189,26 @@
         )
 
 
-def apply_rows(place, chip, own, cross, bands):
-    rows, width = own.shape
+def in_hbm(x):
+    return pltpu.with_memory_space_constraint(x, pltpu.HBM)
+
+
+def apply_rows(place, start, own, chip, cross, bands):
+    rows, width = cross[0].shape
     ext = pltpu.VMEM((3 * rows, width), jnp.bfloat16)
-    args = [held(a) for a in (chip, own, *cross, *bands)]
-    return pl.pallas_call(
-        rows_kernel,
+    hbm = [in_hbm(a) for a in (own, chip, *cross)]
+    landed = pltpu.VMEM((len(hbm), rows, width), jnp.float32)
+    return pl.pallas_call(
+        functools.partial(rows_kernel, start),
         out_shape=pltpu.VMEM((rows, width), jnp.float32),
-        in_specs=[pl.BlockSpec(memory_space=pltpu.SMEM)] + [VMEM_SPEC] * len(args),
+        in_specs=[pl.BlockSpec(memory_space=pltpu.SMEM)]
+        + [pl.BlockSpec(memory_space=pltpu.HBM)] * len(hbm)
+        + [VMEM_SPEC] * 2,
         out_specs=VMEM_SPEC,
-        scratch_shapes=[ext, ext],
+        scratch_shapes=[ext, ext, landed, pltpu.SemaphoreType.DMA((len(hbm),))],
         compiler_params=pltpu.CompilerParams(vmem_limit_bytes=16 << 20),
         name="rows",
-    )(place, *args)
+    )(place, *hbm, *(held(a) for a in bands))
 
 
 def cols_kernel(*refs):
@@ -254,22 +278,18 @@
     forward = lambda n: [(i, i + 1) for i in range(n - 1)]
     backward = lambda n: [(i + 1, i) for i in range(n - 1)]
 
-    def shift(x, axis, pairs):
-        return lax.ppermute(x, axis, pairs)
-
     last = row_count - 1
     middle = row_count // 2
     chip_pairs = [(i, i ^ 1) for i in range(row_count)]
     cross_pairs = [((i + 1 ^ 1) - 1, i) for i in range(1, last)]
     middle_pairs = [(middle - 1, middle), (middle, middle - 1)]
 
-    def from_rows(k, x):
-        chip = shift(x, "row", chip_pairs)
+    def from_across(k, x):
         if k < 3:
-            return chip, [shift(x, "row", cross_pairs)]
+            return [lax.ppermute(x, "row", cross_pairs)]
         ways = [pair for pair in cross_pairs if pair not in middle_pairs]
-        cross = shift(x, "row", ways + [(middle - 1, 0), (middle, last)])
-        return chip, [cross, shift(cross, "row", [(0, middle), (last, middle - 1)])]
+        cross = lax.ppermute(x, "row", ways + [(middle - 1, 0), (middle, last)])
+        return [cross, lax.ppermute(cross, "row", [(0, middle), (last, middle - 1)])]
 
     fields = [
         a.reshape(NLAT, NLON)
@@ -282,16 +302,16 @@
     lat_col = (lax.axis_index("col") * (width // NLON)).astype(jnp.int32).reshape(1)
 
     starts = (0, width - PAIR, PAIR, width - 2 * PAIR)
-    own = list(take_columns(block, starts[:2], PAIR))
-    own += take_columns(block, starts[2:], PAIR)
-    near = [from_rows(k, own[k]) for k in range(4)]
+    chip = lax.ppermute(block, "row", chip_pairs)
+    own = list(take_columns(block, starts[:1], PAIR))
+    own += take_columns(block, starts[1:], PAIR)
+    across = [from_across(k, own[k]) for k in range(4)]
     row_bands = build_bands(lat_row, fields, rows // PAIR, True)
     half, side = [], []
     for k in range(4):
-        chip, cross = near[k]
-        half.append(apply_rows(lat_row, chip, own[k], cross, row_bands))
+        half.append(apply_rows(lat_row, starts[k], block, chip, across[k], row_bands))
         pairs = forward(col_count) if k % 2 else backward(col_count)
-        side.append(shift(half[k], "col", pairs))
+        side.append(lax.ppermute(half[k], "col", pairs))
     col_bands = build_bands(lat_col, fields, width // PAIR, False)
     parts = [side[1], half[0], half[2], half[3], half[1], side[0], side[2]]
     part = apply_cols(parts, col_bands, width)

time: 95.9 us -> 86.2 us (0.90)
  the two profiles are of different devices: /device:TPU:6 before, /device:TPU:4 now
where the time goes in v3:
time: 86.2 us; the launch traced here: 85.6 us
  starting transfers between devices  29.4 us (34%)
  waiting for transfers between devices  28.3 us (33%)
  Pallas kernels  26.9 us (31%)
    ppermute x4, waiting for transfers between devices, body(): side.append(lax.ppermute(half[k], 'col', pairs))  22 us
    ppermute x4, starting transfers between devices, body(): side.append(lax.ppermute(half[k], 'col', pairs))  15.6 us
    pallas_call x4, Pallas kernels, apply_rows(): pl.pallas_call(functools.partial(rows_kernel, start), out_shape=pltpu.VME...  10.7 us
    ppermute x1, starting transfers between devices, from_across(): lax.ppermute(cross, 'row', [(0, middle), (last, middle - 1)])  8.79 us
    pallas_call x1, Pallas kernels, apply_cols(): pl.pallas_call(cols_kernel, out_shape=jax.ShapeDtypeStruct((rows, width),...  6.54 us
    ppermute x1, waiting for transfers between devices, from_across(): cross = lax.ppermute(x, 'row', ways + [(middle - 1, 0), (middle, last)])  6.29 us
    pallas_call x2, Pallas kernels, build_bands(): pl.pallas_call(functools.partial(band_kernel, transposed), out_shape=(ban...  4.98 us
    ppermute x3, starting transfers between devices, from_across(): return [lax.ppermute(x, 'row', cross_pairs)]  3.62 us
  transfers between devices with their start and end apart: 10, of which 4 were waited for; matrix products, arithmetic and copies ran while one was open for 0% of the time, Pallas kernels for 29%

profile of v3, /device:TPU:4, one launch (start us, length us, event | category | flops | bytes accessed | tf_op | source)
XLA Modules:
  0.0 85.6 jit_solution(9169353502038435934)
XLA Ops:
  0.0 0.0 copy-start
  0.0 0.0 copy-start.1
  0.0 0.0 copy-start.2
  0.0 0.0 copy-start.3
  0.0 0.0 copy-start.4
  0.0 0.0 copy-start.5
  0.0 0.1 collective-permute-start
  0.1 1.4 %take.2 = (f32[512,256]{1,0:T(8,128)S(1)}, f32[512,256]{1,0:T(8,128)S(1)}, f32[512,256]{1,0:T(8,128)S(1)}) custom-call(f32[512,1024]{1,0:T(8,128)} %bitcast.23), custom_call_target="tpu_custom_call" | custom-call | tf_op jit(solution)/shard_map/take/pallas_call | solution.py:148
  1.5 1.3 %collective-permute-start.1 = (f32[512,256]{1,0:T(8,128)S(1)}, f32[512,256]{1,0:T(8,128)S(1)}, u32[]{:S(2)}, u32[]{:S(2)}) collective-permute-start(f32[512,256]{1,0:T(8,128)S(1)} %get-tuple-element.12), channel_id=1, source_target_pairs={{16,8},{8,16},{32,24},{24,32},{48,40},{40,48},{80,72},{72,80},{96,... | collective-permute-start | bytes 1572872 | tf_op jit(solution)/shard_map/ppermute | solution.py:291
  2.8 0.7 collective-permute-start.4
  3.5 1.5 %collective-permute-start.7 = (f32[512,256]{1,0:T(8,128)S(1)}, f32[512,256]{1,0:T(8,128)}, u32[]{:S(2)}, u32[]{:S(2)}) collective-permute-start(f32[512,256]{1,0:T(8,128)S(1)} %get-tuple-element.18), channel_id=1, source_target_pairs={{16,8},{8,16},{32,24},{24,32},{48,40},{40,48},{64,56},{56,64},{80,... | collective-permute-start | bytes 1572872 | tf_op jit(solution)/shard_map/ppermute | solution.py:289
  5.0 1.0 %take.3 = f32[512,256]{1,0:T(8,128)S(1)} custom-call(f32[512,1024]{1,0:T(8,128)} %bitcast.24), custom_call_target="tpu_custom_call" | custom-call | tf_op jit(solution)/shard_map/take/pallas_call | solution.py:148
  6.1 1.5 %collective-permute-start.6 = (f32[512,256]{1,0:T(8,128)S(1)}, f32[512,256]{1,0:T(8,128)}, u32[]{:S(2)}, u32[]{:S(2)}) collective-permute-start(f32[512,256]{1,0:T(8,128)S(1)} %take.3), channel_id=1, source_target_pairs={{16,8},{8,16},{32,24},{24,32},{48,40},{40,48},{64,56},{56,64},{80,... | collective-permute-start | bytes 1572872 | tf_op jit(solution)/shard_map/ppermute | solution.py:289
  7.5 6.3 %collective-permute-done.1.refs_0_ = f32[512,256]{1,0:T(8,128)S(1)} collective-permute-done((f32[512,256]{1,0:T(8,128)S(1)}, f32[512,256]{1,0:T(8,128)S(1)}, u32[]{:S(2)}, u32[]{:S(2)}) %collective-permute-start.1) | collective-permute-done | bytes 524320 | tf_op jit(solution)/shard_map/ppermute | solution.py:291
  13.8 0.0 copy-start.6
  13.8 8.8 %collective-permute-start.2 = (f32[512,256]{1,0:T(8,128)S(1)}, f32[512,256]{1,0:T(8,128)}, u32[]{:S(2)}, u32[]{:S(2)}) collective-permute-start(f32[512,256]{1,0:T(8,128)S(1)} %collective-permute-done.1.refs_0_), channel_id=1, source_target_pairs={{0,64},{120,56},{1,65},{121,57},{2,66},{122,58},{3,67},{123,59},{4... | collective-permute-start | bytes 1572872 | tf_op jit(solution)/shard_map/ppermute | solution.py:292
  22.6 0.0 copy-done
  22.6 0.0 copy-done.1
  22.6 0.0 copy-done.2
  22.6 0.0 copy-done.3
  22.6 0.0 copy-done.4
  22.6 0.0 copy-done.5
  22.6 1.9 %row_bands.1 = (bf16[2,256,1280]{2,1,0:T(8,128)(2,1)S(1)}, bf16[2,256,1280]{2,1,0:T(8,128)(2,1)S(1)}) custom-call(s32[1]{0:T(128)} %bitcast.place, s32[64,128]{1,0:T(8,128)S(1)} %bitcast.10, s32[64,128]{1,0:T(8,128)S(1)} %bitcast.12, s32[64,128]{1,0:T(8,128)S(1)} %bitcast.14, f32[64,128]{1,0:T(8,128)S(1)} %bitcast.16, f32[64,128]{1,0:T(8,128)S(1)} %bitcast.18, ...), custom_call_target="tpu_custom_call" | custom-call | tf_op jit(solution)/shard_map/row_bands/pallas_call | solution.py:121
  24.6 0.0 collective-permute-done.4.refs_0_
  24.6 0.0 copy-start.7
  24.6 0.0 collective-permute-done.chip
  24.6 0.8 copy-done.7
  25.4 2.6 %rows.5.refs_4_ = f32[512,256]{1,0:T(8,128)S(1)} custom-call(s32[1]{0:T(128)} %bitcast.place, f32[512,1024]{1,0:T(8,128)} %bitcast.25, f32[512,1024]{1,0:T(8,128)} %collective-permute-done.chip, f32[512,256]{1,0:T(8,128)} %copy-done.7, bf16[2,256,1280]{2,1,0:T(8,128)(2,1)S(1)} %get-tuple-element.13.refs_2_.refs_1_, ...), custom_call_target="tpu_custom_call" | custom-call | tf_op jit(solution)/shard_map/rows/pallas_call | solution.py:201
  28.0 0.0 copy-done.6
  28.0 4.8 %collective-permute-start.5 = (f32[512,256]{1,0:T(8,128)S(1)}, f32[512,256]{1,0:T(8,128)S(1)}, u32[]{:S(2)}, u32[]{:S(2)}) collective-permute-start(f32[512,256]{1,0:T(8,128)S(1)} %rows.5.refs_4_), channel_id=1, source_target_pairs={{0,1},{1,2},{2,3},{3,4},{4,5},{5,6},{6,7},{8,9},{9,10},{10,11},{11... | collective-permute-start | bytes 1572872 | tf_op jit(solution)/shard_map/ppermute | solution.py:314
  32.8 0.0 collective-permute-done.7.refs_0_
  32.8 2.6 %rows.7.refs_2_ = f32[512,256]{1,0:T(8,128)S(1)} custom-call(s32[1]{0:T(128)} %bitcast.place, f32[512,1024]{1,0:T(8,128)} %bitcast.26, f32[512,1024]{1,0:T(8,128)} %collective-permute-done.chip, f32[512,256]{1,0:T(8,128)} %collective-permute-done.7.refs_0_, bf16[2,256,1280]{2,1,0:T(8,128)(2,1)S(1)} %get-tuple-element.13.refs_2_.refs_1_, ...), custom_call_target="tpu_custom_call" | custom-call | tf_op jit(solution)/shard_map/rows/pallas_call | solution.py:201
  35.5 3.4 %collective-permute-start.9 = (f32[512,256]{1,0:T(8,128)S(1)}, f32[512,256]{1,0:T(8,128)}, u32[]{:S(2)}, u32[]{:S(2)}) collective-permute-start(f32[512,256]{1,0:T(8,128)S(1)} %rows.7.refs_2_), channel_id=1, source_target_pairs={{1,0},{2,1},{3,2},{4,3},{5,4},{6,5},{7,6},{9,8},{10,9},{11,10},{12... | collective-permute-start | bytes 1572872 | tf_op jit(solution)/shard_map/ppermute | solution.py:314
  38.9 0.0 collective-permute-done.6.refs_0_
  38.9 2.6 %rows.6.refs_1_ = f32[512,256]{1,0:T(8,128)S(1)} custom-call(s32[1]{0:T(128)} %bitcast.place, f32[512,1024]{1,0:T(8,128)} %bitcast.27, f32[512,1024]{1,0:T(8,128)} %collective-permute-done.chip, f32[512,256]{1,0:T(8,128)} %collective-permute-done.6.refs_0_, bf16[2,256,1280]{2,1,0:T(8,128)(2,1)S(1)} %get-tuple-element.13.refs_2_.refs_1_, ...), custom_call_target="tpu_custom_call" | custom-call | tf_op jit(solution)/shard_map/rows/pallas_call | solution.py:201
  41.6 3.9 %collective-permute-start.8 = (f32[512,256]{1,0:T(8,128)S(1)}, f32[512,256]{1,0:T(8,128)}, u32[]{:S(2)}, u32[]{:S(2)}) collective-permute-start(f32[512,256]{1,0:T(8,128)S(1)} %rows.6.refs_1_), channel_id=1, source_target_pairs={{1,0},{2,1},{3,2},{4,3},{5,4},{6,5},{7,6},{9,8},{10,9},{11,10},{12... | collective-permute-start | bytes 1572872 | tf_op jit(solution)/shard_map/ppermute | solution.py:314
  45.5 0.0 collective-permute-done.2.refs_1_
  45.5 2.8 %rows.4.refs_3_ = f32[512,256]{1,0:T(8,128)S(1)} custom-call(s32[1]{0:T(128)} %bitcast.place, f32[512,1024]{1,0:T(8,128)} %bitcast.28, f32[512,1024]{1,0:T(8,128)} %collective-permute-done.chip, f32[512,256]{1,0:T(8,128)} %copy-done.6, f32[512,256]{1,0:T(8,128)} %collective-permute-done.2.refs_1_, ...), custom_call_target="tpu_custom_call" | custom-call | tf_op jit(solution)/shard_map/rows/pallas_call | solution.py:201
  48.3 3.5 %collective-permute-start.3 = (f32[512,256]{1,0:T(8,128)S(1)}, f32[512,256]{1,0:T(8,128)S(1)}, u32[]{:S(2)}, u32[]{:S(2)}) collective-permute-start(f32[512,256]{1,0:T(8,128)S(1)} %rows.4.refs_3_), channel_id=1, source_target_pairs={{0,1},{1,2},{2,3},{3,4},{4,5},{5,6},{6,7},{8,9},{9,10},{10,11},{11... | collective-permute-start | bytes 1572872 | tf_op jit(solution)/shard_map/ppermute | solution.py:314
  51.8 3.1 %col_bands.1 = (bf16[4,1280,256]{2,1,0:T(8,128)(2,1)S(1)}, bf16[4,1280,256]{2,1,0:T(8,128)(2,1)S(1)}) custom-call(s32[1]{0:T(128)} %bitcast.8.place, s32[64,128]{1,0:T(8,128)S(1)} %bitcast.11, s32[64,128]{1,0:T(8,128)S(1)} %bitcast.13, s32[64,128]{1,0:T(8,128)S(1)} %bitcast.15, f32[64,128]{1,0:T(8,128)S(1)} %bitcast.17, f32[64,128]{1,0:T(8,128)S(1)} %bitcast.19, ...), custom_call_target="tpu_custom_call" | custom-call | tf_op jit(solution)/shard_map/col_bands/pallas_call | solution.py:121
  54.8 11.9 %collective-permute-done.5.refs_0_ = f32[512,256]{1,0:T(8,128)S(1)} collective-permute-done((f32[512,256]{1,0:T(8,128)S(1)}, f32[512,256]{1,0:T(8,128)S(1)}, u32[]{:S(2)}, u32[]{:S(2)}) %collective-permute-start.5) | collective-permute-done | bytes 524320 | tf_op jit(solution)/shard_map/ppermute | solution.py:314
  66.7 1.4 %collective-permute-done.9.refs_6_ = f32[512,256]{1,0:T(8,128)} collective-permute-done((f32[512,256]{1,0:T(8,128)S(1)}, f32[512,256]{1,0:T(8,128)}, u32[]{:S(2)}, u32[]{:S(2)}) %collective-permute-start.9) | collective-permute-done | bytes 524320 | tf_op jit(solution)/shard_map/ppermute | solution.py:314
  68.1 8.8 %collective-permute-done.8.refs_5_ = f32[512,256]{1,0:T(8,128)} collective-permute-done((f32[512,256]{1,0:T(8,128)S(1)}, f32[512,256]{1,0:T(8,128)}, u32[]{:S(2)}, u32[]{:S(2)}) %collective-permute-start.8) | collective-permute-done | bytes 524320 | tf_op jit(solution)/shard_map/ppermute | solution.py:314
  76.9 6.5 %cols.1.part = f32[512,1024]{1,0:T(8,128)} custom-call(f32[512,256]{1,0:T(8,128)S(1)} %collective-permute-done.5.refs_0_, f32[512,256]{1,0:T(8,128)S(1)} %rows.6.refs_1_, f32[512,256]{1,0:T(8,128)S(1)} %rows.7.refs_2_, f32[512,256]{1,0:T(8,128)S(1)} %rows.4.refs_3_, f32[512,256]{1,0:T(8,128)S(1)} %rows.5.refs_4_, f32[512,256]{1,0:T(8,128)} %collective-permute-done.8.refs_5_, ...), custom_call_target="tpu_custom_call" | custom-call | tf_op jit(solution)/shard_map/cols/pallas_call | solution.py:238
  83.4 0.0 collective-permute-done.3.west
  83.4 2.2 %tail.1 = f32[512,1024]{1,0:T(8,128)} custom-call(f32[512,256]{1,0:T(8,128)S(1)} %collective-permute-done.3.west, bf16[4,1280,256]{2,1,0:T(8,128)(2,1)S(1)} %get-tuple-element.15.refs_7_.band_high, bf16[4,1280,256]{2,1,0:T(8,128)(2,1)S(1)} %get-tuple-element.16.refs_8_.band_low, f32[512,1024]{1,0:T(8,128)} %cols.1.part), custom_call_target="tpu_custom_call", output_to_operand_aliasing={{}: (3, {})} | custom-call | tf_op jit(solution)/shard_map/tail/pallas_call | solution.py:259
Async XLA Ops:
  0.0 22.6 %copy-start = (s32[1,1,8192]{2,1,0:T(1,128)S(1)}, s32[1,1,8192]{2,1,0:T(1,128)}, u32[]{:S(2)}) copy-start(s32[1,1,8192]{2,1,0:T(1,128)} %param.8) | copy-start | bytes 98308
  0.0 22.6 %copy-start.1 = (s32[1,1,8192]{2,1,0:T(1,128)S(1)}, s32[1,1,8192]{2,1,0:T(1,128)}, u32[]{:S(2)}) copy-start(s32[1,1,8192]{2,1,0:T(1,128)} %param.9) | copy-start | bytes 98308
  0.0 22.6 %copy-start.2 = (s32[1,1,8192]{2,1,0:T(1,128)S(1)}, s32[1,1,8192]{2,1,0:T(1,128)}, u32[]{:S(2)}) copy-start(s32[1,1,8192]{2,1,0:T(1,128)} %param.10) | copy-start | bytes 98308
  0.0 22.6 %copy-start.3 = (f32[1,1,8192]{2,1,0:T(1,128)S(1)}, f32[1,1,8192]{2,1,0:T(1,128)}, u32[]{:S(2)}) copy-start(f32[1,1,8192]{2,1,0:T(1,128)} %param.11) | copy-start | bytes 98308
  0.0 22.6 %copy-start.4 = (f32[1,8192]{1,0:T(1,128)S(1)}, f32[1,8192]{1,0:T(1,128)}, u32[]{:S(2)}) copy-start(f32[1,8192]{1,0:T(1,128)} %param.12) | copy-start | bytes 98308
  0.0 22.6 %copy-start.5 = (f32[1,8192]{1,0:T(1,128)S(1)}, f32[1,8192]{1,0:T(1,128)}, u32[]{:S(2)}) copy-start(f32[1,8192]{1,0:T(1,128)} %param.13) | copy-start | bytes 98308
  0.0 24.5 %collective-permute-start = (f32[512,1024]{1,0:T(8,128)}, f32[512,1024]{1,0:T(8,128)}, u32[]{:S(2)}, u32[]{:S(2)}) collective-permute-start(f32[512,1024]{1,0:T(8,128)} %bitcast.22), channel_id=1, source_target_pairs={{0,8},{8,0},{16,24},{24,16},{32,40},{40,32},{48,56},{56,48},{64,72... | collective-permute-start | bytes 6291464 | tf_op jit(solution)/shard_map/ppermute | solution.py:305
  1.5 12.3 %collective-permute-start.1 = (f32[512,256]{1,0:T(8,128)S(1)}, f32[512,256]{1,0:T(8,128)S(1)}, u32[]{:S(2)}, u32[]{:S(2)}) collective-permute-start(f32[512,256]{1,0:T(8,128)S(1)} %get-tuple-element.12), channel_id=1, source_target_pairs={{16,8},{8,16},{32,24},{24,32},{48,40},{40,48},{80,72},{72,80},{96,... | collective-permute-start | bytes 1572872 | tf_op jit(solution)/shard_map/ppermute | solution.py:291
  2.8 21.7 %collective-permute-start.4 = (f32[512,256]{1,0:T(8,128)S(1)}, f32[512,256]{1,0:T(8,128)S(1)}, u32[]{:S(2)}, u32[]{:S(2)}) collective-permute-start(f32[512,256]{1,0:T(8,128)S(1)} %get-tuple-element.17), channel_id=1, source_target_pairs={{16,8},{8,16},{32,24},{24,32},{48,40},{40,48},{64,56},{56,64},{80,... | collective-permute-start | bytes 1572872 | tf_op jit(solution)/shard_map/ppermute | solution.py:289
  3.5 29.3 %collective-permute-start.7 = (f32[512,256]{1,0:T(8,128)S(1)}, f32[512,256]{1,0:T(8,128)}, u32[]{:S(2)}, u32[]{:S(2)}) collective-permute-start(f32[512,256]{1,0:T(8,128)S(1)} %get-tuple-element.18), channel_id=1, source_target_pairs={{16,8},{8,16},{32,24},{24,32},{48,40},{40,48},{64,56},{56,64},{80,... | collective-permute-start | bytes 1572872 | tf_op jit(solution)/shard_map/ppermute | solution.py:289
  6.1 32.9 %collective-permute-start.6 = (f32[512,256]{1,0:T(8,128)S(1)}, f32[512,256]{1,0:T(8,128)}, u32[]{:S(2)}, u32[]{:S(2)}) collective-permute-start(f32[512,256]{1,0:T(8,128)S(1)} %take.3), channel_id=1, source_target_pairs={{16,8},{8,16},{32,24},{24,32},{48,40},{40,48},{64,56},{56,64},{80,... | collective-permute-start | bytes 1572872 | tf_op jit(solution)/shard_map/ppermute | solution.py:289
  13.8 14.2 %copy-start.6 = (f32[512,256]{1,0:T(8,128)}, f32[512,256]{1,0:T(8,128)S(1)}, u32[]{:S(2)}) copy-start(f32[512,256]{1,0:T(8,128)S(1)} %collective-permute-done.1.refs_0_) | copy-start | bytes 1572868
  13.8 31.6 %collective-permute-start.2 = (f32[512,256]{1,0:T(8,128)S(1)}, f32[512,256]{1,0:T(8,128)}, u32[]{:S(2)}, u32[]{:S(2)}) collective-permute-start(f32[512,256]{1,0:T(8,128)S(1)} %collective-permute-done.1.refs_0_), channel_id=1, source_target_pairs={{0,64},{120,56},{1,65},{121,57},{2,66},{122,58},{3,67},{123,59},{4... | collective-permute-start | bytes 1572872 | tf_op jit(solution)/shard_map/ppermute | solution.py:292
  24.6 0.8 copy-start.7
  28.0 38.7 %collective-permute-start.5 = (f32[512,256]{1,0:T(8,128)S(1)}, f32[512,256]{1,0:T(8,128)S(1)}, u32[]{:S(2)}, u32[]{:S(2)}) collective-permute-start(f32[512,256]{1,0:T(8,128)S(1)} %rows.5.refs_4_), channel_id=1, source_target_pairs={{0,1},{1,2},{2,3},{3,4},{4,5},{5,6},{6,7},{8,9},{9,10},{10,11},{11... | collective-permute-start | bytes 1572872 | tf_op jit(solution)/shard_map/ppermute | solution.py:314
  35.5 32.6 %collective-permute-start.9 = (f32[512,256]{1,0:T(8,128)S(1)}, f32[512,256]{1,0:T(8,128)}, u32[]{:S(2)}, u32[]{:S(2)}) collective-permute-start(f32[512,256]{1,0:T(8,128)S(1)} %rows.7.refs_2_), channel_id=1, source_target_pairs={{1,0},{2,1},{3,2},{4,3},{5,4},{6,5},{7,6},{9,8},{10,9},{11,10},{12... | collective-permute-start | bytes 1572872 | tf_op jit(solution)/shard_map/ppermute | solution.py:314
  41.6 35.3 %collective-permute-start.8 = (f32[512,256]{1,0:T(8,128)S(1)}, f32[512,256]{1,0:T(8,128)}, u32[]{:S(2)}, u32[]{:S(2)}) collective-permute-start(f32[512,256]{1,0:T(8,128)S(1)} %rows.6.refs_1_), channel_id=1, source_target_pairs={{1,0},{2,1},{3,2},{4,3},{5,4},{6,5},{7,6},{9,8},{10,9},{11,10},{12... | collective-permute-start | bytes 1572872 | tf_op jit(solution)/shard_map/ppermute | solution.py:314
  48.3 35.1 %collective-permute-start.3 = (f32[512,256]{1,0:T(8,128)S(1)}, f32[512,256]{1,0:T(8,128)S(1)}, u32[]{:S(2)}, u32[]{:S(2)}) collective-permute-start(f32[512,256]{1,0:T(8,128)S(1)} %rows.4.refs_3_), channel_id=1, source_target_pairs={{0,1},{1,2},{2,3},{3,4},{4,5},{5,6},{6,7},{8,9},{9,10},{10,11},{11... | collective-permute-start | bytes 1572872 | tf_op jit(solution)/shard_map/ppermute | solution.py:314

commit v4 on v3

--- a/solution.py
+++ b/solution.py
@@ -115,6 +115,10 @@
     return pltpu.with_memory_space_constraint(x, pltpu.VMEM)
 
 
+def in_hbm(x):
+    return pltpu.with_memory_space_constraint(x, pltpu.HBM)
+
+
 def build_bands(place, fields, pairs, transposed):
     shape = (pairs, PAIR, SPAN) if transposed else (pairs, SPAN, PAIR)
     band = pltpu.VMEM(shape, jnp.bfloat16)
@@ -132,37 +136,43 @@
 
 def take_kernel(starts, source, *refs):
     outs, sems = refs[:-1], refs[-1]
-    copies = [
-        pltpu.make_async_copy(source.at[:, pl.ds(at, out.shape[1])], out, sems.at[i])
-        for i, (at, out) in enumerate(zip(starts, outs))
-    ]
+    count = sems.shape[1]
+    piece = source.shape[0] // count
+    copies = []
+    for i, (at, out) in enumerate(zip(starts, outs)):
+        for j in range(count):
+            rows = pl.ds(j * piece, piece)
+            copies.append(
+                pltpu.make_async_copy(
+                    source.at[rows, pl.ds(at, out.shape[1])], out.at[rows], sems.at[i, j]
+                )
+            )
     for copy in copies:
         copy.start()
     for copy in copies:
         copy.wait()
 
 
-def take_columns(source, starts, width):
-    hbm = pl.BlockSpec(memory_space=pltpu.HBM)
-    out = jax.ShapeDtypeStruct((source.shape[0], width), jnp.float32)
+def take_columns(source, ranges):
+    rows = source.shape[0]
+    starts = [start for start, _ in ranges]
     return pl.pallas_call(
         functools.partial(take_kernel, starts),
-        out_shape=(out,) * len(starts),
-        in_specs=[hbm],
-        out_specs=(hbm,) * len(starts),
-        scratch_shapes=[pltpu.SemaphoreType.DMA((len(starts),))],
+        out_shape=tuple(pltpu.VMEM((rows, stop - start), jnp.float32) for start, stop in ranges),
+        in_specs=[pl.BlockSpec(memory_space=pltpu.HBM)],
+        out_specs=(VMEM_SPEC,) * len(ranges),
+        scratch_shapes=[pltpu.SemaphoreType.DMA((len(ranges), 4))],
         compiler_params=pltpu.CompilerParams(vmem_limit_bytes=8 << 20),
         name="take",
     )(in_hbm(source))
 
 
-def rows_kernel(start, place, own, chip, *refs):
-    *cross, band_high, band_low, out, high, low, landed, sems = refs
+def rows_kernel(starts, place, *refs):
+    *sources, band_high, band_low, out, high, low, landed, sems = refs
     rows, width = out.shape
-    sources = [ref.at[:, pl.ds(start, width)] for ref in (own, chip)] + list(cross)
     copies = [
-        pltpu.make_async_copy(source, landed.at[i], sems.at[i])
-        for i, source in enumerate(sources)
+        pltpu.make_async_copy(ref.at[:, pl.ds(start, width)], landed.at[i], sems.at[i])
+        for i, (start, ref) in enumerate(zip(starts, sources))
     ]
     for copy in copies:
         copy.start()
@@ -189,17 +199,13 @@
         )
 
 
-def in_hbm(x):
-    return pltpu.with_memory_space_constraint(x, pltpu.HBM)
-
-
-def apply_rows(place, start, own, chip, cross, bands):
-    rows, width = cross[0].shape
+def apply_rows(place, width, sources, starts, bands):
+    rows = sources[0].shape[0]
     ext = pltpu.VMEM((3 * rows, width), jnp.bfloat16)
-    hbm = [in_hbm(a) for a in (own, chip, *cross)]
+    hbm = [in_hbm(a) for a in sources]
     landed = pltpu.VMEM((len(hbm), rows, width), jnp.float32)
     return pl.pallas_call(
-        functools.partial(rows_kernel, start),
+        functools.partial(rows_kernel, starts),
         out_shape=pltpu.VMEM((rows, width), jnp.float32),
         in_specs=[pl.BlockSpec(memory_space=pltpu.SMEM)]
         + [pl.BlockSpec(memory_space=pltpu.HBM)] * len(hbm)
@@ -284,13 +290,6 @@
     cross_pairs = [((i + 1 ^ 1) - 1, i) for i in range(1, last)]
     middle_pairs = [(middle - 1, middle), (middle, middle - 1)]
 
-    def from_across(k, x):
-        if k < 3:
-            return [lax.ppermute(x, "row", cross_pairs)]
-        ways = [pair for pair in cross_pairs if pair not in middle_pairs]
-        cross = lax.ppermute(x, "row", ways + [(middle - 1, 0), (middle, last)])
-        return [cross, lax.ppermute(cross, "row", [(0, middle), (last, middle - 1)])]
-
     fields = [
         a.reshape(NLAT, NLON)
         for a in (
@@ -303,13 +302,21 @@
 
     starts = (0, width - PAIR, PAIR, width - 2 * PAIR)
     chip = lax.ppermute(block, "row", chip_pairs)
-    own = list(take_columns(block, starts[:1], PAIR))
-    own += take_columns(block, starts[1:], PAIR)
-    across = [from_across(k, own[k]) for k in range(4)]
+    (own0,) = take_columns(block, [(0, PAIR)])
+    own1, own2 = take_columns(block, [(width - PAIR, width), (PAIR, width - PAIR)])
+    across0 = lax.ppermute(own0, "row", cross_pairs)
+    ways = [pair for pair in cross_pairs if pair not in middle_pairs]
+    across1 = lax.ppermute(own1, "row", ways + [(middle - 1, 0), (middle, last)])
+    relay = lax.ppermute(across1, "row", [(0, middle), (last, middle - 1)])
+    across2 = lax.ppermute(own2, "row", cross_pairs)
     row_bands = build_bands(lat_row, fields, rows // PAIR, True)
+    across = ([across0], [across1, relay], [across2], [across2])
+    offset = ([0], [0, 0], [0], [width - 3 * PAIR])
     half, side = [], []
     for k in range(4):
-        half.append(apply_rows(lat_row, starts[k], block, chip, across[k], row_bands))
+        sources = [block, chip] + across[k]
+        begins = [starts[k]] * 2 + offset[k]
+        half.append(apply_rows(lat_row, PAIR, sources, begins, row_bands))
         pairs = forward(col_count) if k % 2 else backward(col_count)
         side.append(lax.ppermute(half[k], "col", pairs))
     col_bands = build_bands(lat_col, fields, width // PAIR, False)

time: 86.2 us -> 85 us (0.986)
  the two profiles are of different devices: /device:TPU:4 before, /device:TPU:103 now
where the time goes in v4:
time: 85 us; the launch traced here: 84.5 us
  starting transfers between devices  31.7 us (37%)
  Pallas kernels  27.1 us (32%)
  waiting for transfers between devices  24.6 us (29%)
    ppermute x4, waiting for transfers between devices, body(): side.append(lax.ppermute(half[k], 'col', pairs))  22.3 us
    ppermute x4, starting transfers between devices, body(): side.append(lax.ppermute(half[k], 'col', pairs))  15.3 us
    pallas_call x4, Pallas kernels, apply_rows(): pl.pallas_call(functools.partial(rows_kernel, starts), out_shape=pltpu.VM...  10.7 us
    ppermute x1, starting transfers between devices, body(): across0 = lax.ppermute(own0, 'row', cross_pairs)  6.61 us
    pallas_call x1, Pallas kernels, apply_cols(): pl.pallas_call(cols_kernel, out_shape=jax.ShapeDtypeStruct((rows, width),...  6.54 us
    ppermute x1, starting transfers between devices, body(): across2 = lax.ppermute(own2, 'row', cross_pairs)  6.49 us
    pallas_call x2, Pallas kernels, build_bands(): pl.pallas_call(functools.partial(band_kernel, transposed), out_shape=(ban...  5.05 us
    pallas_call x2, Pallas kernels, take_columns(): pl.pallas_call(functools.partial(take_kernel, starts), out_shape=tuple((p...  2.65 us
  transfers between devices with their start and end apart: 9, of which 3 were waited for; matrix products, arithmetic and copies ran while one was open for 0% of the time, Pallas kernels for 29%

profile of v4, /device:TPU:103, one launch (start us, length us, event | category | flops | bytes accessed | tf_op | source)
XLA Modules:
  0.0 84.5 jit_solution(7892566921556944218)
XLA Ops:
  0.0 0.0 copy-start
  0.0 0.0 copy-start.1
  0.0 0.0 copy-start.2
  0.0 0.0 copy-start.3
  0.0 0.0 copy-start.4
  0.0 0.0 copy-start.5
  0.0 0.8 collective-permute-start
  0.8 1.5 %take.2 = (f32[512,256]{1,0:T(8,128)S(1)}, f32[512,512]{1,0:T(8,128)S(1)}) custom-call(f32[512,1024]{1,0:T(8,128)} %bitcast.23), custom_call_target="tpu_custom_call" | custom-call | tf_op jit(solution)/shard_map/take/pallas_call | solution.py:159
  2.3 1.3 %collective-permute-start.3 = (f32[512,256]{1,0:T(8,128)S(1)}, f32[512,256]{1,0:T(8,128)S(1)}, u32[]{:S(2)}, u32[]{:S(2)}) collective-permute-start(f32[512,256]{1,0:T(8,128)S(1)} %get-tuple-element.16), channel_id=1, source_target_pairs={{16,8},{8,16},{32,24},{24,32},{48,40},{40,48},{80,72},{72,80},{96,... | collective-permute-start | bytes 1572872 | tf_op jit(solution)/shard_map/ppermute | solution.py:309
  3.7 6.5 %collective-permute-start.1 = (f32[512,512]{1,0:T(8,128)S(1)}, f32[512,512]{1,0:T(8,128)}, u32[]{:S(2)}, u32[]{:S(2)}) collective-permute-start(f32[512,512]{1,0:T(8,128)S(1)} %get-tuple-element.11), channel_id=1, source_target_pairs={{16,8},{8,16},{32,24},{24,32},{48,40},{40,48},{64,56},{56,64},{80,... | collective-permute-start | bytes 3145736 | tf_op jit(solution)/shard_map/ppermute | solution.py:311
  10.2 0.0 collective-permute-done.3.refs_2_
  10.2 0.0 copy-start.6
  10.2 1.3 %collective-permute-start.4 = (f32[512,256]{1,0:T(8,128)S(1)}, f32[512,256]{1,0:T(8,128)S(1)}, u32[]{:S(2)}, u32[]{:S(2)}) collective-permute-start(f32[512,256]{1,0:T(8,128)S(1)} %collective-permute-done.3.refs_2_), channel_id=1, source_target_pairs={{0,64},{120,56},{1,65},{121,57},{2,66},{122,58},{3,67},{123,59},{4... | collective-permute-start | bytes 1572872 | tf_op jit(solution)/shard_map/ppermute | solution.py:310
  11.5 1.1 %take.3 = f32[512,256]{1,0:T(8,128)S(1)} custom-call(f32[512,1024]{1,0:T(8,128)} %bitcast.24), custom_call_target="tpu_custom_call" | custom-call | tf_op jit(solution)/shard_map/take/pallas_call | solution.py:159
  12.6 6.6 %collective-permute-start.6 = (f32[512,256]{1,0:T(8,128)S(1)}, f32[512,256]{1,0:T(8,128)}, u32[]{:S(2)}, u32[]{:S(2)}) collective-permute-start(f32[512,256]{1,0:T(8,128)S(1)} %take.3), channel_id=1, source_target_pairs={{16,8},{8,16},{32,24},{24,32},{48,40},{40,48},{64,56},{56,64},{80,... | collective-permute-start | bytes 1572872 | tf_op jit(solution)/shard_map/ppermute | solution.py:307
  19.2 0.0 copy-done
  19.2 0.0 copy-done.1
  19.3 0.0 copy-done.2
  19.3 0.0 copy-done.3
  19.3 0.0 copy-done.4
  19.3 0.0 copy-done.5
  19.3 1.9 %row_bands.1 = (bf16[2,256,1280]{2,1,0:T(8,128)(2,1)S(1)}, bf16[2,256,1280]{2,1,0:T(8,128)(2,1)S(1)}) custom-call(s32[1]{0:T(128)} %bitcast.place, s32[64,128]{1,0:T(8,128)S(1)} %bitcast.10, s32[64,128]{1,0:T(8,128)S(1)} %bitcast.12, s32[64,128]{1,0:T(8,128)S(1)} %bitcast.14, f32[64,128]{1,0:T(8,128)S(1)} %bitcast.16, f32[64,128]{1,0:T(8,128)S(1)} %bitcast.18, ...), custom_call_target="tpu_custom_call" | custom-call | tf_op jit(solution)/shard_map/row_bands/pallas_call | solution.py:125
  21.2 2.3 %collective-permute-done.4.refs_3_ = f32[512,256]{1,0:T(8,128)S(1)} collective-permute-done((f32[512,256]{1,0:T(8,128)S(1)}, f32[512,256]{1,0:T(8,128)S(1)}, u32[]{:S(2)}, u32[]{:S(2)}) %collective-permute-start.4) | collective-permute-done | bytes 524320 | tf_op jit(solution)/shard_map/ppermute | solution.py:310
  23.6 0.0 copy-start.7
  23.6 0.0 collective-permute-done.refs_1_
  23.6 0.0 copy-done.6
  23.6 0.8 copy-done.7
  24.4 2.8 %rows.5.refs_4_ = f32[512,256]{1,0:T(8,128)S(1)} custom-call(s32[1]{0:T(128)} %bitcast.place, f32[512,1024]{1,0:T(8,128)} %bitcast.25, f32[512,1024]{1,0:T(8,128)} %collective-permute-done.refs_1_, f32[512,256]{1,0:T(8,128)} %copy-done.6, f32[512,256]{1,0:T(8,128)} %copy-done.7, bf16[2,256,1280]{2,1,0:T(8,128)(2,1)S(1)} %get-tuple-element.12.refs_3_.refs_4_, ...), custom_call_target="tpu_custom_call" | custom-call | tf_op jit(solution)/shard_map/rows/pallas_call | solution.py:207
  27.2 4.5 %collective-permute-start.5 = (f32[512,256]{1,0:T(8,128)S(1)}, f32[512,256]{1,0:T(8,128)S(1)}, u32[]{:S(2)}, u32[]{:S(2)}) collective-permute-start(f32[512,256]{1,0:T(8,128)S(1)} %rows.5.refs_4_), channel_id=1, source_target_pairs={{0,1},{1,2},{2,3},{3,4},{4,5},{5,6},{6,7},{8,9},{9,10},{10,11},{11... | collective-permute-start | bytes 1572872 | tf_op jit(solution)/shard_map/ppermute | solution.py:321
  31.7 0.0 collective-permute-done.1.refs_2_
  31.7 2.6 %rows.7.refs_2_ = f32[512,256]{1,0:T(8,128)S(1)} custom-call(s32[1]{0:T(128)} %bitcast.place, f32[512,1024]{1,0:T(8,128)} %bitcast.26, f32[512,1024]{1,0:T(8,128)} %collective-permute-done.refs_1_, f32[512,512]{1,0:T(8,128)} %collective-permute-done.1.refs_2_, bf16[2,256,1280]{2,1,0:T(8,128)(2,1)S(1)} %get-tuple-element.12.refs_3_.refs_4_, ...), custom_call_target="tpu_custom_call" | custom-call | tf_op jit(solution)/shard_map/rows/pallas_call | solution.py:207
  34.4 3.2 %collective-permute-start.8 = (f32[512,256]{1,0:T(8,128)S(1)}, f32[512,256]{1,0:T(8,128)}, u32[]{:S(2)}, u32[]{:S(2)}) collective-permute-start(f32[512,256]{1,0:T(8,128)S(1)} %rows.7.refs_2_), channel_id=1, source_target_pairs={{1,0},{2,1},{3,2},{4,3},{5,4},{6,5},{7,6},{9,8},{10,9},{11,10},{12... | collective-permute-start | bytes 1572872 | tf_op jit(solution)/shard_map/ppermute | solution.py:321
  37.5 0.0 collective-permute-done.6.refs_2_
  37.5 2.6 %rows.6.refs_1_ = f32[512,256]{1,0:T(8,128)S(1)} custom-call(s32[1]{0:T(128)} %bitcast.place, f32[512,1024]{1,0:T(8,128)} %bitcast.27, f32[512,1024]{1,0:T(8,128)} %collective-permute-done.refs_1_, f32[512,256]{1,0:T(8,128)} %collective-permute-done.6.refs_2_, bf16[2,256,1280]{2,1,0:T(8,128)(2,1)S(1)} %get-tuple-element.12.refs_3_.refs_4_, ...), custom_call_target="tpu_custom_call" | custom-call | tf_op jit(solution)/shard_map/rows/pallas_call | solution.py:207
  40.2 3.9 %collective-permute-start.7 = (f32[512,256]{1,0:T(8,128)S(1)}, f32[512,256]{1,0:T(8,128)}, u32[]{:S(2)}, u32[]{:S(2)}) collective-permute-start(f32[512,256]{1,0:T(8,128)S(1)} %rows.6.refs_1_), channel_id=1, source_target_pairs={{1,0},{2,1},{3,2},{4,3},{5,4},{6,5},{7,6},{9,8},{10,9},{11,10},{12... | collective-permute-start | bytes 1572872 | tf_op jit(solution)/shard_map/ppermute | solution.py:321
  44.1 2.6 %rows.4.refs_3_ = f32[512,256]{1,0:T(8,128)S(1)} custom-call(s32[1]{0:T(128)} %bitcast.place, f32[512,1024]{1,0:T(8,128)} %bitcast.28, f32[512,1024]{1,0:T(8,128)} %collective-permute-done.refs_1_, f32[512,512]{1,0:T(8,128)} %collective-permute-done.1.refs_2_, bf16[2,256,1280]{2,1,0:T(8,128)(2,1)S(1)} %get-tuple-element.12.refs_3_.refs_4_, ...), custom_call_target="tpu_custom_call" | custom-call | tf_op jit(solution)/shard_map/rows/pallas_call | solution.py:207
  46.7 3.7 %collective-permute-start.2 = (f32[512,256]{1,0:T(8,128)S(1)}, f32[512,256]{1,0:T(8,128)S(1)}, u32[]{:S(2)}, u32[]{:S(2)}) collective-permute-start(f32[512,256]{1,0:T(8,128)S(1)} %rows.4.refs_3_), channel_id=1, source_target_pairs={{0,1},{1,2},{2,3},{3,4},{4,5},{5,6},{6,7},{8,9},{9,10},{10,11},{11... | collective-permute-start | bytes 1572872 | tf_op jit(solution)/shard_map/ppermute | solution.py:321
  50.4 3.1 %col_bands.1 = (bf16[4,1280,256]{2,1,0:T(8,128)(2,1)S(1)}, bf16[4,1280,256]{2,1,0:T(8,128)(2,1)S(1)}) custom-call(s32[1]{0:T(128)} %bitcast.8.place, s32[64,128]{1,0:T(8,128)S(1)} %bitcast.11, s32[64,128]{1,0:T(8,128)S(1)} %bitcast.13, s32[64,128]{1,0:T(8,128)S(1)} %bitcast.15, f32[64,128]{1,0:T(8,128)S(1)} %bitcast.17, f32[64,128]{1,0:T(8,128)S(1)} %bitcast.19, ...), custom_call_target="tpu_custom_call" | custom-call | tf_op jit(solution)/shard_map/col_bands/pallas_call | solution.py:125
  53.5 0.0 collective-permute-done.5.refs_0_
  53.5 11.3 %collective-permute-done.8.refs_6_ = f32[512,256]{1,0:T(8,128)} collective-permute-done((f32[512,256]{1,0:T(8,128)S(1)}, f32[512,256]{1,0:T(8,128)}, u32[]{:S(2)}, u32[]{:S(2)}) %collective-permute-start.8) | collective-permute-done | bytes 524320 | tf_op jit(solution)/shard_map/ppermute | solution.py:321
  64.8 11.0 %collective-permute-done.7.refs_5_ = f32[512,256]{1,0:T(8,128)} collective-permute-done((f32[512,256]{1,0:T(8,128)S(1)}, f32[512,256]{1,0:T(8,128)}, u32[]{:S(2)}, u32[]{:S(2)}) %collective-permute-start.7) | collective-permute-done | bytes 524320 | tf_op jit(solution)/shard_map/ppermute | solution.py:321
  75.8 6.5 %cols.1.part = f32[512,1024]{1,0:T(8,128)} custom-call(f32[512,256]{1,0:T(8,128)S(1)} %collective-permute-done.5.refs_0_, f32[512,256]{1,0:T(8,128)S(1)} %rows.6.refs_1_, f32[512,256]{1,0:T(8,128)S(1)} %rows.7.refs_2_, f32[512,256]{1,0:T(8,128)S(1)} %rows.4.refs_3_, f32[512,256]{1,0:T(8,128)S(1)} %rows.5.refs_4_, f32[512,256]{1,0:T(8,128)} %collective-permute-done.7.refs_5_, ...), custom_call_target="tpu_custom_call" | custom-call | tf_op jit(solution)/shard_map/cols/pallas_call | solution.py:244
  82.3 0.0 collective-permute-done.2.west
  82.3 2.2 %tail.1 = f32[512,1024]{1,0:T(8,128)} custom-call(f32[512,256]{1,0:T(8,128)S(1)} %collective-permute-done.2.west, bf16[4,1280,256]{2,1,0:T(8,128)(2,1)S(1)} %get-tuple-element.14.refs_7_.band_high, bf16[4,1280,256]{2,1,0:T(8,128)(2,1)S(1)} %get-tuple-element.15.refs_8_.band_low, f32[512,1024]{1,0:T(8,128)} %cols.1.part), custom_call_target="tpu_custom_call", output_to_operand_aliasing={{}: (3, {})} | custom-call | tf_op jit(solution)/shard_map/tail/pallas_call | solution.py:265
Async XLA Ops:
  0.0 19.2 %copy-start = (s32[1,1,8192]{2,1,0:T(1,128)S(1)}, s32[1,1,8192]{2,1,0:T(1,128)}, u32[]{:S(2)}) copy-start(s32[1,1,8192]{2,1,0:T(1,128)} %param.8) | copy-start | bytes 98308
  0.0 19.2 %copy-start.1 = (s32[1,1,8192]{2,1,0:T(1,128)S(1)}, s32[1,1,8192]{2,1,0:T(1,128)}, u32[]{:S(2)}) copy-start(s32[1,1,8192]{2,1,0:T(1,128)} %param.9) | copy-start | bytes 98308
  0.0 19.3 %copy-start.2 = (s32[1,1,8192]{2,1,0:T(1,128)S(1)}, s32[1,1,8192]{2,1,0:T(1,128)}, u32[]{:S(2)}) copy-start(s32[1,1,8192]{2,1,0:T(1,128)} %param.10) | copy-start | bytes 98308
  0.0 19.3 %copy-start.3 = (f32[1,1,8192]{2,1,0:T(1,128)S(1)}, f32[1,1,8192]{2,1,0:T(1,128)}, u32[]{:S(2)}) copy-start(f32[1,1,8192]{2,1,0:T(1,128)} %param.11) | copy-start | bytes 98308
  0.0 19.3 %copy-start.4 = (f32[1,8192]{1,0:T(1,128)S(1)}, f32[1,8192]{1,0:T(1,128)}, u32[]{:S(2)}) copy-start(f32[1,8192]{1,0:T(1,128)} %param.12) | copy-start | bytes 98308
  0.0 19.3 %copy-start.5 = (f32[1,8192]{1,0:T(1,128)S(1)}, f32[1,8192]{1,0:T(1,128)}, u32[]{:S(2)}) copy-start(f32[1,8192]{1,0:T(1,128)} %param.13) | copy-start | bytes 98308
  0.0 23.5 %collective-permute-start = (f32[512,1024]{1,0:T(8,128)}, f32[512,1024]{1,0:T(8,128)}, u32[]{:S(2)}, u32[]{:S(2)}) collective-permute-start(f32[512,1024]{1,0:T(8,128)} %bitcast.22), channel_id=1, source_target_pairs={{0,8},{8,0},{16,24},{24,16},{32,40},{40,32},{48,56},{56,48},{64,72... | collective-permute-start | bytes 6291464 | tf_op jit(solution)/shard_map/ppermute | solution.py:304
  2.3 7.8 %collective-permute-start.3 = (f32[512,256]{1,0:T(8,128)S(1)}, f32[512,256]{1,0:T(8,128)S(1)}, u32[]{:S(2)}, u32[]{:S(2)}) collective-permute-start(f32[512,256]{1,0:T(8,128)S(1)} %get-tuple-element.16), channel_id=1, source_target_pairs={{16,8},{8,16},{32,24},{24,32},{48,40},{40,48},{80,72},{72,80},{96,... | collective-permute-start | bytes 1572872 | tf_op jit(solution)/shard_map/ppermute | solution.py:309
  3.7 28.1 %collective-permute-start.1 = (f32[512,512]{1,0:T(8,128)S(1)}, f32[512,512]{1,0:T(8,128)}, u32[]{:S(2)}, u32[]{:S(2)}) collective-permute-start(f32[512,512]{1,0:T(8,128)S(1)} %get-tuple-element.11), channel_id=1, source_target_pairs={{16,8},{8,16},{32,24},{24,32},{48,40},{40,48},{64,56},{56,64},{80,... | collective-permute-start | bytes 3145736 | tf_op jit(solution)/shard_map/ppermute | solution.py:311
  10.2 13.4 %copy-start.6 = (f32[512,256]{1,0:T(8,128)}, f32[512,256]{1,0:T(8,128)S(1)}, u32[]{:S(2)}) copy-start(f32[512,256]{1,0:T(8,128)S(1)} %collective-permute-done.3.refs_2_) | copy-start | bytes 1572868
  10.2 13.4 %collective-permute-start.4 = (f32[512,256]{1,0:T(8,128)S(1)}, f32[512,256]{1,0:T(8,128)S(1)}, u32[]{:S(2)}, u32[]{:S(2)}) collective-permute-start(f32[512,256]{1,0:T(8,128)S(1)} %collective-permute-done.3.refs_2_), channel_id=1, source_target_pairs={{0,64},{120,56},{1,65},{121,57},{2,66},{122,58},{3,67},{123,59},{4... | collective-permute-start | bytes 1572872 | tf_op jit(solution)/shard_map/ppermute | solution.py:310
  12.6 24.9 %collective-permute-start.6 = (f32[512,256]{1,0:T(8,128)S(1)}, f32[512,256]{1,0:T(8,128)}, u32[]{:S(2)}, u32[]{:S(2)}) collective-permute-start(f32[512,256]{1,0:T(8,128)S(1)} %take.3), channel_id=1, source_target_pairs={{16,8},{8,16},{32,24},{24,32},{48,40},{40,48},{64,56},{56,64},{80,... | collective-permute-start | bytes 1572872 | tf_op jit(solution)/shard_map/ppermute | solution.py:307
  23.6 0.8 copy-start.7
  27.2 26.3 %collective-permute-start.5 = (f32[512,256]{1,0:T(8,128)S(1)}, f32[512,256]{1,0:T(8,128)S(1)}, u32[]{:S(2)}, u32[]{:S(2)}) collective-permute-start(f32[512,256]{1,0:T(8,128)S(1)} %rows.5.refs_4_), channel_id=1, source_target_pairs={{0,1},{1,2},{2,3},{3,4},{4,5},{5,6},{6,7},{8,9},{9,10},{10,11},{11... | collective-permute-start | bytes 1572872 | tf_op jit(solution)/shard_map/ppermute | solution.py:321
  34.4 30.4 %collective-permute-start.8 = (f32[512,256]{1,0:T(8,128)S(1)}, f32[512,256]{1,0:T(8,128)}, u32[]{:S(2)}, u32[]{:S(2)}) collective-permute-start(f32[512,256]{1,0:T(8,128)S(1)} %rows.7.refs_2_), channel_id=1, source_target_pairs={{1,0},{2,1},{3,2},{4,3},{5,4},{6,5},{7,6},{9,8},{10,9},{11,10},{12... | collective-permute-start | bytes 1572872 | tf_op jit(solution)/shard_map/ppermute | solution.py:321
  40.2 35.6 %collective-permute-start.7 = (f32[512,256]{1,0:T(8,128)S(1)}, f32[512,256]{1,0:T(8,128)}, u32[]{:S(2)}, u32[]{:S(2)}) collective-permute-start(f32[512,256]{1,0:T(8,128)S(1)} %rows.6.refs_1_), channel_id=1, source_target_pairs={{1,0},{2,1},{3,2},{4,3},{5,4},{6,5},{7,6},{9,8},{10,9},{11,10},{12... | collective-permute-start | bytes 1572872 | tf_op jit(solution)/shard_map/ppermute | solution.py:321
  46.7 35.6 %collective-permute-start.2 = (f32[512,256]{1,0:T(8,128)S(1)}, f32[512,256]{1,0:T(8,128)S(1)}, u32[]{:S(2)}, u32[]{:S(2)}) collective-permute-start(f32[512,256]{1,0:T(8,128)S(1)} %rows.4.refs_3_), channel_id=1, source_target_pairs={{0,1},{1,2},{2,3},{3,4},{4,5},{5,6},{6,7},{8,9},{9,10},{10,11},{11... | collective-permute-start | bytes 1572872 | tf_op jit(solution)/shard_map/ppermute | solution.py:321

commit v5 on v4

--- a/solution.py
+++ b/solution.py
@@ -252,18 +252,17 @@
     )(*args)
 
 
-def tail_kernel(west, band_high, band_low, part, out):
-    h, l = split(west[...])
-    band = slice(0, west.shape[1])
-    out[...] = part[...] + dot3(h, l, band_high[0, band], band_low[0, band])
-
-
-def apply_tail(west, bands, part):
+def tail_kernel(pair, band_rows, side, band_high, band_low, part, out):
+    h, l = split(side[...])
+    out[...] = part[...] + dot3(h, l, band_high[pair, band_rows], band_low[pair, band_rows])
+
+
+def apply_tail(side, bands, part, pair, band_rows):
     rows, width = part.shape
-    block = pl.BlockSpec((rows, PAIR), lambda i: (0, 0))
-    args = [held(a) for a in (west, *bands)]
-    return pl.pallas_call(
-        tail_kernel,
+    block = pl.BlockSpec((rows, PAIR), lambda i: (0, pair))
+    args = [held(a) for a in (side, *bands)]
+    return pl.pallas_call(
+        functools.partial(tail_kernel, pair, band_rows),
         grid=(1,),
         out_shape=jax.ShapeDtypeStruct((rows, width), jnp.float32),
         in_specs=[VMEM_SPEC] * 3 + [block],
@@ -302,12 +301,13 @@
 
     starts = (0, width - PAIR, PAIR, width - 2 * PAIR)
     chip = lax.ppermute(block, "row", chip_pairs)
-    (own0,) = take_columns(block, [(0, PAIR)])
-    own1, own2 = take_columns(block, [(width - PAIR, width), (PAIR, width - PAIR)])
+    own0, own1 = take_columns(block, [(0, PAIR), (width - PAIR, width)])
+    (own2,) = take_columns(block, [(PAIR, width - PAIR)])
     across0 = lax.ppermute(own0, "row", cross_pairs)
     ways = [pair for pair in cross_pairs if pair not in middle_pairs]
-    across1 = lax.ppermute(own1, "row", ways + [(middle - 1, 0), (middle, last)])
-    relay = lax.ppermute(across1, "row", [(0, middle), (last, middle - 1)])
+    across1 = lax.ppermute(own1, "row", ways)
+    ends = lax.ppermute(own1, "row", [(middle - 1, 0), (middle, last)])
+    relay = lax.ppermute(ends, "row", [(0, middle), (last, middle - 1)])
     across2 = lax.ppermute(own2, "row", cross_pairs)
     row_bands = build_bands(lat_row, fields, rows // PAIR, True)
     across = ([across0], [across1, relay], [across2], [across2])
@@ -320,9 +320,11 @@
         pairs = forward(col_count) if k % 2 else backward(col_count)
         side.append(lax.ppermute(half[k], "col", pairs))
     col_bands = build_bands(lat_col, fields, width // PAIR, False)
-    parts = [side[1], half[0], half[2], half[3], half[1], side[0], side[2]]
+    parts = [side[1], half[0], half[2], half[3], half[1], side[0]]
     part = apply_cols(parts, col_bands, width)
-    return apply_tail(side[3], col_bands, part)[None]
+    pairs = width // PAIR
+    part = apply_tail(side[2], col_bands, part, pairs - 1, slice(SPAN - PAIR, SPAN))
+    return apply_tail(side[3], col_bands, part, 0, slice(0, PAIR))[None]
 
 
 def solution(mesh):

time: 85 us -> 87.9 us (1.034)
  the two profiles are of different devices: /device:TPU:103 before, /device:TPU:45 now
where the time goes in v5:
time: 87.9 us; the launch traced here: 87.3 us
  waiting for transfers between devices  30.2 us (34%)
  Pallas kernels  28.1 us (32%)
  starting transfers between devices  27.2 us (31%)
  local copies, waits for them, and re-layouts  1.61 us (2%)
    ppermute x4, waiting for transfers between devices, body(): side.append(lax.ppermute(half[k], 'col', pairs))  20.6 us
    ppermute x4, starting transfers between devices, body(): side.append(lax.ppermute(half[k], 'col', pairs))  14.5 us
    pallas_call x4, Pallas kernels, apply_rows(): pl.pallas_call(functools.partial(rows_kernel, starts), out_shape=pltpu.VM...  10.7 us
    ppermute x1, waiting for transfers between devices, body(): across1 = lax.ppermute(own1, 'row', ways)  9.52 us
    pallas_call x1, Pallas kernels, apply_cols(): pl.pallas_call(cols_kernel, out_shape=jax.ShapeDtypeStruct((rows, width),...  5.14 us
    pallas_call x2, Pallas kernels, build_bands(): pl.pallas_call(functools.partial(band_kernel, transposed), out_shape=(ban...  5.01 us
    pallas_call x2, Pallas kernels, apply_tail(): pl.pallas_call(functools.partial(tail_kernel, pair, band_rows), grid=(1,)...  4.74 us
    ppermute x1, starting transfers between devices, body(): across2 = lax.ppermute(own2, 'row', cross_pairs)  3.44 us
  transfers between devices with their start and end apart: 10, of which 4 were waited for; matrix products, arithmetic and copies ran while one was open for 0% of the time, Pallas kernels for 30%

profile of v5, /device:TPU:45, one launch (start us, length us, event | category | flops | bytes accessed | tf_op | source)
XLA Modules:
  0.0 87.3 jit_solution(13598026281808020866)
XLA Ops:
  0.0 0.7 collective-permute-start
  0.7 1.4 %take.3 = (f32[512,256]{1,0:T(8,128)S(1)}, f32[512,256]{1,0:T(8,128)S(1)}) custom-call(f32[512,1024]{1,0:T(8,128)} %bitcast.23), custom_call_target="tpu_custom_call" | custom-call | tf_op jit(solution)/shard_map/take/pallas_call | solution.py:159
  2.0 0.0 copy-start
  2.1 0.0 copy-start.1
  2.1 0.0 copy-start.2
  2.1 0.0 copy-start.3
  2.1 0.0 copy-start.4
  2.1 0.0 copy-start.5
  2.1 1.6 %collective-permute-start.5 = (f32[512,256]{1,0:T(8,128)S(1)}, f32[512,256]{1,0:T(8,128)}, u32[]{:S(2)}, u32[]{:S(2)}) collective-permute-start(f32[512,256]{1,0:T(8,128)S(1)} %get-tuple-element.15), channel_id=1, source_target_pairs={{56,0},{64,120},{57,1},{65,121},{58,2},{66,122},{59,3},{67,123},{6... | collective-permute-start | bytes 1572872 | tf_op jit(solution)/shard_map/ppermute | solution.py:309
  3.7 1.2 %take.2 = f32[512,512]{1,0:T(8,128)S(1)} custom-call(f32[512,1024]{1,0:T(8,128)} %bitcast.24), custom_call_target="tpu_custom_call" | custom-call | tf_op jit(solution)/shard_map/take/pallas_call | solution.py:159
  4.9 3.4 %collective-permute-start.1 = (f32[512,512]{1,0:T(8,128)S(1)}, f32[512,512]{1,0:T(8,128)}, u32[]{:S(2)}, u32[]{:S(2)}) collective-permute-start(f32[512,512]{1,0:T(8,128)S(1)} %take.2), channel_id=1, source_target_pairs={{16,8},{8,16},{32,24},{24,32},{48,40},{40,48},{64,56},{56,64},{80,... | collective-permute-start | bytes 3145736 | tf_op jit(solution)/shard_map/ppermute | solution.py:311
  8.4 2.1 %collective-permute-start.4 = (f32[512,256]{1,0:T(8,128)S(1)}, f32[512,256]{1,0:T(8,128)S(1)}, u32[]{:S(2)}, u32[]{:S(2)}) collective-permute-start(f32[512,256]{1,0:T(8,128)S(1)} %get-tuple-element.15), channel_id=1, source_target_pairs={{16,8},{8,16},{32,24},{24,32},{48,40},{40,48},{80,72},{72,80},{96,... | collective-permute-start | bytes 1572872 | tf_op jit(solution)/shard_map/ppermute | solution.py:308
  10.5 0.0 collective-permute-done.5
  10.5 1.5 %collective-permute-start.6 = (f32[512,256]{1,0:T(8,128)}, f32[512,256]{1,0:T(8,128)}, u32[]{:S(2)}, u32[]{:S(2)}) collective-permute-start(f32[512,256]{1,0:T(8,128)} %collective-permute-done.5), channel_id=1, source_target_pairs={{0,64},{120,56},{1,65},{121,57},{2,66},{122,58},{3,67},{123,59},{4... | collective-permute-start | bytes 1572872 | tf_op jit(solution)/shard_map/ppermute | solution.py:310
  12.0 3.4 %collective-permute-start.8 = (f32[512,256]{1,0:T(8,128)S(1)}, f32[512,256]{1,0:T(8,128)S(1)}, u32[]{:S(2)}, u32[]{:S(2)}) collective-permute-start(f32[512,256]{1,0:T(8,128)S(1)} %get-tuple-element.16), channel_id=1, source_target_pairs={{16,8},{8,16},{32,24},{24,32},{48,40},{40,48},{64,56},{56,64},{80,... | collective-permute-start | bytes 1572872 | tf_op jit(solution)/shard_map/ppermute | solution.py:306
  15.4 0.0 copy-done
  15.4 0.0 copy-done.1
  15.4 0.0 copy-done.2
  15.4 0.0 copy-done.3
  15.5 0.0 copy-done.4
  15.5 0.0 copy-done.5
  15.5 2.0 %row_bands.1 = (bf16[2,256,1280]{2,1,0:T(8,128)(2,1)S(1)}, bf16[2,256,1280]{2,1,0:T(8,128)(2,1)S(1)}) custom-call(s32[1]{0:T(128)} %bitcast.place, s32[64,128]{1,0:T(8,128)S(1)} %bitcast.10, s32[64,128]{1,0:T(8,128)S(1)} %bitcast.12, s32[64,128]{1,0:T(8,128)S(1)} %bitcast.14, f32[64,128]{1,0:T(8,128)S(1)} %bitcast.16, f32[64,128]{1,0:T(8,128)S(1)} %bitcast.18, ...), custom_call_target="tpu_custom_call" | custom-call | tf_op jit(solution)/shard_map/row_bands/pallas_call | solution.py:125
  17.4 9.5 %collective-permute-done.4.refs_2_ = f32[512,256]{1,0:T(8,128)S(1)} collective-permute-done((f32[512,256]{1,0:T(8,128)S(1)}, f32[512,256]{1,0:T(8,128)S(1)}, u32[]{:S(2)}, u32[]{:S(2)}) %collective-permute-start.4) | collective-permute-done | bytes 524320 | tf_op jit(solution)/shard_map/ppermute | solution.py:308
  27.0 0.0 copy-start.6
  27.0 0.0 collective-permute-done.6.refs_3_
  27.0 0.0 collective-permute-done.refs_1_
  27.0 0.8 copy-done.6
  27.8 2.8 %rows.6.refs_4_ = f32[512,256]{1,0:T(8,128)S(1)} custom-call(s32[1]{0:T(128)} %bitcast.place, f32[512,1024]{1,0:T(8,128)} %bitcast.25, f32[512,1024]{1,0:T(8,128)} %collective-permute-done.refs_1_, f32[512,256]{1,0:T(8,128)} %copy-done.6, f32[512,256]{1,0:T(8,128)} %collective-permute-done.6.refs_3_, ...), custom_call_target="tpu_custom_call" | custom-call | tf_op jit(solution)/shard_map/rows/pallas_call | solution.py:207
  30.6 3.9 %collective-permute-start.7 = (f32[512,256]{1,0:T(8,128)S(1)}, f32[512,256]{1,0:T(8,128)S(1)}, u32[]{:S(2)}, u32[]{:S(2)}) collective-permute-start(f32[512,256]{1,0:T(8,128)S(1)} %rows.6.refs_4_), channel_id=1, source_target_pairs={{0,1},{1,2},{2,3},{3,4},{4,5},{5,6},{6,7},{8,9},{9,10},{10,11},{11... | collective-permute-start | bytes 1572872 | tf_op jit(solution)/shard_map/ppermute | solution.py:321
  34.5 0.0 collective-permute-done.8.refs_2_
  34.5 0.0 copy-start.7
  34.5 0.8 copy-done.7
  35.3 2.6 %rows.7.refs_1_ = f32[512,256]{1,0:T(8,128)S(1)} custom-call(s32[1]{0:T(128)} %bitcast.place, f32[512,1024]{1,0:T(8,128)} %bitcast.26, f32[512,1024]{1,0:T(8,128)} %collective-permute-done.refs_1_, f32[512,256]{1,0:T(8,128)} %copy-done.7, bf16[2,256,1280]{2,1,0:T(8,128)(2,1)S(1)} %get-tuple-element.11.refs_3_.refs_4_, ...), custom_call_target="tpu_custom_call" | custom-call | tf_op jit(solution)/shard_map/rows/pallas_call | solution.py:207
  37.9 3.8 %collective-permute-start.9 = (f32[512,256]{1,0:T(8,128)S(1)}, f32[512,256]{1,0:T(8,128)S(1)}, u32[]{:S(2)}, u32[]{:S(2)}) collective-permute-start(f32[512,256]{1,0:T(8,128)S(1)} %rows.7.refs_1_), channel_id=1, source_target_pairs={{1,0},{2,1},{3,2},{4,3},{5,4},{6,5},{7,6},{9,8},{10,9},{11,10},{12... | collective-permute-start | bytes 1572872 | tf_op jit(solution)/shard_map/ppermute | solution.py:321
  41.7 0.0 collective-permute-done.1.refs_2_
  41.7 2.6 %rows.5.refs_2_ = f32[512,256]{1,0:T(8,128)S(1)} custom-call(s32[1]{0:T(128)} %bitcast.place, f32[512,1024]{1,0:T(8,128)} %bitcast.27, f32[512,1024]{1,0:T(8,128)} %collective-permute-done.refs_1_, f32[512,512]{1,0:T(8,128)} %collective-permute-done.1.refs_2_, bf16[2,256,1280]{2,1,0:T(8,128)(2,1)S(1)} %get-tuple-element.11.refs_3_.refs_4_, ...), custom_call_target="tpu_custom_call" | custom-call | tf_op jit(solution)/shard_map/rows/pallas_call | solution.py:207
  44.3 3.0 %collective-permute-start.3 = (f32[512,256]{1,0:T(8,128)S(1)}, f32[512,256]{1,0:T(8,128)}, u32[]{:S(2)}, u32[]{:S(2)}) collective-permute-start(f32[512,256]{1,0:T(8,128)S(1)} %rows.5.refs_2_), channel_id=1, source_target_pairs={{1,0},{2,1},{3,2},{4,3},{5,4},{6,5},{7,6},{9,8},{10,9},{11,10},{12... | collective-permute-start | bytes 1572872 | tf_op jit(solution)/shard_map/ppermute | solution.py:321
  47.4 2.6 %rows.4.refs_3_ = f32[512,256]{1,0:T(8,128)S(1)} custom-call(s32[1]{0:T(128)} %bitcast.place, f32[512,1024]{1,0:T(8,128)} %bitcast.28, f32[512,1024]{1,0:T(8,128)} %collective-permute-done.refs_1_, f32[512,512]{1,0:T(8,128)} %collective-permute-done.1.refs_2_, bf16[2,256,1280]{2,1,0:T(8,128)(2,1)S(1)} %get-tuple-element.11.refs_3_.refs_4_, ...), custom_call_target="tpu_custom_call" | custom-call | tf_op jit(solution)/shard_map/rows/pallas_call | solution.py:207
  50.0 3.8 %collective-permute-start.2 = (f32[512,256]{1,0:T(8,128)S(1)}, f32[512,256]{1,0:T(8,128)}, u32[]{:S(2)}, u32[]{:S(2)}) collective-permute-start(f32[512,256]{1,0:T(8,128)S(1)} %rows.4.refs_3_), channel_id=1, source_target_pairs={{0,1},{1,2},{2,3},{3,4},{4,5},{5,6},{6,7},{8,9},{9,10},{10,11},{11... | collective-permute-start | bytes 1572872 | tf_op jit(solution)/shard_map/ppermute | solution.py:321
  53.8 3.1 %col_bands.1 = (bf16[4,1280,256]{2,1,0:T(8,128)(2,1)S(1)}, bf16[4,1280,256]{2,1,0:T(8,128)(2,1)S(1)}) custom-call(s32[1]{0:T(128)} %bitcast.8.place, s32[64,128]{1,0:T(8,128)S(1)} %bitcast.11, s32[64,128]{1,0:T(8,128)S(1)} %bitcast.13, s32[64,128]{1,0:T(8,128)S(1)} %bitcast.15, f32[64,128]{1,0:T(8,128)S(1)} %bitcast.17, f32[64,128]{1,0:T(8,128)S(1)} %bitcast.19, ...), custom_call_target="tpu_custom_call" | custom-call | tf_op jit(solution)/shard_map/col_bands/pallas_call | solution.py:125
  56.8 11.7 %collective-permute-done.7.refs_0_ = f32[512,256]{1,0:T(8,128)S(1)} collective-permute-done((f32[512,256]{1,0:T(8,128)S(1)}, f32[512,256]{1,0:T(8,128)S(1)}, u32[]{:S(2)}, u32[]{:S(2)}) %collective-permute-start.7) | collective-permute-done | bytes 524320 | tf_op jit(solution)/shard_map/ppermute | solution.py:321
  68.5 2.7 %collective-permute-done.9.refs_5_ = f32[512,256]{1,0:T(8,128)S(1)} collective-permute-done((f32[512,256]{1,0:T(8,128)S(1)}, f32[512,256]{1,0:T(8,128)S(1)}, u32[]{:S(2)}, u32[]{:S(2)}) %collective-permute-start.9) | collective-permute-done | bytes 524320 | tf_op jit(solution)/shard_map/ppermute | solution.py:321
  71.3 5.1 %cols.1.part = f32[512,1024]{1,0:T(8,128)} custom-call(f32[512,256]{1,0:T(8,128)S(1)} %collective-permute-done.7.refs_0_, f32[512,256]{1,0:T(8,128)S(1)} %rows.7.refs_1_, f32[512,256]{1,0:T(8,128)S(1)} %rows.5.refs_2_, f32[512,256]{1,0:T(8,128)S(1)} %rows.4.refs_3_, f32[512,256]{1,0:T(8,128)S(1)} %rows.6.refs_4_, ...), custom_call_target="tpu_custom_call" | custom-call | tf_op jit(solution)/shard_map/cols/pallas_call | solution.py:244
  76.4 6.2 %collective-permute-done.3.side = f32[512,256]{1,0:T(8,128)} collective-permute-done((f32[512,256]{1,0:T(8,128)S(1)}, f32[512,256]{1,0:T(8,128)}, u32[]{:S(2)}, u32[]{:S(2)}) %collective-permute-start.3) | collective-permute-done | bytes 524320 | tf_op jit(solution)/shard_map/ppermute | solution.py:321
  82.6 2.4 %tail.2.part = f32[512,1024]{1,0:T(8,128)} custom-call(f32[512,256]{1,0:T(8,128)} %collective-permute-done.3.side, bf16[4,1280,256]{2,1,0:T(8,128)(2,1)S(1)} %get-tuple-element.13.refs_6_.band_high, bf16[4,1280,256]{2,1,0:T(8,128)(2,1)S(1)} %get-tuple-element.14.refs_7_.band_low, f32[512,1024]{1,0:T(8,128)} %cols.1.part), custom_call_target="tpu_custom_call", output_to_operand_aliasing={{}: (3, {})} | custom-call | tf_op jit(solution)/shard_map/tail/pallas_call | solution.py:264
  85.0 0.0 collective-permute-done.2.side
  85.0 2.4 %tail.3 = f32[512,1024]{1,0:T(8,128)} custom-call(f32[512,256]{1,0:T(8,128)} %collective-permute-done.2.side, bf16[4,1280,256]{2,1,0:T(8,128)(2,1)S(1)} %get-tuple-element.13.refs_6_.band_high, bf16[4,1280,256]{2,1,0:T(8,128)(2,1)S(1)} %get-tuple-element.14.refs_7_.band_low, f32[512,1024]{1,0:T(8,128)} %tail.2.part), custom_call_target="tpu_custom_call", output_to_operand_aliasing={{}: (3, {})} | custom-call | tf_op jit(solution)/shard_map/tail/pallas_call | solution.py:264
Async XLA Ops:
  0.0 27.0 %collective-permute-start = (f32[512,1024]{1,0:T(8,128)}, f32[512,1024]{1,0:T(8,128)}, u32[]{:S(2)}, u32[]{:S(2)}) collective-permute-start(f32[512,1024]{1,0:T(8,128)} %bitcast.22), channel_id=1, source_target_pairs={{0,8},{8,0},{16,24},{24,16},{32,40},{40,32},{48,56},{56,48},{64,72... | collective-permute-start | bytes 6291464 | tf_op jit(solution)/shard_map/ppermute | solution.py:303
  2.0 13.4 %copy-start = (s32[1,1,8192]{2,1,0:T(1,128)S(1)}, s32[1,1,8192]{2,1,0:T(1,128)}, u32[]{:S(2)}) copy-start(s32[1,1,8192]{2,1,0:T(1,128)} %param.8) | copy-start | bytes 98308
  2.1 13.4 %copy-start.1 = (s32[1,1,8192]{2,1,0:T(1,128)S(1)}, s32[1,1,8192]{2,1,0:T(1,128)}, u32[]{:S(2)}) copy-start(s32[1,1,8192]{2,1,0:T(1,128)} %param.9) | copy-start | bytes 98308
  2.1 13.4 %copy-start.2 = (s32[1,1,8192]{2,1,0:T(1,128)S(1)}, s32[1,1,8192]{2,1,0:T(1,128)}, u32[]{:S(2)}) copy-start(s32[1,1,8192]{2,1,0:T(1,128)} %param.10) | copy-start | bytes 98308
  2.1 13.4 %copy-start.3 = (f32[1,1,8192]{2,1,0:T(1,128)S(1)}, f32[1,1,8192]{2,1,0:T(1,128)}, u32[]{:S(2)}) copy-start(f32[1,1,8192]{2,1,0:T(1,128)} %param.11) | copy-start | bytes 98308
  2.1 13.4 %copy-start.4 = (f32[1,8192]{1,0:T(1,128)S(1)}, f32[1,8192]{1,0:T(1,128)}, u32[]{:S(2)}) copy-start(f32[1,8192]{1,0:T(1,128)} %param.12) | copy-start | bytes 98308
  2.1 13.4 %copy-start.5 = (f32[1,8192]{1,0:T(1,128)S(1)}, f32[1,8192]{1,0:T(1,128)}, u32[]{:S(2)}) copy-start(f32[1,8192]{1,0:T(1,128)} %param.13) | copy-start | bytes 98308
  2.1 8.4 %collective-permute-start.5 = (f32[512,256]{1,0:T(8,128)S(1)}, f32[512,256]{1,0:T(8,128)}, u32[]{:S(2)}, u32[]{:S(2)}) collective-permute-start(f32[512,256]{1,0:T(8,128)S(1)} %get-tuple-element.15), channel_id=1, source_target_pairs={{56,0},{64,120},{57,1},{65,121},{58,2},{66,122},{59,3},{67,123},{6... | collective-permute-start | bytes 1572872 | tf_op jit(solution)/shard_map/ppermute | solution.py:309
  4.9 36.8 %collective-permute-start.1 = (f32[512,512]{1,0:T(8,128)S(1)}, f32[512,512]{1,0:T(8,128)}, u32[]{:S(2)}, u32[]{:S(2)}) collective-permute-start(f32[512,512]{1,0:T(8,128)S(1)} %take.2), channel_id=1, source_target_pairs={{16,8},{8,16},{32,24},{24,32},{48,40},{40,48},{64,56},{56,64},{80,... | collective-permute-start | bytes 3145736 | tf_op jit(solution)/shard_map/ppermute | solution.py:311
  8.4 18.6 %collective-permute-start.4 = (f32[512,256]{1,0:T(8,128)S(1)}, f32[512,256]{1,0:T(8,128)S(1)}, u32[]{:S(2)}, u32[]{:S(2)}) collective-permute-start(f32[512,256]{1,0:T(8,128)S(1)} %get-tuple-element.15), channel_id=1, source_target_pairs={{16,8},{8,16},{32,24},{24,32},{48,40},{40,48},{80,72},{72,80},{96,... | collective-permute-start | bytes 1572872 | tf_op jit(solution)/shard_map/ppermute | solution.py:308
  10.5 16.4 %collective-permute-start.6 = (f32[512,256]{1,0:T(8,128)}, f32[512,256]{1,0:T(8,128)}, u32[]{:S(2)}, u32[]{:S(2)}) collective-permute-start(f32[512,256]{1,0:T(8,128)} %collective-permute-done.5), channel_id=1, source_target_pairs={{0,64},{120,56},{1,65},{121,57},{2,66},{122,58},{3,67},{123,59},{4... | collective-permute-start | bytes 1572872 | tf_op jit(solution)/shard_map/ppermute | solution.py:310
  12.0 22.5 %collective-permute-start.8 = (f32[512,256]{1,0:T(8,128)S(1)}, f32[512,256]{1,0:T(8,128)S(1)}, u32[]{:S(2)}, u32[]{:S(2)}) collective-permute-start(f32[512,256]{1,0:T(8,128)S(1)} %get-tuple-element.16), channel_id=1, source_target_pairs={{16,8},{8,16},{32,24},{24,32},{48,40},{40,48},{64,56},{56,64},{80,... | collective-permute-start | bytes 1572872 | tf_op jit(solution)/shard_map/ppermute | solution.py:306
  27.0 0.8 copy-start.6
  30.6 37.9 %collective-permute-start.7 = (f32[512,256]{1,0:T(8,128)S(1)}, f32[512,256]{1,0:T(8,128)S(1)}, u32[]{:S(2)}, u32[]{:S(2)}) collective-permute-start(f32[512,256]{1,0:T(8,128)S(1)} %rows.6.refs_4_), channel_id=1, source_target_pairs={{0,1},{1,2},{2,3},{3,4},{4,5},{5,6},{6,7},{8,9},{9,10},{10,11},{11... | collective-permute-start | bytes 1572872 | tf_op jit(solution)/shard_map/ppermute | solution.py:321
  34.5 0.8 copy-start.7
  37.9 33.3 %collective-permute-start.9 = (f32[512,256]{1,0:T(8,128)S(1)}, f32[512,256]{1,0:T(8,128)S(1)}, u32[]{:S(2)}, u32[]{:S(2)}) collective-permute-start(f32[512,256]{1,0:T(8,128)S(1)} %rows.7.refs_1_), channel_id=1, source_target_pairs={{1,0},{2,1},{3,2},{4,3},{5,4},{6,5},{7,6},{9,8},{10,9},{11,10},{12... | collective-permute-start | bytes 1572872 | tf_op jit(solution)/shard_map/ppermute | solution.py:321
  44.3 38.3 %collective-permute-start.3 = (f32[512,256]{1,0:T(8,128)S(1)}, f32[512,256]{1,0:T(8,128)}, u32[]{:S(2)}, u32[]{:S(2)}) collective-permute-start(f32[512,256]{1,0:T(8,128)S(1)} %rows.5.refs_2_), channel_id=1, source_target_pairs={{1,0},{2,1},{3,2},{4,3},{5,4},{6,5},{7,6},{9,8},{10,9},{11,10},{12... | collective-permute-start | bytes 1572872 | tf_op jit(solution)/shard_map/ppermute | solution.py:321
  50.0 35.0 %collective-permute-start.2 = (f32[512,256]{1,0:T(8,128)S(1)}, f32[512,256]{1,0:T(8,128)}, u32[]{:S(2)}, u32[]{:S(2)}) collective-permute-start(f32[512,256]{1,0:T(8,128)S(1)} %rows.4.refs_3_), channel_id=1, source_target_pairs={{0,1},{1,2},{2,3},{3,4},{4,5},{5,6},{6,7},{8,9},{9,10},{10,11},{11... | collective-permute-start | bytes 1572872 | tf_op jit(solution)/shard_map/ppermute | solution.py:321

commit v6 on v5

--- a/solution.py
+++ b/solution.py
@@ -283,11 +283,8 @@
     forward = lambda n: [(i, i + 1) for i in range(n - 1)]
     backward = lambda n: [(i + 1, i) for i in range(n - 1)]
 
-    last = row_count - 1
-    middle = row_count // 2
     chip_pairs = [(i, i ^ 1) for i in range(row_count)]
-    cross_pairs = [((i + 1 ^ 1) - 1, i) for i in range(1, last)]
-    middle_pairs = [(middle - 1, middle), (middle, middle - 1)]
+    cross_pairs = [((i + 1 ^ 1) - 1, i) for i in range(1, row_count - 1)]
 
     fields = [
         a.reshape(NLAT, NLON)
@@ -301,21 +298,15 @@
 
     starts = (0, width - PAIR, PAIR, width - 2 * PAIR)
     chip = lax.ppermute(block, "row", chip_pairs)
-    own0, own1 = take_columns(block, [(0, PAIR), (width - PAIR, width)])
-    (own2,) = take_columns(block, [(PAIR, width - PAIR)])
+    (own0,) = take_columns(block, [(0, PAIR)])
+    (own1,) = take_columns(block, [(PAIR, width)])
     across0 = lax.ppermute(own0, "row", cross_pairs)
-    ways = [pair for pair in cross_pairs if pair not in middle_pairs]
-    across1 = lax.ppermute(own1, "row", ways)
-    ends = lax.ppermute(own1, "row", [(middle - 1, 0), (middle, last)])
-    relay = lax.ppermute(ends, "row", [(0, middle), (last, middle - 1)])
-    across2 = lax.ppermute(own2, "row", cross_pairs)
+    across1 = lax.ppermute(own1, "row", cross_pairs)
     row_bands = build_bands(lat_row, fields, rows // PAIR, True)
-    across = ([across0], [across1, relay], [across2], [across2])
-    offset = ([0], [0, 0], [0], [width - 3 * PAIR])
     half, side = [], []
     for k in range(4):
-        sources = [block, chip] + across[k]
-        begins = [starts[k]] * 2 + offset[k]
+        sources = [block, chip, across1 if k else across0]
+        begins = [starts[k], starts[k], starts[k] - PAIR if k else 0]
         half.append(apply_rows(lat_row, PAIR, sources, begins, row_bands))
         pairs = forward(col_count) if k % 2 else backward(col_count)
         side.append(lax.ppermute(half[k], "col", pairs))

time: 87.9 us -> 84.9 us (0.966)
  the two profiles are of different devices: /device:TPU:45 before, /device:TPU:10 now
where the time goes in v6:
time: 84.9 us; the launch traced here: 84.3 us
  starting transfers between devices  30.4 us (36%)
  Pallas kernels  28.8 us (34%)
  waiting for transfers between devices  24.1 us (28%)
    ppermute x4, starting transfers between devices, body(): side.append(lax.ppermute(half[k], 'col', pairs))  22.4 us
    ppermute x1, waiting for transfers between devices, body(): across1 = lax.ppermute(own1, 'row', cross_pairs)  13.1 us
    ppermute x4, waiting for transfers between devices, body(): side.append(lax.ppermute(half[k], 'col', pairs))  10.9 us
    pallas_call x4, Pallas kernels, apply_rows(): pl.pallas_call(functools.partial(rows_kernel, starts), out_shape=pltpu.VM...  10.5 us
    pallas_call x1, Pallas kernels, apply_cols(): pl.pallas_call(cols_kernel, out_shape=jax.ShapeDtypeStruct((rows, width),...  6.18 us
    ppermute x1, starting transfers between devices, body(): across1 = lax.ppermute(own1, 'row', cross_pairs)  6.08 us
    pallas_call x2, Pallas kernels, build_bands(): pl.pallas_call(functools.partial(band_kernel, transposed), out_shape=(ban...  5.03 us
    pallas_call x2, Pallas kernels, apply_tail(): pl.pallas_call(functools.partial(tail_kernel, pair, band_rows), grid=(1,)...  4.58 us
  transfers between devices with their start and end apart: 7, of which 3 were waited for; matrix products, arithmetic and copies ran while one was open for 0% of the time, Pallas kernels for 31%

profile of v6, /device:TPU:10, one launch (start us, length us, event | category | flops | bytes accessed | tf_op | source)
XLA Modules:
  0.0 84.3 jit_solution(1898189602630539674)
XLA Ops:
  0.0 0.0 collective-permute-start
  0.0 1.4 %take.2 = f32[512,768]{1,0:T(8,128)S(1)} custom-call(f32[512,1024]{1,0:T(8,128)} %bitcast.23), custom_call_target="tpu_custom_call" | custom-call | tf_op jit(solution)/shard_map/take/pallas_call | solution.py:159
  1.4 0.0 copy-start
  1.4 0.0 copy-start.1
  1.4 0.0 copy-start.2
  1.4 0.0 copy-start.3
  1.4 0.0 copy-start.4
  1.5 0.0 copy-start.5
  1.5 6.1 %collective-permute-start.1 = (f32[512,768]{1,0:T(8,128)S(1)}, f32[512,768]{1,0:T(8,128)}, u32[]{:S(2)}, u32[]{:S(2)}) collective-permute-start(f32[512,768]{1,0:T(8,128)S(1)} %take.2), channel_id=1, source_target_pairs={{16,8},{8,16},{32,24},{24,32},{48,40},{40,48},{64,56},{56,64},{80,... | collective-permute-start | bytes 4718600 | tf_op jit(solution)/shard_map/ppermute | solution.py:304
  7.6 1.1 %take.3 = f32[512,256]{1,0:T(8,128)S(1)} custom-call(f32[512,1024]{1,0:T(8,128)} %bitcast.24), custom_call_target="tpu_custom_call" | custom-call | tf_op jit(solution)/shard_map/take/pallas_call | solution.py:159
  8.7 1.9 %collective-permute-start.5 = (f32[512,256]{1,0:T(8,128)S(1)}, f32[512,256]{1,0:T(8,128)S(1)}, u32[]{:S(2)}, u32[]{:S(2)}) collective-permute-start(f32[512,256]{1,0:T(8,128)S(1)} %take.3), channel_id=1, source_target_pairs={{16,8},{8,16},{32,24},{24,32},{48,40},{40,48},{64,56},{56,64},{80,... | collective-permute-start | bytes 1572872 | tf_op jit(solution)/shard_map/ppermute | solution.py:303
  10.6 0.0 copy-done
  10.6 0.0 copy-done.1
  10.6 0.0 copy-done.2
  10.7 0.0 copy-done.3
  10.7 0.0 copy-done.4
  10.7 0.0 copy-done.5
  10.7 1.9 %row_bands.1 = (bf16[2,256,1280]{2,1,0:T(8,128)(2,1)S(1)}, bf16[2,256,1280]{2,1,0:T(8,128)(2,1)S(1)}) custom-call(s32[1]{0:T(128)} %bitcast.place, s32[64,128]{1,0:T(8,128)S(1)} %bitcast.10, s32[64,128]{1,0:T(8,128)S(1)} %bitcast.12, s32[64,128]{1,0:T(8,128)S(1)} %bitcast.14, f32[64,128]{1,0:T(8,128)S(1)} %bitcast.16, f32[64,128]{1,0:T(8,128)S(1)} %bitcast.18, ...), custom_call_target="tpu_custom_call" | custom-call | tf_op jit(solution)/shard_map/row_bands/pallas_call | solution.py:125
  12.6 13.1 %collective-permute-done.1.refs_2_ = f32[512,768]{1,0:T(8,128)} collective-permute-done((f32[512,768]{1,0:T(8,128)S(1)}, f32[512,768]{1,0:T(8,128)}, u32[]{:S(2)}, u32[]{:S(2)}) %collective-permute-start.1) | collective-permute-done | bytes 1572896 | tf_op jit(solution)/shard_map/ppermute | solution.py:304
  25.7 0.0 collective-permute-done.refs_1_
  25.7 2.6 %rows.6.refs_4_ = f32[512,256]{1,0:T(8,128)S(1)} custom-call(s32[1]{0:T(128)} %bitcast.place, f32[512,1024]{1,0:T(8,128)} %bitcast.25, f32[512,1024]{1,0:T(8,128)} %collective-permute-done.refs_1_, f32[512,768]{1,0:T(8,128)} %collective-permute-done.1.refs_2_, bf16[2,256,1280]{2,1,0:T(8,128)(2,1)S(1)} %get-tuple-element.9.refs_3_, ...), custom_call_target="tpu_custom_call" | custom-call | tf_op jit(solution)/shard_map/rows/pallas_call | solution.py:207
  28.4 4.5 %collective-permute-start.4 = (f32[512,256]{1,0:T(8,128)S(1)}, f32[512,256]{1,0:T(8,128)S(1)}, u32[]{:S(2)}, u32[]{:S(2)}) collective-permute-start(f32[512,256]{1,0:T(8,128)S(1)} %rows.6.refs_4_), channel_id=1, source_target_pairs={{0,1},{1,2},{2,3},{3,4},{4,5},{5,6},{6,7},{8,9},{9,10},{10,11},{11... | collective-permute-start | bytes 1572872 | tf_op jit(solution)/shard_map/ppermute | solution.py:312
  32.9 0.0 collective-permute-done.5.refs_2_
  32.9 0.0 copy-start.6
  32.9 0.8 copy-done.6
  33.7 2.6 %rows.7.refs_1_ = f32[512,256]{1,0:T(8,128)S(1)} custom-call(s32[1]{0:T(128)} %bitcast.place, f32[512,1024]{1,0:T(8,128)} %bitcast.26, f32[512,1024]{1,0:T(8,128)} %collective-permute-done.refs_1_, f32[512,256]{1,0:T(8,128)} %copy-done.6, bf16[2,256,1280]{2,1,0:T(8,128)(2,1)S(1)} %get-tuple-element.9.refs_3_, bf16[2,256,1280]{2,1,0:T(8,128)(2,1)S(1)} %get-tuple-element.10.refs_4_), custom_call_target="tpu_custom_call" | custom-call | tf_op jit(solution)/shard_map/rows/pallas_call | solution.py:207
  36.3 3.8 %collective-permute-start.6 = (f32[512,256]{1,0:T(8,128)S(1)}, f32[512,256]{1,0:T(8,128)}, u32[]{:S(2)}, u32[]{:S(2)}) collective-permute-start(f32[512,256]{1,0:T(8,128)S(1)} %rows.7.refs_1_), channel_id=1, source_target_pairs={{1,0},{2,1},{3,2},{4,3},{5,4},{6,5},{7,6},{9,8},{10,9},{11,10},{12... | collective-permute-start | bytes 1572872 | tf_op jit(solution)/shard_map/ppermute | solution.py:312
  40.1 2.6 %rows.5.refs_2_ = f32[512,256]{1,0:T(8,128)S(1)} custom-call(s32[1]{0:T(128)} %bitcast.place, f32[512,1024]{1,0:T(8,128)} %bitcast.27, f32[512,1024]{1,0:T(8,128)} %collective-permute-done.refs_1_, f32[512,768]{1,0:T(8,128)} %collective-permute-done.1.refs_2_, bf16[2,256,1280]{2,1,0:T(8,128)(2,1)S(1)} %get-tuple-element.9.refs_3_, ...), custom_call_target="tpu_custom_call" | custom-call | tf_op jit(solution)/shard_map/rows/pallas_call | solution.py:207
  42.7 3.6 %collective-permute-start.3 = (f32[512,256]{1,0:T(8,128)S(1)}, f32[512,256]{1,0:T(8,128)S(1)}, u32[]{:S(2)}, u32[]{:S(2)}) collective-permute-start(f32[512,256]{1,0:T(8,128)S(1)} %rows.5.refs_2_), channel_id=1, source_target_pairs={{1,0},{2,1},{3,2},{4,3},{5,4},{6,5},{7,6},{9,8},{10,9},{11,10},{12... | collective-permute-start | bytes 1572872 | tf_op jit(solution)/shard_map/ppermute | solution.py:312
  46.3 2.6 %rows.4.refs_3_ = f32[512,256]{1,0:T(8,128)S(1)} custom-call(s32[1]{0:T(128)} %bitcast.place, f32[512,1024]{1,0:T(8,128)} %bitcast.28, f32[512,1024]{1,0:T(8,128)} %collective-permute-done.refs_1_, f32[512,768]{1,0:T(8,128)} %collective-permute-done.1.refs_2_, bf16[2,256,1280]{2,1,0:T(8,128)(2,1)S(1)} %get-tuple-element.9.refs_3_, ...), custom_call_target="tpu_custom_call" | custom-call | tf_op jit(solution)/shard_map/rows/pallas_call | solution.py:207
  49.0 10.5 %collective-permute-start.2 = (f32[512,256]{1,0:T(8,128)S(1)}, f32[512,256]{1,0:T(8,128)}, u32[]{:S(2)}, u32[]{:S(2)}) collective-permute-start(f32[512,256]{1,0:T(8,128)S(1)} %rows.4.refs_3_), channel_id=1, source_target_pairs={{0,1},{1,2},{2,3},{3,4},{4,5},{5,6},{6,7},{8,9},{9,10},{10,11},{11... | collective-permute-start | bytes 1572872 | tf_op jit(solution)/shard_map/ppermute | solution.py:312
  59.5 3.1 %col_bands.1 = (bf16[4,1280,256]{2,1,0:T(8,128)(2,1)S(1)}, bf16[4,1280,256]{2,1,0:T(8,128)(2,1)S(1)}) custom-call(s32[1]{0:T(128)} %bitcast.8.place, s32[64,128]{1,0:T(8,128)S(1)} %bitcast.11, s32[64,128]{1,0:T(8,128)S(1)} %bitcast.13, s32[64,128]{1,0:T(8,128)S(1)} %bitcast.15, f32[64,128]{1,0:T(8,128)S(1)} %bitcast.17, f32[64,128]{1,0:T(8,128)S(1)} %bitcast.19, ...), custom_call_target="tpu_custom_call" | custom-call | tf_op jit(solution)/shard_map/col_bands/pallas_call | solution.py:125
  62.6 5.0 %collective-permute-done.4.refs_0_ = f32[512,256]{1,0:T(8,128)S(1)} collective-permute-done((f32[512,256]{1,0:T(8,128)S(1)}, f32[512,256]{1,0:T(8,128)S(1)}, u32[]{:S(2)}, u32[]{:S(2)}) %collective-permute-start.4) | collective-permute-done | bytes 524320 | tf_op jit(solution)/shard_map/ppermute | solution.py:312
  67.6 5.9 %collective-permute-done.6.refs_5_ = f32[512,256]{1,0:T(8,128)} collective-permute-done((f32[512,256]{1,0:T(8,128)S(1)}, f32[512,256]{1,0:T(8,128)}, u32[]{:S(2)}, u32[]{:S(2)}) %collective-permute-start.6) | collective-permute-done | bytes 524320 | tf_op jit(solution)/shard_map/ppermute | solution.py:312
  73.6 6.2 %cols.1.part = f32[512,1024]{1,0:T(8,128)} custom-call(f32[512,256]{1,0:T(8,128)S(1)} %collective-permute-done.4.refs_0_, f32[512,256]{1,0:T(8,128)S(1)} %rows.7.refs_1_, f32[512,256]{1,0:T(8,128)S(1)} %rows.5.refs_2_, f32[512,256]{1,0:T(8,128)S(1)} %rows.4.refs_3_, f32[512,256]{1,0:T(8,128)S(1)} %rows.6.refs_4_, f32[512,256]{1,0:T(8,128)} %collective-permute-done.6.refs_5_, ...), custom_call_target="tpu_custom_call" | custom-call | tf_op jit(solution)/shard_map/cols/pallas_call | solution.py:244
  79.7 0.0 collective-permute-done.3.side
  79.7 2.2 %tail.2.part = f32[512,1024]{1,0:T(8,128)} custom-call(f32[512,256]{1,0:T(8,128)S(1)} %collective-permute-done.3.side, bf16[4,1280,256]{2,1,0:T(8,128)(2,1)S(1)} %get-tuple-element.11.refs_6_.band_high, bf16[4,1280,256]{2,1,0:T(8,128)(2,1)S(1)} %get-tuple-element.12.refs_7_.band_low, f32[512,1024]{1,0:T(8,128)} %cols.1.part), custom_call_target="tpu_custom_call", output_to_operand_aliasing={{}: (3, {})} | custom-call | tf_op jit(solution)/shard_map/tail/pallas_call | solution.py:264
  82.0 0.0 collective-permute-done.2.side
  82.0 2.4 %tail.3 = f32[512,1024]{1,0:T(8,128)} custom-call(f32[512,256]{1,0:T(8,128)} %collective-permute-done.2.side, bf16[4,1280,256]{2,1,0:T(8,128)(2,1)S(1)} %get-tuple-element.11.refs_6_.band_high, bf16[4,1280,256]{2,1,0:T(8,128)(2,1)S(1)} %get-tuple-element.12.refs_7_.band_low, f32[512,1024]{1,0:T(8,128)} %tail.2.part), custom_call_target="tpu_custom_call", output_to_operand_aliasing={{}: (3, {})} | custom-call | tf_op jit(solution)/shard_map/tail/pallas_call | solution.py:264
Async XLA Ops:
  0.0 25.7 %collective-permute-start = (f32[512,1024]{1,0:T(8,128)}, f32[512,1024]{1,0:T(8,128)}, u32[]{:S(2)}, u32[]{:S(2)}) collective-permute-start(f32[512,1024]{1,0:T(8,128)} %bitcast.22), channel_id=1, source_target_pairs={{0,8},{8,0},{16,24},{24,16},{32,40},{40,32},{48,56},{56,48},{64,72... | collective-permute-start | bytes 6291464 | tf_op jit(solution)/shard_map/ppermute | solution.py:300
  1.4 9.2 %copy-start = (s32[1,1,8192]{2,1,0:T(1,128)S(1)}, s32[1,1,8192]{2,1,0:T(1,128)}, u32[]{:S(2)}) copy-start(s32[1,1,8192]{2,1,0:T(1,128)} %param.8) | copy-start | bytes 98308
  1.4 9.2 %copy-start.1 = (s32[1,1,8192]{2,1,0:T(1,128)S(1)}, s32[1,1,8192]{2,1,0:T(1,128)}, u32[]{:S(2)}) copy-start(s32[1,1,8192]{2,1,0:T(1,128)} %param.9) | copy-start | bytes 98308
  1.4 9.2 %copy-start.2 = (s32[1,1,8192]{2,1,0:T(1,128)S(1)}, s32[1,1,8192]{2,1,0:T(1,128)}, u32[]{:S(2)}) copy-start(s32[1,1,8192]{2,1,0:T(1,128)} %param.10) | copy-start | bytes 98308
  1.4 9.2 %copy-start.3 = (f32[1,1,8192]{2,1,0:T(1,128)S(1)}, f32[1,1,8192]{2,1,0:T(1,128)}, u32[]{:S(2)}) copy-start(f32[1,1,8192]{2,1,0:T(1,128)} %param.11) | copy-start | bytes 98308
  1.4 9.2 %copy-start.4 = (f32[1,8192]{1,0:T(1,128)S(1)}, f32[1,8192]{1,0:T(1,128)}, u32[]{:S(2)}) copy-start(f32[1,8192]{1,0:T(1,128)} %param.12) | copy-start | bytes 98308
  1.5 9.2 %copy-start.5 = (f32[1,8192]{1,0:T(1,128)S(1)}, f32[1,8192]{1,0:T(1,128)}, u32[]{:S(2)}) copy-start(f32[1,8192]{1,0:T(1,128)} %param.13) | copy-start | bytes 98308
  1.5 24.3 %collective-permute-start.1 = (f32[512,768]{1,0:T(8,128)S(1)}, f32[512,768]{1,0:T(8,128)}, u32[]{:S(2)}, u32[]{:S(2)}) collective-permute-start(f32[512,768]{1,0:T(8,128)S(1)} %take.2), channel_id=1, source_target_pairs={{16,8},{8,16},{32,24},{24,32},{48,40},{40,48},{64,56},{56,64},{80,... | collective-permute-start | bytes 4718600 | tf_op jit(solution)/shard_map/ppermute | solution.py:304
  8.7 24.2 %collective-permute-start.5 = (f32[512,256]{1,0:T(8,128)S(1)}, f32[512,256]{1,0:T(8,128)S(1)}, u32[]{:S(2)}, u32[]{:S(2)}) collective-permute-start(f32[512,256]{1,0:T(8,128)S(1)} %take.3), channel_id=1, source_target_pairs={{16,8},{8,16},{32,24},{24,32},{48,40},{40,48},{64,56},{56,64},{80,... | collective-permute-start | bytes 1572872 | tf_op jit(solution)/shard_map/ppermute | solution.py:303
  28.4 39.3 %collective-permute-start.4 = (f32[512,256]{1,0:T(8,128)S(1)}, f32[512,256]{1,0:T(8,128)S(1)}, u32[]{:S(2)}, u32[]{:S(2)}) collective-permute-start(f32[512,256]{1,0:T(8,128)S(1)} %rows.6.refs_4_), channel_id=1, source_target_pairs={{0,1},{1,2},{2,3},{3,4},{4,5},{5,6},{6,7},{8,9},{9,10},{10,11},{11... | collective-permute-start | bytes 1572872 | tf_op jit(solution)/shard_map/ppermute | solution.py:312
  32.9 0.8 copy-start.6
  36.3 37.2 %collective-permute-start.6 = (f32[512,256]{1,0:T(8,128)S(1)}, f32[512,256]{1,0:T(8,128)}, u32[]{:S(2)}, u32[]{:S(2)}) collective-permute-start(f32[512,256]{1,0:T(8,128)S(1)} %rows.7.refs_1_), channel_id=1, source_target_pairs={{1,0},{2,1},{3,2},{4,3},{5,4},{6,5},{7,6},{9,8},{10,9},{11,10},{12... | collective-permute-start | bytes 1572872 | tf_op jit(solution)/shard_map/ppermute | solution.py:312
  42.7 37.0 %collective-permute-start.3 = (f32[512,256]{1,0:T(8,128)S(1)}, f32[512,256]{1,0:T(8,128)S(1)}, u32[]{:S(2)}, u32[]{:S(2)}) collective-permute-start(f32[512,256]{1,0:T(8,128)S(1)} %rows.5.refs_2_), channel_id=1, source_target_pairs={{1,0},{2,1},{3,2},{4,3},{5,4},{6,5},{7,6},{9,8},{10,9},{11,10},{12... | collective-permute-start | bytes 1572872 | tf_op jit(solution)/shard_map/ppermute | solution.py:312
  49.0 33.0 %collective-permute-start.2 = (f32[512,256]{1,0:T(8,128)S(1)}, f32[512,256]{1,0:T(8,128)}, u32[]{:S(2)}, u32[]{:S(2)}) collective-permute-start(f32[512,256]{1,0:T(8,128)S(1)} %rows.4.refs_3_), channel_id=1, source_target_pairs={{0,1},{1,2},{2,3},{3,4},{4,5},{5,6},{6,7},{8,9},{9,10},{10,11},{11... | collective-permute-start | bytes 1572872 | tf_op jit(solution)/shard_map/ppermute | solution.py:312

commit v7 on v6

--- a/solution.py
+++ b/solution.py
@@ -299,14 +299,17 @@
     starts = (0, width - PAIR, PAIR, width - 2 * PAIR)
     chip = lax.ppermute(block, "row", chip_pairs)
     (own0,) = take_columns(block, [(0, PAIR)])
-    (own1,) = take_columns(block, [(PAIR, width)])
-    across0 = lax.ppermute(own0, "row", cross_pairs)
-    across1 = lax.ppermute(own1, "row", cross_pairs)
+    own1, own2 = take_columns(block, [(width - PAIR, width), (PAIR, width - PAIR)])
+    across0, across1, across2 = (
+        lax.ppermute(x, "row", cross_pairs) for x in (own0, own1, own2)
+    )
+    across = (across0, across1, across2, across2)
+    offset = (0, 0, 0, width - 3 * PAIR)
     row_bands = build_bands(lat_row, fields, rows // PAIR, True)
     half, side = [], []
     for k in range(4):
-        sources = [block, chip, across1 if k else across0]
-        begins = [starts[k], starts[k], starts[k] - PAIR if k else 0]
+        sources = [block, chip, across[k]]
+        begins = [starts[k], starts[k], offset[k]]
         half.append(apply_rows(lat_row, PAIR, sources, begins, row_bands))
         pairs = forward(col_count) if k % 2 else backward(col_count)
         side.append(lax.ppermute(half[k], "col", pairs))

time: 84.9 us -> 85.1 us (level)
  the two profiles are of different devices: /device:TPU:10 before, /device:TPU:101 now
where the time goes in v7:
time: 85.1 us; the launch traced here: 84.7 us
  waiting for transfers between devices  30 us (35%)
  Pallas kernels  28 us (33%)
  starting transfers between devices  24.8 us (29%)
  local copies, waits for them, and re-layouts  1.6 us (2%)
    ppermute x4, waiting for transfers between devices, body(): side.append(lax.ppermute(half[k], 'col', pairs))  19 us
    ppermute x4, starting transfers between devices, body(): side.append(lax.ppermute(half[k], 'col', pairs))  14.5 us
    ppermute x3, waiting for transfers between devices, body(): lax.ppermute(x, 'row', cross_pairs)  11.1 us
    pallas_call x4, Pallas kernels, apply_rows(): pl.pallas_call(functools.partial(rows_kernel, starts), out_shape=pltpu.VM...  10.4 us
    ppermute x3, starting transfers between devices, body(): lax.ppermute(x, 'row', cross_pairs)  9.59 us
    pallas_call x1, Pallas kernels, apply_cols(): pl.pallas_call(cols_kernel, out_shape=jax.ShapeDtypeStruct((rows, width),...  5.14 us
    pallas_call x2, Pallas kernels, build_bands(): pl.pallas_call(functools.partial(band_kernel, transposed), out_shape=(ban...  5 us
    pallas_call x2, Pallas kernels, apply_tail(): pl.pallas_call(functools.partial(tail_kernel, pair, band_rows), grid=(1,)...  4.74 us
  transfers between devices with their start and end apart: 8, of which 4 were waited for; matrix products, arithmetic and copies ran while one was open for 0% of the time, Pallas kernels for 30%

profile of v7, /device:TPU:101, one launch (start us, length us, event | category | flops | bytes accessed | tf_op | source)
XLA Modules:
  0.0 84.7 jit_solution(15373227004830570212)
XLA Ops:
  0.0 0.0 copy-start
  0.0 0.0 copy-start.1
  0.0 0.0 copy-start.2
  0.0 0.0 copy-start.3
  0.0 0.0 copy-start.4
  0.0 0.0 copy-start.5
  0.0 0.8 collective-permute-start
  0.8 1.5 %take.2 = (f32[512,256]{1,0:T(8,128)S(1)}, f32[512,512]{1,0:T(8,128)S(1)}) custom-call(f32[512,1024]{1,0:T(8,128)} %bitcast.23), custom_call_target="tpu_custom_call" | custom-call | tf_op jit(solution)/shard_map/take/pallas_call | solution.py:159
  2.3 1.9 %collective-permute-start.1 = (f32[512,512]{1,0:T(8,128)S(1)}, f32[512,512]{1,0:T(8,128)}, u32[]{:S(2)}, u32[]{:S(2)}) collective-permute-start(f32[512,512]{1,0:T(8,128)S(1)} %get-tuple-element.11), channel_id=1, source_target_pairs={{16,8},{8,16},{32,24},{24,32},{48,40},{40,48},{64,56},{56,64},{80,... | collective-permute-start | bytes 3145736 | tf_op jit(solution)/shard_map/ppermute | solution.py:304
  4.3 5.8 %collective-permute-start.4 = (f32[512,256]{1,0:T(8,128)S(1)}, f32[512,256]{1,0:T(8,128)S(1)}, u32[]{:S(2)}, u32[]{:S(2)}) collective-permute-start(f32[512,256]{1,0:T(8,128)S(1)} %get-tuple-element.16), channel_id=1, source_target_pairs={{16,8},{8,16},{32,24},{24,32},{48,40},{40,48},{64,56},{56,64},{80,... | collective-permute-start | bytes 1572872 | tf_op jit(solution)/shard_map/ppermute | solution.py:304
  10.0 1.1 %take.3 = f32[512,256]{1,0:T(8,128)S(1)} custom-call(f32[512,1024]{1,0:T(8,128)} %bitcast.24), custom_call_target="tpu_custom_call" | custom-call | tf_op jit(solution)/shard_map/take/pallas_call | solution.py:159
  11.2 1.9 %collective-permute-start.6 = (f32[512,256]{1,0:T(8,128)S(1)}, f32[512,256]{1,0:T(8,128)S(1)}, u32[]{:S(2)}, u32[]{:S(2)}) collective-permute-start(f32[512,256]{1,0:T(8,128)S(1)} %take.3), channel_id=1, source_target_pairs={{16,8},{8,16},{32,24},{24,32},{48,40},{40,48},{64,56},{56,64},{80,... | collective-permute-start | bytes 1572872 | tf_op jit(solution)/shard_map/ppermute | solution.py:304
  13.1 0.0 copy-done
  13.1 0.0 copy-done.1
  13.1 0.0 copy-done.2
  13.1 0.0 copy-done.3
  13.1 0.0 copy-done.4
  13.1 0.0 copy-done.5
  13.1 1.9 %row_bands.1 = (bf16[2,256,1280]{2,1,0:T(8,128)(2,1)S(1)}, bf16[2,256,1280]{2,1,0:T(8,128)(2,1)S(1)}) custom-call(s32[1]{0:T(128)} %bitcast.place, s32[64,128]{1,0:T(8,128)S(1)} %bitcast.10, s32[64,128]{1,0:T(8,128)S(1)} %bitcast.12, s32[64,128]{1,0:T(8,128)S(1)} %bitcast.14, f32[64,128]{1,0:T(8,128)S(1)} %bitcast.16, f32[64,128]{1,0:T(8,128)S(1)} %bitcast.18, ...), custom_call_target="tpu_custom_call" | custom-call | tf_op jit(solution)/shard_map/row_bands/pallas_call | solution.py:125
  15.1 11.1 %collective-permute-done.4.refs_2_ = f32[512,256]{1,0:T(8,128)S(1)} collective-permute-done((f32[512,256]{1,0:T(8,128)S(1)}, f32[512,256]{1,0:T(8,128)S(1)}, u32[]{:S(2)}, u32[]{:S(2)}) %collective-permute-start.4) | collective-permute-done | bytes 524320 | tf_op jit(solution)/shard_map/ppermute | solution.py:304
  26.2 0.0 copy-start.7
  26.2 0.0 collective-permute-done.refs_1_
  26.2 0.8 copy-done.7
  27.0 2.6 %rows.6.refs_4_ = f32[512,256]{1,0:T(8,128)S(1)} custom-call(s32[1]{0:T(128)} %bitcast.place, f32[512,1024]{1,0:T(8,128)} %bitcast.25, f32[512,1024]{1,0:T(8,128)} %collective-permute-done.refs_1_, f32[512,256]{1,0:T(8,128)} %copy-done.7, bf16[2,256,1280]{2,1,0:T(8,128)(2,1)S(1)} %get-tuple-element.12.refs_3_, ...), custom_call_target="tpu_custom_call" | custom-call | tf_op jit(solution)/shard_map/rows/pallas_call | solution.py:207
  29.6 4.8 %collective-permute-start.5 = (f32[512,256]{1,0:T(8,128)S(1)}, f32[512,256]{1,0:T(8,128)S(1)}, u32[]{:S(2)}, u32[]{:S(2)}) collective-permute-start(f32[512,256]{1,0:T(8,128)S(1)} %rows.6.refs_4_), channel_id=1, source_target_pairs={{0,1},{1,2},{2,3},{3,4},{4,5},{5,6},{6,7},{8,9},{9,10},{10,11},{11... | collective-permute-start | bytes 1572872 | tf_op jit(solution)/shard_map/ppermute | solution.py:315
  34.4 0.0 collective-permute-done.6.refs_2_
  34.4 0.0 copy-start.6
  34.4 0.8 copy-done.6
  35.2 2.6 %rows.7.refs_1_ = f32[512,256]{1,0:T(8,128)S(1)} custom-call(s32[1]{0:T(128)} %bitcast.place, f32[512,1024]{1,0:T(8,128)} %bitcast.26, f32[512,1024]{1,0:T(8,128)} %collective-permute-done.refs_1_, f32[512,256]{1,0:T(8,128)} %copy-done.6, bf16[2,256,1280]{2,1,0:T(8,128)(2,1)S(1)} %get-tuple-element.12.refs_3_, ...), custom_call_target="tpu_custom_call" | custom-call | tf_op jit(solution)/shard_map/rows/pallas_call | solution.py:207
  37.8 2.9 %collective-permute-start.7 = (f32[512,256]{1,0:T(8,128)S(1)}, f32[512,256]{1,0:T(8,128)S(1)}, u32[]{:S(2)}, u32[]{:S(2)}) collective-permute-start(f32[512,256]{1,0:T(8,128)S(1)} %rows.7.refs_1_), channel_id=1, source_target_pairs={{1,0},{2,1},{3,2},{4,3},{5,4},{6,5},{7,6},{9,8},{10,9},{11,10},{12... | collective-permute-start | bytes 1572872 | tf_op jit(solution)/shard_map/ppermute | solution.py:315
  40.7 0.0 collective-permute-done.1.refs_2_
  40.7 2.6 %rows.5.refs_2_ = f32[512,256]{1,0:T(8,128)S(1)} custom-call(s32[1]{0:T(128)} %bitcast.place, f32[512,1024]{1,0:T(8,128)} %bitcast.27, f32[512,1024]{1,0:T(8,128)} %collective-permute-done.refs_1_, f32[512,512]{1,0:T(8,128)} %collective-permute-done.1.refs_2_, bf16[2,256,1280]{2,1,0:T(8,128)(2,1)S(1)} %get-tuple-element.12.refs_3_, ...), custom_call_target="tpu_custom_call" | custom-call | tf_op jit(solution)/shard_map/rows/pallas_call | solution.py:207
  43.3 3.9 %collective-permute-start.3 = (f32[512,256]{1,0:T(8,128)S(1)}, f32[512,256]{1,0:T(8,128)}, u32[]{:S(2)}, u32[]{:S(2)}) collective-permute-start(f32[512,256]{1,0:T(8,128)S(1)} %rows.5.refs_2_), channel_id=1, source_target_pairs={{1,0},{2,1},{3,2},{4,3},{5,4},{6,5},{7,6},{9,8},{10,9},{11,10},{12... | collective-permute-start | bytes 1572872 | tf_op jit(solution)/shard_map/ppermute | solution.py:315
  47.2 2.6 %rows.4.refs_3_ = f32[512,256]{1,0:T(8,128)S(1)} custom-call(s32[1]{0:T(128)} %bitcast.place, f32[512,1024]{1,0:T(8,128)} %bitcast.28, f32[512,1024]{1,0:T(8,128)} %collective-permute-done.refs_1_, f32[512,512]{1,0:T(8,128)} %collective-permute-done.1.refs_2_, bf16[2,256,1280]{2,1,0:T(8,128)(2,1)S(1)} %get-tuple-element.12.refs_3_, ...), custom_call_target="tpu_custom_call" | custom-call | tf_op jit(solution)/shard_map/rows/pallas_call | solution.py:207
  49.9 2.9 %collective-permute-start.2 = (f32[512,256]{1,0:T(8,128)S(1)}, f32[512,256]{1,0:T(8,128)}, u32[]{:S(2)}, u32[]{:S(2)}) collective-permute-start(f32[512,256]{1,0:T(8,128)S(1)} %rows.4.refs_3_), channel_id=1, source_target_pairs={{0,1},{1,2},{2,3},{3,4},{4,5},{5,6},{6,7},{8,9},{9,10},{10,11},{11... | collective-permute-start | bytes 1572872 | tf_op jit(solution)/shard_map/ppermute | solution.py:315
  52.8 3.1 %col_bands.1 = (bf16[4,1280,256]{2,1,0:T(8,128)(2,1)S(1)}, bf16[4,1280,256]{2,1,0:T(8,128)(2,1)S(1)}) custom-call(s32[1]{0:T(128)} %bitcast.8.place, s32[64,128]{1,0:T(8,128)S(1)} %bitcast.11, s32[64,128]{1,0:T(8,128)S(1)} %bitcast.13, s32[64,128]{1,0:T(8,128)S(1)} %bitcast.15, f32[64,128]{1,0:T(8,128)S(1)} %bitcast.17, f32[64,128]{1,0:T(8,128)S(1)} %bitcast.19, ...), custom_call_target="tpu_custom_call" | custom-call | tf_op jit(solution)/shard_map/col_bands/pallas_call | solution.py:125
  55.8 12.8 %collective-permute-done.5.refs_0_ = f32[512,256]{1,0:T(8,128)S(1)} collective-permute-done((f32[512,256]{1,0:T(8,128)S(1)}, f32[512,256]{1,0:T(8,128)S(1)}, u32[]{:S(2)}, u32[]{:S(2)}) %collective-permute-start.5) | collective-permute-done | bytes 524320 | tf_op jit(solution)/shard_map/ppermute | solution.py:315
  68.6 0.3 collective-permute-done.7.refs_5_
  68.9 5.1 %cols.1.part = f32[512,1024]{1,0:T(8,128)} custom-call(f32[512,256]{1,0:T(8,128)S(1)} %collective-permute-done.5.refs_0_, f32[512,256]{1,0:T(8,128)S(1)} %rows.7.refs_1_, f32[512,256]{1,0:T(8,128)S(1)} %rows.5.refs_2_, f32[512,256]{1,0:T(8,128)S(1)} %rows.4.refs_3_, f32[512,256]{1,0:T(8,128)S(1)} %rows.6.refs_4_, ...), custom_call_target="tpu_custom_call" | custom-call | tf_op jit(solution)/shard_map/cols/pallas_call | solution.py:244
  74.0 5.9 %collective-permute-done.3.side = f32[512,256]{1,0:T(8,128)} collective-permute-done((f32[512,256]{1,0:T(8,128)S(1)}, f32[512,256]{1,0:T(8,128)}, u32[]{:S(2)}, u32[]{:S(2)}) %collective-permute-start.3) | collective-permute-done | bytes 524320 | tf_op jit(solution)/shard_map/ppermute | solution.py:315
  79.9 2.4 %tail.2.part = f32[512,1024]{1,0:T(8,128)} custom-call(f32[512,256]{1,0:T(8,128)} %collective-permute-done.3.side, bf16[4,1280,256]{2,1,0:T(8,128)(2,1)S(1)} %get-tuple-element.14.refs_6_.band_high, bf16[4,1280,256]{2,1,0:T(8,128)(2,1)S(1)} %get-tuple-element.15.refs_7_.band_low, f32[512,1024]{1,0:T(8,128)} %cols.1.part), custom_call_target="tpu_custom_call", output_to_operand_aliasing={{}: (3, {})} | custom-call | tf_op jit(solution)/shard_map/tail/pallas_call | solution.py:264
  82.3 0.0 collective-permute-done.2.side
  82.3 2.4 %tail.3 = f32[512,1024]{1,0:T(8,128)} custom-call(f32[512,256]{1,0:T(8,128)} %collective-permute-done.2.side, bf16[4,1280,256]{2,1,0:T(8,128)(2,1)S(1)} %get-tuple-element.14.refs_6_.band_high, bf16[4,1280,256]{2,1,0:T(8,128)(2,1)S(1)} %get-tuple-element.15.refs_7_.band_low, f32[512,1024]{1,0:T(8,128)} %tail.2.part), custom_call_target="tpu_custom_call", output_to_operand_aliasing={{}: (3, {})} | custom-call | tf_op jit(solution)/shard_map/tail/pallas_call | solution.py:264
Async XLA Ops:
  0.0 13.1 %copy-start = (s32[1,1,8192]{2,1,0:T(1,128)S(1)}, s32[1,1,8192]{2,1,0:T(1,128)}, u32[]{:S(2)}) copy-start(s32[1,1,8192]{2,1,0:T(1,128)} %param.8) | copy-start | bytes 98308
  0.0 13.1 %copy-start.1 = (s32[1,1,8192]{2,1,0:T(1,128)S(1)}, s32[1,1,8192]{2,1,0:T(1,128)}, u32[]{:S(2)}) copy-start(s32[1,1,8192]{2,1,0:T(1,128)} %param.9) | copy-start | bytes 98308
  0.0 13.1 %copy-start.2 = (s32[1,1,8192]{2,1,0:T(1,128)S(1)}, s32[1,1,8192]{2,1,0:T(1,128)}, u32[]{:S(2)}) copy-start(s32[1,1,8192]{2,1,0:T(1,128)} %param.10) | copy-start | bytes 98308
  0.0 13.1 %copy-start.3 = (f32[1,1,8192]{2,1,0:T(1,128)S(1)}, f32[1,1,8192]{2,1,0:T(1,128)}, u32[]{:S(2)}) copy-start(f32[1,1,8192]{2,1,0:T(1,128)} %param.11) | copy-start | bytes 98308
  0.0 13.1 %copy-start.4 = (f32[1,8192]{1,0:T(1,128)S(1)}, f32[1,8192]{1,0:T(1,128)}, u32[]{:S(2)}) copy-start(f32[1,8192]{1,0:T(1,128)} %param.12) | copy-start | bytes 98308
  0.0 13.1 %copy-start.5 = (f32[1,8192]{1,0:T(1,128)S(1)}, f32[1,8192]{1,0:T(1,128)}, u32[]{:S(2)}) copy-start(f32[1,8192]{1,0:T(1,128)} %param.13) | copy-start | bytes 98308
  0.0 26.1 %collective-permute-start = (f32[512,1024]{1,0:T(8,128)}, f32[512,1024]{1,0:T(8,128)}, u32[]{:S(2)}, u32[]{:S(2)}) collective-permute-start(f32[512,1024]{1,0:T(8,128)} %bitcast.22), channel_id=1, source_target_pairs={{0,8},{8,0},{16,24},{24,16},{32,40},{40,32},{48,56},{56,48},{64,72... | collective-permute-start | bytes 6291464 | tf_op jit(solution)/shard_map/ppermute | solution.py:300
  2.3 38.4 %collective-permute-start.1 = (f32[512,512]{1,0:T(8,128)S(1)}, f32[512,512]{1,0:T(8,128)}, u32[]{:S(2)}, u32[]{:S(2)}) collective-permute-start(f32[512,512]{1,0:T(8,128)S(1)} %get-tuple-element.11), channel_id=1, source_target_pairs={{16,8},{8,16},{32,24},{24,32},{48,40},{40,48},{64,56},{56,64},{80,... | collective-permute-start | bytes 3145736 | tf_op jit(solution)/shard_map/ppermute | solution.py:304
  4.3 21.9 %collective-permute-start.4 = (f32[512,256]{1,0:T(8,128)S(1)}, f32[512,256]{1,0:T(8,128)S(1)}, u32[]{:S(2)}, u32[]{:S(2)}) collective-permute-start(f32[512,256]{1,0:T(8,128)S(1)} %get-tuple-element.16), channel_id=1, source_target_pairs={{16,8},{8,16},{32,24},{24,32},{48,40},{40,48},{64,56},{56,64},{80,... | collective-permute-start | bytes 1572872 | tf_op jit(solution)/shard_map/ppermute | solution.py:304
  11.2 23.3 %collective-permute-start.6 = (f32[512,256]{1,0:T(8,128)S(1)}, f32[512,256]{1,0:T(8,128)S(1)}, u32[]{:S(2)}, u32[]{:S(2)}) collective-permute-start(f32[512,256]{1,0:T(8,128)S(1)} %take.3), channel_id=1, source_target_pairs={{16,8},{8,16},{32,24},{24,32},{48,40},{40,48},{64,56},{56,64},{80,... | collective-permute-start | bytes 1572872 | tf_op jit(solution)/shard_map/ppermute | solution.py:304
  26.2 0.8 copy-start.7
  29.6 39.0 %collective-permute-start.5 = (f32[512,256]{1,0:T(8,128)S(1)}, f32[512,256]{1,0:T(8,128)S(1)}, u32[]{:S(2)}, u32[]{:S(2)}) collective-permute-start(f32[512,256]{1,0:T(8,128)S(1)} %rows.6.refs_4_), channel_id=1, source_target_pairs={{0,1},{1,2},{2,3},{3,4},{4,5},{5,6},{6,7},{8,9},{9,10},{10,11},{11... | collective-permute-start | bytes 1572872 | tf_op jit(solution)/shard_map/ppermute | solution.py:315
  34.4 0.8 copy-start.6
  37.8 31.0 %collective-permute-start.7 = (f32[512,256]{1,0:T(8,128)S(1)}, f32[512,256]{1,0:T(8,128)S(1)}, u32[]{:S(2)}, u32[]{:S(2)}) collective-permute-start(f32[512,256]{1,0:T(8,128)S(1)} %rows.7.refs_1_), channel_id=1, source_target_pairs={{1,0},{2,1},{3,2},{4,3},{5,4},{6,5},{7,6},{9,8},{10,9},{11,10},{12... | collective-permute-start | bytes 1572872 | tf_op jit(solution)/shard_map/ppermute | solution.py:315
  43.3 36.6 %collective-permute-start.3 = (f32[512,256]{1,0:T(8,128)S(1)}, f32[512,256]{1,0:T(8,128)}, u32[]{:S(2)}, u32[]{:S(2)}) collective-permute-start(f32[512,256]{1,0:T(8,128)S(1)} %rows.5.refs_2_), channel_id=1, source_target_pairs={{1,0},{2,1},{3,2},{4,3},{5,4},{6,5},{7,6},{9,8},{10,9},{11,10},{12... | collective-permute-start | bytes 1572872 | tf_op jit(solution)/shard_map/ppermute | solution.py:315
  49.9 32.4 %collective-permute-start.2 = (f32[512,256]{1,0:T(8,128)S(1)}, f32[512,256]{1,0:T(8,128)}, u32[]{:S(2)}, u32[]{:S(2)}) collective-permute-start(f32[512,256]{1,0:T(8,128)S(1)} %rows.4.refs_3_), channel_id=1, source_target_pairs={{0,1},{1,2},{2,3},{3,4},{4,5},{5,6},{6,7},{8,9},{9,10},{10,11},{11... | collective-permute-start | bytes 1572872 | tf_op jit(solution)/shard_map/ppermute | solution.py:315

commit v8 on v6

--- a/solution.py
+++ b/solution.py
@@ -285,6 +285,9 @@
 
     chip_pairs = [(i, i ^ 1) for i in range(row_count)]
     cross_pairs = [((i + 1 ^ 1) - 1, i) for i in range(1, row_count - 1)]
+    middle = row_count // 2
+    middle_pairs = [(middle - 1, middle), (middle, middle - 1)]
+    other_pairs = [pair for pair in cross_pairs if pair not in middle_pairs]
 
     fields = [
         a.reshape(NLAT, NLON)
@@ -299,14 +302,17 @@
     starts = (0, width - PAIR, PAIR, width - 2 * PAIR)
     chip = lax.ppermute(block, "row", chip_pairs)
     (own0,) = take_columns(block, [(0, PAIR)])
-    (own1,) = take_columns(block, [(PAIR, width)])
+    own1, own2 = take_columns(block, [(width - PAIR, width), (PAIR, width - PAIR)])
     across0 = lax.ppermute(own0, "row", cross_pairs)
     across1 = lax.ppermute(own1, "row", cross_pairs)
+    across2 = [lax.ppermute(own2, "row", middle_pairs), lax.ppermute(own2, "row", other_pairs)]
+    across = ([across0], [across1], across2, across2)
+    offset = (0, 0, 0, width - 3 * PAIR)
     row_bands = build_bands(lat_row, fields, rows // PAIR, True)
     half, side = [], []
     for k in range(4):
-        sources = [block, chip, across1 if k else across0]
-        begins = [starts[k], starts[k], starts[k] - PAIR if k else 0]
+        sources = [block, chip] + across[k]
+        begins = [starts[k]] * 2 + [offset[k]] * len(across[k])
         half.append(apply_rows(lat_row, PAIR, sources, begins, row_bands))
         pairs = forward(col_count) if k % 2 else backward(col_count)
         side.append(lax.ppermute(half[k], "col", pairs))

time: 84.9 us -> 86.8 us (1.022)
  the two profiles are of different devices: /device:TPU:10 before, /device:TPU:101 now
where the time goes in v8:
time: 86.8 us; the launch traced here: 86.3 us
  waiting for transfers between devices  29.6 us (34%)
  Pallas kernels  28.4 us (33%)
  starting transfers between devices  26.5 us (31%)
  local copies, waits for them, and re-layouts  1.6 us (2%)
    ppermute x4, waiting for transfers between devices, body(): side.append(lax.ppermute(half[k], 'col', pairs))  20.2 us
    ppermute x4, starting transfers between devices, body(): side.append(lax.ppermute(half[k], 'col', pairs))  14.5 us
    pallas_call x4, Pallas kernels, apply_rows(): pl.pallas_call(functools.partial(rows_kernel, starts), out_shape=pltpu.VM...  10.9 us
    ppermute x1, waiting for transfers between devices, body(): across1 = lax.ppermute(own1, 'row', cross_pairs)  9.42 us
    ppermute x1, starting transfers between devices, body(): across1 = lax.ppermute(own1, 'row', cross_pairs)  5.74 us
    pallas_call x1, Pallas kernels, apply_cols(): pl.pallas_call(cols_kernel, out_shape=jax.ShapeDtypeStruct((rows, width),...  5.14 us
    pallas_call x2, Pallas kernels, build_bands(): pl.pallas_call(functools.partial(band_kernel, transposed), out_shape=(ban...  5 us
    pallas_call x2, Pallas kernels, apply_tail(): pl.pallas_call(functools.partial(tail_kernel, pair, band_rows), grid=(1,)...  4.74 us
  transfers between devices with their start and end apart: 9, of which 4 were waited for; matrix products, arithmetic and copies ran while one was open for 0% of the time, Pallas kernels for 30%

profile of v8, /device:TPU:101, one launch (start us, length us, event | category | flops | bytes accessed | tf_op | source)
XLA Modules:
  0.0 86.3 jit_solution(3588842856552945954)
XLA Ops:
  0.0 0.0 copy-start
  0.0 0.0 copy-start.1
  0.0 0.0 copy-start.2
  0.0 0.0 copy-start.3
  0.0 0.0 copy-start.4
  0.0 0.0 copy-start.5
  0.0 0.8 collective-permute-start
  0.8 1.5 %take.2 = (f32[512,256]{1,0:T(8,128)S(1)}, f32[512,512]{1,0:T(8,128)S(1)}) custom-call(f32[512,1024]{1,0:T(8,128)} %bitcast.23), custom_call_target="tpu_custom_call" | custom-call | tf_op jit(solution)/shard_map/take/pallas_call | solution.py:159
  2.3 1.9 %collective-permute-start.1 = (f32[512,512]{1,0:T(8,128)S(1)}, f32[512,512]{1,0:T(8,128)}, u32[]{:S(2)}, u32[]{:S(2)}) collective-permute-start(f32[512,512]{1,0:T(8,128)S(1)} %get-tuple-element.11), channel_id=1, source_target_pairs={{56,64},{64,56},{57,65},{65,57},{58,66},{66,58},{59,67},{67,59},{6... | collective-permute-start | bytes 3145736 | tf_op jit(solution)/shard_map/ppermute | solution.py:308
  4.3 1.7 %collective-permute-start.2 = (f32[512,512]{1,0:T(8,128)S(1)}, f32[512,512]{1,0:T(8,128)}, u32[]{:S(2)}, u32[]{:S(2)}) collective-permute-start(f32[512,512]{1,0:T(8,128)S(1)} %get-tuple-element.11), channel_id=1, source_target_pairs={{16,8},{8,16},{32,24},{24,32},{48,40},{40,48},{80,72},{72,80},{96,... | collective-permute-start | bytes 3145736 | tf_op jit(solution)/shard_map/ppermute | solution.py:308
  5.9 5.7 %collective-permute-start.5 = (f32[512,256]{1,0:T(8,128)S(1)}, f32[512,256]{1,0:T(8,128)S(1)}, u32[]{:S(2)}, u32[]{:S(2)}) collective-permute-start(f32[512,256]{1,0:T(8,128)S(1)} %get-tuple-element.16), channel_id=1, source_target_pairs={{16,8},{8,16},{32,24},{24,32},{48,40},{40,48},{64,56},{56,64},{80,... | collective-permute-start | bytes 1572872 | tf_op jit(solution)/shard_map/ppermute | solution.py:307
  11.7 1.1 %take.3 = f32[512,256]{1,0:T(8,128)S(1)} custom-call(f32[512,1024]{1,0:T(8,128)} %bitcast.24), custom_call_target="tpu_custom_call" | custom-call | tf_op jit(solution)/shard_map/take/pallas_call | solution.py:159
  12.8 1.9 %collective-permute-start.7 = (f32[512,256]{1,0:T(8,128)S(1)}, f32[512,256]{1,0:T(8,128)S(1)}, u32[]{:S(2)}, u32[]{:S(2)}) collective-permute-start(f32[512,256]{1,0:T(8,128)S(1)} %take.3), channel_id=1, source_target_pairs={{16,8},{8,16},{32,24},{24,32},{48,40},{40,48},{64,56},{56,64},{80,... | collective-permute-start | bytes 1572872 | tf_op jit(solution)/shard_map/ppermute | solution.py:306
  14.7 0.0 copy-done
  14.7 0.0 copy-done.1
  14.8 0.0 copy-done.2
  14.8 0.0 copy-done.3
  14.8 0.0 copy-done.4
  14.8 0.0 copy-done.5
  14.8 1.9 %row_bands.1 = (bf16[2,256,1280]{2,1,0:T(8,128)(2,1)S(1)}, bf16[2,256,1280]{2,1,0:T(8,128)(2,1)S(1)}) custom-call(s32[1]{0:T(128)} %bitcast.place, s32[64,128]{1,0:T(8,128)S(1)} %bitcast.10, s32[64,128]{1,0:T(8,128)S(1)} %bitcast.12, s32[64,128]{1,0:T(8,128)S(1)} %bitcast.14, f32[64,128]{1,0:T(8,128)S(1)} %bitcast.16, f32[64,128]{1,0:T(8,128)S(1)} %bitcast.18, ...), custom_call_target="tpu_custom_call" | custom-call | tf_op jit(solution)/shard_map/row_bands/pallas_call | solution.py:125
  16.7 9.4 %collective-permute-done.5.refs_2_ = f32[512,256]{1,0:T(8,128)S(1)} collective-permute-done((f32[512,256]{1,0:T(8,128)S(1)}, f32[512,256]{1,0:T(8,128)S(1)}, u32[]{:S(2)}, u32[]{:S(2)}) %collective-permute-start.5) | collective-permute-done | bytes 524320 | tf_op jit(solution)/shard_map/ppermute | solution.py:307
  26.2 0.0 copy-start.7
  26.2 0.0 collective-permute-done.refs_1_
  26.2 0.8 copy-done.7
  27.0 2.6 %rows.6.refs_4_ = f32[512,256]{1,0:T(8,128)S(1)} custom-call(s32[1]{0:T(128)} %bitcast.place, f32[512,1024]{1,0:T(8,128)} %bitcast.25, f32[512,1024]{1,0:T(8,128)} %collective-permute-done.refs_1_, f32[512,256]{1,0:T(8,128)} %copy-done.7, bf16[2,256,1280]{2,1,0:T(8,128)(2,1)S(1)} %get-tuple-element.12.refs_4_.refs_3_, ...), custom_call_target="tpu_custom_call" | custom-call | tf_op jit(solution)/shard_map/rows/pallas_call | solution.py:207
  29.6 4.8 %collective-permute-start.6 = (f32[512,256]{1,0:T(8,128)S(1)}, f32[512,256]{1,0:T(8,128)S(1)}, u32[]{:S(2)}, u32[]{:S(2)}) collective-permute-start(f32[512,256]{1,0:T(8,128)S(1)} %rows.6.refs_4_), channel_id=1, source_target_pairs={{0,1},{1,2},{2,3},{3,4},{4,5},{5,6},{6,7},{8,9},{9,10},{10,11},{11... | collective-permute-start | bytes 1572872 | tf_op jit(solution)/shard_map/ppermute | solution.py:318
  34.4 0.0 collective-permute-done.7.refs_2_
  34.4 0.0 copy-start.6
  34.4 0.8 copy-done.6
  35.2 2.6 %rows.7.refs_1_ = f32[512,256]{1,0:T(8,128)S(1)} custom-call(s32[1]{0:T(128)} %bitcast.place, f32[512,1024]{1,0:T(8,128)} %bitcast.26, f32[512,1024]{1,0:T(8,128)} %collective-permute-done.refs_1_, f32[512,256]{1,0:T(8,128)} %copy-done.6, bf16[2,256,1280]{2,1,0:T(8,128)(2,1)S(1)} %get-tuple-element.12.refs_4_.refs_3_, ...), custom_call_target="tpu_custom_call" | custom-call | tf_op jit(solution)/shard_map/rows/pallas_call | solution.py:207
  37.8 2.9 %collective-permute-start.8 = (f32[512,256]{1,0:T(8,128)S(1)}, f32[512,256]{1,0:T(8,128)S(1)}, u32[]{:S(2)}, u32[]{:S(2)}) collective-permute-start(f32[512,256]{1,0:T(8,128)S(1)} %rows.7.refs_1_), channel_id=1, source_target_pairs={{1,0},{2,1},{3,2},{4,3},{5,4},{6,5},{7,6},{9,8},{10,9},{11,10},{12... | collective-permute-start | bytes 1572872 | tf_op jit(solution)/shard_map/ppermute | solution.py:318
  40.7 0.0 collective-permute-done.1.refs_2_
  40.7 0.0 collective-permute-done.2.refs_3_
  40.7 2.8 %rows.5.refs_2_ = f32[512,256]{1,0:T(8,128)S(1)} custom-call(s32[1]{0:T(128)} %bitcast.place, f32[512,1024]{1,0:T(8,128)} %bitcast.27, f32[512,1024]{1,0:T(8,128)} %collective-permute-done.refs_1_, f32[512,512]{1,0:T(8,128)} %collective-permute-done.1.refs_2_, f32[512,512]{1,0:T(8,128)} %collective-permute-done.2.refs_3_, ...), custom_call_target="tpu_custom_call" | custom-call | tf_op jit(solution)/shard_map/rows/pallas_call | solution.py:207
  43.6 3.9 %collective-permute-start.4 = (f32[512,256]{1,0:T(8,128)S(1)}, f32[512,256]{1,0:T(8,128)}, u32[]{:S(2)}, u32[]{:S(2)}) collective-permute-start(f32[512,256]{1,0:T(8,128)S(1)} %rows.5.refs_2_), channel_id=1, source_target_pairs={{1,0},{2,1},{3,2},{4,3},{5,4},{6,5},{7,6},{9,8},{10,9},{11,10},{12... | collective-permute-start | bytes 1572872 | tf_op jit(solution)/shard_map/ppermute | solution.py:318
  47.5 2.8 %rows.4.refs_3_ = f32[512,256]{1,0:T(8,128)S(1)} custom-call(s32[1]{0:T(128)} %bitcast.place, f32[512,1024]{1,0:T(8,128)} %bitcast.28, f32[512,1024]{1,0:T(8,128)} %collective-permute-done.refs_1_, f32[512,512]{1,0:T(8,128)} %collective-permute-done.1.refs_2_, f32[512,512]{1,0:T(8,128)} %collective-permute-done.2.refs_3_, ...), custom_call_target="tpu_custom_call" | custom-call | tf_op jit(solution)/shard_map/rows/pallas_call | solution.py:207
  50.3 2.9 %collective-permute-start.3 = (f32[512,256]{1,0:T(8,128)S(1)}, f32[512,256]{1,0:T(8,128)}, u32[]{:S(2)}, u32[]{:S(2)}) collective-permute-start(f32[512,256]{1,0:T(8,128)S(1)} %rows.4.refs_3_), channel_id=1, source_target_pairs={{0,1},{1,2},{2,3},{3,4},{4,5},{5,6},{6,7},{8,9},{9,10},{10,11},{11... | collective-permute-start | bytes 1572872 | tf_op jit(solution)/shard_map/ppermute | solution.py:318
  53.2 3.1 %col_bands.1 = (bf16[4,1280,256]{2,1,0:T(8,128)(2,1)S(1)}, bf16[4,1280,256]{2,1,0:T(8,128)(2,1)S(1)}) custom-call(s32[1]{0:T(128)} %bitcast.8.place, s32[64,128]{1,0:T(8,128)S(1)} %bitcast.11, s32[64,128]{1,0:T(8,128)S(1)} %bitcast.13, s32[64,128]{1,0:T(8,128)S(1)} %bitcast.15, f32[64,128]{1,0:T(8,128)S(1)} %bitcast.17, f32[64,128]{1,0:T(8,128)S(1)} %bitcast.19, ...), custom_call_target="tpu_custom_call" | custom-call | tf_op jit(solution)/shard_map/col_bands/pallas_call | solution.py:125
  56.3 12.3 %collective-permute-done.6.refs_0_ = f32[512,256]{1,0:T(8,128)S(1)} collective-permute-done((f32[512,256]{1,0:T(8,128)S(1)}, f32[512,256]{1,0:T(8,128)S(1)}, u32[]{:S(2)}, u32[]{:S(2)}) %collective-permute-start.6) | collective-permute-done | bytes 524320 | tf_op jit(solution)/shard_map/ppermute | solution.py:318
  68.6 1.7 %collective-permute-done.8.refs_5_ = f32[512,256]{1,0:T(8,128)S(1)} collective-permute-done((f32[512,256]{1,0:T(8,128)S(1)}, f32[512,256]{1,0:T(8,128)S(1)}, u32[]{:S(2)}, u32[]{:S(2)}) %collective-permute-start.8) | collective-permute-done | bytes 524320 | tf_op jit(solution)/shard_map/ppermute | solution.py:318
  70.3 5.1 %cols.1.part = f32[512,1024]{1,0:T(8,128)} custom-call(f32[512,256]{1,0:T(8,128)S(1)} %collective-permute-done.6.refs_0_, f32[512,256]{1,0:T(8,128)S(1)} %rows.7.refs_1_, f32[512,256]{1,0:T(8,128)S(1)} %rows.5.refs_2_, f32[512,256]{1,0:T(8,128)S(1)} %rows.4.refs_3_, f32[512,256]{1,0:T(8,128)S(1)} %rows.6.refs_4_, ...), custom_call_target="tpu_custom_call" | custom-call | tf_op jit(solution)/shard_map/cols/pallas_call | solution.py:244
  75.4 6.2 %collective-permute-done.4.side = f32[512,256]{1,0:T(8,128)} collective-permute-done((f32[512,256]{1,0:T(8,128)S(1)}, f32[512,256]{1,0:T(8,128)}, u32[]{:S(2)}, u32[]{:S(2)}) %collective-permute-start.4) | collective-permute-done | bytes 524320 | tf_op jit(solution)/shard_map/ppermute | solution.py:318
  81.6 2.4 %tail.2.part = f32[512,1024]{1,0:T(8,128)} custom-call(f32[512,256]{1,0:T(8,128)} %collective-permute-done.4.side, bf16[4,1280,256]{2,1,0:T(8,128)(2,1)S(1)} %get-tuple-element.14.refs_6_.band_high, bf16[4,1280,256]{2,1,0:T(8,128)(2,1)S(1)} %get-tuple-element.15.refs_7_.band_low, f32[512,1024]{1,0:T(8,128)} %cols.1.part), custom_call_target="tpu_custom_call", output_to_operand_aliasing={{}: (3, {})} | custom-call | tf_op jit(solution)/shard_map/tail/pallas_call | solution.py:264
  84.0 0.0 collective-permute-done.3.side
  84.0 2.4 %tail.3 = f32[512,1024]{1,0:T(8,128)} custom-call(f32[512,256]{1,0:T(8,128)} %collective-permute-done.3.side, bf16[4,1280,256]{2,1,0:T(8,128)(2,1)S(1)} %get-tuple-element.14.refs_6_.band_high, bf16[4,1280,256]{2,1,0:T(8,128)(2,1)S(1)} %get-tuple-element.15.refs_7_.band_low, f32[512,1024]{1,0:T(8,128)} %tail.2.part), custom_call_target="tpu_custom_call", output_to_operand_aliasing={{}: (3, {})} | custom-call | tf_op jit(solution)/shard_map/tail/pallas_call | solution.py:264
Async XLA Ops:
  0.0 14.7 %copy-start = (s32[1,1,8192]{2,1,0:T(1,128)S(1)}, s32[1,1,8192]{2,1,0:T(1,128)}, u32[]{:S(2)}) copy-start(s32[1,1,8192]{2,1,0:T(1,128)} %param.8) | copy-start | bytes 98308
  0.0 14.7 %copy-start.1 = (s32[1,1,8192]{2,1,0:T(1,128)S(1)}, s32[1,1,8192]{2,1,0:T(1,128)}, u32[]{:S(2)}) copy-start(s32[1,1,8192]{2,1,0:T(1,128)} %param.9) | copy-start | bytes 98308
  0.0 14.8 %copy-start.2 = (s32[1,1,8192]{2,1,0:T(1,128)S(1)}, s32[1,1,8192]{2,1,0:T(1,128)}, u32[]{:S(2)}) copy-start(s32[1,1,8192]{2,1,0:T(1,128)} %param.10) | copy-start | bytes 98308
  0.0 14.8 %copy-start.3 = (f32[1,1,8192]{2,1,0:T(1,128)S(1)}, f32[1,1,8192]{2,1,0:T(1,128)}, u32[]{:S(2)}) copy-start(f32[1,1,8192]{2,1,0:T(1,128)} %param.11) | copy-start | bytes 98308
  0.0 14.8 %copy-start.4 = (f32[1,8192]{1,0:T(1,128)S(1)}, f32[1,8192]{1,0:T(1,128)}, u32[]{:S(2)}) copy-start(f32[1,8192]{1,0:T(1,128)} %param.12) | copy-start | bytes 98308
  0.0 14.8 %copy-start.5 = (f32[1,8192]{1,0:T(1,128)S(1)}, f32[1,8192]{1,0:T(1,128)}, u32[]{:S(2)}) copy-start(f32[1,8192]{1,0:T(1,128)} %param.13) | copy-start | bytes 98308
  0.0 26.1 %collective-permute-start = (f32[512,1024]{1,0:T(8,128)}, f32[512,1024]{1,0:T(8,128)}, u32[]{:S(2)}, u32[]{:S(2)}) collective-permute-start(f32[512,1024]{1,0:T(8,128)} %bitcast.22), channel_id=1, source_target_pairs={{0,8},{8,0},{16,24},{24,16},{32,40},{40,32},{48,56},{56,48},{64,72... | collective-permute-start | bytes 6291464 | tf_op jit(solution)/shard_map/ppermute | solution.py:303
  2.3 38.4 %collective-permute-start.1 = (f32[512,512]{1,0:T(8,128)S(1)}, f32[512,512]{1,0:T(8,128)}, u32[]{:S(2)}, u32[]{:S(2)}) collective-permute-start(f32[512,512]{1,0:T(8,128)S(1)} %get-tuple-element.11), channel_id=1, source_target_pairs={{56,64},{64,56},{57,65},{65,57},{58,66},{66,58},{59,67},{67,59},{6... | collective-permute-start | bytes 3145736 | tf_op jit(solution)/shard_map/ppermute | solution.py:308
  4.3 36.5 %collective-permute-start.2 = (f32[512,512]{1,0:T(8,128)S(1)}, f32[512,512]{1,0:T(8,128)}, u32[]{:S(2)}, u32[]{:S(2)}) collective-permute-start(f32[512,512]{1,0:T(8,128)S(1)} %get-tuple-element.11), channel_id=1, source_target_pairs={{16,8},{8,16},{32,24},{24,32},{48,40},{40,48},{80,72},{72,80},{96,... | collective-permute-start | bytes 3145736 | tf_op jit(solution)/shard_map/ppermute | solution.py:308
  5.9 20.3 %collective-permute-start.5 = (f32[512,256]{1,0:T(8,128)S(1)}, f32[512,256]{1,0:T(8,128)S(1)}, u32[]{:S(2)}, u32[]{:S(2)}) collective-permute-start(f32[512,256]{1,0:T(8,128)S(1)} %get-tuple-element.16), channel_id=1, source_target_pairs={{16,8},{8,16},{32,24},{24,32},{48,40},{40,48},{64,56},{56,64},{80,... | collective-permute-start | bytes 1572872 | tf_op jit(solution)/shard_map/ppermute | solution.py:307
  12.8 21.6 %collective-permute-start.7 = (f32[512,256]{1,0:T(8,128)S(1)}, f32[512,256]{1,0:T(8,128)S(1)}, u32[]{:S(2)}, u32[]{:S(2)}) collective-permute-start(f32[512,256]{1,0:T(8,128)S(1)} %take.3), channel_id=1, source_target_pairs={{16,8},{8,16},{32,24},{24,32},{48,40},{40,48},{64,56},{56,64},{80,... | collective-permute-start | bytes 1572872 | tf_op jit(solution)/shard_map/ppermute | solution.py:306
  26.2 0.8 copy-start.7
  29.6 39.0 %collective-permute-start.6 = (f32[512,256]{1,0:T(8,128)S(1)}, f32[512,256]{1,0:T(8,128)S(1)}, u32[]{:S(2)}, u32[]{:S(2)}) collective-permute-start(f32[512,256]{1,0:T(8,128)S(1)} %rows.6.refs_4_), channel_id=1, source_target_pairs={{0,1},{1,2},{2,3},{3,4},{4,5},{5,6},{6,7},{8,9},{9,10},{10,11},{11... | collective-permute-start | bytes 1572872 | tf_op jit(solution)/shard_map/ppermute | solution.py:318
  34.4 0.8 copy-start.6
  37.8 32.4 %collective-permute-start.8 = (f32[512,256]{1,0:T(8,128)S(1)}, f32[512,256]{1,0:T(8,128)S(1)}, u32[]{:S(2)}, u32[]{:S(2)}) collective-permute-start(f32[512,256]{1,0:T(8,128)S(1)} %rows.7.refs_1_), channel_id=1, source_target_pairs={{1,0},{2,1},{3,2},{4,3},{5,4},{6,5},{7,6},{9,8},{10,9},{11,10},{12... | collective-permute-start | bytes 1572872 | tf_op jit(solution)/shard_map/ppermute | solution.py:318
  43.6 38.0 %collective-permute-start.4 = (f32[512,256]{1,0:T(8,128)S(1)}, f32[512,256]{1,0:T(8,128)}, u32[]{:S(2)}, u32[]{:S(2)}) collective-permute-start(f32[512,256]{1,0:T(8,128)S(1)} %rows.5.refs_2_), channel_id=1, source_target_pairs={{1,0},{2,1},{3,2},{4,3},{5,4},{6,5},{7,6},{9,8},{10,9},{11,10},{12... | collective-permute-start | bytes 1572872 | tf_op jit(solution)/shard_map/ppermute | solution.py:318
  50.3 33.7 %collective-permute-start.3 = (f32[512,256]{1,0:T(8,128)S(1)}, f32[512,256]{1,0:T(8,128)}, u32[]{:S(2)}, u32[]{:S(2)}) collective-permute-start(f32[512,256]{1,0:T(8,128)S(1)} %rows.4.refs_3_), channel_id=1, source_target_pairs={{0,1},{1,2},{2,3},{3,4},{4,5},{5,6},{6,7},{8,9},{9,10},{10,11},{11... | collective-permute-start | bytes 1572872 | tf_op jit(solution)/shard_map/ppermute | solution.py:318

commit v9 on v7

--- a/solution.py
+++ b/solution.py
@@ -285,6 +285,7 @@
 
     chip_pairs = [(i, i ^ 1) for i in range(row_count)]
     cross_pairs = [((i + 1 ^ 1) - 1, i) for i in range(1, row_count - 1)]
+    copy_pairs = [(source ^ 1, target) for source, target in cross_pairs]
 
     fields = [
         a.reshape(NLAT, NLON)
@@ -299,10 +300,11 @@
     starts = (0, width - PAIR, PAIR, width - 2 * PAIR)
     chip = lax.ppermute(block, "row", chip_pairs)
     (own0,) = take_columns(block, [(0, PAIR)])
-    own1, own2 = take_columns(block, [(width - PAIR, width), (PAIR, width - PAIR)])
-    across0, across1, across2 = (
-        lax.ppermute(x, "row", cross_pairs) for x in (own0, own1, own2)
-    )
+    (own1,) = take_columns(block, [(width - PAIR, width)])
+    (copy2,) = take_columns(chip, [(PAIR, width - PAIR)])
+    across0 = lax.ppermute(own0, "row", cross_pairs)
+    across1 = lax.ppermute(own1, "row", cross_pairs)
+    across2 = lax.ppermute(copy2, "row", copy_pairs)
     across = (across0, across1, across2, across2)
     offset = (0, 0, 0, width - 3 * PAIR)
     row_bands = build_bands(lat_row, fields, rows // PAIR, True)

time: 85.1 us -> 89.8 us (1.055)
  the two profiles are of different devices: /device:TPU:101 before, /device:TPU:15 now
where the time goes in v9:
time: 89.8 us; the launch traced here: 89.3 us
  waiting for transfers between devices  30 us (33%)
  Pallas kernels  28.8 us (32%)
  starting transfers between devices  27.2 us (30%)
  local copies, waits for them, and re-layouts  2.99 us (3%)
    ppermute x4, waiting for transfers between devices, body(): side.append(lax.ppermute(half[k], 'col', pairs))  19.7 us
    ppermute x4, starting transfers between devices, body(): side.append(lax.ppermute(half[k], 'col', pairs))  15.3 us
    pallas_call x4, Pallas kernels, apply_rows(): pl.pallas_call(functools.partial(rows_kernel, starts), out_shape=pltpu.VM...  10.4 us
    ppermute x1, waiting for transfers between devices, body(): across1 = lax.ppermute(own1, 'row', cross_pairs)  6.32 us
    ppermute x1, starting transfers between devices, body(): across2 = lax.ppermute(copy2, 'row', copy_pairs)  5.68 us
    pallas_call x1, Pallas kernels, apply_cols(): pl.pallas_call(cols_kernel, out_shape=jax.ShapeDtypeStruct((rows, width),...  5.14 us
    pallas_call x2, Pallas kernels, build_bands(): pl.pallas_call(functools.partial(band_kernel, transposed), out_shape=(ban...  5.03 us
    pallas_call x2, Pallas kernels, apply_tail(): pl.pallas_call(functools.partial(tail_kernel, pair, band_rows), grid=(1,)...  4.74 us
  transfers between devices with their start and end apart: 8, of which 4 were waited for; matrix products, arithmetic and copies ran while one was open for 0% of the time, Pallas kernels for 28%

profile of v9, /device:TPU:15, one launch (start us, length us, event | category | flops | bytes accessed | tf_op | source)
XLA Modules:
  0.0 89.3 jit_solution(2950013049855263539)
XLA Ops:
  0.0 0.7 collective-permute-start
  0.7 4.0 %collective-permute-done.source.refs_1_ = f32[512,1024]{1,0:T(8,128)S(1)} collective-permute-done((f32[512,1024]{1,0:T(8,128)}, f32[512,1024]{1,0:T(8,128)S(1)}, u32[]{:S(2)}, u32[]{:S(2)}) %collective-permute-start) | collective-permute-done | bytes 2097184 | tf_op jit(solution)/shard_map/ppermute | solution.py:301
  4.7 0.0 copy-start.6
  4.7 1.3 %copy-done.6 = f32[512,1024]{1,0:T(8,128)} copy-done((f32[512,1024]{1,0:T(8,128)}, f32[512,1024]{1,0:T(8,128)S(1)}, u32[]{:S(2)}) %copy-start.6) | copy-done | bytes 2097176
  6.0 1.2 %take.3 = f32[512,512]{1,0:T(8,128)S(1)} custom-call(f32[512,1024]{1,0:T(8,128)} %copy-done.6), custom_call_target="tpu_custom_call" | custom-call | tf_op jit(solution)/shard_map/take/pallas_call | solution.py:159
  7.2 0.0 copy-start
  7.2 0.0 copy-start.1
  7.2 0.0 copy-start.2
  7.3 0.0 copy-start.3
  7.3 0.0 copy-start.4
  7.3 0.0 copy-start.5
  7.3 5.7 %collective-permute-start.1 = (f32[512,512]{1,0:T(8,128)S(1)}, f32[512,512]{1,0:T(8,128)}, u32[]{:S(2)}, u32[]{:S(2)}) collective-permute-start(f32[512,512]{1,0:T(8,128)S(1)} %take.3), channel_id=1, source_target_pairs={{24,8},{0,16},{40,24},{16,32},{56,40},{32,48},{72,56},{48,64},{88,... | collective-permute-start | bytes 3145736 | tf_op jit(solution)/shard_map/ppermute | solution.py:307
  13.0 1.1 %take.4 = f32[512,256]{1,0:T(8,128)S(1)} custom-call(f32[512,1024]{1,0:T(8,128)} %bitcast.23), custom_call_target="tpu_custom_call" | custom-call | tf_op jit(solution)/shard_map/take/pallas_call | solution.py:159
  14.1 2.1 %collective-permute-start.4 = (f32[512,256]{1,0:T(8,128)S(1)}, f32[512,256]{1,0:T(8,128)S(1)}, u32[]{:S(2)}, u32[]{:S(2)}) collective-permute-start(f32[512,256]{1,0:T(8,128)S(1)} %take.4), channel_id=1, source_target_pairs={{16,8},{8,16},{32,24},{24,32},{48,40},{40,48},{64,56},{56,64},{80,... | collective-permute-start | bytes 1572872 | tf_op jit(solution)/shard_map/ppermute | solution.py:306
  16.2 1.1 %take.5 = f32[512,256]{1,0:T(8,128)S(1)} custom-call(f32[512,1024]{1,0:T(8,128)} %bitcast.24), custom_call_target="tpu_custom_call" | custom-call | tf_op jit(solution)/shard_map/take/pallas_call | solution.py:159
  17.4 3.5 %collective-permute-start.6 = (f32[512,256]{1,0:T(8,128)S(1)}, f32[512,256]{1,0:T(8,128)S(1)}, u32[]{:S(2)}, u32[]{:S(2)}) collective-permute-start(f32[512,256]{1,0:T(8,128)S(1)} %take.5), channel_id=1, source_target_pairs={{16,8},{8,16},{32,24},{24,32},{48,40},{40,48},{64,56},{56,64},{80,... | collective-permute-start | bytes 1572872 | tf_op jit(solution)/shard_map/ppermute | solution.py:305
  20.9 0.0 copy-done
  20.9 0.0 copy-done.1
  20.9 0.0 copy-done.2
  20.9 0.0 copy-done.3
  20.9 0.0 copy-done.4
  20.9 0.0 copy-done.5
  20.9 1.9 %row_bands.1 = (bf16[2,256,1280]{2,1,0:T(8,128)(2,1)S(1)}, bf16[2,256,1280]{2,1,0:T(8,128)(2,1)S(1)}) custom-call(s32[1]{0:T(128)} %bitcast.place, s32[64,128]{1,0:T(8,128)S(1)} %bitcast.10, s32[64,128]{1,0:T(8,128)S(1)} %bitcast.12, s32[64,128]{1,0:T(8,128)S(1)} %bitcast.14, f32[64,128]{1,0:T(8,128)S(1)} %bitcast.16, f32[64,128]{1,0:T(8,128)S(1)} %bitcast.18, ...), custom_call_target="tpu_custom_call" | custom-call | tf_op jit(solution)/shard_map/row_bands/pallas_call | solution.py:125
  22.8 6.3 %collective-permute-done.4.refs_2_ = f32[512,256]{1,0:T(8,128)S(1)} collective-permute-done((f32[512,256]{1,0:T(8,128)S(1)}, f32[512,256]{1,0:T(8,128)S(1)}, u32[]{:S(2)}, u32[]{:S(2)}) %collective-permute-start.4) | collective-permute-done | bytes 524320 | tf_op jit(solution)/shard_map/ppermute | solution.py:306
  29.2 0.0 copy-start.8
  29.2 0.8 copy-done.8
  30.0 2.6 %rows.6.refs_4_ = f32[512,256]{1,0:T(8,128)S(1)} custom-call(s32[1]{0:T(128)} %bitcast.place, f32[512,1024]{1,0:T(8,128)} %bitcast.25, f32[512,1024]{1,0:T(8,128)} %copy-done.6, f32[512,256]{1,0:T(8,128)} %copy-done.8, bf16[2,256,1280]{2,1,0:T(8,128)(2,1)S(1)} %get-tuple-element.9.refs_3_, bf16[2,256,1280]{2,1,0:T(8,128)(2,1)S(1)} %get-tuple-element.10.refs_4_), custom_call_target="tpu_custom_call" | custom-call | tf_op jit(solution)/shard_map/rows/pallas_call | solution.py:207
  32.6 3.9 %collective-permute-start.5 = (f32[512,256]{1,0:T(8,128)S(1)}, f32[512,256]{1,0:T(8,128)S(1)}, u32[]{:S(2)}, u32[]{:S(2)}) collective-permute-start(f32[512,256]{1,0:T(8,128)S(1)} %rows.6.refs_4_), channel_id=1, source_target_pairs={{0,1},{1,2},{2,3},{3,4},{4,5},{5,6},{6,7},{8,9},{9,10},{10,11},{11... | collective-permute-start | bytes 1572872 | tf_op jit(solution)/shard_map/ppermute | solution.py:317
  36.5 0.0 collective-permute-done.6.refs_2_
  36.5 0.0 copy-start.7
  36.6 0.8 copy-done.7
  37.4 2.6 %rows.7.refs_1_ = f32[512,256]{1,0:T(8,128)S(1)} custom-call(s32[1]{0:T(128)} %bitcast.place, f32[512,1024]{1,0:T(8,128)} %bitcast.26, f32[512,1024]{1,0:T(8,128)} %copy-done.6, f32[512,256]{1,0:T(8,128)} %copy-done.7, bf16[2,256,1280]{2,1,0:T(8,128)(2,1)S(1)} %get-tuple-element.9.refs_3_, bf16[2,256,1280]{2,1,0:T(8,128)(2,1)S(1)} %get-tuple-element.10.refs_4_), custom_call_target="tpu_custom_call" | custom-call | tf_op jit(solution)/shard_map/rows/pallas_call | solution.py:207
  40.0 3.8 %collective-permute-start.7 = (f32[512,256]{1,0:T(8,128)S(1)}, f32[512,256]{1,0:T(8,128)S(1)}, u32[]{:S(2)}, u32[]{:S(2)}) collective-permute-start(f32[512,256]{1,0:T(8,128)S(1)} %rows.7.refs_1_), channel_id=1, source_target_pairs={{1,0},{2,1},{3,2},{4,3},{5,4},{6,5},{7,6},{9,8},{10,9},{11,10},{12... | collective-permute-start | bytes 1572872 | tf_op jit(solution)/shard_map/ppermute | solution.py:317
  43.8 0.0 collective-permute-done.1.refs_2_
  43.8 2.6 %rows.5.refs_2_ = f32[512,256]{1,0:T(8,128)S(1)} custom-call(s32[1]{0:T(128)} %bitcast.place, f32[512,1024]{1,0:T(8,128)} %bitcast.27, f32[512,1024]{1,0:T(8,128)} %copy-done.6, f32[512,512]{1,0:T(8,128)} %collective-permute-done.1.refs_2_, bf16[2,256,1280]{2,1,0:T(8,128)(2,1)S(1)} %get-tuple-element.9.refs_3_, ...), custom_call_target="tpu_custom_call" | custom-call | tf_op jit(solution)/shard_map/rows/pallas_call | solution.py:207
  46.4 3.3 %collective-permute-start.3 = (f32[512,256]{1,0:T(8,128)S(1)}, f32[512,256]{1,0:T(8,128)}, u32[]{:S(2)}, u32[]{:S(2)}) collective-permute-start(f32[512,256]{1,0:T(8,128)S(1)} %rows.5.refs_2_), channel_id=1, source_target_pairs={{1,0},{2,1},{3,2},{4,3},{5,4},{6,5},{7,6},{9,8},{10,9},{11,10},{12... | collective-permute-start | bytes 1572872 | tf_op jit(solution)/shard_map/ppermute | solution.py:317
  49.7 2.6 %rows.4.refs_3_ = f32[512,256]{1,0:T(8,128)S(1)} custom-call(s32[1]{0:T(128)} %bitcast.place, f32[512,1024]{1,0:T(8,128)} %bitcast.28, f32[512,1024]{1,0:T(8,128)} %copy-done.6, f32[512,512]{1,0:T(8,128)} %collective-permute-done.1.refs_2_, bf16[2,256,1280]{2,1,0:T(8,128)(2,1)S(1)} %get-tuple-element.9.refs_3_, ...), custom_call_target="tpu_custom_call" | custom-call | tf_op jit(solution)/shard_map/rows/pallas_call | solution.py:207
  52.3 4.3 %collective-permute-start.2 = (f32[512,256]{1,0:T(8,128)S(1)}, f32[512,256]{1,0:T(8,128)}, u32[]{:S(2)}, u32[]{:S(2)}) collective-permute-start(f32[512,256]{1,0:T(8,128)S(1)} %rows.4.refs_3_), channel_id=1, source_target_pairs={{0,1},{1,2},{2,3},{3,4},{4,5},{5,6},{6,7},{8,9},{9,10},{10,11},{11... | collective-permute-start | bytes 1572872 | tf_op jit(solution)/shard_map/ppermute | solution.py:317
  56.6 3.1 %col_bands.1 = (bf16[4,1280,256]{2,1,0:T(8,128)(2,1)S(1)}, bf16[4,1280,256]{2,1,0:T(8,128)(2,1)S(1)}) custom-call(s32[1]{0:T(128)} %bitcast.8.place, s32[64,128]{1,0:T(8,128)S(1)} %bitcast.11, s32[64,128]{1,0:T(8,128)S(1)} %bitcast.13, s32[64,128]{1,0:T(8,128)S(1)} %bitcast.15, f32[64,128]{1,0:T(8,128)S(1)} %bitcast.17, f32[64,128]{1,0:T(8,128)S(1)} %bitcast.19, ...), custom_call_target="tpu_custom_call" | custom-call | tf_op jit(solution)/shard_map/col_bands/pallas_call | solution.py:125
  59.7 0.0 collective-permute-done.5.refs_0_
  59.8 13.5 %collective-permute-done.7.refs_5_ = f32[512,256]{1,0:T(8,128)S(1)} collective-permute-done((f32[512,256]{1,0:T(8,128)S(1)}, f32[512,256]{1,0:T(8,128)S(1)}, u32[]{:S(2)}, u32[]{:S(2)}) %collective-permute-start.7) | collective-permute-done | bytes 524320 | tf_op jit(solution)/shard_map/ppermute | solution.py:317
  73.2 5.1 %cols.1.part = f32[512,1024]{1,0:T(8,128)} custom-call(f32[512,256]{1,0:T(8,128)S(1)} %collective-permute-done.5.refs_0_, f32[512,256]{1,0:T(8,128)S(1)} %rows.7.refs_1_, f32[512,256]{1,0:T(8,128)S(1)} %rows.5.refs_2_, f32[512,256]{1,0:T(8,128)S(1)} %rows.4.refs_3_, f32[512,256]{1,0:T(8,128)S(1)} %rows.6.refs_4_, ...), custom_call_target="tpu_custom_call" | custom-call | tf_op jit(solution)/shard_map/cols/pallas_call | solution.py:244
  78.4 6.2 %collective-permute-done.3.side = f32[512,256]{1,0:T(8,128)} collective-permute-done((f32[512,256]{1,0:T(8,128)S(1)}, f32[512,256]{1,0:T(8,128)}, u32[]{:S(2)}, u32[]{:S(2)}) %collective-permute-start.3) | collective-permute-done | bytes 524320 | tf_op jit(solution)/shard_map/ppermute | solution.py:317
  84.6 2.4 %tail.2.part = f32[512,1024]{1,0:T(8,128)} custom-call(f32[512,256]{1,0:T(8,128)} %collective-permute-done.3.side, bf16[4,1280,256]{2,1,0:T(8,128)(2,1)S(1)} %get-tuple-element.11.refs_6_.band_high, bf16[4,1280,256]{2,1,0:T(8,128)(2,1)S(1)} %get-tuple-element.12.refs_7_.band_low, f32[512,1024]{1,0:T(8,128)} %cols.1.part), custom_call_target="tpu_custom_call", output_to_operand_aliasing={{}: (3, {})} | custom-call | tf_op jit(solution)/shard_map/tail/pallas_call | solution.py:264
  86.9 0.0 collective-permute-done.2.side
  86.9 2.4 %tail.3 = f32[512,1024]{1,0:T(8,128)} custom-call(f32[512,256]{1,0:T(8,128)} %collective-permute-done.2.side, bf16[4,1280,256]{2,1,0:T(8,128)(2,1)S(1)} %get-tuple-element.11.refs_6_.band_high, bf16[4,1280,256]{2,1,0:T(8,128)(2,1)S(1)} %get-tuple-element.12.refs_7_.band_low, f32[512,1024]{1,0:T(8,128)} %tail.2.part), custom_call_target="tpu_custom_call", output_to_operand_aliasing={{}: (3, {})} | custom-call | tf_op jit(solution)/shard_map/tail/pallas_call | solution.py:264
Async XLA Ops:
  0.0 4.7 %collective-permute-start = (f32[512,1024]{1,0:T(8,128)}, f32[512,1024]{1,0:T(8,128)S(1)}, u32[]{:S(2)}, u32[]{:S(2)}) collective-permute-start(f32[512,1024]{1,0:T(8,128)} %bitcast.22), channel_id=1, source_target_pairs={{0,8},{8,0},{16,24},{24,16},{32,40},{40,32},{48,56},{56,48},{64,72... | collective-permute-start | bytes 6291464 | tf_op jit(solution)/shard_map/ppermute | solution.py:301
  4.7 1.3 %copy-start.6 = (f32[512,1024]{1,0:T(8,128)}, f32[512,1024]{1,0:T(8,128)S(1)}, u32[]{:S(2)}) copy-start(f32[512,1024]{1,0:T(8,128)S(1)} %collective-permute-done.source.refs_1_) | copy-start | bytes 6291460
  7.2 13.6 %copy-start = (s32[1,1,8192]{2,1,0:T(1,128)S(1)}, s32[1,1,8192]{2,1,0:T(1,128)}, u32[]{:S(2)}) copy-start(s32[1,1,8192]{2,1,0:T(1,128)} %param.8) | copy-start | bytes 98308
  7.2 13.6 %copy-start.1 = (s32[1,1,8192]{2,1,0:T(1,128)S(1)}, s32[1,1,8192]{2,1,0:T(1,128)}, u32[]{:S(2)}) copy-start(s32[1,1,8192]{2,1,0:T(1,128)} %param.9) | copy-start | bytes 98308
  7.2 13.6 %copy-start.2 = (s32[1,1,8192]{2,1,0:T(1,128)S(1)}, s32[1,1,8192]{2,1,0:T(1,128)}, u32[]{:S(2)}) copy-start(s32[1,1,8192]{2,1,0:T(1,128)} %param.10) | copy-start | bytes 98308
  7.3 13.6 %copy-start.3 = (f32[1,1,8192]{2,1,0:T(1,128)S(1)}, f32[1,1,8192]{2,1,0:T(1,128)}, u32[]{:S(2)}) copy-start(f32[1,1,8192]{2,1,0:T(1,128)} %param.11) | copy-start | bytes 98308
  7.3 13.6 %copy-start.4 = (f32[1,8192]{1,0:T(1,128)S(1)}, f32[1,8192]{1,0:T(1,128)}, u32[]{:S(2)}) copy-start(f32[1,8192]{1,0:T(1,128)} %param.12) | copy-start | bytes 98308
  7.3 13.6 %copy-start.5 = (f32[1,8192]{1,0:T(1,128)S(1)}, f32[1,8192]{1,0:T(1,128)}, u32[]{:S(2)}) copy-start(f32[1,8192]{1,0:T(1,128)} %param.13) | copy-start | bytes 98308
  7.3 36.5 %collective-permute-start.1 = (f32[512,512]{1,0:T(8,128)S(1)}, f32[512,512]{1,0:T(8,128)}, u32[]{:S(2)}, u32[]{:S(2)}) collective-permute-start(f32[512,512]{1,0:T(8,128)S(1)} %take.3), channel_id=1, source_target_pairs={{24,8},{0,16},{40,24},{16,32},{56,40},{32,48},{72,56},{48,64},{88,... | collective-permute-start | bytes 3145736 | tf_op jit(solution)/shard_map/ppermute | solution.py:307
  14.1 15.0 %collective-permute-start.4 = (f32[512,256]{1,0:T(8,128)S(1)}, f32[512,256]{1,0:T(8,128)S(1)}, u32[]{:S(2)}, u32[]{:S(2)}) collective-permute-start(f32[512,256]{1,0:T(8,128)S(1)} %take.4), channel_id=1, source_target_pairs={{16,8},{8,16},{32,24},{24,32},{48,40},{40,48},{64,56},{56,64},{80,... | collective-permute-start | bytes 1572872 | tf_op jit(solution)/shard_map/ppermute | solution.py:306
  17.4 19.2 %collective-permute-start.6 = (f32[512,256]{1,0:T(8,128)S(1)}, f32[512,256]{1,0:T(8,128)S(1)}, u32[]{:S(2)}, u32[]{:S(2)}) collective-permute-start(f32[512,256]{1,0:T(8,128)S(1)} %take.5), channel_id=1, source_target_pairs={{16,8},{8,16},{32,24},{24,32},{48,40},{40,48},{64,56},{56,64},{80,... | collective-permute-start | bytes 1572872 | tf_op jit(solution)/shard_map/ppermute | solution.py:305
  29.2 0.8 copy-start.8
  32.6 27.1 %collective-permute-start.5 = (f32[512,256]{1,0:T(8,128)S(1)}, f32[512,256]{1,0:T(8,128)S(1)}, u32[]{:S(2)}, u32[]{:S(2)}) collective-permute-start(f32[512,256]{1,0:T(8,128)S(1)} %rows.6.refs_4_), channel_id=1, source_target_pairs={{0,1},{1,2},{2,3},{3,4},{4,5},{5,6},{6,7},{8,9},{9,10},{10,11},{11... | collective-permute-start | bytes 1572872 | tf_op jit(solution)/shard_map/ppermute | solution.py:317
  36.5 0.8 copy-start.7
  40.0 33.2 %collective-permute-start.7 = (f32[512,256]{1,0:T(8,128)S(1)}, f32[512,256]{1,0:T(8,128)S(1)}, u32[]{:S(2)}, u32[]{:S(2)}) collective-permute-start(f32[512,256]{1,0:T(8,128)S(1)} %rows.7.refs_1_), channel_id=1, source_target_pairs={{1,0},{2,1},{3,2},{4,3},{5,4},{6,5},{7,6},{9,8},{10,9},{11,10},{12... | collective-permute-start | bytes 1572872 | tf_op jit(solution)/shard_map/ppermute | solution.py:317
  46.4 38.2 %collective-permute-start.3 = (f32[512,256]{1,0:T(8,128)S(1)}, f32[512,256]{1,0:T(8,128)}, u32[]{:S(2)}, u32[]{:S(2)}) collective-permute-start(f32[512,256]{1,0:T(8,128)S(1)} %rows.5.refs_2_), channel_id=1, source_target_pairs={{1,0},{2,1},{3,2},{4,3},{5,4},{6,5},{7,6},{9,8},{10,9},{11,10},{12... | collective-permute-start | bytes 1572872 | tf_op jit(solution)/shard_map/ppermute | solution.py:317
  52.3 34.6 %collective-permute-start.2 = (f32[512,256]{1,0:T(8,128)S(1)}, f32[512,256]{1,0:T(8,128)}, u32[]{:S(2)}, u32[]{:S(2)}) collective-permute-start(f32[512,256]{1,0:T(8,128)S(1)} %rows.4.refs_3_), channel_id=1, source_target_pairs={{0,1},{1,2},{2,3},{3,4},{4,5},{5,6},{6,7},{8,9},{9,10},{10,11},{11... | collective-permute-start | bytes 1572872 | tf_op jit(solution)/shard_map/ppermute | solution.py:317

commit v10 on v9

--- a/solution.py
+++ b/solution.py
@@ -153,18 +153,18 @@
         copy.wait()
 
 
-def take_columns(source, ranges):
+def take_columns(source, space, ranges):
     rows = source.shape[0]
     starts = [start for start, _ in ranges]
     return pl.pallas_call(
         functools.partial(take_kernel, starts),
         out_shape=tuple(pltpu.VMEM((rows, stop - start), jnp.float32) for start, stop in ranges),
-        in_specs=[pl.BlockSpec(memory_space=pltpu.HBM)],
+        in_specs=[pl.BlockSpec(memory_space=space)],
         out_specs=(VMEM_SPEC,) * len(ranges),
         scratch_shapes=[pltpu.SemaphoreType.DMA((len(ranges), 4))],
         compiler_params=pltpu.CompilerParams(vmem_limit_bytes=8 << 20),
         name="take",
-    )(in_hbm(source))
+    )(source)
 
 
 def rows_kernel(starts, place, *refs):
@@ -202,19 +202,19 @@
 def apply_rows(place, width, sources, starts, bands):
     rows = sources[0].shape[0]
     ext = pltpu.VMEM((3 * rows, width), jnp.bfloat16)
-    hbm = [in_hbm(a) for a in sources]
-    landed = pltpu.VMEM((len(hbm), rows, width), jnp.float32)
+    landed = pltpu.VMEM((len(sources), rows, width), jnp.float32)
     return pl.pallas_call(
         functools.partial(rows_kernel, starts),
         out_shape=pltpu.VMEM((rows, width), jnp.float32),
         in_specs=[pl.BlockSpec(memory_space=pltpu.SMEM)]
-        + [pl.BlockSpec(memory_space=pltpu.HBM)] * len(hbm)
+        + [pl.BlockSpec(memory_space=pltpu.HBM)]
+        + [pl.BlockSpec(memory_space=pl.ANY)] * (len(sources) - 1)
         + [VMEM_SPEC] * 2,
         out_specs=VMEM_SPEC,
-        scratch_shapes=[ext, ext, landed, pltpu.SemaphoreType.DMA((len(hbm),))],
+        scratch_shapes=[ext, ext, landed, pltpu.SemaphoreType.DMA((len(sources),))],
         compiler_params=pltpu.CompilerParams(vmem_limit_bytes=16 << 20),
         name="rows",
-    )(place, *hbm, *(held(a) for a in bands))
+    )(place, in_hbm(sources[0]), *sources[1:], *(held(a) for a in bands))
 
 
 def cols_kernel(*refs):
@@ -252,22 +252,33 @@
     )(*args)
 
 
-def tail_kernel(pair, band_rows, side, band_high, band_low, part, out):
-    h, l = split(side[...])
-    out[...] = part[...] + dot3(h, l, band_high[pair, band_rows], band_low[pair, band_rows])
-
-
-def apply_tail(side, bands, part, pair, band_rows):
+def tail_kernel(west, east, band_high, band_low, part, out):
+    last = band_high.shape[0] - 1
+
+    def add(ref, pair, rows):
+        h, l = split(ref[...])
+        out[...] = part[...] + dot3(h, l, band_high[pair, rows], band_low[pair, rows])
+
+    @pl.when(pl.program_id(0) == 0)
+    def _():
+        add(east, last, slice(SPAN - east.shape[1], SPAN))
+
+    @pl.when(pl.program_id(0) == 1)
+    def _():
+        add(west, 0, slice(0, west.shape[1]))
+
+
+def apply_tail(west, east, bands, part):
     rows, width = part.shape
-    block = pl.BlockSpec((rows, PAIR), lambda i: (0, pair))
-    args = [held(a) for a in (side, *bands)]
-    return pl.pallas_call(
-        functools.partial(tail_kernel, pair, band_rows),
-        grid=(1,),
+    block = pl.BlockSpec((rows, PAIR), lambda i: (0, (1 - i) * (width // PAIR - 1)))
+    args = [held(a) for a in (west, east, *bands)]
+    return pl.pallas_call(
+        tail_kernel,
+        grid=(2,),
         out_shape=jax.ShapeDtypeStruct((rows, width), jnp.float32),
-        in_specs=[VMEM_SPEC] * 3 + [block],
+        in_specs=[VMEM_SPEC] * 4 + [block],
         out_specs=block,
-        input_output_aliases={3: 0},
+        input_output_aliases={4: 0},
         compiler_params=pltpu.CompilerParams(vmem_limit_bytes=16 << 20),
         name="tail",
     )(*args, part)
@@ -299,9 +310,9 @@
 
     starts = (0, width - PAIR, PAIR, width - 2 * PAIR)
     chip = lax.ppermute(block, "row", chip_pairs)
-    (own0,) = take_columns(block, [(0, PAIR)])
-    (own1,) = take_columns(block, [(width - PAIR, width)])
-    (copy2,) = take_columns(chip, [(PAIR, width - PAIR)])
+    (own0,) = take_columns(in_hbm(block), pltpu.HBM, [(0, PAIR)])
+    (own1,) = take_columns(in_hbm(block), pltpu.HBM, [(width - PAIR, width)])
+    (copy2,) = take_columns(chip, pl.ANY, [(PAIR, width - PAIR)])
     across0 = lax.ppermute(own0, "row", cross_pairs)
     across1 = lax.ppermute(own1, "row", cross_pairs)
     across2 = lax.ppermute(copy2, "row", copy_pairs)
@@ -318,9 +329,7 @@
     col_bands = build_bands(lat_col, fields, width // PAIR, False)
     parts = [side[1], half[0], half[2], half[3], half[1], side[0]]
     part = apply_cols(parts, col_bands, width)
-    pairs = width // PAIR
-    part = apply_tail(side[2], col_bands, part, pairs - 1, slice(SPAN - PAIR, SPAN))
-    return apply_tail(side[3], col_bands, part, 0, slice(0, PAIR))[None]
+    return apply_tail(side[3], side[2], col_bands, part)[None]
 
 
 def solution(mesh):

time: 89.8 us -> 86.7 us (0.965)
  the two profiles are of different devices: /device:TPU:15 before, /device:TPU:13 now
where the time goes in v10:
time: 86.7 us; the launch traced here: 86.2 us
  Pallas kernels  32.7 us (38%)
  waiting for transfers between devices  26.8 us (31%)
  starting transfers between devices  26.4 us (30%)
    ppermute x4, waiting for transfers between devices, body(): side.append(lax.ppermute(half[k], 'col', pairs))  17.8 us
    ppermute x4, starting transfers between devices, body(): side.append(lax.ppermute(half[k], 'col', pairs))  14.5 us
    pallas_call x4, Pallas kernels, apply_rows(): pl.pallas_call(functools.partial(rows_kernel, starts), out_shape=pltpu.VM...  13 us
    pallas_call x1, Pallas kernels, apply_cols(): pl.pallas_call(cols_kernel, out_shape=jax.ShapeDtypeStruct((rows, width),...  6.97 us
    ppermute x1, starting transfers between devices, body(): across2 = lax.ppermute(copy2, 'row', copy_pairs)  5.68 us
    pallas_call x2, Pallas kernels, build_bands(): pl.pallas_call(functools.partial(band_kernel, transposed), out_shape=(ban...  4.98 us
    pallas_call x3, Pallas kernels, take_columns(): pl.pallas_call(functools.partial(take_kernel, starts), out_shape=tuple((p...  4.95 us
    ppermute x1, waiting for transfers between devices, body(): across1 = lax.ppermute(own1, 'row', cross_pairs)  4.93 us
  transfers between devices with their start and end apart: 8, of which 4 were waited for; matrix products, arithmetic and copies ran while one was open for 0% of the time, Pallas kernels for 33%

profile of v10, /device:TPU:13, one launch (start us, length us, event | category | flops | bytes accessed | tf_op | source)
XLA Modules:
  0.0 86.2 jit_solution(3546639685374300039)
XLA Ops:
  0.0 0.7 collective-permute-start
  0.7 4.0 %collective-permute-done.source.refs_1_ = f32[512,1024]{1,0:T(8,128)S(1)} collective-permute-done((f32[512,1024]{1,0:T(8,128)}, f32[512,1024]{1,0:T(8,128)S(1)}, u32[]{:S(2)}, u32[]{:S(2)}) %collective-permute-start) | collective-permute-done | bytes 2097184 | tf_op jit(solution)/shard_map/ppermute | solution.py:312
  4.7 1.1 %take.3 = f32[512,512]{1,0:T(8,128)} custom-call(f32[512,1024]{1,0:T(8,128)S(1)} %collective-permute-done.source.refs_1_), custom_call_target="tpu_custom_call" | custom-call | tf_op jit(solution)/shard_map/take/pallas_call | solution.py:159
  5.8 0.0 copy-start
  5.8 0.0 copy-start.1
  5.8 0.0 copy-start.2
  5.8 0.0 copy-start.3
  5.8 0.0 copy-start.4
  5.8 0.0 copy-start.5
  5.8 5.7 %collective-permute-start.1 = (f32[512,512]{1,0:T(8,128)}, f32[512,512]{1,0:T(8,128)S(1)}, u32[]{:S(2)}, u32[]{:S(2)}) collective-permute-start(f32[512,512]{1,0:T(8,128)} %take.3), channel_id=1, source_target_pairs={{24,8},{0,16},{40,24},{16,32},{56,40},{32,48},{72,56},{48,64},{88,... | collective-permute-start | bytes 3145736 | tf_op jit(solution)/shard_map/ppermute | solution.py:318
  11.5 1.9 %take.4 = f32[512,256]{1,0:T(8,128)} custom-call(f32[512,1024]{1,0:T(8,128)} %bitcast.23), custom_call_target="tpu_custom_call" | custom-call | tf_op jit(solution)/shard_map/take/pallas_call | solution.py:159
  13.5 2.1 %collective-permute-start.4 = (f32[512,256]{1,0:T(8,128)}, f32[512,256]{1,0:T(8,128)}, u32[]{:S(2)}, u32[]{:S(2)}) collective-permute-start(f32[512,256]{1,0:T(8,128)} %take.4), channel_id=1, source_target_pairs={{16,8},{8,16},{32,24},{24,32},{48,40},{40,48},{64,56},{56,64},{80,... | collective-permute-start | bytes 1572872 | tf_op jit(solution)/shard_map/ppermute | solution.py:317
  15.5 1.9 %take.5 = f32[512,256]{1,0:T(8,128)} custom-call(f32[512,1024]{1,0:T(8,128)} %bitcast.24), custom_call_target="tpu_custom_call" | custom-call | tf_op jit(solution)/shard_map/take/pallas_call | solution.py:159
  17.5 3.5 %collective-permute-start.6 = (f32[512,256]{1,0:T(8,128)}, f32[512,256]{1,0:T(8,128)}, u32[]{:S(2)}, u32[]{:S(2)}) collective-permute-start(f32[512,256]{1,0:T(8,128)} %take.5), channel_id=1, source_target_pairs={{16,8},{8,16},{32,24},{24,32},{48,40},{40,48},{64,56},{56,64},{80,... | collective-permute-start | bytes 1572872 | tf_op jit(solution)/shard_map/ppermute | solution.py:316
  21.0 0.0 copy-done
  21.0 0.0 copy-done.1
  21.0 0.0 copy-done.2
  21.0 0.0 copy-done.3
  21.0 0.0 copy-done.4
  21.0 0.0 copy-done.5
  21.1 1.9 %row_bands.1 = (bf16[2,256,1280]{2,1,0:T(8,128)(2,1)S(1)}, bf16[2,256,1280]{2,1,0:T(8,128)(2,1)S(1)}) custom-call(s32[1]{0:T(128)} %bitcast.place, s32[64,128]{1,0:T(8,128)S(1)} %bitcast.10, s32[64,128]{1,0:T(8,128)S(1)} %bitcast.12, s32[64,128]{1,0:T(8,128)S(1)} %bitcast.14, f32[64,128]{1,0:T(8,128)S(1)} %bitcast.16, f32[64,128]{1,0:T(8,128)S(1)} %bitcast.18, ...), custom_call_target="tpu_custom_call" | custom-call | tf_op jit(solution)/shard_map/row_bands/pallas_call | solution.py:125
  23.0 4.9 %collective-permute-done.4.refs_2_ = f32[512,256]{1,0:T(8,128)} collective-permute-done((f32[512,256]{1,0:T(8,128)}, f32[512,256]{1,0:T(8,128)}, u32[]{:S(2)}, u32[]{:S(2)}) %collective-permute-start.4) | collective-permute-done | bytes 524320 | tf_op jit(solution)/shard_map/ppermute | solution.py:317
  27.9 3.3 %rows.6.refs_4_ = f32[512,256]{1,0:T(8,128)} custom-call(s32[1]{0:T(128)} %bitcast.place, f32[512,1024]{1,0:T(8,128)} %bitcast.25, f32[512,1024]{1,0:T(8,128)S(1)} %collective-permute-done.source.refs_1_, f32[512,256]{1,0:T(8,128)} %collective-permute-done.4.refs_2_, bf16[2,256,1280]{2,1,0:T(8,128)(2,1)S(1)} %get-tuple-element.9.refs_3_, ...), custom_call_target="tpu_custom_call" | custom-call | tf_op jit(solution)/shard_map/rows/pallas_call | solution.py:206
  31.2 3.9 %collective-permute-start.5 = (f32[512,256]{1,0:T(8,128)}, f32[512,256]{1,0:T(8,128)}, u32[]{:S(2)}, u32[]{:S(2)}) collective-permute-start(f32[512,256]{1,0:T(8,128)} %rows.6.refs_4_), channel_id=1, source_target_pairs={{0,1},{1,2},{2,3},{3,4},{4,5},{5,6},{6,7},{8,9},{9,10},{10,11},{11... | collective-permute-start | bytes 1572872 | tf_op jit(solution)/shard_map/ppermute | solution.py:328
  35.1 0.0 collective-permute-done.6.refs_2_
  35.1 3.3 %rows.7.refs_1_ = f32[512,256]{1,0:T(8,128)} custom-call(s32[1]{0:T(128)} %bitcast.place, f32[512,1024]{1,0:T(8,128)} %bitcast.26, f32[512,1024]{1,0:T(8,128)S(1)} %collective-permute-done.source.refs_1_, f32[512,256]{1,0:T(8,128)} %collective-permute-done.6.refs_2_, bf16[2,256,1280]{2,1,0:T(8,128)(2,1)S(1)} %get-tuple-element.9.refs_3_, ...), custom_call_target="tpu_custom_call" | custom-call | tf_op jit(solution)/shard_map/rows/pallas_call | solution.py:206
  38.4 3.8 %collective-permute-start.7 = (f32[512,256]{1,0:T(8,128)}, f32[512,256]{1,0:T(8,128)}, u32[]{:S(2)}, u32[]{:S(2)}) collective-permute-start(f32[512,256]{1,0:T(8,128)} %rows.7.refs_1_), channel_id=1, source_target_pairs={{1,0},{2,1},{3,2},{4,3},{5,4},{6,5},{7,6},{9,8},{10,9},{11,10},{12... | collective-permute-start | bytes 1572872 | tf_op jit(solution)/shard_map/ppermute | solution.py:328
  42.2 0.0 collective-permute-done.1.refs_2_
  42.2 3.2 %rows.5.refs_2_ = f32[512,256]{1,0:T(8,128)} custom-call(s32[1]{0:T(128)} %bitcast.place, f32[512,1024]{1,0:T(8,128)} %bitcast.27, f32[512,1024]{1,0:T(8,128)S(1)} %collective-permute-done.source.refs_1_, f32[512,512]{1,0:T(8,128)S(1)} %collective-permute-done.1.refs_2_, bf16[2,256,1280]{2,1,0:T(8,128)(2,1)S(1)} %get-tuple-element.9.refs_3_, ...), custom_call_target="tpu_custom_call" | custom-call | tf_op jit(solution)/shard_map/rows/pallas_call | solution.py:206
  45.4 3.0 %collective-permute-start.3 = (f32[512,256]{1,0:T(8,128)}, f32[512,256]{1,0:T(8,128)}, u32[]{:S(2)}, u32[]{:S(2)}) collective-permute-start(f32[512,256]{1,0:T(8,128)} %rows.5.refs_2_), channel_id=1, source_target_pairs={{1,0},{2,1},{3,2},{4,3},{5,4},{6,5},{7,6},{9,8},{10,9},{11,10},{12... | collective-permute-start | bytes 1572872 | tf_op jit(solution)/shard_map/ppermute | solution.py:328
  48.5 3.2 %rows.4.refs_3_ = f32[512,256]{1,0:T(8,128)} custom-call(s32[1]{0:T(128)} %bitcast.place, f32[512,1024]{1,0:T(8,128)} %bitcast.28, f32[512,1024]{1,0:T(8,128)S(1)} %collective-permute-done.source.refs_1_, f32[512,512]{1,0:T(8,128)S(1)} %collective-permute-done.1.refs_2_, bf16[2,256,1280]{2,1,0:T(8,128)(2,1)S(1)} %get-tuple-element.9.refs_3_, ...), custom_call_target="tpu_custom_call" | custom-call | tf_op jit(solution)/shard_map/rows/pallas_call | solution.py:206
  51.7 3.8 %collective-permute-start.2 = (f32[512,256]{1,0:T(8,128)}, f32[512,256]{1,0:T(8,128)S(1)}, u32[]{:S(2)}, u32[]{:S(2)}) collective-permute-start(f32[512,256]{1,0:T(8,128)} %rows.4.refs_3_), channel_id=1, source_target_pairs={{0,1},{1,2},{2,3},{3,4},{4,5},{5,6},{6,7},{8,9},{9,10},{10,11},{11... | collective-permute-start | bytes 1572872 | tf_op jit(solution)/shard_map/ppermute | solution.py:328
  55.5 3.1 %col_bands.1 = (bf16[4,1280,256]{2,1,0:T(8,128)(2,1)S(1)}, bf16[4,1280,256]{2,1,0:T(8,128)(2,1)S(1)}) custom-call(s32[1]{0:T(128)} %bitcast.8.place, s32[64,128]{1,0:T(8,128)S(1)} %bitcast.11, s32[64,128]{1,0:T(8,128)S(1)} %bitcast.13, s32[64,128]{1,0:T(8,128)S(1)} %bitcast.15, f32[64,128]{1,0:T(8,128)S(1)} %bitcast.17, f32[64,128]{1,0:T(8,128)S(1)} %bitcast.19, ...), custom_call_target="tpu_custom_call" | custom-call | tf_op jit(solution)/shard_map/col_bands/pallas_call | solution.py:125
  58.5 0.0 collective-permute-done.5.refs_0_
  58.6 13.6 %collective-permute-done.7.refs_5_ = f32[512,256]{1,0:T(8,128)} collective-permute-done((f32[512,256]{1,0:T(8,128)}, f32[512,256]{1,0:T(8,128)}, u32[]{:S(2)}, u32[]{:S(2)}) %collective-permute-start.7) | collective-permute-done | bytes 524320 | tf_op jit(solution)/shard_map/ppermute | solution.py:328
  72.1 7.0 %cols.1.part = f32[512,1024]{1,0:T(8,128)} custom-call(f32[512,256]{1,0:T(8,128)} %collective-permute-done.5.refs_0_, f32[512,256]{1,0:T(8,128)} %rows.7.refs_1_, f32[512,256]{1,0:T(8,128)} %rows.5.refs_2_, f32[512,256]{1,0:T(8,128)} %rows.4.refs_3_, f32[512,256]{1,0:T(8,128)} %rows.6.refs_4_, f32[512,256]{1,0:T(8,128)} %collective-permute-done.7.refs_5_, ...), custom_call_target="tpu_custom_call" | custom-call | tf_op jit(solution)/shard_map/cols/pallas_call | solution.py:244
  79.1 4.3 %collective-permute-done.3.east = f32[512,256]{1,0:T(8,128)} collective-permute-done((f32[512,256]{1,0:T(8,128)}, f32[512,256]{1,0:T(8,128)}, u32[]{:S(2)}, u32[]{:S(2)}) %collective-permute-start.3) | collective-permute-done | bytes 524320 | tf_op jit(solution)/shard_map/ppermute | solution.py:328
  83.4 0.0 collective-permute-done.2.west
  83.4 2.8 %tail.1 = f32[512,1024]{1,0:T(8,128)} custom-call(f32[512,256]{1,0:T(8,128)S(1)} %collective-permute-done.2.west, f32[512,256]{1,0:T(8,128)} %collective-permute-done.3.east, bf16[4,1280,256]{2,1,0:T(8,128)(2,1)S(1)} %get-tuple-element.11.refs_6_.band_high, ...), custom_call_target="tpu_custom_call", output_to_operand_aliasing={{}: (4, {})} | custom-call | tf_op jit(solution)/shard_map/tail/pallas_call | solution.py:275
Async XLA Ops:
  0.0 4.7 %collective-permute-start = (f32[512,1024]{1,0:T(8,128)}, f32[512,1024]{1,0:T(8,128)S(1)}, u32[]{:S(2)}, u32[]{:S(2)}) collective-permute-start(f32[512,1024]{1,0:T(8,128)} %bitcast.22), channel_id=1, source_target_pairs={{0,8},{8,0},{16,24},{24,16},{32,40},{40,32},{48,56},{56,48},{64,72... | collective-permute-start | bytes 6291464 | tf_op jit(solution)/shard_map/ppermute | solution.py:312
  5.8 15.2 %copy-start = (s32[1,1,8192]{2,1,0:T(1,128)S(1)}, s32[1,1,8192]{2,1,0:T(1,128)}, u32[]{:S(2)}) copy-start(s32[1,1,8192]{2,1,0:T(1,128)} %param.8) | copy-start | bytes 98308
  5.8 15.2 %copy-start.1 = (s32[1,1,8192]{2,1,0:T(1,128)S(1)}, s32[1,1,8192]{2,1,0:T(1,128)}, u32[]{:S(2)}) copy-start(s32[1,1,8192]{2,1,0:T(1,128)} %param.9) | copy-start | bytes 98308
  5.8 15.2 %copy-start.2 = (s32[1,1,8192]{2,1,0:T(1,128)S(1)}, s32[1,1,8192]{2,1,0:T(1,128)}, u32[]{:S(2)}) copy-start(s32[1,1,8192]{2,1,0:T(1,128)} %param.10) | copy-start | bytes 98308
  5.8 15.2 %copy-start.3 = (f32[1,1,8192]{2,1,0:T(1,128)S(1)}, f32[1,1,8192]{2,1,0:T(1,128)}, u32[]{:S(2)}) copy-start(f32[1,1,8192]{2,1,0:T(1,128)} %param.11) | copy-start | bytes 98308
  5.8 15.2 %copy-start.4 = (f32[1,8192]{1,0:T(1,128)S(1)}, f32[1,8192]{1,0:T(1,128)}, u32[]{:S(2)}) copy-start(f32[1,8192]{1,0:T(1,128)} %param.12) | copy-start | bytes 98308
  5.8 15.2 %copy-start.5 = (f32[1,8192]{1,0:T(1,128)S(1)}, f32[1,8192]{1,0:T(1,128)}, u32[]{:S(2)}) copy-start(f32[1,8192]{1,0:T(1,128)} %param.13) | copy-start | bytes 98308
  5.8 36.4 %collective-permute-start.1 = (f32[512,512]{1,0:T(8,128)}, f32[512,512]{1,0:T(8,128)S(1)}, u32[]{:S(2)}, u32[]{:S(2)}) collective-permute-start(f32[512,512]{1,0:T(8,128)} %take.3), channel_id=1, source_target_pairs={{24,8},{0,16},{40,24},{16,32},{56,40},{32,48},{72,56},{48,64},{88,... | collective-permute-start | bytes 3145736 | tf_op jit(solution)/shard_map/ppermute | solution.py:318
  13.5 14.5 %collective-permute-start.4 = (f32[512,256]{1,0:T(8,128)}, f32[512,256]{1,0:T(8,128)}, u32[]{:S(2)}, u32[]{:S(2)}) collective-permute-start(f32[512,256]{1,0:T(8,128)} %take.4), channel_id=1, source_target_pairs={{16,8},{8,16},{32,24},{24,32},{48,40},{40,48},{64,56},{56,64},{80,... | collective-permute-start | bytes 1572872 | tf_op jit(solution)/shard_map/ppermute | solution.py:317
  17.5 17.6 %collective-permute-start.6 = (f32[512,256]{1,0:T(8,128)}, f32[512,256]{1,0:T(8,128)}, u32[]{:S(2)}, u32[]{:S(2)}) collective-permute-start(f32[512,256]{1,0:T(8,128)} %take.5), channel_id=1, source_target_pairs={{16,8},{8,16},{32,24},{24,32},{48,40},{40,48},{64,56},{56,64},{80,... | collective-permute-start | bytes 1572872 | tf_op jit(solution)/shard_map/ppermute | solution.py:316
  31.2 27.4 %collective-permute-start.5 = (f32[512,256]{1,0:T(8,128)}, f32[512,256]{1,0:T(8,128)}, u32[]{:S(2)}, u32[]{:S(2)}) collective-permute-start(f32[512,256]{1,0:T(8,128)} %rows.6.refs_4_), channel_id=1, source_target_pairs={{0,1},{1,2},{2,3},{3,4},{4,5},{5,6},{6,7},{8,9},{9,10},{10,11},{11... | collective-permute-start | bytes 1572872 | tf_op jit(solution)/shard_map/ppermute | solution.py:328
  38.4 33.7 %collective-permute-start.7 = (f32[512,256]{1,0:T(8,128)}, f32[512,256]{1,0:T(8,128)}, u32[]{:S(2)}, u32[]{:S(2)}) collective-permute-start(f32[512,256]{1,0:T(8,128)} %rows.7.refs_1_), channel_id=1, source_target_pairs={{1,0},{2,1},{3,2},{4,3},{5,4},{6,5},{7,6},{9,8},{10,9},{11,10},{12... | collective-permute-start | bytes 1572872 | tf_op jit(solution)/shard_map/ppermute | solution.py:328
  45.4 37.9 %collective-permute-start.3 = (f32[512,256]{1,0:T(8,128)}, f32[512,256]{1,0:T(8,128)}, u32[]{:S(2)}, u32[]{:S(2)}) collective-permute-start(f32[512,256]{1,0:T(8,128)} %rows.5.refs_2_), channel_id=1, source_target_pairs={{1,0},{2,1},{3,2},{4,3},{5,4},{6,5},{7,6},{9,8},{10,9},{11,10},{12... | collective-permute-start | bytes 1572872 | tf_op jit(solution)/shard_map/ppermute | solution.py:328
  51.7 31.7 %collective-permute-start.2 = (f32[512,256]{1,0:T(8,128)}, f32[512,256]{1,0:T(8,128)S(1)}, u32[]{:S(2)}, u32[]{:S(2)}) collective-permute-start(f32[512,256]{1,0:T(8,128)} %rows.4.refs_3_), channel_id=1, source_target_pairs={{0,1},{1,2},{2,3},{3,4},{4,5},{5,6},{6,7},{8,9},{9,10},{10,11},{11... | collective-permute-start | bytes 1572872 | tf_op jit(solution)/shard_map/ppermute | solution.py:328

commit v11 on v10

--- a/solution.py
+++ b/solution.py
@@ -296,6 +296,10 @@
 
     chip_pairs = [(i, i ^ 1) for i in range(row_count)]
     cross_pairs = [((i + 1 ^ 1) - 1, i) for i in range(1, row_count - 1)]
+    middle = row_count // 2
+    last = row_count - 1
+    middle_pairs = [(middle - 1, middle), (middle, middle - 1)]
+    other_pairs = [pair for pair in cross_pairs if pair not in middle_pairs]
     copy_pairs = [(source ^ 1, target) for source, target in cross_pairs]
 
     fields = [
@@ -310,19 +314,20 @@
 
     starts = (0, width - PAIR, PAIR, width - 2 * PAIR)
     chip = lax.ppermute(block, "row", chip_pairs)
-    (own0,) = take_columns(in_hbm(block), pltpu.HBM, [(0, PAIR)])
-    (own1,) = take_columns(in_hbm(block), pltpu.HBM, [(width - PAIR, width)])
+    own0, own1 = take_columns(in_hbm(block), pltpu.HBM, [(0, PAIR), (width - PAIR, width)])
     (copy2,) = take_columns(chip, pl.ANY, [(PAIR, width - PAIR)])
     across0 = lax.ppermute(own0, "row", cross_pairs)
-    across1 = lax.ppermute(own1, "row", cross_pairs)
+    ends = lax.ppermute(own1, "row", [(middle - 1, 0), (middle, last)])
+    relay = lax.ppermute(ends, "row", [(0, middle), (last, middle - 1)])
+    across1 = lax.ppermute(own1, "row", other_pairs)
     across2 = lax.ppermute(copy2, "row", copy_pairs)
-    across = (across0, across1, across2, across2)
+    across = ([across0], [across1, relay], [across2], [across2])
     offset = (0, 0, 0, width - 3 * PAIR)
     row_bands = build_bands(lat_row, fields, rows // PAIR, True)
     half, side = [], []
     for k in range(4):
-        sources = [block, chip, across[k]]
-        begins = [starts[k], starts[k], offset[k]]
+        sources = [block, chip] + across[k]
+        begins = [starts[k]] * 2 + [offset[k]] * len(across[k])
         half.append(apply_rows(lat_row, PAIR, sources, begins, row_bands))
         pairs = forward(col_count) if k % 2 else backward(col_count)
         side.append(lax.ppermute(half[k], "col", pairs))

time: 86.7 us -> 86.8 us (level)
  starting transfers between devices: 26.4 us -> 30.1 us
  waiting for transfers between devices: 26.8 us -> 24.5 us
  Pallas kernels: 32.7 us -> 31.4 us
    ppermute x1, waiting for transfers between devices: 4 us -> 0.01 us  [body(): chip = lax.ppermute(block, 'row', chip_pairs)]
    ppermute x1 -> x3, starting transfers between devices: 2.08 us -> 4.99 us  [the longest x1 1.92 us: body(): across1 = lax.ppermute(own1, 'row', other_pairs)]
    ppermute x1 -> x3, waiting for transfers between devices: 4.93 us -> 6.72 us  [the longest x1 6.71 us: body(): across1 = lax.ppermute(own1, 'row', other_pairs)]
    pallas_call x3 -> x2, Pallas kernels: 4.95 us -> 3.42 us  [take_columns(): pl.pallas_call(functools.partial(take_kernel, starts), out_shape=tuple((p...]
    ppermute x4, waiting for transfers between devices: 17.8 us -> 16.4 us  [body(): side.append(lax.ppermute(half[k], 'col', pairs))]
    ppermute x1, waiting for transfers between devices: 0.01 us -> 1.4 us  [body(): across0 = lax.ppermute(own0, 'row', cross_pairs)]
  transfers between devices with their start and end apart: 8 -> 10, of which waited for: 4 -> 5; matrix products, arithmetic and copies ran while one was open for 0% -> 0% of each run, Pallas kernels for 33% -> 33%
where the time goes in v11:
time: 86.8 us; the launch traced here: 86.3 us
  Pallas kernels  31.4 us (36%)
  starting transfers between devices  30.1 us (35%)
  waiting for transfers between devices  24.5 us (28%)
    ppermute x4, waiting for transfers between devices, body(): side.append(lax.ppermute(half[k], 'col', pairs))  16.4 us
    ppermute x4, starting transfers between devices, body(): side.append(lax.ppermute(half[k], 'col', pairs))  14.6 us
    pallas_call x4, Pallas kernels, apply_rows(): pl.pallas_call(functools.partial(rows_kernel, starts), out_shape=pltpu.VM...  13.2 us
    pallas_call x1, Pallas kernels, apply_cols(): pl.pallas_call(cols_kernel, out_shape=jax.ShapeDtypeStruct((rows, width),...  6.96 us
    ppermute x1, waiting for transfers between devices, body(): across1 = lax.ppermute(own1, 'row', other_pairs)  6.71 us
    ppermute x1, starting transfers between devices, body(): across2 = lax.ppermute(copy2, 'row', copy_pairs)  6.18 us
    pallas_call x2, Pallas kernels, build_bands(): pl.pallas_call(functools.partial(band_kernel, transposed), out_shape=(ban...  4.98 us
    ppermute x1, starting transfers between devices, body(): across0 = lax.ppermute(own0, 'row', cross_pairs)  3.63 us
  transfers between devices with their start and end apart: 10, of which 5 were waited for; matrix products, arithmetic and copies ran while one was open for 0% of the time, Pallas kernels for 33%

profile of v11, /device:TPU:13, one launch (start us, length us, event | category | flops | bytes accessed | tf_op | source)
XLA Modules:
  0.0 86.3 jit_solution(17595265880038949173)
XLA Ops:
  0.0 0.7 collective-permute-start
  0.7 2.3 %take.3 = (f32[512,256]{1,0:T(8,128)}, f32[512,256]{1,0:T(8,128)}) custom-call(f32[512,1024]{1,0:T(8,128)} %bitcast.23), custom_call_target="tpu_custom_call" | custom-call | tf_op jit(solution)/shard_map/take/pallas_call | solution.py:159
  3.0 0.0 copy-start
  3.0 0.0 copy-start.1
  3.0 0.0 copy-start.2
  3.1 0.0 copy-start.3
  3.1 0.0 copy-start.4
  3.1 0.0 copy-start.5
  3.1 1.6 %collective-permute-start.5 = (f32[512,256]{1,0:T(8,128)}, f32[512,256]{1,0:T(8,128)}, u32[]{:S(2)}, u32[]{:S(2)}) collective-permute-start(f32[512,256]{1,0:T(8,128)} %get-tuple-element.15), channel_id=1, source_target_pairs={{56,0},{64,120},{57,1},{65,121},{58,2},{66,122},{59,3},{67,123},{6... | collective-permute-start | bytes 1572872 | tf_op jit(solution)/shard_map/ppermute | solution.py:320
  4.7 0.0 collective-permute-done.source.refs_1_
  4.7 1.1 %take.2 = f32[512,512]{1,0:T(8,128)} custom-call(f32[512,1024]{1,0:T(8,128)S(1)} %collective-permute-done.source.refs_1_), custom_call_target="tpu_custom_call" | custom-call | tf_op jit(solution)/shard_map/take/pallas_call | solution.py:159
  5.8 6.2 %collective-permute-start.1 = (f32[512,512]{1,0:T(8,128)}, f32[512,512]{1,0:T(8,128)S(1)}, u32[]{:S(2)}, u32[]{:S(2)}) collective-permute-start(f32[512,512]{1,0:T(8,128)} %take.2), channel_id=1, source_target_pairs={{24,8},{0,16},{40,24},{16,32},{56,40},{32,48},{72,56},{48,64},{88,... | collective-permute-start | bytes 3145736 | tf_op jit(solution)/shard_map/ppermute | solution.py:323
  12.0 1.9 %collective-permute-start.4 = (f32[512,256]{1,0:T(8,128)}, f32[512,256]{1,0:T(8,128)}, u32[]{:S(2)}, u32[]{:S(2)}) collective-permute-start(f32[512,256]{1,0:T(8,128)} %get-tuple-element.15), channel_id=1, source_target_pairs={{16,8},{8,16},{32,24},{24,32},{48,40},{40,48},{80,72},{72,80},{96,... | collective-permute-start | bytes 1572872 | tf_op jit(solution)/shard_map/ppermute | solution.py:322
  13.9 0.0 collective-permute-done.5
  13.9 1.5 %collective-permute-start.6 = (f32[512,256]{1,0:T(8,128)}, f32[512,256]{1,0:T(8,128)}, u32[]{:S(2)}, u32[]{:S(2)}) collective-permute-start(f32[512,256]{1,0:T(8,128)} %collective-permute-done.5), channel_id=1, source_target_pairs={{0,64},{120,56},{1,65},{121,57},{2,66},{122,58},{3,67},{123,59},{4... | collective-permute-start | bytes 1572872 | tf_op jit(solution)/shard_map/ppermute | solution.py:321
  15.4 3.6 %collective-permute-start.8 = (f32[512,256]{1,0:T(8,128)}, f32[512,256]{1,0:T(8,128)}, u32[]{:S(2)}, u32[]{:S(2)}) collective-permute-start(f32[512,256]{1,0:T(8,128)} %get-tuple-element.16), channel_id=1, source_target_pairs={{16,8},{8,16},{32,24},{24,32},{48,40},{40,48},{64,56},{56,64},{80,... | collective-permute-start | bytes 1572872 | tf_op jit(solution)/shard_map/ppermute | solution.py:319
  19.0 0.0 copy-done
  19.0 0.0 copy-done.1
  19.1 0.0 copy-done.2
  19.1 0.0 copy-done.3
  19.1 0.0 copy-done.4
  19.1 0.0 copy-done.5
  19.1 1.9 %row_bands.1 = (bf16[2,256,1280]{2,1,0:T(8,128)(2,1)S(1)}, bf16[2,256,1280]{2,1,0:T(8,128)(2,1)S(1)}) custom-call(s32[1]{0:T(128)} %bitcast.place, s32[64,128]{1,0:T(8,128)S(1)} %bitcast.10, s32[64,128]{1,0:T(8,128)S(1)} %bitcast.12, s32[64,128]{1,0:T(8,128)S(1)} %bitcast.14, f32[64,128]{1,0:T(8,128)S(1)} %bitcast.16, f32[64,128]{1,0:T(8,128)S(1)} %bitcast.18, ...), custom_call_target="tpu_custom_call" | custom-call | tf_op jit(solution)/shard_map/row_bands/pallas_call | solution.py:125
  21.0 6.7 %collective-permute-done.4.refs_2_ = f32[512,256]{1,0:T(8,128)} collective-permute-done((f32[512,256]{1,0:T(8,128)}, f32[512,256]{1,0:T(8,128)}, u32[]{:S(2)}, u32[]{:S(2)}) %collective-permute-start.4) | collective-permute-done | bytes 524320 | tf_op jit(solution)/shard_map/ppermute | solution.py:322
  27.7 0.0 collective-permute-done.6.refs_3_
  27.7 3.5 %rows.6.refs_4_ = f32[512,256]{1,0:T(8,128)} custom-call(s32[1]{0:T(128)} %bitcast.place, f32[512,1024]{1,0:T(8,128)} %bitcast.24, f32[512,1024]{1,0:T(8,128)S(1)} %collective-permute-done.source.refs_1_, f32[512,256]{1,0:T(8,128)} %collective-permute-done.4.refs_2_, f32[512,256]{1,0:T(8,128)} %collective-permute-done.6.refs_3_, ...), custom_call_target="tpu_custom_call" | custom-call | tf_op jit(solution)/shard_map/rows/pallas_call | solution.py:206
  31.2 3.9 %collective-permute-start.7 = (f32[512,256]{1,0:T(8,128)}, f32[512,256]{1,0:T(8,128)}, u32[]{:S(2)}, u32[]{:S(2)}) collective-permute-start(f32[512,256]{1,0:T(8,128)} %rows.6.refs_4_), channel_id=1, source_target_pairs={{0,1},{1,2},{2,3},{3,4},{4,5},{5,6},{6,7},{8,9},{9,10},{10,11},{11... | collective-permute-start | bytes 1572872 | tf_op jit(solution)/shard_map/ppermute | solution.py:333
  35.2 1.4 %collective-permute-done.8.refs_2_ = f32[512,256]{1,0:T(8,128)} collective-permute-done((f32[512,256]{1,0:T(8,128)}, f32[512,256]{1,0:T(8,128)}, u32[]{:S(2)}, u32[]{:S(2)}) %collective-permute-start.8) | collective-permute-done | bytes 524320 | tf_op jit(solution)/shard_map/ppermute | solution.py:319
  36.6 3.3 %rows.7.refs_1_ = f32[512,256]{1,0:T(8,128)} custom-call(s32[1]{0:T(128)} %bitcast.place, f32[512,1024]{1,0:T(8,128)} %bitcast.25, f32[512,1024]{1,0:T(8,128)S(1)} %collective-permute-done.source.refs_1_, f32[512,256]{1,0:T(8,128)} %collective-permute-done.8.refs_2_, bf16[2,256,1280]{2,1,0:T(8,128)(2,1)S(1)} %get-tuple-element.11.refs_3_.refs_4_, ...), custom_call_target="tpu_custom_call" | custom-call | tf_op jit(solution)/shard_map/rows/pallas_call | solution.py:206
  39.8 3.9 %collective-permute-start.9 = (f32[512,256]{1,0:T(8,128)}, f32[512,256]{1,0:T(8,128)}, u32[]{:S(2)}, u32[]{:S(2)}) collective-permute-start(f32[512,256]{1,0:T(8,128)} %rows.7.refs_1_), channel_id=1, source_target_pairs={{1,0},{2,1},{3,2},{4,3},{5,4},{6,5},{7,6},{9,8},{10,9},{11,10},{12... | collective-permute-start | bytes 1572872 | tf_op jit(solution)/shard_map/ppermute | solution.py:333
  43.7 0.0 collective-permute-done.1.refs_2_
  43.8 3.2 %rows.5.refs_2_ = f32[512,256]{1,0:T(8,128)} custom-call(s32[1]{0:T(128)} %bitcast.place, f32[512,1024]{1,0:T(8,128)} %bitcast.26, f32[512,1024]{1,0:T(8,128)S(1)} %collective-permute-done.source.refs_1_, f32[512,512]{1,0:T(8,128)S(1)} %collective-permute-done.1.refs_2_, bf16[2,256,1280]{2,1,0:T(8,128)(2,1)S(1)} %get-tuple-element.11.refs_3_.refs_4_, ...), custom_call_target="tpu_custom_call" | custom-call | tf_op jit(solution)/shard_map/rows/pallas_call | solution.py:206
  47.0 2.9 %collective-permute-start.3 = (f32[512,256]{1,0:T(8,128)}, f32[512,256]{1,0:T(8,128)}, u32[]{:S(2)}, u32[]{:S(2)}) collective-permute-start(f32[512,256]{1,0:T(8,128)} %rows.5.refs_2_), channel_id=1, source_target_pairs={{1,0},{2,1},{3,2},{4,3},{5,4},{6,5},{7,6},{9,8},{10,9},{11,10},{12... | collective-permute-start | bytes 1572872 | tf_op jit(solution)/shard_map/ppermute | solution.py:333
  49.9 3.2 %rows.4.refs_3_ = f32[512,256]{1,0:T(8,128)} custom-call(s32[1]{0:T(128)} %bitcast.place, f32[512,1024]{1,0:T(8,128)} %bitcast.27, f32[512,1024]{1,0:T(8,128)S(1)} %collective-permute-done.source.refs_1_, f32[512,512]{1,0:T(8,128)S(1)} %collective-permute-done.1.refs_2_, bf16[2,256,1280]{2,1,0:T(8,128)(2,1)S(1)} %get-tuple-element.11.refs_3_.refs_4_, ...), custom_call_target="tpu_custom_call" | custom-call | tf_op jit(solution)/shard_map/rows/pallas_call | solution.py:206
  53.1 3.9 %collective-permute-start.2 = (f32[512,256]{1,0:T(8,128)}, f32[512,256]{1,0:T(8,128)S(1)}, u32[]{:S(2)}, u32[]{:S(2)}) collective-permute-start(f32[512,256]{1,0:T(8,128)} %rows.4.refs_3_), channel_id=1, source_target_pairs={{0,1},{1,2},{2,3},{3,4},{4,5},{5,6},{6,7},{8,9},{9,10},{10,11},{11... | collective-permute-start | bytes 1572872 | tf_op jit(solution)/shard_map/ppermute | solution.py:333
  57.0 3.1 %col_bands.1 = (bf16[4,1280,256]{2,1,0:T(8,128)(2,1)S(1)}, bf16[4,1280,256]{2,1,0:T(8,128)(2,1)S(1)}) custom-call(s32[1]{0:T(128)} %bitcast.8.place, s32[64,128]{1,0:T(8,128)S(1)} %bitcast.11, s32[64,128]{1,0:T(8,128)S(1)} %bitcast.13, s32[64,128]{1,0:T(8,128)S(1)} %bitcast.15, f32[64,128]{1,0:T(8,128)S(1)} %bitcast.17, f32[64,128]{1,0:T(8,128)S(1)} %bitcast.19, ...), custom_call_target="tpu_custom_call" | custom-call | tf_op jit(solution)/shard_map/col_bands/pallas_call | solution.py:125
  60.1 9.2 %collective-permute-done.7.refs_0_ = f32[512,256]{1,0:T(8,128)} collective-permute-done((f32[512,256]{1,0:T(8,128)}, f32[512,256]{1,0:T(8,128)}, u32[]{:S(2)}, u32[]{:S(2)}) %collective-permute-start.7) | collective-permute-done | bytes 524320 | tf_op jit(solution)/shard_map/ppermute | solution.py:333
  69.3 3.0 %collective-permute-done.9.refs_5_ = f32[512,256]{1,0:T(8,128)} collective-permute-done((f32[512,256]{1,0:T(8,128)}, f32[512,256]{1,0:T(8,128)}, u32[]{:S(2)}, u32[]{:S(2)}) %collective-permute-start.9) | collective-permute-done | bytes 524320 | tf_op jit(solution)/shard_map/ppermute | solution.py:333
  72.3 7.0 %cols.1.part = f32[512,1024]{1,0:T(8,128)} custom-call(f32[512,256]{1,0:T(8,128)} %collective-permute-done.7.refs_0_, f32[512,256]{1,0:T(8,128)} %rows.7.refs_1_, f32[512,256]{1,0:T(8,128)} %rows.5.refs_2_, f32[512,256]{1,0:T(8,128)} %rows.4.refs_3_, f32[512,256]{1,0:T(8,128)} %rows.6.refs_4_, f32[512,256]{1,0:T(8,128)} %collective-permute-done.9.refs_5_, ...), custom_call_target="tpu_custom_call" | custom-call | tf_op jit(solution)/shard_map/cols/pallas_call | solution.py:244
  79.2 4.2 %collective-permute-done.3.east = f32[512,256]{1,0:T(8,128)} collective-permute-done((f32[512,256]{1,0:T(8,128)}, f32[512,256]{1,0:T(8,128)}, u32[]{:S(2)}, u32[]{:S(2)}) %collective-permute-start.3) | collective-permute-done | bytes 524320 | tf_op jit(solution)/shard_map/ppermute | solution.py:333
  83.5 0.0 collective-permute-done.2.west
  83.5 2.8 %tail.1 = f32[512,1024]{1,0:T(8,128)} custom-call(f32[512,256]{1,0:T(8,128)S(1)} %collective-permute-done.2.west, f32[512,256]{1,0:T(8,128)} %collective-permute-done.3.east, bf16[4,1280,256]{2,1,0:T(8,128)(2,1)S(1)} %get-tuple-element.13.refs_6_.band_high, ...), custom_call_target="tpu_custom_call", output_to_operand_aliasing={{}: (4, {})} | custom-call | tf_op jit(solution)/shard_map/tail/pallas_call | solution.py:275
Async XLA Ops:
  0.0 4.7 %collective-permute-start = (f32[512,1024]{1,0:T(8,128)}, f32[512,1024]{1,0:T(8,128)S(1)}, u32[]{:S(2)}, u32[]{:S(2)}) collective-permute-start(f32[512,1024]{1,0:T(8,128)} %bitcast.22), channel_id=1, source_target_pairs={{0,8},{8,0},{16,24},{24,16},{32,40},{40,32},{48,56},{56,48},{64,72... | collective-permute-start | bytes 6291464 | tf_op jit(solution)/shard_map/ppermute | solution.py:316
  3.0 16.0 %copy-start = (s32[1,1,8192]{2,1,0:T(1,128)S(1)}, s32[1,1,8192]{2,1,0:T(1,128)}, u32[]{:S(2)}) copy-start(s32[1,1,8192]{2,1,0:T(1,128)} %param.8) | copy-start | bytes 98308
  3.0 16.0 %copy-start.1 = (s32[1,1,8192]{2,1,0:T(1,128)S(1)}, s32[1,1,8192]{2,1,0:T(1,128)}, u32[]{:S(2)}) copy-start(s32[1,1,8192]{2,1,0:T(1,128)} %param.9) | copy-start | bytes 98308
  3.0 16.0 %copy-start.2 = (s32[1,1,8192]{2,1,0:T(1,128)S(1)}, s32[1,1,8192]{2,1,0:T(1,128)}, u32[]{:S(2)}) copy-start(s32[1,1,8192]{2,1,0:T(1,128)} %param.10) | copy-start | bytes 98308
  3.1 16.0 %copy-start.3 = (f32[1,1,8192]{2,1,0:T(1,128)S(1)}, f32[1,1,8192]{2,1,0:T(1,128)}, u32[]{:S(2)}) copy-start(f32[1,1,8192]{2,1,0:T(1,128)} %param.11) | copy-start | bytes 98308
  3.1 16.0 %copy-start.4 = (f32[1,8192]{1,0:T(1,128)S(1)}, f32[1,8192]{1,0:T(1,128)}, u32[]{:S(2)}) copy-start(f32[1,8192]{1,0:T(1,128)} %param.12) | copy-start | bytes 98308
  3.1 16.0 %copy-start.5 = (f32[1,8192]{1,0:T(1,128)S(1)}, f32[1,8192]{1,0:T(1,128)}, u32[]{:S(2)}) copy-start(f32[1,8192]{1,0:T(1,128)} %param.13) | copy-start | bytes 98308
  3.1 10.8 %collective-permute-start.5 = (f32[512,256]{1,0:T(8,128)}, f32[512,256]{1,0:T(8,128)}, u32[]{:S(2)}, u32[]{:S(2)}) collective-permute-start(f32[512,256]{1,0:T(8,128)} %get-tuple-element.15), channel_id=1, source_target_pairs={{56,0},{64,120},{57,1},{65,121},{58,2},{66,122},{59,3},{67,123},{6... | collective-permute-start | bytes 1572872 | tf_op jit(solution)/shard_map/ppermute | solution.py:320
  5.8 38.0 %collective-permute-start.1 = (f32[512,512]{1,0:T(8,128)}, f32[512,512]{1,0:T(8,128)S(1)}, u32[]{:S(2)}, u32[]{:S(2)}) collective-permute-start(f32[512,512]{1,0:T(8,128)} %take.2), channel_id=1, source_target_pairs={{24,8},{0,16},{40,24},{16,32},{56,40},{32,48},{72,56},{48,64},{88,... | collective-permute-start | bytes 3145736 | tf_op jit(solution)/shard_map/ppermute | solution.py:323
  12.0 15.8 %collective-permute-start.4 = (f32[512,256]{1,0:T(8,128)}, f32[512,256]{1,0:T(8,128)}, u32[]{:S(2)}, u32[]{:S(2)}) collective-permute-start(f32[512,256]{1,0:T(8,128)} %get-tuple-element.15), channel_id=1, source_target_pairs={{16,8},{8,16},{32,24},{24,32},{48,40},{40,48},{80,72},{72,80},{96,... | collective-permute-start | bytes 1572872 | tf_op jit(solution)/shard_map/ppermute | solution.py:322
  13.9 13.8 %collective-permute-start.6 = (f32[512,256]{1,0:T(8,128)}, f32[512,256]{1,0:T(8,128)}, u32[]{:S(2)}, u32[]{:S(2)}) collective-permute-start(f32[512,256]{1,0:T(8,128)} %collective-permute-done.5), channel_id=1, source_target_pairs={{0,64},{120,56},{1,65},{121,57},{2,66},{122,58},{3,67},{123,59},{4... | collective-permute-start | bytes 1572872 | tf_op jit(solution)/shard_map/ppermute | solution.py:321
  15.4 21.2 %collective-permute-start.8 = (f32[512,256]{1,0:T(8,128)}, f32[512,256]{1,0:T(8,128)}, u32[]{:S(2)}, u32[]{:S(2)}) collective-permute-start(f32[512,256]{1,0:T(8,128)} %get-tuple-element.16), channel_id=1, source_target_pairs={{16,8},{8,16},{32,24},{24,32},{48,40},{40,48},{64,56},{56,64},{80,... | collective-permute-start | bytes 1572872 | tf_op jit(solution)/shard_map/ppermute | solution.py:319
  31.2 38.1 %collective-permute-start.7 = (f32[512,256]{1,0:T(8,128)}, f32[512,256]{1,0:T(8,128)}, u32[]{:S(2)}, u32[]{:S(2)}) collective-permute-start(f32[512,256]{1,0:T(8,128)} %rows.6.refs_4_), channel_id=1, source_target_pairs={{0,1},{1,2},{2,3},{3,4},{4,5},{5,6},{6,7},{8,9},{9,10},{10,11},{11... | collective-permute-start | bytes 1572872 | tf_op jit(solution)/shard_map/ppermute | solution.py:333
  39.8 32.4 %collective-permute-start.9 = (f32[512,256]{1,0:T(8,128)}, f32[512,256]{1,0:T(8,128)}, u32[]{:S(2)}, u32[]{:S(2)}) collective-permute-start(f32[512,256]{1,0:T(8,128)} %rows.7.refs_1_), channel_id=1, source_target_pairs={{1,0},{2,1},{3,2},{4,3},{5,4},{6,5},{7,6},{9,8},{10,9},{11,10},{12... | collective-permute-start | bytes 1572872 | tf_op jit(solution)/shard_map/ppermute | solution.py:333
  47.0 36.5 %collective-permute-start.3 = (f32[512,256]{1,0:T(8,128)}, f32[512,256]{1,0:T(8,128)}, u32[]{:S(2)}, u32[]{:S(2)}) collective-permute-start(f32[512,256]{1,0:T(8,128)} %rows.5.refs_2_), channel_id=1, source_target_pairs={{1,0},{2,1},{3,2},{4,3},{5,4},{6,5},{7,6},{9,8},{10,9},{11,10},{12... | collective-permute-start | bytes 1572872 | tf_op jit(solution)/shard_map/ppermute | solution.py:333
  53.1 30.4 %collective-permute-start.2 = (f32[512,256]{1,0:T(8,128)}, f32[512,256]{1,0:T(8,128)S(1)}, u32[]{:S(2)}, u32[]{:S(2)}) collective-permute-start(f32[512,256]{1,0:T(8,128)} %rows.4.refs_3_), channel_id=1, source_target_pairs={{0,1},{1,2},{2,3},{3,4},{4,5},{5,6},{6,7},{8,9},{9,10},{10,11},{11... | collective-permute-start | bytes 1572872 | tf_op jit(solution)/shard_map/ppermute | solution.py:333

commit v12 on v11

--- a/solution.py
+++ b/solution.py
@@ -294,6 +294,9 @@
     forward = lambda n: [(i, i + 1) for i in range(n - 1)]
     backward = lambda n: [(i + 1, i) for i in range(n - 1)]
 
+    def shift(x, axis, pairs):
+        return lax.ppermute(x, axis, pairs)
+
     chip_pairs = [(i, i ^ 1) for i in range(row_count)]
     cross_pairs = [((i + 1 ^ 1) - 1, i) for i in range(1, row_count - 1)]
     middle = row_count // 2
@@ -313,15 +316,17 @@
     lat_col = (lax.axis_index("col") * (width // NLON)).astype(jnp.int32).reshape(1)
 
     starts = (0, width - PAIR, PAIR, width - 2 * PAIR)
-    chip = lax.ppermute(block, "row", chip_pairs)
-    own0, own1 = take_columns(in_hbm(block), pltpu.HBM, [(0, PAIR), (width - PAIR, width)])
+    chip = shift(block, "row", chip_pairs)
+    (own0,) = take_columns(in_hbm(block), pltpu.HBM, [(0, PAIR)])
+    (own1,) = take_columns(in_hbm(block), pltpu.HBM, [(width - PAIR, width)])
     (copy2,) = take_columns(chip, pl.ANY, [(PAIR, width - PAIR)])
-    across0 = lax.ppermute(own0, "row", cross_pairs)
-    ends = lax.ppermute(own1, "row", [(middle - 1, 0), (middle, last)])
-    relay = lax.ppermute(ends, "row", [(0, middle), (last, middle - 1)])
-    across1 = lax.ppermute(own1, "row", other_pairs)
-    across2 = lax.ppermute(copy2, "row", copy_pairs)
-    across = ([across0], [across1, relay], [across2], [across2])
+    across0 = shift(own0, "row", cross_pairs)
+    ends = shift(own1, "row", [(middle - 1, 0), (middle, last)])
+    relay = shift(ends, "row", [(0, middle), (last, middle - 1)])
+    across1 = shift(own1, "row", other_pairs)
+    mid = shift(copy2, "row", [p for p in copy_pairs if p[1] in (middle - 1, middle)])
+    across2 = shift(copy2, "row", [p for p in copy_pairs if p[1] not in (middle - 1, middle)])
+    across = ([across0], [across1, relay], [mid, across2], [mid, across2])
     offset = (0, 0, 0, width - 3 * PAIR)
     row_bands = build_bands(lat_row, fields, rows // PAIR, True)
     half, side = [], []
@@ -330,7 +335,7 @@
         begins = [starts[k]] * 2 + [offset[k]] * len(across[k])
         half.append(apply_rows(lat_row, PAIR, sources, begins, row_bands))
         pairs = forward(col_count) if k % 2 else backward(col_count)
-        side.append(lax.ppermute(half[k], "col", pairs))
+        side.append(shift(half[k], "col", pairs))
     col_bands = build_bands(lat_col, fields, width // PAIR, False)
     parts = [side[1], half[0], half[2], half[3], half[1], side[0]]
     part = apply_cols(parts, col_bands, width)

time: 86.8 us -> 88.5 us (1.020)
  the two profiles are of different devices: /device:TPU:13 before, /device:TPU:67 now
where the time goes in v12:
time: 88.5 us; the launch traced here: 87.9 us
  Pallas kernels  33.2 us (38%)
  starting transfers between devices  32.9 us (37%)
  waiting for transfers between devices  21.5 us (24%)
    ppermute x11, starting transfers between devices, shift(): return lax.ppermute(x, axis, pairs)  32.9 us
    ppermute x11, waiting for transfers between devices, shift(): return lax.ppermute(x, axis, pairs)  21.5 us
    pallas_call x4, Pallas kernels, apply_rows(): pl.pallas_call(functools.partial(rows_kernel, starts), out_shape=pltpu.VM...  13.5 us
    pallas_call x1, Pallas kernels, apply_cols(): pl.pallas_call(cols_kernel, out_shape=jax.ShapeDtypeStruct((rows, width),...  6.97 us
    pallas_call x2, Pallas kernels, build_bands(): pl.pallas_call(functools.partial(band_kernel, transposed), out_shape=(ban...  5.06 us
    pallas_call x3, Pallas kernels, take_columns(): pl.pallas_call(functools.partial(take_kernel, starts), out_shape=tuple((p...  4.96 us
    pallas_call x1, Pallas kernels, apply_tail(): pl.pallas_call(tail_kernel, grid=(2,), out_shape=jax.ShapeDtypeStruct((ro...  2.8 us
  transfers between devices with their start and end apart: 11, of which 5 were waited for; matrix products, arithmetic and copies ran while one was open for 0% of the time, Pallas kernels for 35%

profile of v12, /device:TPU:67, one launch (start us, length us, event | category | flops | bytes accessed | tf_op | source)
XLA Modules:
  0.0 87.9 jit_solution(10445868521509051156)
XLA Ops:
  0.0 0.7 collective-permute-start
  0.7 1.9 %take.4 = f32[512,256]{1,0:T(8,128)} custom-call(f32[512,1024]{1,0:T(8,128)} %bitcast.23), custom_call_target="tpu_custom_call" | custom-call | tf_op jit(solution)/shard_map/take/pallas_call | solution.py:159
  2.6 1.5 %collective-permute-start.6 = (f32[512,256]{1,0:T(8,128)}, f32[512,256]{1,0:T(8,128)}, u32[]{:S(2)}, u32[]{:S(2)}) collective-permute-start(f32[512,256]{1,0:T(8,128)} %take.4), channel_id=1, source_target_pairs={{56,0},{64,120},{57,1},{65,121},{58,2},{66,122},{59,3},{67,123},{6... | collective-permute-start | bytes 1572872 | tf_op jit(solution)/shard_map/ppermute | solution.py:298
  4.1 0.6 collective-permute-done.source.refs_1_
  4.7 1.1 %take.3 = f32[512,512]{1,0:T(8,128)} custom-call(f32[512,1024]{1,0:T(8,128)S(1)} %collective-permute-done.source.refs_1_), custom_call_target="tpu_custom_call" | custom-call | tf_op jit(solution)/shard_map/take/pallas_call | solution.py:159
  5.8 0.0 copy-start
  5.8 0.0 copy-start.1
  5.8 0.0 copy-start.2
  5.8 0.0 copy-start.3
  5.8 0.0 copy-start.4
  5.8 0.0 copy-start.5
  5.8 0.9 collective-permute-start.1
  6.7 1.9 %collective-permute-start.2 = (f32[512,512]{1,0:T(8,128)}, f32[512,512]{1,0:T(8,128)}, u32[]{:S(2)}, u32[]{:S(2)}) collective-permute-start(f32[512,512]{1,0:T(8,128)} %take.3), channel_id=1, source_target_pairs={{24,8},{0,16},{40,24},{16,32},{56,40},{32,48},{88,72},{64,80},{104... | collective-permute-start | bytes 3145736 | tf_op jit(solution)/shard_map/ppermute | solution.py:298
  8.6 8.8 %collective-permute-start.5 = (f32[512,256]{1,0:T(8,128)}, f32[512,256]{1,0:T(8,128)}, u32[]{:S(2)}, u32[]{:S(2)}) collective-permute-start(f32[512,256]{1,0:T(8,128)} %take.4), channel_id=1, source_target_pairs={{16,8},{8,16},{32,24},{24,32},{48,40},{40,48},{80,72},{72,80},{96,... | collective-permute-start | bytes 1572872 | tf_op jit(solution)/shard_map/ppermute | solution.py:298
  17.4 0.0 collective-permute-done.6
  17.4 1.5 %collective-permute-start.7 = (f32[512,256]{1,0:T(8,128)}, f32[512,256]{1,0:T(8,128)}, u32[]{:S(2)}, u32[]{:S(2)}) collective-permute-start(f32[512,256]{1,0:T(8,128)} %collective-permute-done.6), channel_id=1, source_target_pairs={{0,64},{120,56},{1,65},{121,57},{2,66},{122,58},{3,67},{123,59},{4... | collective-permute-start | bytes 1572872 | tf_op jit(solution)/shard_map/ppermute | solution.py:298
  18.9 1.9 %take.5 = f32[512,256]{1,0:T(8,128)} custom-call(f32[512,1024]{1,0:T(8,128)} %bitcast.24), custom_call_target="tpu_custom_call" | custom-call | tf_op jit(solution)/shard_map/take/pallas_call | solution.py:159
  20.8 1.9 %collective-permute-start.9 = (f32[512,256]{1,0:T(8,128)}, f32[512,256]{1,0:T(8,128)}, u32[]{:S(2)}, u32[]{:S(2)}) collective-permute-start(f32[512,256]{1,0:T(8,128)} %take.5), channel_id=1, source_target_pairs={{16,8},{8,16},{32,24},{24,32},{48,40},{40,48},{64,56},{56,64},{80,... | collective-permute-start | bytes 1572872 | tf_op jit(solution)/shard_map/ppermute | solution.py:298
  22.8 0.0 copy-done
  22.8 0.0 copy-done.1
  22.8 0.0 copy-done.2
  22.8 0.0 copy-done.3
  22.8 0.0 copy-done.4
  22.8 0.0 copy-done.5
  22.8 2.0 %row_bands.1 = (bf16[2,256,1280]{2,1,0:T(8,128)(2,1)S(1)}, bf16[2,256,1280]{2,1,0:T(8,128)(2,1)S(1)}) custom-call(s32[1]{0:T(128)} %bitcast.place, s32[64,128]{1,0:T(8,128)S(1)} %bitcast.10, s32[64,128]{1,0:T(8,128)S(1)} %bitcast.12, s32[64,128]{1,0:T(8,128)S(1)} %bitcast.14, f32[64,128]{1,0:T(8,128)S(1)} %bitcast.16, f32[64,128]{1,0:T(8,128)S(1)} %bitcast.18, ...), custom_call_target="tpu_custom_call" | custom-call | tf_op jit(solution)/shard_map/row_bands/pallas_call | solution.py:125
  24.8 4.7 %collective-permute-done.5.refs_2_ = f32[512,256]{1,0:T(8,128)} collective-permute-done((f32[512,256]{1,0:T(8,128)}, f32[512,256]{1,0:T(8,128)}, u32[]{:S(2)}, u32[]{:S(2)}) %collective-permute-start.5) | collective-permute-done | bytes 524320 | tf_op jit(solution)/shard_map/ppermute | solution.py:298
  29.5 0.0 collective-permute-done.7.refs_3_
  29.5 3.5 %rows.6.refs_4_ = f32[512,256]{1,0:T(8,128)} custom-call(s32[1]{0:T(128)} %bitcast.place, f32[512,1024]{1,0:T(8,128)} %bitcast.25, f32[512,1024]{1,0:T(8,128)S(1)} %collective-permute-done.source.refs_1_, f32[512,256]{1,0:T(8,128)} %collective-permute-done.5.refs_2_, f32[512,256]{1,0:T(8,128)} %collective-permute-done.7.refs_3_, ...), custom_call_target="tpu_custom_call" | custom-call | tf_op jit(solution)/shard_map/rows/pallas_call | solution.py:206
  33.0 4.5 %collective-permute-start.8 = (f32[512,256]{1,0:T(8,128)}, f32[512,256]{1,0:T(8,128)}, u32[]{:S(2)}, u32[]{:S(2)}) collective-permute-start(f32[512,256]{1,0:T(8,128)} %rows.6.refs_4_), channel_id=1, source_target_pairs={{0,1},{1,2},{2,3},{3,4},{4,5},{5,6},{6,7},{8,9},{9,10},{10,11},{11... | collective-permute-start | bytes 1572872 | tf_op jit(solution)/shard_map/ppermute | solution.py:298
  37.5 2.5 %collective-permute-done.9.refs_2_ = f32[512,256]{1,0:T(8,128)} collective-permute-done((f32[512,256]{1,0:T(8,128)}, f32[512,256]{1,0:T(8,128)}, u32[]{:S(2)}, u32[]{:S(2)}) %collective-permute-start.9) | collective-permute-done | bytes 524320 | tf_op jit(solution)/shard_map/ppermute | solution.py:298
  40.0 3.3 %rows.7.refs_1_ = f32[512,256]{1,0:T(8,128)} custom-call(s32[1]{0:T(128)} %bitcast.place, f32[512,1024]{1,0:T(8,128)} %bitcast.26, f32[512,1024]{1,0:T(8,128)S(1)} %collective-permute-done.source.refs_1_, f32[512,256]{1,0:T(8,128)} %collective-permute-done.9.refs_2_, bf16[2,256,1280]{2,1,0:T(8,128)(2,1)S(1)} %get-tuple-element.9.refs_4_.refs_3_, ...), custom_call_target="tpu_custom_call" | custom-call | tf_op jit(solution)/shard_map/rows/pallas_call | solution.py:206
  43.2 4.5 %collective-permute-start.10 = (f32[512,256]{1,0:T(8,128)}, f32[512,256]{1,0:T(8,128)}, u32[]{:S(2)}, u32[]{:S(2)}) collective-permute-start(f32[512,256]{1,0:T(8,128)} %rows.7.refs_1_), channel_id=1, source_target_pairs={{1,0},{2,1},{3,2},{4,3},{5,4},{6,5},{7,6},{9,8},{10,9},{11,10},{12... | collective-permute-start | bytes 1572872 | tf_op jit(solution)/shard_map/ppermute | solution.py:298
  47.8 0.0 collective-permute-done.1.refs_2_
  47.8 0.0 collective-permute-done.2.refs_3_
  47.8 3.3 %rows.5.refs_2_ = f32[512,256]{1,0:T(8,128)} custom-call(s32[1]{0:T(128)} %bitcast.place, f32[512,1024]{1,0:T(8,128)} %bitcast.27, f32[512,1024]{1,0:T(8,128)S(1)} %collective-permute-done.source.refs_1_, f32[512,512]{1,0:T(8,128)S(1)} %collective-permute-done.1.refs_2_, f32[512,512]{1,0:T(8,128)} %collective-permute-done.2.refs_3_, ...), custom_call_target="tpu_custom_call" | custom-call | tf_op jit(solution)/shard_map/rows/pallas_call | solution.py:206
  51.1 2.3 %collective-permute-start.4 = (f32[512,256]{1,0:T(8,128)}, f32[512,256]{1,0:T(8,128)}, u32[]{:S(2)}, u32[]{:S(2)}) collective-permute-start(f32[512,256]{1,0:T(8,128)} %rows.5.refs_2_), channel_id=1, source_target_pairs={{1,0},{2,1},{3,2},{4,3},{5,4},{6,5},{7,6},{9,8},{10,9},{11,10},{12... | collective-permute-start | bytes 1572872 | tf_op jit(solution)/shard_map/ppermute | solution.py:298
  53.4 3.3 %rows.4.refs_3_ = f32[512,256]{1,0:T(8,128)} custom-call(s32[1]{0:T(128)} %bitcast.place, f32[512,1024]{1,0:T(8,128)} %bitcast.28, f32[512,1024]{1,0:T(8,128)S(1)} %collective-permute-done.source.refs_1_, f32[512,512]{1,0:T(8,128)S(1)} %collective-permute-done.1.refs_2_, f32[512,512]{1,0:T(8,128)} %collective-permute-done.2.refs_3_, ...), custom_call_target="tpu_custom_call" | custom-call | tf_op jit(solution)/shard_map/rows/pallas_call | solution.py:206
  56.8 4.5 %collective-permute-start.3 = (f32[512,256]{1,0:T(8,128)}, f32[512,256]{1,0:T(8,128)S(1)}, u32[]{:S(2)}, u32[]{:S(2)}) collective-permute-start(f32[512,256]{1,0:T(8,128)} %rows.4.refs_3_), channel_id=1, source_target_pairs={{0,1},{1,2},{2,3},{3,4},{4,5},{5,6},{6,7},{8,9},{9,10},{10,11},{11... | collective-permute-start | bytes 1572872 | tf_op jit(solution)/shard_map/ppermute | solution.py:298
  61.3 3.1 %col_bands.1 = (bf16[4,1280,256]{2,1,0:T(8,128)(2,1)S(1)}, bf16[4,1280,256]{2,1,0:T(8,128)(2,1)S(1)}) custom-call(s32[1]{0:T(128)} %bitcast.8.place, s32[64,128]{1,0:T(8,128)S(1)} %bitcast.11, s32[64,128]{1,0:T(8,128)S(1)} %bitcast.13, s32[64,128]{1,0:T(8,128)S(1)} %bitcast.15, f32[64,128]{1,0:T(8,128)S(1)} %bitcast.17, f32[64,128]{1,0:T(8,128)S(1)} %bitcast.19, ...), custom_call_target="tpu_custom_call" | custom-call | tf_op jit(solution)/shard_map/col_bands/pallas_call | solution.py:125
  64.4 6.6 %collective-permute-done.8.refs_0_ = f32[512,256]{1,0:T(8,128)} collective-permute-done((f32[512,256]{1,0:T(8,128)}, f32[512,256]{1,0:T(8,128)}, u32[]{:S(2)}, u32[]{:S(2)}) %collective-permute-start.8) | collective-permute-done | bytes 524320 | tf_op jit(solution)/shard_map/ppermute | solution.py:298
  71.0 0.0 collective-permute-done.10.refs_5_
  71.0 7.0 %cols.1.part = f32[512,1024]{1,0:T(8,128)} custom-call(f32[512,256]{1,0:T(8,128)} %collective-permute-done.8.refs_0_, f32[512,256]{1,0:T(8,128)} %rows.7.refs_1_, f32[512,256]{1,0:T(8,128)} %rows.5.refs_2_, f32[512,256]{1,0:T(8,128)} %rows.4.refs_3_, f32[512,256]{1,0:T(8,128)} %rows.6.refs_4_, f32[512,256]{1,0:T(8,128)} %collective-permute-done.10.refs_5_, ...), custom_call_target="tpu_custom_call" | custom-call | tf_op jit(solution)/shard_map/cols/pallas_call | solution.py:244
  78.0 7.2 %collective-permute-done.4.east = f32[512,256]{1,0:T(8,128)} collective-permute-done((f32[512,256]{1,0:T(8,128)}, f32[512,256]{1,0:T(8,128)}, u32[]{:S(2)}, u32[]{:S(2)}) %collective-permute-start.4) | collective-permute-done | bytes 524320 | tf_op jit(solution)/shard_map/ppermute | solution.py:298
  85.1 0.0 collective-permute-done.3.west
  85.1 2.8 %tail.1 = f32[512,1024]{1,0:T(8,128)} custom-call(f32[512,256]{1,0:T(8,128)S(1)} %collective-permute-done.3.west, f32[512,256]{1,0:T(8,128)} %collective-permute-done.4.east, bf16[4,1280,256]{2,1,0:T(8,128)(2,1)S(1)} %get-tuple-element.11.refs_6_.band_high, ...), custom_call_target="tpu_custom_call", output_to_operand_aliasing={{}: (4, {})} | custom-call | tf_op jit(solution)/shard_map/tail/pallas_call | solution.py:275
Async XLA Ops:
  0.0 4.7 %collective-permute-start = (f32[512,1024]{1,0:T(8,128)}, f32[512,1024]{1,0:T(8,128)S(1)}, u32[]{:S(2)}, u32[]{:S(2)}) collective-permute-start(f32[512,1024]{1,0:T(8,128)} %bitcast.22), channel_id=1, source_target_pairs={{0,8},{8,0},{16,24},{24,16},{32,40},{40,32},{48,56},{56,48},{64,72... | collective-permute-start | bytes 6291464 | tf_op jit(solution)/shard_map/ppermute | solution.py:298
  2.6 14.8 %collective-permute-start.6 = (f32[512,256]{1,0:T(8,128)}, f32[512,256]{1,0:T(8,128)}, u32[]{:S(2)}, u32[]{:S(2)}) collective-permute-start(f32[512,256]{1,0:T(8,128)} %take.4), channel_id=1, source_target_pairs={{56,0},{64,120},{57,1},{65,121},{58,2},{66,122},{59,3},{67,123},{6... | collective-permute-start | bytes 1572872 | tf_op jit(solution)/shard_map/ppermute | solution.py:298
  5.8 17.0 %copy-start = (s32[1,1,8192]{2,1,0:T(1,128)S(1)}, s32[1,1,8192]{2,1,0:T(1,128)}, u32[]{:S(2)}) copy-start(s32[1,1,8192]{2,1,0:T(1,128)} %param.8) | copy-start | bytes 98308
  5.8 17.0 %copy-start.1 = (s32[1,1,8192]{2,1,0:T(1,128)S(1)}, s32[1,1,8192]{2,1,0:T(1,128)}, u32[]{:S(2)}) copy-start(s32[1,1,8192]{2,1,0:T(1,128)} %param.9) | copy-start | bytes 98308
  5.8 17.0 %copy-start.2 = (s32[1,1,8192]{2,1,0:T(1,128)S(1)}, s32[1,1,8192]{2,1,0:T(1,128)}, u32[]{:S(2)}) copy-start(s32[1,1,8192]{2,1,0:T(1,128)} %param.10) | copy-start | bytes 98308
  5.8 17.0 %copy-start.3 = (f32[1,1,8192]{2,1,0:T(1,128)S(1)}, f32[1,1,8192]{2,1,0:T(1,128)}, u32[]{:S(2)}) copy-start(f32[1,1,8192]{2,1,0:T(1,128)} %param.11) | copy-start | bytes 98308
  5.8 17.0 %copy-start.4 = (f32[1,8192]{1,0:T(1,128)S(1)}, f32[1,8192]{1,0:T(1,128)}, u32[]{:S(2)}) copy-start(f32[1,8192]{1,0:T(1,128)} %param.12) | copy-start | bytes 98308
  5.8 17.0 %copy-start.5 = (f32[1,8192]{1,0:T(1,128)S(1)}, f32[1,8192]{1,0:T(1,128)}, u32[]{:S(2)}) copy-start(f32[1,8192]{1,0:T(1,128)} %param.13) | copy-start | bytes 98308
  5.8 41.9 %collective-permute-start.1 = (f32[512,512]{1,0:T(8,128)}, f32[512,512]{1,0:T(8,128)S(1)}, u32[]{:S(2)}, u32[]{:S(2)}) collective-permute-start(f32[512,512]{1,0:T(8,128)} %take.3), channel_id=1, source_target_pairs={{72,56},{48,64},{73,57},{49,65},{74,58},{50,66},{75,59},{51,67},{7... | collective-permute-start | bytes 3145736 | tf_op jit(solution)/shard_map/ppermute | solution.py:298
  6.7 41.1 %collective-permute-start.2 = (f32[512,512]{1,0:T(8,128)}, f32[512,512]{1,0:T(8,128)}, u32[]{:S(2)}, u32[]{:S(2)}) collective-permute-start(f32[512,512]{1,0:T(8,128)} %take.3), channel_id=1, source_target_pairs={{24,8},{0,16},{40,24},{16,32},{56,40},{32,48},{88,72},{64,80},{104... | collective-permute-start | bytes 3145736 | tf_op jit(solution)/shard_map/ppermute | solution.py:298
  8.6 20.8 %collective-permute-start.5 = (f32[512,256]{1,0:T(8,128)}, f32[512,256]{1,0:T(8,128)}, u32[]{:S(2)}, u32[]{:S(2)}) collective-permute-start(f32[512,256]{1,0:T(8,128)} %take.4), channel_id=1, source_target_pairs={{16,8},{8,16},{32,24},{24,32},{48,40},{40,48},{80,72},{72,80},{96,... | collective-permute-start | bytes 1572872 | tf_op jit(solution)/shard_map/ppermute | solution.py:298
  17.4 12.0 %collective-permute-start.7 = (f32[512,256]{1,0:T(8,128)}, f32[512,256]{1,0:T(8,128)}, u32[]{:S(2)}, u32[]{:S(2)}) collective-permute-start(f32[512,256]{1,0:T(8,128)} %collective-permute-done.6), channel_id=1, source_target_pairs={{0,64},{120,56},{1,65},{121,57},{2,66},{122,58},{3,67},{123,59},{4... | collective-permute-start | bytes 1572872 | tf_op jit(solution)/shard_map/ppermute | solution.py:298
  20.8 19.1 %collective-permute-start.9 = (f32[512,256]{1,0:T(8,128)}, f32[512,256]{1,0:T(8,128)}, u32[]{:S(2)}, u32[]{:S(2)}) collective-permute-start(f32[512,256]{1,0:T(8,128)} %take.5), channel_id=1, source_target_pairs={{16,8},{8,16},{32,24},{24,32},{48,40},{40,48},{64,56},{56,64},{80,... | collective-permute-start | bytes 1572872 | tf_op jit(solution)/shard_map/ppermute | solution.py:298
  33.0 38.0 %collective-permute-start.8 = (f32[512,256]{1,0:T(8,128)}, f32[512,256]{1,0:T(8,128)}, u32[]{:S(2)}, u32[]{:S(2)}) collective-permute-start(f32[512,256]{1,0:T(8,128)} %rows.6.refs_4_), channel_id=1, source_target_pairs={{0,1},{1,2},{2,3},{3,4},{4,5},{5,6},{6,7},{8,9},{9,10},{10,11},{11... | collective-permute-start | bytes 1572872 | tf_op jit(solution)/shard_map/ppermute | solution.py:298
  43.2 27.8 %collective-permute-start.10 = (f32[512,256]{1,0:T(8,128)}, f32[512,256]{1,0:T(8,128)}, u32[]{:S(2)}, u32[]{:S(2)}) collective-permute-start(f32[512,256]{1,0:T(8,128)} %rows.7.refs_1_), channel_id=1, source_target_pairs={{1,0},{2,1},{3,2},{4,3},{5,4},{6,5},{7,6},{9,8},{10,9},{11,10},{12... | collective-permute-start | bytes 1572872 | tf_op jit(solution)/shard_map/ppermute | solution.py:298
  51.1 34.0 %collective-permute-start.4 = (f32[512,256]{1,0:T(8,128)}, f32[512,256]{1,0:T(8,128)}, u32[]{:S(2)}, u32[]{:S(2)}) collective-permute-start(f32[512,256]{1,0:T(8,128)} %rows.5.refs_2_), channel_id=1, source_target_pairs={{1,0},{2,1},{3,2},{4,3},{5,4},{6,5},{7,6},{9,8},{10,9},{11,10},{12... | collective-permute-start | bytes 1572872 | tf_op jit(solution)/shard_map/ppermute | solution.py:298
  56.8 28.4 %collective-permute-start.3 = (f32[512,256]{1,0:T(8,128)}, f32[512,256]{1,0:T(8,128)S(1)}, u32[]{:S(2)}, u32[]{:S(2)}) collective-permute-start(f32[512,256]{1,0:T(8,128)} %rows.4.refs_3_), channel_id=1, source_target_pairs={{0,1},{1,2},{2,3},{3,4},{4,5},{5,6},{6,7},{8,9},{9,10},{10,11},{11... | collective-permute-start | bytes 1572872 | tf_op jit(solution)/shard_map/ppermute | solution.py:298

commit v13 on v11

--- a/solution.py
+++ b/solution.py
@@ -314,20 +314,23 @@
 
     starts = (0, width - PAIR, PAIR, width - 2 * PAIR)
     chip = lax.ppermute(block, "row", chip_pairs)
-    own0, own1 = take_columns(in_hbm(block), pltpu.HBM, [(0, PAIR), (width - PAIR, width)])
-    (copy2,) = take_columns(chip, pl.ANY, [(PAIR, width - PAIR)])
+    (own0,) = take_columns(in_hbm(block), pltpu.HBM, [(0, PAIR)])
+    own1, own3 = take_columns(
+        in_hbm(block), pltpu.HBM,
+        [(width - PAIR, width), (width - 2 * PAIR, width - PAIR)],
+    )
+    (copy2,) = take_columns(chip, pl.ANY, [(PAIR, 2 * PAIR)])
     across0 = lax.ppermute(own0, "row", cross_pairs)
-    ends = lax.ppermute(own1, "row", [(middle - 1, 0), (middle, last)])
-    relay = lax.ppermute(ends, "row", [(0, middle), (last, middle - 1)])
-    across1 = lax.ppermute(own1, "row", other_pairs)
+    across1 = lax.ppermute(own1, "row", cross_pairs)
     across2 = lax.ppermute(copy2, "row", copy_pairs)
-    across = ([across0], [across1, relay], [across2], [across2])
-    offset = (0, 0, 0, width - 3 * PAIR)
+    across3 = lax.ppermute(own3, "row", other_pairs + [(middle - 1, 0), (middle, last)])
+    relay = lax.ppermute(across3, "row", [(0, middle), (last, middle - 1)])
+    across = ([across0], [across1], [across2], [across3, relay])
     row_bands = build_bands(lat_row, fields, rows // PAIR, True)
     half, side = [], []
     for k in range(4):
         sources = [block, chip] + across[k]
-        begins = [starts[k]] * 2 + [offset[k]] * len(across[k])
+        begins = [starts[k]] * 2 + [0] * len(across[k])
         half.append(apply_rows(lat_row, PAIR, sources, begins, row_bands))
         pairs = forward(col_count) if k % 2 else backward(col_count)
         side.append(lax.ppermute(half[k], "col", pairs))

time: 86.8 us -> 84.9 us (0.978)
  the two profiles are of different devices: /device:TPU:13 before, /device:TPU:11 now
where the time goes in v13:
time: 84.9 us; the launch traced here: 84.2 us
  starting transfers between devices  33.5 us (39%)
  Pallas kernels  31.1 us (37%)
  waiting for transfers between devices  15.6 us (18%)
  local copies, waits for them, and re-layouts  3.7 us (4%)
    ppermute x4, waiting for transfers between devices, body(): side.append(lax.ppermute(half[k], 'col', pairs))  15.6 us
    ppermute x4, starting transfers between devices, body(): side.append(lax.ppermute(half[k], 'col', pairs))  15.4 us
    pallas_call x4, Pallas kernels, apply_rows(): pl.pallas_call(functools.partial(rows_kernel, starts), out_shape=pltpu.VM...  11.6 us
    ppermute x1, starting transfers between devices, body(): across2 = lax.ppermute(copy2, 'row', copy_pairs)  6.85 us
    pallas_call x1, Pallas kernels, apply_cols(): pl.pallas_call(cols_kernel, out_shape=jax.ShapeDtypeStruct((rows, width),...  6.65 us
    pallas_call x2, Pallas kernels, build_bands(): pl.pallas_call(functools.partial(band_kernel, transposed), out_shape=(ban...  5.03 us
    pallas_call x3, Pallas kernels, take_columns(): pl.pallas_call(functools.partial(take_kernel, starts), out_shape=tuple((p...  5 us
    unnamed x20, local copies, waits for them, and re-layouts  3.7 us
  transfers between devices with their start and end apart: 10, of which 3 were waited for; matrix products, arithmetic and copies ran while one was open for 0% of the time, Pallas kernels for 34%

profile of v13, /device:TPU:11, one launch (start us, length us, event | category | flops | bytes accessed | tf_op | source)
XLA Modules:
  0.0 84.2 jit_solution(11602380809931468634)
XLA Ops:
  0.0 0.7 collective-permute-start
  0.7 2.1 %take.3 = (f32[512,256]{1,0:T(8,128)}, f32[512,256]{1,0:T(8,128)S(1)}) custom-call(f32[512,1024]{1,0:T(8,128)} %bitcast.23), custom_call_target="tpu_custom_call" | custom-call | tf_op jit(solution)/shard_map/take/pallas_call | solution.py:159
  2.8 3.4 %collective-permute-start.1 = (f32[512,256]{1,0:T(8,128)S(1)}, f32[512,256]{1,0:T(8,128)}, u32[]{:S(2)}, u32[]{:S(2)}) collective-permute-start(f32[512,256]{1,0:T(8,128)S(1)} %get-tuple-element.11), channel_id=1, source_target_pairs={{16,8},{8,16},{32,24},{24,32},{48,40},{40,48},{80,72},{72,80},{96,... | collective-permute-start | bytes 1572872 | tf_op jit(solution)/shard_map/ppermute | solution.py:326
  6.3 0.0 copy-start.4
  6.3 0.0 copy-start.5
  6.3 0.0 copy-start.6
  6.3 0.0 copy-start.7
  6.3 0.0 copy-start.8
  6.3 0.0 copy-start.9
  6.3 2.3 %collective-permute-start.6 = (f32[512,256]{1,0:T(8,128)}, f32[512,256]{1,0:T(8,128)S(1)}, u32[]{:S(2)}, u32[]{:S(2)}) collective-permute-start(f32[512,256]{1,0:T(8,128)} %get-tuple-element.16), channel_id=1, source_target_pairs={{16,8},{8,16},{32,24},{24,32},{48,40},{40,48},{64,56},{56,64},{80,... | collective-permute-start | bytes 1572872 | tf_op jit(solution)/shard_map/ppermute | solution.py:324
  8.6 1.9 %take.5 = f32[512,256]{1,0:T(8,128)} custom-call(f32[512,1024]{1,0:T(8,128)} %bitcast.24), custom_call_target="tpu_custom_call" | custom-call | tf_op jit(solution)/shard_map/take/pallas_call | solution.py:159
  10.6 3.4 %collective-permute-start.8 = (f32[512,256]{1,0:T(8,128)}, f32[512,256]{1,0:T(8,128)S(1)}, u32[]{:S(2)}, u32[]{:S(2)}) collective-permute-start(f32[512,256]{1,0:T(8,128)} %take.5), channel_id=1, source_target_pairs={{16,8},{8,16},{32,24},{24,32},{48,40},{40,48},{64,56},{56,64},{80,... | collective-permute-start | bytes 1572872 | tf_op jit(solution)/shard_map/ppermute | solution.py:323
  14.0 0.0 collective-permute-done.1.refs_2_
  14.0 1.5 %collective-permute-start.2 = (f32[512,256]{1,0:T(8,128)}, f32[512,256]{1,0:T(8,128)}, u32[]{:S(2)}, u32[]{:S(2)}) collective-permute-start(f32[512,256]{1,0:T(8,128)} %collective-permute-done.1.refs_2_), channel_id=1, source_target_pairs={{0,64},{120,56},{1,65},{121,57},{2,66},{122,58},{3,67},{123,59},{4... | collective-permute-start | bytes 1572872 | tf_op jit(solution)/shard_map/ppermute | solution.py:327
  15.5 0.0 collective-permute-done.refs_1_.source
  15.5 0.9 %take.4 = f32[512,256]{1,0:T(8,128)} custom-call(f32[512,1024]{1,0:T(8,128)S(1)} %collective-permute-done.refs_1_.source), custom_call_target="tpu_custom_call" | custom-call | tf_op jit(solution)/shard_map/take/pallas_call | solution.py:159
  16.4 6.9 %collective-permute-start.4 = (f32[512,256]{1,0:T(8,128)}, f32[512,256]{1,0:T(8,128)}, u32[]{:S(2)}, u32[]{:S(2)}) collective-permute-start(f32[512,256]{1,0:T(8,128)} %take.4), channel_id=1, source_target_pairs={{24,8},{0,16},{40,24},{16,32},{56,40},{32,48},{72,56},{48,64},{88,... | collective-permute-start | bytes 1572872 | tf_op jit(solution)/shard_map/ppermute | solution.py:325
  23.3 0.0 copy-done.4
  23.3 0.0 copy-done.5
  23.3 0.0 copy-done.6
  23.3 0.0 copy-done.7
  23.3 0.0 copy-done.8
  23.3 0.0 copy-done.9
  23.3 1.9 %row_bands.1 = (bf16[2,256,1280]{2,1,0:T(8,128)(2,1)S(1)}, bf16[2,256,1280]{2,1,0:T(8,128)(2,1)S(1)}) custom-call(s32[1]{0:T(128)} %bitcast.place, s32[64,128]{1,0:T(8,128)S(1)} %bitcast.10, s32[64,128]{1,0:T(8,128)S(1)} %bitcast.12, s32[64,128]{1,0:T(8,128)S(1)} %bitcast.14, f32[64,128]{1,0:T(8,128)S(1)} %bitcast.16, f32[64,128]{1,0:T(8,128)S(1)} %bitcast.18, ...), custom_call_target="tpu_custom_call" | custom-call | tf_op jit(solution)/shard_map/row_bands/pallas_call | solution.py:125
  25.3 0.0 collective-permute-done.6.refs_2_
  25.3 0.0 copy-start.2
  25.3 0.8 copy-done.2
  26.1 0.0 copy-start.3
  26.1 1.0 %copy-done.3 = f32[512,256]{1,0:T(8,128)S(1)} copy-done((f32[512,256]{1,0:T(8,128)S(1)}, f32[512,256]{1,0:T(8,128)}, u32[]{:S(2)}) %copy-start.3) | copy-done | bytes 524312
  27.1 2.4 %rows.6.refs_4_ = f32[512,256]{1,0:T(8,128)S(1)} custom-call(s32[1]{0:T(128)} %bitcast.place, f32[512,1024]{1,0:T(8,128)} %bitcast.25, f32[512,1024]{1,0:T(8,128)S(1)} %collective-permute-done.refs_1_.source, f32[512,256]{1,0:T(8,128)S(1)} %copy-done.3, bf16[2,256,1280]{2,1,0:T(8,128)(2,1)S(1)} %get-tuple-element.12.refs_4_.refs_3_, ...), custom_call_target="tpu_custom_call" | custom-call | tf_op jit(solution)/shard_map/rows/pallas_call | solution.py:206
  29.5 3.9 %collective-permute-start.7 = (f32[512,256]{1,0:T(8,128)S(1)}, f32[512,256]{1,0:T(8,128)}, u32[]{:S(2)}, u32[]{:S(2)}) collective-permute-start(f32[512,256]{1,0:T(8,128)S(1)} %rows.6.refs_4_), channel_id=1, source_target_pairs={{0,1},{1,2},{2,3},{3,4},{4,5},{5,6},{6,7},{8,9},{9,10},{10,11},{11... | collective-permute-start | bytes 1572872 | tf_op jit(solution)/shard_map/ppermute | solution.py:336
  33.5 0.0 collective-permute-done.8.refs_2_
  33.5 0.0 copy-start
  33.5 0.8 copy-done
  34.3 0.0 copy-start.1
  34.3 1.0 %copy-done.1 = f32[512,256]{1,0:T(8,128)S(1)} copy-done((f32[512,256]{1,0:T(8,128)S(1)}, f32[512,256]{1,0:T(8,128)}, u32[]{:S(2)}) %copy-start.1) | copy-done | bytes 524312
  35.3 2.4 %rows.7.refs_1_ = f32[512,256]{1,0:T(8,128)S(1)} custom-call(s32[1]{0:T(128)} %bitcast.place, f32[512,1024]{1,0:T(8,128)} %bitcast.26, f32[512,1024]{1,0:T(8,128)S(1)} %collective-permute-done.refs_1_.source, f32[512,256]{1,0:T(8,128)S(1)} %copy-done.1, bf16[2,256,1280]{2,1,0:T(8,128)(2,1)S(1)} %get-tuple-element.12.refs_4_.refs_3_, ...), custom_call_target="tpu_custom_call" | custom-call | tf_op jit(solution)/shard_map/rows/pallas_call | solution.py:206
  37.7 3.8 %collective-permute-start.9 = (f32[512,256]{1,0:T(8,128)S(1)}, f32[512,256]{1,0:T(8,128)}, u32[]{:S(2)}, u32[]{:S(2)}) collective-permute-start(f32[512,256]{1,0:T(8,128)S(1)} %rows.7.refs_1_), channel_id=1, source_target_pairs={{1,0},{2,1},{3,2},{4,3},{5,4},{6,5},{7,6},{9,8},{10,9},{11,10},{12... | collective-permute-start | bytes 1572872 | tf_op jit(solution)/shard_map/ppermute | solution.py:336
  41.5 0.0 collective-permute-done.2.refs_3_
  41.5 3.5 %rows.4.refs_3_ = f32[512,256]{1,0:T(8,128)} custom-call(s32[1]{0:T(128)} %bitcast.place, f32[512,1024]{1,0:T(8,128)} %bitcast.27, f32[512,1024]{1,0:T(8,128)S(1)} %collective-permute-done.refs_1_.source, f32[512,256]{1,0:T(8,128)} %collective-permute-done.1.refs_2_, f32[512,256]{1,0:T(8,128)} %collective-permute-done.2.refs_3_, ...), custom_call_target="tpu_custom_call" | custom-call | tf_op jit(solution)/shard_map/rows/pallas_call | solution.py:206
  45.0 3.0 %collective-permute-start.3 = (f32[512,256]{1,0:T(8,128)}, f32[512,256]{1,0:T(8,128)}, u32[]{:S(2)}, u32[]{:S(2)}) collective-permute-start(f32[512,256]{1,0:T(8,128)} %rows.4.refs_3_), channel_id=1, source_target_pairs={{0,1},{1,2},{2,3},{3,4},{4,5},{5,6},{6,7},{8,9},{9,10},{10,11},{11... | collective-permute-start | bytes 1572872 | tf_op jit(solution)/shard_map/ppermute | solution.py:336
  48.1 0.0 collective-permute-done.4.refs_2_
  48.1 3.3 %rows.5.refs_2_ = f32[512,256]{1,0:T(8,128)} custom-call(s32[1]{0:T(128)} %bitcast.place, f32[512,1024]{1,0:T(8,128)} %bitcast.28, f32[512,1024]{1,0:T(8,128)S(1)} %collective-permute-done.refs_1_.source, f32[512,256]{1,0:T(8,128)} %collective-permute-done.4.refs_2_, bf16[2,256,1280]{2,1,0:T(8,128)(2,1)S(1)} %get-tuple-element.12.refs_4_.refs_3_, ...), custom_call_target="tpu_custom_call" | custom-call | tf_op jit(solution)/shard_map/rows/pallas_call | solution.py:206
  51.3 4.7 %collective-permute-start.5 = (f32[512,256]{1,0:T(8,128)}, f32[512,256]{1,0:T(8,128)S(1)}, u32[]{:S(2)}, u32[]{:S(2)}) collective-permute-start(f32[512,256]{1,0:T(8,128)} %rows.5.refs_2_), channel_id=1, source_target_pairs={{1,0},{2,1},{3,2},{4,3},{5,4},{6,5},{7,6},{9,8},{10,9},{11,10},{12... | collective-permute-start | bytes 1572872 | tf_op jit(solution)/shard_map/ppermute | solution.py:336
  56.0 3.1 %col_bands.1 = (bf16[4,1280,256]{2,1,0:T(8,128)(2,1)S(1)}, bf16[4,1280,256]{2,1,0:T(8,128)(2,1)S(1)}) custom-call(s32[1]{0:T(128)} %bitcast.8.place, s32[64,128]{1,0:T(8,128)S(1)} %bitcast.11, s32[64,128]{1,0:T(8,128)S(1)} %bitcast.13, s32[64,128]{1,0:T(8,128)S(1)} %bitcast.15, f32[64,128]{1,0:T(8,128)S(1)} %bitcast.17, f32[64,128]{1,0:T(8,128)S(1)} %bitcast.19, ...), custom_call_target="tpu_custom_call" | custom-call | tf_op jit(solution)/shard_map/col_bands/pallas_call | solution.py:125
  59.1 0.0 collective-permute-done.7.refs_0_
  59.1 11.1 %collective-permute-done.9.refs_5_ = f32[512,256]{1,0:T(8,128)} collective-permute-done((f32[512,256]{1,0:T(8,128)S(1)}, f32[512,256]{1,0:T(8,128)}, u32[]{:S(2)}, u32[]{:S(2)}) %collective-permute-start.9) | collective-permute-done | bytes 524320 | tf_op jit(solution)/shard_map/ppermute | solution.py:336
  70.3 6.6 %cols.1.part = f32[512,1024]{1,0:T(8,128)} custom-call(f32[512,256]{1,0:T(8,128)} %collective-permute-done.7.refs_0_, f32[512,256]{1,0:T(8,128)S(1)} %rows.7.refs_1_, f32[512,256]{1,0:T(8,128)} %rows.5.refs_2_, f32[512,256]{1,0:T(8,128)} %rows.4.refs_3_, f32[512,256]{1,0:T(8,128)S(1)} %rows.6.refs_4_, f32[512,256]{1,0:T(8,128)} %collective-permute-done.9.refs_5_, ...), custom_call_target="tpu_custom_call" | custom-call | tf_op jit(solution)/shard_map/cols/pallas_call | solution.py:244
  76.9 1.2 %collective-permute-done.3.west = f32[512,256]{1,0:T(8,128)} collective-permute-done((f32[512,256]{1,0:T(8,128)}, f32[512,256]{1,0:T(8,128)}, u32[]{:S(2)}, u32[]{:S(2)}) %collective-permute-start.3) | collective-permute-done | bytes 524320 | tf_op jit(solution)/shard_map/ppermute | solution.py:336
  78.1 3.3 %collective-permute-done.5.east = f32[512,256]{1,0:T(8,128)S(1)} collective-permute-done((f32[512,256]{1,0:T(8,128)}, f32[512,256]{1,0:T(8,128)S(1)}, u32[]{:S(2)}, u32[]{:S(2)}) %collective-permute-start.5) | collective-permute-done | bytes 524320 | tf_op jit(solution)/shard_map/ppermute | solution.py:336
  81.4 2.8 %tail.1 = f32[512,1024]{1,0:T(8,128)} custom-call(f32[512,256]{1,0:T(8,128)} %collective-permute-done.3.west, f32[512,256]{1,0:T(8,128)S(1)} %collective-permute-done.5.east, bf16[4,1280,256]{2,1,0:T(8,128)(2,1)S(1)} %get-tuple-element.14.refs_6_.band_high, ...), custom_call_target="tpu_custom_call", output_to_operand_aliasing={{}: (4, {})} | custom-call | tf_op jit(solution)/shard_map/tail/pallas_call | solution.py:275
Async XLA Ops:
  0.0 15.5 %collective-permute-start = (f32[512,1024]{1,0:T(8,128)}, f32[512,1024]{1,0:T(8,128)S(1)}, u32[]{:S(2)}, u32[]{:S(2)}) collective-permute-start(f32[512,1024]{1,0:T(8,128)} %bitcast.22), channel_id=1, source_target_pairs={{0,8},{8,0},{16,24},{24,16},{32,40},{40,32},{48,56},{56,48},{64,72... | collective-permute-start | bytes 6291464 | tf_op jit(solution)/shard_map/ppermute | solution.py:316
  2.8 11.2 %collective-permute-start.1 = (f32[512,256]{1,0:T(8,128)S(1)}, f32[512,256]{1,0:T(8,128)}, u32[]{:S(2)}, u32[]{:S(2)}) collective-permute-start(f32[512,256]{1,0:T(8,128)S(1)} %get-tuple-element.11), channel_id=1, source_target_pairs={{16,8},{8,16},{32,24},{24,32},{48,40},{40,48},{80,72},{72,80},{96,... | collective-permute-start | bytes 1572872 | tf_op jit(solution)/shard_map/ppermute | solution.py:326
  6.3 17.0 %copy-start.4 = (s32[1,1,8192]{2,1,0:T(1,128)S(1)}, s32[1,1,8192]{2,1,0:T(1,128)}, u32[]{:S(2)}) copy-start(s32[1,1,8192]{2,1,0:T(1,128)} %param.8) | copy-start | bytes 98308
  6.3 17.0 %copy-start.5 = (s32[1,1,8192]{2,1,0:T(1,128)S(1)}, s32[1,1,8192]{2,1,0:T(1,128)}, u32[]{:S(2)}) copy-start(s32[1,1,8192]{2,1,0:T(1,128)} %param.9) | copy-start | bytes 98308
  6.3 17.0 %copy-start.6 = (s32[1,1,8192]{2,1,0:T(1,128)S(1)}, s32[1,1,8192]{2,1,0:T(1,128)}, u32[]{:S(2)}) copy-start(s32[1,1,8192]{2,1,0:T(1,128)} %param.10) | copy-start | bytes 98308
  6.3 17.0 %copy-start.7 = (f32[1,1,8192]{2,1,0:T(1,128)S(1)}, f32[1,1,8192]{2,1,0:T(1,128)}, u32[]{:S(2)}) copy-start(f32[1,1,8192]{2,1,0:T(1,128)} %param.11) | copy-start | bytes 98308
  6.3 17.0 %copy-start.8 = (f32[1,8192]{1,0:T(1,128)S(1)}, f32[1,8192]{1,0:T(1,128)}, u32[]{:S(2)}) copy-start(f32[1,8192]{1,0:T(1,128)} %param.12) | copy-start | bytes 98308
  6.3 17.0 %copy-start.9 = (f32[1,8192]{1,0:T(1,128)S(1)}, f32[1,8192]{1,0:T(1,128)}, u32[]{:S(2)}) copy-start(f32[1,8192]{1,0:T(1,128)} %param.13) | copy-start | bytes 98308
  6.3 18.9 %collective-permute-start.6 = (f32[512,256]{1,0:T(8,128)}, f32[512,256]{1,0:T(8,128)S(1)}, u32[]{:S(2)}, u32[]{:S(2)}) collective-permute-start(f32[512,256]{1,0:T(8,128)} %get-tuple-element.16), channel_id=1, source_target_pairs={{16,8},{8,16},{32,24},{24,32},{48,40},{40,48},{64,56},{56,64},{80,... | collective-permute-start | bytes 1572872 | tf_op jit(solution)/shard_map/ppermute | solution.py:324
  10.6 22.9 %collective-permute-start.8 = (f32[512,256]{1,0:T(8,128)}, f32[512,256]{1,0:T(8,128)S(1)}, u32[]{:S(2)}, u32[]{:S(2)}) collective-permute-start(f32[512,256]{1,0:T(8,128)} %take.5), channel_id=1, source_target_pairs={{16,8},{8,16},{32,24},{24,32},{48,40},{40,48},{64,56},{56,64},{80,... | collective-permute-start | bytes 1572872 | tf_op jit(solution)/shard_map/ppermute | solution.py:323
  14.0 27.5 %collective-permute-start.2 = (f32[512,256]{1,0:T(8,128)}, f32[512,256]{1,0:T(8,128)}, u32[]{:S(2)}, u32[]{:S(2)}) collective-permute-start(f32[512,256]{1,0:T(8,128)} %collective-permute-done.1.refs_2_), channel_id=1, source_target_pairs={{0,64},{120,56},{1,65},{121,57},{2,66},{122,58},{3,67},{123,59},{4... | collective-permute-start | bytes 1572872 | tf_op jit(solution)/shard_map/ppermute | solution.py:327
  16.4 31.7 %collective-permute-start.4 = (f32[512,256]{1,0:T(8,128)}, f32[512,256]{1,0:T(8,128)}, u32[]{:S(2)}, u32[]{:S(2)}) collective-permute-start(f32[512,256]{1,0:T(8,128)} %take.4), channel_id=1, source_target_pairs={{24,8},{0,16},{40,24},{16,32},{56,40},{32,48},{72,56},{48,64},{88,... | collective-permute-start | bytes 1572872 | tf_op jit(solution)/shard_map/ppermute | solution.py:325
  25.3 0.8 copy-start.2
  26.1 1.0 %copy-start.3 = (f32[512,256]{1,0:T(8,128)S(1)}, f32[512,256]{1,0:T(8,128)}, u32[]{:S(2)}) copy-start(f32[512,256]{1,0:T(8,128)} %copy-done.2) | copy-start | bytes 1572868
  29.5 29.6 %collective-permute-start.7 = (f32[512,256]{1,0:T(8,128)S(1)}, f32[512,256]{1,0:T(8,128)}, u32[]{:S(2)}, u32[]{:S(2)}) collective-permute-start(f32[512,256]{1,0:T(8,128)S(1)} %rows.6.refs_4_), channel_id=1, source_target_pairs={{0,1},{1,2},{2,3},{3,4},{4,5},{5,6},{6,7},{8,9},{9,10},{10,11},{11... | collective-permute-start | bytes 1572872 | tf_op jit(solution)/shard_map/ppermute | solution.py:336
  33.5 0.8 copy-start
  34.3 1.0 %copy-start.1 = (f32[512,256]{1,0:T(8,128)S(1)}, f32[512,256]{1,0:T(8,128)}, u32[]{:S(2)}) copy-start(f32[512,256]{1,0:T(8,128)} %copy-done) | copy-start | bytes 1572868
  37.7 32.5 %collective-permute-start.9 = (f32[512,256]{1,0:T(8,128)S(1)}, f32[512,256]{1,0:T(8,128)}, u32[]{:S(2)}, u32[]{:S(2)}) collective-permute-start(f32[512,256]{1,0:T(8,128)S(1)} %rows.7.refs_1_), channel_id=1, source_target_pairs={{1,0},{2,1},{3,2},{4,3},{5,4},{6,5},{7,6},{9,8},{10,9},{11,10},{12... | collective-permute-start | bytes 1572872 | tf_op jit(solution)/shard_map/ppermute | solution.py:336
  45.0 33.1 %collective-permute-start.3 = (f32[512,256]{1,0:T(8,128)}, f32[512,256]{1,0:T(8,128)}, u32[]{:S(2)}, u32[]{:S(2)}) collective-permute-start(f32[512,256]{1,0:T(8,128)} %rows.4.refs_3_), channel_id=1, source_target_pairs={{0,1},{1,2},{2,3},{3,4},{4,5},{5,6},{6,7},{8,9},{9,10},{10,11},{11... | collective-permute-start | bytes 1572872 | tf_op jit(solution)/shard_map/ppermute | solution.py:336
  51.3 30.0 %collective-permute-start.5 = (f32[512,256]{1,0:T(8,128)}, f32[512,256]{1,0:T(8,128)S(1)}, u32[]{:S(2)}, u32[]{:S(2)}) collective-permute-start(f32[512,256]{1,0:T(8,128)} %rows.5.refs_2_), channel_id=1, source_target_pairs={{1,0},{2,1},{3,2},{4,3},{5,4},{6,5},{7,6},{9,8},{10,9},{11,10},{12... | collective-permute-start | bytes 1572872 | tf_op jit(solution)/shard_map/ppermute | solution.py:336

commit v14 on v11

--- a/solution.py
+++ b/solution.py
@@ -135,33 +135,44 @@
 
 
 def take_kernel(starts, source, *refs):
-    outs, sems = refs[:-1], refs[-1]
-    count = sems.shape[1]
-    piece = source.shape[0] // count
-    copies = []
+    count = len(starts)
+    outs, landed, sems = refs[:count], refs[count:-1], refs[-1]
+    pieces = sems.shape[2]
+    size = source.shape[0] // pieces
+    moves = []
     for i, (at, out) in enumerate(zip(starts, outs)):
-        for j in range(count):
-            rows = pl.ds(j * piece, piece)
-            copies.append(
-                pltpu.make_async_copy(
-                    source.at[rows, pl.ds(at, out.shape[1])], out.at[rows], sems.at[i, j]
+        for j in range(pieces):
+            rows = pl.ds(j * size, size)
+            here = landed[i].at[rows]
+            moves.append(
+                (
+                    pltpu.make_async_copy(
+                        source.at[rows, pl.ds(at, out.shape[1])], here, sems.at[0, i, j]
+                    ),
+                    pltpu.make_async_copy(here, out.at[rows], sems.at[1, i, j]),
                 )
             )
-    for copy in copies:
-        copy.start()
-    for copy in copies:
-        copy.wait()
+    for arrive, _ in moves:
+        arrive.start()
+    for arrive, leave in moves:
+        arrive.wait()
+        leave.start()
+    for _, leave in moves:
+        leave.wait()
 
 
 def take_columns(source, space, ranges):
     rows = source.shape[0]
     starts = [start for start, _ in ranges]
+    shapes = [(rows, stop - start) for start, stop in ranges]
+    hbm = pl.BlockSpec(memory_space=pltpu.HBM)
     return pl.pallas_call(
         functools.partial(take_kernel, starts),
-        out_shape=tuple(pltpu.VMEM((rows, stop - start), jnp.float32) for start, stop in ranges),
+        out_shape=tuple(jax.ShapeDtypeStruct(shape, jnp.float32) for shape in shapes),
         in_specs=[pl.BlockSpec(memory_space=space)],
-        out_specs=(VMEM_SPEC,) * len(ranges),
-        scratch_shapes=[pltpu.SemaphoreType.DMA((len(ranges), 4))],
+        out_specs=(hbm,) * len(ranges),
+        scratch_shapes=[pltpu.VMEM(shape, jnp.float32) for shape in shapes]
+        + [pltpu.SemaphoreType.DMA((2, len(ranges), 4))],
         compiler_params=pltpu.CompilerParams(vmem_limit_bytes=8 << 20),
         name="take",
     )(source)
@@ -254,9 +265,11 @@
 
 def tail_kernel(west, east, band_high, band_low, part, out):
     last = band_high.shape[0] - 1
+    tile = out.shape[0]
+    here = pl.ds(pl.multiple_of(pl.program_id(1) * tile, tile), tile)
 
     def add(ref, pair, rows):
-        h, l = split(ref[...])
+        h, l = split(ref[here, :])
         out[...] = part[...] + dot3(h, l, band_high[pair, rows], band_low[pair, rows])
 
     @pl.when(pl.program_id(0) == 0)
@@ -270,11 +283,12 @@
 
 def apply_tail(west, east, bands, part):
     rows, width = part.shape
-    block = pl.BlockSpec((rows, PAIR), lambda i: (0, (1 - i) * (width // PAIR - 1)))
+    tile = rows // 2
+    block = pl.BlockSpec((tile, PAIR), lambda i, j: (j, (1 - i) * (width // PAIR - 1)))
     args = [held(a) for a in (west, east, *bands)]
     return pl.pallas_call(
         tail_kernel,
-        grid=(2,),
+        grid=(2, rows // tile),
         out_shape=jax.ShapeDtypeStruct((rows, width), jnp.float32),
         in_specs=[VMEM_SPEC] * 4 + [block],
         out_specs=block,

time: 86.8 us -> 88.1 us (1.015)
  the two profiles are of different devices: /device:TPU:13 before, /device:TPU:11 now
where the time goes in v14:
time: 88.1 us; the launch traced here: 87.5 us
  Pallas kernels  32.5 us (37%)
  starting transfers between devices  29.9 us (34%)
  waiting for transfers between devices  24.9 us (28%)
    ppermute x4, waiting for transfers between devices, body(): side.append(lax.ppermute(half[k], 'col', pairs))  16.6 us
    ppermute x4, starting transfers between devices, body(): side.append(lax.ppermute(half[k], 'col', pairs))  14.6 us
    pallas_call x4, Pallas kernels, apply_rows(): pl.pallas_call(functools.partial(rows_kernel, starts), out_shape=pltpu.VM...  13.2 us
    pallas_call x1, Pallas kernels, apply_cols(): pl.pallas_call(cols_kernel, out_shape=jax.ShapeDtypeStruct((rows, width),...  6.97 us
    ppermute x1, waiting for transfers between devices, body(): across1 = lax.ppermute(own1, 'row', other_pairs)  6.92 us
    ppermute x1, starting transfers between devices, body(): across2 = lax.ppermute(copy2, 'row', copy_pairs)  5.98 us
    pallas_call x2, Pallas kernels, build_bands(): pl.pallas_call(functools.partial(band_kernel, transposed), out_shape=(ban...  5.03 us
    pallas_call x1, Pallas kernels, apply_tail(): pl.pallas_call(tail_kernel, grid=(2, rows // tile), out_shape=jax.ShapeDt...  4.06 us
  transfers between devices with their start and end apart: 10, of which 6 were waited for; matrix products, arithmetic and copies ran while one was open for 0% of the time, Pallas kernels for 32%

profile of v14, /device:TPU:11, one launch (start us, length us, event | category | flops | bytes accessed | tf_op | source)
XLA Modules:
  0.0 87.5 jit_solution(1135954749365153638)
XLA Ops:
  0.0 0.7 collective-permute-start
  0.7 2.1 %take.3 = (f32[512,256]{1,0:T(8,128)}, f32[512,256]{1,0:T(8,128)}) custom-call(f32[512,1024]{1,0:T(8,128)} %bitcast.23), custom_call_target="tpu_custom_call" | custom-call | tf_op jit(solution)/shard_map/take/pallas_call | solution.py:169
  2.8 0.0 copy-start
  2.8 0.0 copy-start.1
  2.8 0.0 copy-start.2
  2.8 0.0 copy-start.3
  2.8 0.0 copy-start.4
  2.9 0.0 copy-start.5
  2.9 1.6 %collective-permute-start.5 = (f32[512,256]{1,0:T(8,128)}, f32[512,256]{1,0:T(8,128)}, u32[]{:S(2)}, u32[]{:S(2)}) collective-permute-start(f32[512,256]{1,0:T(8,128)} %get-tuple-element.15), channel_id=1, source_target_pairs={{56,0},{64,120},{57,1},{65,121},{58,2},{66,122},{59,3},{67,123},{6... | collective-permute-start | bytes 1572872 | tf_op jit(solution)/shard_map/ppermute | solution.py:334
  4.5 0.2 collective-permute-done.source.refs_1_
  4.7 1.1 %take.2 = f32[512,512]{1,0:T(8,128)} custom-call(f32[512,1024]{1,0:T(8,128)S(1)} %collective-permute-done.source.refs_1_), custom_call_target="tpu_custom_call" | custom-call | tf_op jit(solution)/shard_map/take/pallas_call | solution.py:169
  5.8 6.0 %collective-permute-start.1 = (f32[512,512]{1,0:T(8,128)}, f32[512,512]{1,0:T(8,128)S(1)}, u32[]{:S(2)}, u32[]{:S(2)}) collective-permute-start(f32[512,512]{1,0:T(8,128)} %take.2), channel_id=1, source_target_pairs={{24,8},{0,16},{40,24},{16,32},{56,40},{32,48},{72,56},{48,64},{88,... | collective-permute-start | bytes 3145736 | tf_op jit(solution)/shard_map/ppermute | solution.py:337
  11.8 1.9 %collective-permute-start.4 = (f32[512,256]{1,0:T(8,128)}, f32[512,256]{1,0:T(8,128)}, u32[]{:S(2)}, u32[]{:S(2)}) collective-permute-start(f32[512,256]{1,0:T(8,128)} %get-tuple-element.15), channel_id=1, source_target_pairs={{16,8},{8,16},{32,24},{24,32},{48,40},{40,48},{80,72},{72,80},{96,... | collective-permute-start | bytes 1572872 | tf_op jit(solution)/shard_map/ppermute | solution.py:336
  13.7 0.0 collective-permute-done.5
  13.7 1.5 %collective-permute-start.6 = (f32[512,256]{1,0:T(8,128)}, f32[512,256]{1,0:T(8,128)}, u32[]{:S(2)}, u32[]{:S(2)}) collective-permute-start(f32[512,256]{1,0:T(8,128)} %collective-permute-done.5), channel_id=1, source_target_pairs={{0,64},{120,56},{1,65},{121,57},{2,66},{122,58},{3,67},{123,59},{4... | collective-permute-start | bytes 1572872 | tf_op jit(solution)/shard_map/ppermute | solution.py:335
  15.2 3.6 %collective-permute-start.8 = (f32[512,256]{1,0:T(8,128)}, f32[512,256]{1,0:T(8,128)}, u32[]{:S(2)}, u32[]{:S(2)}) collective-permute-start(f32[512,256]{1,0:T(8,128)} %get-tuple-element.16), channel_id=1, source_target_pairs={{16,8},{8,16},{32,24},{24,32},{48,40},{40,48},{64,56},{56,64},{80,... | collective-permute-start | bytes 1572872 | tf_op jit(solution)/shard_map/ppermute | solution.py:333
  18.8 0.0 copy-done
  18.8 0.0 copy-done.1
  18.8 0.0 copy-done.2
  18.9 0.0 copy-done.3
  18.9 0.0 copy-done.4
  18.9 0.0 copy-done.5
  18.9 1.9 %row_bands.1 = (bf16[2,256,1280]{2,1,0:T(8,128)(2,1)S(1)}, bf16[2,256,1280]{2,1,0:T(8,128)(2,1)S(1)}) custom-call(s32[1]{0:T(128)} %bitcast.place, s32[64,128]{1,0:T(8,128)S(1)} %bitcast.10, s32[64,128]{1,0:T(8,128)S(1)} %bitcast.12, s32[64,128]{1,0:T(8,128)S(1)} %bitcast.14, f32[64,128]{1,0:T(8,128)S(1)} %bitcast.16, f32[64,128]{1,0:T(8,128)S(1)} %bitcast.18, ...), custom_call_target="tpu_custom_call" | custom-call | tf_op jit(solution)/shard_map/row_bands/pallas_call | solution.py:125
  20.8 6.9 %collective-permute-done.4.refs_2_ = f32[512,256]{1,0:T(8,128)} collective-permute-done((f32[512,256]{1,0:T(8,128)}, f32[512,256]{1,0:T(8,128)}, u32[]{:S(2)}, u32[]{:S(2)}) %collective-permute-start.4) | collective-permute-done | bytes 524320 | tf_op jit(solution)/shard_map/ppermute | solution.py:336
  27.7 0.0 collective-permute-done.6.refs_3_
  27.7 3.5 %rows.6.refs_4_ = f32[512,256]{1,0:T(8,128)} custom-call(s32[1]{0:T(128)} %bitcast.place, f32[512,1024]{1,0:T(8,128)} %bitcast.24, f32[512,1024]{1,0:T(8,128)S(1)} %collective-permute-done.source.refs_1_, f32[512,256]{1,0:T(8,128)} %collective-permute-done.4.refs_2_, f32[512,256]{1,0:T(8,128)} %collective-permute-done.6.refs_3_, ...), custom_call_target="tpu_custom_call" | custom-call | tf_op jit(solution)/shard_map/rows/pallas_call | solution.py:217
  31.2 3.9 %collective-permute-start.7 = (f32[512,256]{1,0:T(8,128)}, f32[512,256]{1,0:T(8,128)}, u32[]{:S(2)}, u32[]{:S(2)}) collective-permute-start(f32[512,256]{1,0:T(8,128)} %rows.6.refs_4_), channel_id=1, source_target_pairs={{0,1},{1,2},{2,3},{3,4},{4,5},{5,6},{6,7},{8,9},{9,10},{10,11},{11... | collective-permute-start | bytes 1572872 | tf_op jit(solution)/shard_map/ppermute | solution.py:347
  35.2 1.2 %collective-permute-done.8.refs_2_ = f32[512,256]{1,0:T(8,128)} collective-permute-done((f32[512,256]{1,0:T(8,128)}, f32[512,256]{1,0:T(8,128)}, u32[]{:S(2)}, u32[]{:S(2)}) %collective-permute-start.8) | collective-permute-done | bytes 524320 | tf_op jit(solution)/shard_map/ppermute | solution.py:333
  36.4 3.3 %rows.7.refs_1_ = f32[512,256]{1,0:T(8,128)} custom-call(s32[1]{0:T(128)} %bitcast.place, f32[512,1024]{1,0:T(8,128)} %bitcast.25, f32[512,1024]{1,0:T(8,128)S(1)} %collective-permute-done.source.refs_1_, f32[512,256]{1,0:T(8,128)} %collective-permute-done.8.refs_2_, bf16[2,256,1280]{2,1,0:T(8,128)(2,1)S(1)} %get-tuple-element.11.refs_3_.refs_4_, ...), custom_call_target="tpu_custom_call" | custom-call | tf_op jit(solution)/shard_map/rows/pallas_call | solution.py:217
  39.6 3.9 %collective-permute-start.9 = (f32[512,256]{1,0:T(8,128)}, f32[512,256]{1,0:T(8,128)}, u32[]{:S(2)}, u32[]{:S(2)}) collective-permute-start(f32[512,256]{1,0:T(8,128)} %rows.7.refs_1_), channel_id=1, source_target_pairs={{1,0},{2,1},{3,2},{4,3},{5,4},{6,5},{7,6},{9,8},{10,9},{11,10},{12... | collective-permute-start | bytes 1572872 | tf_op jit(solution)/shard_map/ppermute | solution.py:347
  43.5 0.0 collective-permute-done.1.refs_2_
  43.5 3.2 %rows.5.refs_2_ = f32[512,256]{1,0:T(8,128)} custom-call(s32[1]{0:T(128)} %bitcast.place, f32[512,1024]{1,0:T(8,128)} %bitcast.26, f32[512,1024]{1,0:T(8,128)S(1)} %collective-permute-done.source.refs_1_, f32[512,512]{1,0:T(8,128)S(1)} %collective-permute-done.1.refs_2_, bf16[2,256,1280]{2,1,0:T(8,128)(2,1)S(1)} %get-tuple-element.11.refs_3_.refs_4_, ...), custom_call_target="tpu_custom_call" | custom-call | tf_op jit(solution)/shard_map/rows/pallas_call | solution.py:217
  46.8 2.9 %collective-permute-start.3 = (f32[512,256]{1,0:T(8,128)}, f32[512,256]{1,0:T(8,128)}, u32[]{:S(2)}, u32[]{:S(2)}) collective-permute-start(f32[512,256]{1,0:T(8,128)} %rows.5.refs_2_), channel_id=1, source_target_pairs={{1,0},{2,1},{3,2},{4,3},{5,4},{6,5},{7,6},{9,8},{10,9},{11,10},{12... | collective-permute-start | bytes 1572872 | tf_op jit(solution)/shard_map/ppermute | solution.py:347
  49.7 3.2 %rows.4.refs_3_ = f32[512,256]{1,0:T(8,128)} custom-call(s32[1]{0:T(128)} %bitcast.place, f32[512,1024]{1,0:T(8,128)} %bitcast.27, f32[512,1024]{1,0:T(8,128)S(1)} %collective-permute-done.source.refs_1_, f32[512,512]{1,0:T(8,128)S(1)} %collective-permute-done.1.refs_2_, bf16[2,256,1280]{2,1,0:T(8,128)(2,1)S(1)} %get-tuple-element.11.refs_3_.refs_4_, ...), custom_call_target="tpu_custom_call" | custom-call | tf_op jit(solution)/shard_map/rows/pallas_call | solution.py:217
  52.9 3.9 %collective-permute-start.2 = (f32[512,256]{1,0:T(8,128)}, f32[512,256]{1,0:T(8,128)S(1)}, u32[]{:S(2)}, u32[]{:S(2)}) collective-permute-start(f32[512,256]{1,0:T(8,128)} %rows.4.refs_3_), channel_id=1, source_target_pairs={{0,1},{1,2},{2,3},{3,4},{4,5},{5,6},{6,7},{8,9},{9,10},{10,11},{11... | collective-permute-start | bytes 1572872 | tf_op jit(solution)/shard_map/ppermute | solution.py:347
  56.8 3.1 %col_bands.1 = (bf16[4,1280,256]{2,1,0:T(8,128)(2,1)S(1)}, bf16[4,1280,256]{2,1,0:T(8,128)(2,1)S(1)}) custom-call(s32[1]{0:T(128)} %bitcast.8.place, s32[64,128]{1,0:T(8,128)S(1)} %bitcast.11, s32[64,128]{1,0:T(8,128)S(1)} %bitcast.13, s32[64,128]{1,0:T(8,128)S(1)} %bitcast.15, f32[64,128]{1,0:T(8,128)S(1)} %bitcast.17, f32[64,128]{1,0:T(8,128)S(1)} %bitcast.19, ...), custom_call_target="tpu_custom_call" | custom-call | tf_op jit(solution)/shard_map/col_bands/pallas_call | solution.py:125
  59.9 9.6 %collective-permute-done.7.refs_0_ = f32[512,256]{1,0:T(8,128)} collective-permute-done((f32[512,256]{1,0:T(8,128)}, f32[512,256]{1,0:T(8,128)}, u32[]{:S(2)}, u32[]{:S(2)}) %collective-permute-start.7) | collective-permute-done | bytes 524320 | tf_op jit(solution)/shard_map/ppermute | solution.py:347
  69.5 2.8 %collective-permute-done.9.refs_5_ = f32[512,256]{1,0:T(8,128)} collective-permute-done((f32[512,256]{1,0:T(8,128)}, f32[512,256]{1,0:T(8,128)}, u32[]{:S(2)}, u32[]{:S(2)}) %collective-permute-start.9) | collective-permute-done | bytes 524320 | tf_op jit(solution)/shard_map/ppermute | solution.py:347
  72.3 7.0 %cols.1.part = f32[512,1024]{1,0:T(8,128)} custom-call(f32[512,256]{1,0:T(8,128)} %collective-permute-done.7.refs_0_, f32[512,256]{1,0:T(8,128)} %rows.7.refs_1_, f32[512,256]{1,0:T(8,128)} %rows.5.refs_2_, f32[512,256]{1,0:T(8,128)} %rows.4.refs_3_, f32[512,256]{1,0:T(8,128)} %rows.6.refs_4_, f32[512,256]{1,0:T(8,128)} %collective-permute-done.9.refs_5_, ...), custom_call_target="tpu_custom_call" | custom-call | tf_op jit(solution)/shard_map/cols/pallas_call | solution.py:255
  79.2 4.3 %collective-permute-done.3.east = f32[512,256]{1,0:T(8,128)} collective-permute-done((f32[512,256]{1,0:T(8,128)}, f32[512,256]{1,0:T(8,128)}, u32[]{:S(2)}, u32[]{:S(2)}) %collective-permute-start.3) | collective-permute-done | bytes 524320 | tf_op jit(solution)/shard_map/ppermute | solution.py:347
  83.5 0.0 collective-permute-done.2.west
  83.5 4.1 %tail.1 = f32[512,1024]{1,0:T(8,128)} custom-call(f32[512,256]{1,0:T(8,128)S(1)} %collective-permute-done.2.west, f32[512,256]{1,0:T(8,128)} %collective-permute-done.3.east, bf16[4,1280,256]{2,1,0:T(8,128)(2,1)S(1)} %get-tuple-element.13.refs_6_.band_high, ...), custom_call_target="tpu_custom_call", output_to_operand_aliasing={{}: (4, {})} | custom-call | tf_op jit(solution)/shard_map/tail/pallas_call | solution.py:289
Async XLA Ops:
  0.0 4.7 %collective-permute-start = (f32[512,1024]{1,0:T(8,128)}, f32[512,1024]{1,0:T(8,128)S(1)}, u32[]{:S(2)}, u32[]{:S(2)}) collective-permute-start(f32[512,1024]{1,0:T(8,128)} %bitcast.22), channel_id=1, source_target_pairs={{0,8},{8,0},{16,24},{24,16},{32,40},{40,32},{48,56},{56,48},{64,72... | collective-permute-start | bytes 6291464 | tf_op jit(solution)/shard_map/ppermute | solution.py:330
  2.8 16.0 %copy-start = (s32[1,1,8192]{2,1,0:T(1,128)S(1)}, s32[1,1,8192]{2,1,0:T(1,128)}, u32[]{:S(2)}) copy-start(s32[1,1,8192]{2,1,0:T(1,128)} %param.8) | copy-start | bytes 98308
  2.8 16.0 %copy-start.1 = (s32[1,1,8192]{2,1,0:T(1,128)S(1)}, s32[1,1,8192]{2,1,0:T(1,128)}, u32[]{:S(2)}) copy-start(s32[1,1,8192]{2,1,0:T(1,128)} %param.9) | copy-start | bytes 98308
  2.8 16.0 %copy-start.2 = (s32[1,1,8192]{2,1,0:T(1,128)S(1)}, s32[1,1,8192]{2,1,0:T(1,128)}, u32[]{:S(2)}) copy-start(s32[1,1,8192]{2,1,0:T(1,128)} %param.10) | copy-start | bytes 98308
  2.8 16.0 %copy-start.3 = (f32[1,1,8192]{2,1,0:T(1,128)S(1)}, f32[1,1,8192]{2,1,0:T(1,128)}, u32[]{:S(2)}) copy-start(f32[1,1,8192]{2,1,0:T(1,128)} %param.11) | copy-start | bytes 98308
  2.8 16.0 %copy-start.4 = (f32[1,8192]{1,0:T(1,128)S(1)}, f32[1,8192]{1,0:T(1,128)}, u32[]{:S(2)}) copy-start(f32[1,8192]{1,0:T(1,128)} %param.12) | copy-start | bytes 98308
  2.9 16.0 %copy-start.5 = (f32[1,8192]{1,0:T(1,128)S(1)}, f32[1,8192]{1,0:T(1,128)}, u32[]{:S(2)}) copy-start(f32[1,8192]{1,0:T(1,128)} %param.13) | copy-start | bytes 98308
  2.9 10.8 %collective-permute-start.5 = (f32[512,256]{1,0:T(8,128)}, f32[512,256]{1,0:T(8,128)}, u32[]{:S(2)}, u32[]{:S(2)}) collective-permute-start(f32[512,256]{1,0:T(8,128)} %get-tuple-element.15), channel_id=1, source_target_pairs={{56,0},{64,120},{57,1},{65,121},{58,2},{66,122},{59,3},{67,123},{6... | collective-permute-start | bytes 1572872 | tf_op jit(solution)/shard_map/ppermute | solution.py:334
  5.8 37.8 %collective-permute-start.1 = (f32[512,512]{1,0:T(8,128)}, f32[512,512]{1,0:T(8,128)S(1)}, u32[]{:S(2)}, u32[]{:S(2)}) collective-permute-start(f32[512,512]{1,0:T(8,128)} %take.2), channel_id=1, source_target_pairs={{24,8},{0,16},{40,24},{16,32},{56,40},{32,48},{72,56},{48,64},{88,... | collective-permute-start | bytes 3145736 | tf_op jit(solution)/shard_map/ppermute | solution.py:337
  11.8 16.0 %collective-permute-start.4 = (f32[512,256]{1,0:T(8,128)}, f32[512,256]{1,0:T(8,128)}, u32[]{:S(2)}, u32[]{:S(2)}) collective-permute-start(f32[512,256]{1,0:T(8,128)} %get-tuple-element.15), channel_id=1, source_target_pairs={{16,8},{8,16},{32,24},{24,32},{48,40},{40,48},{80,72},{72,80},{96,... | collective-permute-start | bytes 1572872 | tf_op jit(solution)/shard_map/ppermute | solution.py:336
  13.7 14.0 %collective-permute-start.6 = (f32[512,256]{1,0:T(8,128)}, f32[512,256]{1,0:T(8,128)}, u32[]{:S(2)}, u32[]{:S(2)}) collective-permute-start(f32[512,256]{1,0:T(8,128)} %collective-permute-done.5), channel_id=1, source_target_pairs={{0,64},{120,56},{1,65},{121,57},{2,66},{122,58},{3,67},{123,59},{4... | collective-permute-start | bytes 1572872 | tf_op jit(solution)/shard_map/ppermute | solution.py:335
  15.2 21.2 %collective-permute-start.8 = (f32[512,256]{1,0:T(8,128)}, f32[512,256]{1,0:T(8,128)}, u32[]{:S(2)}, u32[]{:S(2)}) collective-permute-start(f32[512,256]{1,0:T(8,128)} %get-tuple-element.16), channel_id=1, source_target_pairs={{16,8},{8,16},{32,24},{24,32},{48,40},{40,48},{64,56},{56,64},{80,... | collective-permute-start | bytes 1572872 | tf_op jit(solution)/shard_map/ppermute | solution.py:333
  31.2 38.3 %collective-permute-start.7 = (f32[512,256]{1,0:T(8,128)}, f32[512,256]{1,0:T(8,128)}, u32[]{:S(2)}, u32[]{:S(2)}) collective-permute-start(f32[512,256]{1,0:T(8,128)} %rows.6.refs_4_), channel_id=1, source_target_pairs={{0,1},{1,2},{2,3},{3,4},{4,5},{5,6},{6,7},{8,9},{9,10},{10,11},{11... | collective-permute-start | bytes 1572872 | tf_op jit(solution)/shard_map/ppermute | solution.py:347
  39.6 32.6 %collective-permute-start.9 = (f32[512,256]{1,0:T(8,128)}, f32[512,256]{1,0:T(8,128)}, u32[]{:S(2)}, u32[]{:S(2)}) collective-permute-start(f32[512,256]{1,0:T(8,128)} %rows.7.refs_1_), channel_id=1, source_target_pairs={{1,0},{2,1},{3,2},{4,3},{5,4},{6,5},{7,6},{9,8},{10,9},{11,10},{12... | collective-permute-start | bytes 1572872 | tf_op jit(solution)/shard_map/ppermute | solution.py:347
  46.8 36.7 %collective-permute-start.3 = (f32[512,256]{1,0:T(8,128)}, f32[512,256]{1,0:T(8,128)}, u32[]{:S(2)}, u32[]{:S(2)}) collective-permute-start(f32[512,256]{1,0:T(8,128)} %rows.5.refs_2_), channel_id=1, source_target_pairs={{1,0},{2,1},{3,2},{4,3},{5,4},{6,5},{7,6},{9,8},{10,9},{11,10},{12... | collective-permute-start | bytes 1572872 | tf_op jit(solution)/shard_map/ppermute | solution.py:347
  52.9 30.6 %collective-permute-start.2 = (f32[512,256]{1,0:T(8,128)}, f32[512,256]{1,0:T(8,128)S(1)}, u32[]{:S(2)}, u32[]{:S(2)}) collective-permute-start(f32[512,256]{1,0:T(8,128)} %rows.4.refs_3_), channel_id=1, source_target_pairs={{0,1},{1,2},{2,3},{3,4},{4,5},{5,6},{6,7},{8,9},{9,10},{10,11},{11... | collective-permute-start | bytes 1572872 | tf_op jit(solution)/shard_map/ppermute | solution.py:347

commit v15 on v14

--- a/solution.py
+++ b/solution.py
@@ -161,7 +161,7 @@
         leave.wait()
 
 
-def take_columns(source, space, ranges):
+def take_columns(source, ranges):
     rows = source.shape[0]
     starts = [start for start, _ in ranges]
     shapes = [(rows, stop - start) for start, stop in ranges]
@@ -169,13 +169,13 @@
     return pl.pallas_call(
         functools.partial(take_kernel, starts),
         out_shape=tuple(jax.ShapeDtypeStruct(shape, jnp.float32) for shape in shapes),
-        in_specs=[pl.BlockSpec(memory_space=space)],
+        in_specs=[hbm],
         out_specs=(hbm,) * len(ranges),
         scratch_shapes=[pltpu.VMEM(shape, jnp.float32) for shape in shapes]
         + [pltpu.SemaphoreType.DMA((2, len(ranges), 4))],
         compiler_params=pltpu.CompilerParams(vmem_limit_bytes=8 << 20),
         name="take",
-    )(source)
+    )(in_hbm(source))
 
 
 def rows_kernel(starts, place, *refs):
@@ -218,14 +218,13 @@
         functools.partial(rows_kernel, starts),
         out_shape=pltpu.VMEM((rows, width), jnp.float32),
         in_specs=[pl.BlockSpec(memory_space=pltpu.SMEM)]
-        + [pl.BlockSpec(memory_space=pltpu.HBM)]
-        + [pl.BlockSpec(memory_space=pl.ANY)] * (len(sources) - 1)
+        + [pl.BlockSpec(memory_space=pltpu.HBM)] * len(sources)
         + [VMEM_SPEC] * 2,
         out_specs=VMEM_SPEC,
         scratch_shapes=[ext, ext, landed, pltpu.SemaphoreType.DMA((len(sources),))],
         compiler_params=pltpu.CompilerParams(vmem_limit_bytes=16 << 20),
         name="rows",
-    )(place, in_hbm(sources[0]), *sources[1:], *(held(a) for a in bands))
+    )(place, *(in_hbm(a) for a in sources), *(held(a) for a in bands))
 
 
 def cols_kernel(*refs):
@@ -265,11 +264,9 @@
 
 def tail_kernel(west, east, band_high, band_low, part, out):
     last = band_high.shape[0] - 1
-    tile = out.shape[0]
-    here = pl.ds(pl.multiple_of(pl.program_id(1) * tile, tile), tile)
 
     def add(ref, pair, rows):
-        h, l = split(ref[here, :])
+        h, l = split(ref[...])
         out[...] = part[...] + dot3(h, l, band_high[pair, rows], band_low[pair, rows])
 
     @pl.when(pl.program_id(0) == 0)
@@ -283,12 +280,11 @@
 
 def apply_tail(west, east, bands, part):
     rows, width = part.shape
-    tile = rows // 2
-    block = pl.BlockSpec((tile, PAIR), lambda i, j: (j, (1 - i) * (width // PAIR - 1)))
+    block = pl.BlockSpec((rows, PAIR), lambda i: (0, (1 - i) * (width // PAIR - 1)))
     args = [held(a) for a in (west, east, *bands)]
     return pl.pallas_call(
         tail_kernel,
-        grid=(2, rows // tile),
+        grid=(2,),
         out_shape=jax.ShapeDtypeStruct((rows, width), jnp.float32),
         in_specs=[VMEM_SPEC] * 4 + [block],
         out_specs=block,
@@ -328,15 +324,17 @@
 
     starts = (0, width - PAIR, PAIR, width - 2 * PAIR)
     chip = lax.ppermute(block, "row", chip_pairs)
-    own0, own1 = take_columns(in_hbm(block), pltpu.HBM, [(0, PAIR), (width - PAIR, width)])
-    (copy2,) = take_columns(chip, pl.ANY, [(PAIR, width - PAIR)])
+    own0, own1, own2 = take_columns(
+        block, [(0, PAIR), (PAIR, 2 * PAIR), (2 * PAIR, width)]
+    )
+    copy2 = lax.ppermute(own2, "row", chip_pairs)
     across0 = lax.ppermute(own0, "row", cross_pairs)
     ends = lax.ppermute(own1, "row", [(middle - 1, 0), (middle, last)])
     relay = lax.ppermute(ends, "row", [(0, middle), (last, middle - 1)])
     across1 = lax.ppermute(own1, "row", other_pairs)
     across2 = lax.ppermute(copy2, "row", copy_pairs)
-    across = ([across0], [across1, relay], [across2], [across2])
-    offset = (0, 0, 0, width - 3 * PAIR)
+    across = ([across0], [across2], [across1, relay], [across2])
+    offset = (0, width - 3 * PAIR, 0, width - 4 * PAIR)
     row_bands = build_bands(lat_row, fields, rows // PAIR, True)
     half, side = [], []
     for k in range(4):
@@ -354,4 +352,6 @@
 def solution(mesh):
     in_specs = (P(None, "row", "col"), P(), P(), P(), P(), P(), P())
     out_specs = P(None, "row", "col")
-    return jax.shard_map(body, mesh=mesh, in_specs=in_specs, out_specs=out_specs, check_vma=False)
+    return jax.shard_map(
+        body, mesh=mesh, in_specs=in_specs, out_specs=out_specs, check_vma=False
+    )

time: 88.1 us -> 89 us (1.010)
  the two profiles are of different devices: /device:TPU:11 before, /device:TPU:77 now
where the time goes in v15:
time: 89 us; the launch traced here: 88.6 us
  waiting for transfers between devices  34.6 us (39%)
  Pallas kernels  26.3 us (30%)
  starting transfers between devices  25.7 us (29%)
  local copies, waits for them, and re-layouts  1.77 us (2%)
    ppermute x4, waiting for transfers between devices, body(): side.append(lax.ppermute(half[k], 'col', pairs))  20.4 us
    ppermute x4, starting transfers between devices, body(): side.append(lax.ppermute(half[k], 'col', pairs))  14.5 us
    ppermute x1, waiting for transfers between devices, body(): across2 = lax.ppermute(copy2, 'row', copy_pairs)  11.2 us
    pallas_call x4, Pallas kernels, apply_rows(): pl.pallas_call(functools.partial(rows_kernel, starts), out_shape=pltpu.VM...  10.7 us
    pallas_call x1, Pallas kernels, apply_cols(): pl.pallas_call(cols_kernel, out_shape=jax.ShapeDtypeStruct((rows, width),...  5.14 us
    pallas_call x2, Pallas kernels, build_bands(): pl.pallas_call(functools.partial(band_kernel, transposed), out_shape=(ban...  5.01 us
    ppermute x1, waiting for transfers between devices, body(): copy2 = lax.ppermute(own2, 'row', chip_pairs)  2.99 us
    pallas_call x1, Pallas kernels, apply_tail(): pl.pallas_call(tail_kernel, grid=(2,), out_shape=jax.ShapeDtypeStruct((ro...  2.96 us
  transfers between devices with their start and end apart: 11, of which 5 were waited for; matrix products, arithmetic and copies ran while one was open for 0% of the time, Pallas kernels for 26%

profile of v15, /device:TPU:77, one launch (start us, length us, event | category | flops | bytes accessed | tf_op | source)
XLA Modules:
  0.0 88.6 jit_solution(5158776282803458105)
XLA Ops:
  0.0 0.0 copy-start
  0.0 0.0 copy-start.1
  0.0 0.0 copy-start.2
  0.0 0.0 copy-start.3
  0.0 0.0 copy-start.4
  0.0 0.0 copy-start.5
  0.0 0.8 collective-permute-start
  0.8 2.5 %take.1 = (f32[512,256]{1,0:T(8,128)S(1)}, f32[512,256]{1,0:T(8,128)S(1)}, f32[512,512]{1,0:T(8,128)S(1)}) custom-call(f32[512,1024]{1,0:T(8,128)} %bitcast.23), custom_call_target="tpu_custom_call" | custom-call | tf_op jit(solution)/shard_map/take/pallas_call | solution.py:169
  3.3 0.1 collective-permute-start.1
  3.4 3.0 %collective-permute-done.1 = f32[512,512]{1,0:T(8,128)} collective-permute-done((f32[512,512]{1,0:T(8,128)S(1)}, f32[512,512]{1,0:T(8,128)}, u32[]{:S(2)}, u32[]{:S(2)}) %collective-permute-start.1) | collective-permute-done | bytes 1048608 | tf_op jit(solution)/shard_map/ppermute | solution.py:330
  6.4 1.9 %collective-permute-start.2 = (f32[512,512]{1,0:T(8,128)}, f32[512,512]{1,0:T(8,128)S(1)}, u32[]{:S(2)}, u32[]{:S(2)}) collective-permute-start(f32[512,512]{1,0:T(8,128)} %collective-permute-done.1), channel_id=1, source_target_pairs={{24,8},{0,16},{40,24},{16,32},{56,40},{32,48},{72,56},{48,64},{88,... | collective-permute-start | bytes 3145736 | tf_op jit(solution)/shard_map/ppermute | solution.py:335
  8.3 1.5 %collective-permute-start.5 = (f32[512,256]{1,0:T(8,128)S(1)}, f32[512,256]{1,0:T(8,128)}, u32[]{:S(2)}, u32[]{:S(2)}) collective-permute-start(f32[512,256]{1,0:T(8,128)S(1)} %get-tuple-element.15), channel_id=1, source_target_pairs={{56,0},{64,120},{57,1},{65,121},{58,2},{66,122},{59,3},{67,123},{6... | collective-permute-start | bytes 1572872 | tf_op jit(solution)/shard_map/ppermute | solution.py:332
  9.8 2.9 %collective-permute-start.9 = (f32[512,256]{1,0:T(8,128)S(1)}, f32[512,256]{1,0:T(8,128)S(1)}, u32[]{:S(2)}, u32[]{:S(2)}) collective-permute-start(f32[512,256]{1,0:T(8,128)S(1)} %get-tuple-element.18), channel_id=1, source_target_pairs={{16,8},{8,16},{32,24},{24,32},{48,40},{40,48},{64,56},{56,64},{80,... | collective-permute-start | bytes 1572872 | tf_op jit(solution)/shard_map/ppermute | solution.py:331
  12.7 2.7 %collective-permute-start.4 = (f32[512,256]{1,0:T(8,128)S(1)}, f32[512,256]{1,0:T(8,128)}, u32[]{:S(2)}, u32[]{:S(2)}) collective-permute-start(f32[512,256]{1,0:T(8,128)S(1)} %get-tuple-element.15), channel_id=1, source_target_pairs={{16,8},{8,16},{32,24},{24,32},{48,40},{40,48},{80,72},{72,80},{96,... | collective-permute-start | bytes 1572872 | tf_op jit(solution)/shard_map/ppermute | solution.py:334
  15.4 0.0 collective-permute-done.5
  15.4 1.5 %collective-permute-start.6 = (f32[512,256]{1,0:T(8,128)}, f32[512,256]{1,0:T(8,128)}, u32[]{:S(2)}, u32[]{:S(2)}) collective-permute-start(f32[512,256]{1,0:T(8,128)} %collective-permute-done.5), channel_id=1, source_target_pairs={{0,64},{120,56},{1,65},{121,57},{2,66},{122,58},{3,67},{123,59},{4... | collective-permute-start | bytes 1572872 | tf_op jit(solution)/shard_map/ppermute | solution.py:333
  16.8 0.0 copy-done
  16.8 0.0 copy-done.1
  16.8 0.0 copy-done.2
  16.9 0.0 copy-done.3
  16.9 0.0 copy-done.4
  16.9 0.0 copy-done.5
  16.9 2.0 %row_bands.1 = (bf16[2,256,1280]{2,1,0:T(8,128)(2,1)S(1)}, bf16[2,256,1280]{2,1,0:T(8,128)(2,1)S(1)}) custom-call(s32[1]{0:T(128)} %bitcast.place, s32[64,128]{1,0:T(8,128)S(1)} %bitcast.10, s32[64,128]{1,0:T(8,128)S(1)} %bitcast.12, s32[64,128]{1,0:T(8,128)S(1)} %bitcast.14, f32[64,128]{1,0:T(8,128)S(1)} %bitcast.16, f32[64,128]{1,0:T(8,128)S(1)} %bitcast.18, ...), custom_call_target="tpu_custom_call" | custom-call | tf_op jit(solution)/shard_map/row_bands/pallas_call | solution.py:125
  18.8 0.0 collective-permute-done.refs_1_
  18.8 11.2 %collective-permute-done.2.refs_2_ = f32[512,512]{1,0:T(8,128)S(1)} collective-permute-done((f32[512,512]{1,0:T(8,128)}, f32[512,512]{1,0:T(8,128)S(1)}, u32[]{:S(2)}, u32[]{:S(2)}) %collective-permute-start.2) | collective-permute-done | bytes 1048608 | tf_op jit(solution)/shard_map/ppermute | solution.py:335
  30.1 0.0 copy-start.6
  30.1 1.0 %copy-done.6 = f32[512,512]{1,0:T(8,128)} copy-done((f32[512,512]{1,0:T(8,128)}, f32[512,512]{1,0:T(8,128)S(1)}, u32[]{:S(2)}) %copy-start.6) | copy-done | bytes 1048600
  31.0 2.6 %rows.6.refs_4_ = f32[512,256]{1,0:T(8,128)S(1)} custom-call(s32[1]{0:T(128)} %bitcast.place, f32[512,1024]{1,0:T(8,128)} %bitcast.24, f32[512,1024]{1,0:T(8,128)} %collective-permute-done.refs_1_, f32[512,512]{1,0:T(8,128)} %copy-done.6, bf16[2,256,1280]{2,1,0:T(8,128)(2,1)S(1)} %get-tuple-element.13.refs_3_.refs_4_, ...), custom_call_target="tpu_custom_call" | custom-call | tf_op jit(solution)/shard_map/rows/pallas_call | solution.py:217
  33.6 3.9 %collective-permute-start.8 = (f32[512,256]{1,0:T(8,128)S(1)}, f32[512,256]{1,0:T(8,128)S(1)}, u32[]{:S(2)}, u32[]{:S(2)}) collective-permute-start(f32[512,256]{1,0:T(8,128)S(1)} %rows.6.refs_4_), channel_id=1, source_target_pairs={{0,1},{1,2},{2,3},{3,4},{4,5},{5,6},{6,7},{8,9},{9,10},{10,11},{11... | collective-permute-start | bytes 1572872 | tf_op jit(solution)/shard_map/ppermute | solution.py:345
  37.6 0.0 collective-permute-done.9.refs_2_
  37.6 0.0 copy-start.7
  37.6 0.8 copy-done.7
  38.4 2.6 %rows.7.refs_1_ = f32[512,256]{1,0:T(8,128)S(1)} custom-call(s32[1]{0:T(128)} %bitcast.place, f32[512,1024]{1,0:T(8,128)} %bitcast.25, f32[512,1024]{1,0:T(8,128)} %collective-permute-done.refs_1_, f32[512,256]{1,0:T(8,128)} %copy-done.7, bf16[2,256,1280]{2,1,0:T(8,128)(2,1)S(1)} %get-tuple-element.13.refs_3_.refs_4_, ...), custom_call_target="tpu_custom_call" | custom-call | tf_op jit(solution)/shard_map/rows/pallas_call | solution.py:217
  41.0 3.8 %collective-permute-start.10 = (f32[512,256]{1,0:T(8,128)S(1)}, f32[512,256]{1,0:T(8,128)S(1)}, u32[]{:S(2)}, u32[]{:S(2)}) collective-permute-start(f32[512,256]{1,0:T(8,128)S(1)} %rows.7.refs_1_), channel_id=1, source_target_pairs={{1,0},{2,1},{3,2},{4,3},{5,4},{6,5},{7,6},{9,8},{10,9},{11,10},{12... | collective-permute-start | bytes 1572872 | tf_op jit(solution)/shard_map/ppermute | solution.py:345
  44.8 0.0 collective-permute-done.4.refs_2_
  44.8 0.0 collective-permute-done.6.refs_3_
  44.8 2.8 %rows.5.refs_2_ = f32[512,256]{1,0:T(8,128)S(1)} custom-call(s32[1]{0:T(128)} %bitcast.place, f32[512,1024]{1,0:T(8,128)} %bitcast.26, f32[512,1024]{1,0:T(8,128)} %collective-permute-done.refs_1_, f32[512,256]{1,0:T(8,128)} %collective-permute-done.4.refs_2_, f32[512,256]{1,0:T(8,128)} %collective-permute-done.6.refs_3_, ...), custom_call_target="tpu_custom_call" | custom-call | tf_op jit(solution)/shard_map/rows/pallas_call | solution.py:217
  47.6 3.0 %collective-permute-start.7 = (f32[512,256]{1,0:T(8,128)S(1)}, f32[512,256]{1,0:T(8,128)}, u32[]{:S(2)}, u32[]{:S(2)}) collective-permute-start(f32[512,256]{1,0:T(8,128)S(1)} %rows.5.refs_2_), channel_id=1, source_target_pairs={{1,0},{2,1},{3,2},{4,3},{5,4},{6,5},{7,6},{9,8},{10,9},{11,10},{12... | collective-permute-start | bytes 1572872 | tf_op jit(solution)/shard_map/ppermute | solution.py:345
  50.6 2.6 %rows.4.refs_3_ = f32[512,256]{1,0:T(8,128)S(1)} custom-call(s32[1]{0:T(128)} %bitcast.place, f32[512,1024]{1,0:T(8,128)} %bitcast.27, f32[512,1024]{1,0:T(8,128)} %collective-permute-done.refs_1_, f32[512,512]{1,0:T(8,128)} %copy-done.6, bf16[2,256,1280]{2,1,0:T(8,128)(2,1)S(1)} %get-tuple-element.13.refs_3_.refs_4_, ...), custom_call_target="tpu_custom_call" | custom-call | tf_op jit(solution)/shard_map/rows/pallas_call | solution.py:217
  53.3 3.8 %collective-permute-start.3 = (f32[512,256]{1,0:T(8,128)S(1)}, f32[512,256]{1,0:T(8,128)}, u32[]{:S(2)}, u32[]{:S(2)}) collective-permute-start(f32[512,256]{1,0:T(8,128)S(1)} %rows.4.refs_3_), channel_id=1, source_target_pairs={{0,1},{1,2},{2,3},{3,4},{4,5},{5,6},{6,7},{8,9},{9,10},{10,11},{11... | collective-permute-start | bytes 1572872 | tf_op jit(solution)/shard_map/ppermute | solution.py:345
  57.1 3.1 %col_bands.1 = (bf16[4,1280,256]{2,1,0:T(8,128)(2,1)S(1)}, bf16[4,1280,256]{2,1,0:T(8,128)(2,1)S(1)}) custom-call(s32[1]{0:T(128)} %bitcast.8.place, s32[64,128]{1,0:T(8,128)S(1)} %bitcast.11, s32[64,128]{1,0:T(8,128)S(1)} %bitcast.13, s32[64,128]{1,0:T(8,128)S(1)} %bitcast.15, f32[64,128]{1,0:T(8,128)S(1)} %bitcast.17, f32[64,128]{1,0:T(8,128)S(1)} %bitcast.19, ...), custom_call_target="tpu_custom_call" | custom-call | tf_op jit(solution)/shard_map/col_bands/pallas_call | solution.py:125
  60.1 8.9 %collective-permute-done.8.refs_0_ = f32[512,256]{1,0:T(8,128)S(1)} collective-permute-done((f32[512,256]{1,0:T(8,128)S(1)}, f32[512,256]{1,0:T(8,128)S(1)}, u32[]{:S(2)}, u32[]{:S(2)}) %collective-permute-start.8) | collective-permute-done | bytes 524320 | tf_op jit(solution)/shard_map/ppermute | solution.py:345
  69.0 5.3 %collective-permute-done.10.refs_5_ = f32[512,256]{1,0:T(8,128)S(1)} collective-permute-done((f32[512,256]{1,0:T(8,128)S(1)}, f32[512,256]{1,0:T(8,128)S(1)}, u32[]{:S(2)}, u32[]{:S(2)}) %collective-permute-start.10) | collective-permute-done | bytes 524320 | tf_op jit(solution)/shard_map/ppermute | solution.py:345
  74.3 5.1 %cols.1.part = f32[512,1024]{1,0:T(8,128)} custom-call(f32[512,256]{1,0:T(8,128)S(1)} %collective-permute-done.8.refs_0_, f32[512,256]{1,0:T(8,128)S(1)} %rows.7.refs_1_, f32[512,256]{1,0:T(8,128)S(1)} %rows.5.refs_2_, f32[512,256]{1,0:T(8,128)S(1)} %rows.4.refs_3_, f32[512,256]{1,0:T(8,128)S(1)} %rows.6.refs_4_, ...), custom_call_target="tpu_custom_call" | custom-call | tf_op jit(solution)/shard_map/cols/pallas_call | solution.py:254
  79.4 6.2 %collective-permute-done.7.east = f32[512,256]{1,0:T(8,128)} collective-permute-done((f32[512,256]{1,0:T(8,128)S(1)}, f32[512,256]{1,0:T(8,128)}, u32[]{:S(2)}, u32[]{:S(2)}) %collective-permute-start.7) | collective-permute-done | bytes 524320 | tf_op jit(solution)/shard_map/ppermute | solution.py:345
  85.6 0.0 collective-permute-done.3.west
  85.6 3.0 %tail.1 = f32[512,1024]{1,0:T(8,128)} custom-call(f32[512,256]{1,0:T(8,128)} %collective-permute-done.3.west, f32[512,256]{1,0:T(8,128)} %collective-permute-done.7.east, bf16[4,1280,256]{2,1,0:T(8,128)(2,1)S(1)} %get-tuple-element.16.refs_6_.band_high, bf16[4,1280,256]{2,1,0:T(8,128)(2,1)S(1)} %get-tuple-element.17.refs_7_.band_low, ...), custom_call_target="tpu_custom_call", output_to_operand_aliasing={{}: (4, {})} | custom-call | tf_op jit(solution)/shard_map/tail/pallas_call | solution.py:285
Async XLA Ops:
  0.0 16.8 %copy-start = (s32[1,1,8192]{2,1,0:T(1,128)S(1)}, s32[1,1,8192]{2,1,0:T(1,128)}, u32[]{:S(2)}) copy-start(s32[1,1,8192]{2,1,0:T(1,128)} %param.8) | copy-start | bytes 98308
  0.0 16.8 %copy-start.1 = (s32[1,1,8192]{2,1,0:T(1,128)S(1)}, s32[1,1,8192]{2,1,0:T(1,128)}, u32[]{:S(2)}) copy-start(s32[1,1,8192]{2,1,0:T(1,128)} %param.9) | copy-start | bytes 98308
  0.0 16.8 %copy-start.2 = (s32[1,1,8192]{2,1,0:T(1,128)S(1)}, s32[1,1,8192]{2,1,0:T(1,128)}, u32[]{:S(2)}) copy-start(s32[1,1,8192]{2,1,0:T(1,128)} %param.10) | copy-start | bytes 98308
  0.0 16.8 %copy-start.3 = (f32[1,1,8192]{2,1,0:T(1,128)S(1)}, f32[1,1,8192]{2,1,0:T(1,128)}, u32[]{:S(2)}) copy-start(f32[1,1,8192]{2,1,0:T(1,128)} %param.11) | copy-start | bytes 98308
  0.0 16.8 %copy-start.4 = (f32[1,8192]{1,0:T(1,128)S(1)}, f32[1,8192]{1,0:T(1,128)}, u32[]{:S(2)}) copy-start(f32[1,8192]{1,0:T(1,128)} %param.12) | copy-start | bytes 98308
  0.0 16.8 %copy-start.5 = (f32[1,8192]{1,0:T(1,128)S(1)}, f32[1,8192]{1,0:T(1,128)}, u32[]{:S(2)}) copy-start(f32[1,8192]{1,0:T(1,128)} %param.13) | copy-start | bytes 98308
  0.0 18.8 %collective-permute-start = (f32[512,1024]{1,0:T(8,128)}, f32[512,1024]{1,0:T(8,128)}, u32[]{:S(2)}, u32[]{:S(2)}) collective-permute-start(f32[512,1024]{1,0:T(8,128)} %bitcast.22), channel_id=1, source_target_pairs={{0,8},{8,0},{16,24},{24,16},{32,40},{40,32},{48,56},{56,48},{64,72... | collective-permute-start | bytes 6291464 | tf_op jit(solution)/shard_map/ppermute | solution.py:326
  3.3 3.1 %collective-permute-start.1 = (f32[512,512]{1,0:T(8,128)S(1)}, f32[512,512]{1,0:T(8,128)}, u32[]{:S(2)}, u32[]{:S(2)}) collective-permute-start(f32[512,512]{1,0:T(8,128)S(1)} %get-tuple-element.12), channel_id=1, source_target_pairs={{0,8},{8,0},{16,24},{24,16},{32,40},{40,32},{48,56},{56,48},{64,72... | collective-permute-start | bytes 3145736 | tf_op jit(solution)/shard_map/ppermute | solution.py:330
  6.4 23.6 %collective-permute-start.2 = (f32[512,512]{1,0:T(8,128)}, f32[512,512]{1,0:T(8,128)S(1)}, u32[]{:S(2)}, u32[]{:S(2)}) collective-permute-start(f32[512,512]{1,0:T(8,128)} %collective-permute-done.1), channel_id=1, source_target_pairs={{24,8},{0,16},{40,24},{16,32},{56,40},{32,48},{72,56},{48,64},{88,... | collective-permute-start | bytes 3145736 | tf_op jit(solution)/shard_map/ppermute | solution.py:335
  8.3 7.0 %collective-permute-start.5 = (f32[512,256]{1,0:T(8,128)S(1)}, f32[512,256]{1,0:T(8,128)}, u32[]{:S(2)}, u32[]{:S(2)}) collective-permute-start(f32[512,256]{1,0:T(8,128)S(1)} %get-tuple-element.15), channel_id=1, source_target_pairs={{56,0},{64,120},{57,1},{65,121},{58,2},{66,122},{59,3},{67,123},{6... | collective-permute-start | bytes 1572872 | tf_op jit(solution)/shard_map/ppermute | solution.py:332
  9.8 27.8 %collective-permute-start.9 = (f32[512,256]{1,0:T(8,128)S(1)}, f32[512,256]{1,0:T(8,128)S(1)}, u32[]{:S(2)}, u32[]{:S(2)}) collective-permute-start(f32[512,256]{1,0:T(8,128)S(1)} %get-tuple-element.18), channel_id=1, source_target_pairs={{16,8},{8,16},{32,24},{24,32},{48,40},{40,48},{64,56},{56,64},{80,... | collective-permute-start | bytes 1572872 | tf_op jit(solution)/shard_map/ppermute | solution.py:331
  12.7 32.1 %collective-permute-start.4 = (f32[512,256]{1,0:T(8,128)S(1)}, f32[512,256]{1,0:T(8,128)}, u32[]{:S(2)}, u32[]{:S(2)}) collective-permute-start(f32[512,256]{1,0:T(8,128)S(1)} %get-tuple-element.15), channel_id=1, source_target_pairs={{16,8},{8,16},{32,24},{24,32},{48,40},{40,48},{80,72},{72,80},{96,... | collective-permute-start | bytes 1572872 | tf_op jit(solution)/shard_map/ppermute | solution.py:334
  15.4 29.4 %collective-permute-start.6 = (f32[512,256]{1,0:T(8,128)}, f32[512,256]{1,0:T(8,128)}, u32[]{:S(2)}, u32[]{:S(2)}) collective-permute-start(f32[512,256]{1,0:T(8,128)} %collective-permute-done.5), channel_id=1, source_target_pairs={{0,64},{120,56},{1,65},{121,57},{2,66},{122,58},{3,67},{123,59},{4... | collective-permute-start | bytes 1572872 | tf_op jit(solution)/shard_map/ppermute | solution.py:333
  30.1 1.0 %copy-start.6 = (f32[512,512]{1,0:T(8,128)}, f32[512,512]{1,0:T(8,128)S(1)}, u32[]{:S(2)}) copy-start(f32[512,512]{1,0:T(8,128)S(1)} %collective-permute-done.2.refs_2_) | copy-start | bytes 3145732
  33.6 35.4 %collective-permute-start.8 = (f32[512,256]{1,0:T(8,128)S(1)}, f32[512,256]{1,0:T(8,128)S(1)}, u32[]{:S(2)}, u32[]{:S(2)}) collective-permute-start(f32[512,256]{1,0:T(8,128)S(1)} %rows.6.refs_4_), channel_id=1, source_target_pairs={{0,1},{1,2},{2,3},{3,4},{4,5},{5,6},{6,7},{8,9},{9,10},{10,11},{11... | collective-permute-start | bytes 1572872 | tf_op jit(solution)/shard_map/ppermute | solution.py:345
  37.6 0.8 copy-start.7
  41.0 33.3 %collective-permute-start.10 = (f32[512,256]{1,0:T(8,128)S(1)}, f32[512,256]{1,0:T(8,128)S(1)}, u32[]{:S(2)}, u32[]{:S(2)}) collective-permute-start(f32[512,256]{1,0:T(8,128)S(1)} %rows.7.refs_1_), channel_id=1, source_target_pairs={{1,0},{2,1},{3,2},{4,3},{5,4},{6,5},{7,6},{9,8},{10,9},{11,10},{12... | collective-permute-start | bytes 1572872 | tf_op jit(solution)/shard_map/ppermute | solution.py:345
  47.6 38.0 %collective-permute-start.7 = (f32[512,256]{1,0:T(8,128)S(1)}, f32[512,256]{1,0:T(8,128)}, u32[]{:S(2)}, u32[]{:S(2)}) collective-permute-start(f32[512,256]{1,0:T(8,128)S(1)} %rows.5.refs_2_), channel_id=1, source_target_pairs={{1,0},{2,1},{3,2},{4,3},{5,4},{6,5},{7,6},{9,8},{10,9},{11,10},{12... | collective-permute-start | bytes 1572872 | tf_op jit(solution)/shard_map/ppermute | solution.py:345
  53.3 32.4 %collective-permute-start.3 = (f32[512,256]{1,0:T(8,128)S(1)}, f32[512,256]{1,0:T(8,128)}, u32[]{:S(2)}, u32[]{:S(2)}) collective-permute-start(f32[512,256]{1,0:T(8,128)S(1)} %rows.4.refs_3_), channel_id=1, source_target_pairs={{0,1},{1,2},{2,3},{3,4},{4,5},{5,6},{6,7},{8,9},{9,10},{10,11},{11... | collective-permute-start | bytes 1572872 | tf_op jit(solution)/shard_map/ppermute | solution.py:345

commit v16 on v15

--- a/solution.py
+++ b/solution.py
@@ -262,36 +262,46 @@
     )(*args)
 
 
-def tail_kernel(west, east, band_high, band_low, part, out):
+def tail_kernel(west, east, band_high, band_low, part, out, landed, sems):
     last = band_high.shape[0] - 1
-
-    def add(ref, pair, rows):
-        h, l = split(ref[...])
-        out[...] = part[...] + dot3(h, l, band_high[pair, rows], band_low[pair, rows])
-
-    @pl.when(pl.program_id(0) == 0)
-    def _():
-        add(east, last, slice(SPAN - east.shape[1], SPAN))
-
-    @pl.when(pl.program_id(0) == 1)
-    def _():
-        add(west, 0, slice(0, west.shape[1]))
+    jobs = ((east, last, slice(SPAN - east.shape[1], SPAN)), (west, 0, slice(0, west.shape[1])))
+    here = [pl.ds(pair * PAIR, PAIR) for _, pair, _ in jobs]
+    arrive = [
+        pltpu.make_async_copy(part.at[:, cols], landed.at[i], sems.at[0, i])
+        for i, cols in enumerate(here)
+    ]
+    leave = [
+        pltpu.make_async_copy(landed.at[i], out.at[:, cols], sems.at[1, i])
+        for i, cols in enumerate(here)
+    ]
+    for copy in arrive:
+        copy.start()
+    for i, (side, pair, rows) in enumerate(jobs):
+        h, l = split(side[...])
+        value = dot3(h, l, band_high[pair, rows], band_low[pair, rows])
+        arrive[i].wait()
+        landed[i] = landed[i] + value
+        leave[i].start()
+    for copy in leave:
+        copy.wait()
 
 
 def apply_tail(west, east, bands, part):
     rows, width = part.shape
-    block = pl.BlockSpec((rows, PAIR), lambda i: (0, (1 - i) * (width // PAIR - 1)))
     args = [held(a) for a in (west, east, *bands)]
+    hbm = pl.BlockSpec(memory_space=pltpu.HBM)
     return pl.pallas_call(
         tail_kernel,
-        grid=(2,),
         out_shape=jax.ShapeDtypeStruct((rows, width), jnp.float32),
-        in_specs=[VMEM_SPEC] * 4 + [block],
-        out_specs=block,
+        in_specs=[VMEM_SPEC] * 4 + [hbm],
+        out_specs=hbm,
+        scratch_shapes=[
+            pltpu.VMEM((2, rows, PAIR), jnp.float32), pltpu.SemaphoreType.DMA((2, 2)),
+        ],
         input_output_aliases={4: 0},
         compiler_params=pltpu.CompilerParams(vmem_limit_bytes=16 << 20),
         name="tail",
-    )(*args, part)
+    )(*args, in_hbm(part))
 
 
 def body(
@@ -324,9 +334,7 @@
 
     starts = (0, width - PAIR, PAIR, width - 2 * PAIR)
     chip = lax.ppermute(block, "row", chip_pairs)
-    own0, own1, own2 = take_columns(
-        block, [(0, PAIR), (PAIR, 2 * PAIR), (2 * PAIR, width)]
-    )
+    own0, own1, own2 = take_columns(block, [(0, PAIR), (PAIR, 2 * PAIR), (2 * PAIR, width)])
     copy2 = lax.ppermute(own2, "row", chip_pairs)
     across0 = lax.ppermute(own0, "row", cross_pairs)
     ends = lax.ppermute(own1, "row", [(middle - 1, 0), (middle, last)])
@@ -352,6 +360,4 @@
 def solution(mesh):
     in_specs = (P(None, "row", "col"), P(), P(), P(), P(), P(), P())
     out_specs = P(None, "row", "col")
-    return jax.shard_map(
-        body, mesh=mesh, in_specs=in_specs, out_specs=out_specs, check_vma=False
-    )
+    return jax.shard_map(body, mesh=mesh, in_specs=in_specs, out_specs=out_specs, check_vma=False)

time: 89 us -> 89.8 us (level)
  no operation moved by 1% of the time
where the time goes in v16:
time: 89.8 us; the launch traced here: 89.4 us
  waiting for transfers between devices  34.6 us (39%)
  Pallas kernels  27.1 us (30%)
  starting transfers between devices  25.7 us (29%)
  local copies, waits for them, and re-layouts  1.77 us (2%)
    ppermute x4, waiting for transfers between devices, body(): side.append(lax.ppermute(half[k], 'col', pairs))  20.4 us
    ppermute x4, starting transfers between devices, body(): side.append(lax.ppermute(half[k], 'col', pairs))  14.5 us
    ppermute x1, waiting for transfers between devices, body(): across2 = lax.ppermute(copy2, 'row', copy_pairs)  11.2 us
    pallas_call x4, Pallas kernels, apply_rows(): pl.pallas_call(functools.partial(rows_kernel, starts), out_shape=pltpu.VM...  10.7 us
    pallas_call x1, Pallas kernels, apply_cols(): pl.pallas_call(cols_kernel, out_shape=jax.ShapeDtypeStruct((rows, width),...  5.14 us
    pallas_call x2, Pallas kernels, build_bands(): pl.pallas_call(functools.partial(band_kernel, transposed), out_shape=(ban...  5.01 us
    pallas_call x1, Pallas kernels, apply_tail(): pl.pallas_call(tail_kernel, out_shape=jax.ShapeDtypeStruct((rows, width),...  3.78 us
    ppermute x1, waiting for transfers between devices, body(): copy2 = lax.ppermute(own2, 'row', chip_pairs)  2.99 us
  transfers between devices with their start and end apart: 11, of which 5 were waited for; matrix products, arithmetic and copies ran while one was open for 0% of the time, Pallas kernels for 26%

profile of v16, /device:TPU:77, one launch (start us, length us, event | category | flops | bytes accessed | tf_op | source)
XLA Modules:
  0.0 89.4 jit_solution(13991952920756860815)
XLA Ops:
  0.0 0.0 copy-start
  0.0 0.0 copy-start.1
  0.0 0.0 copy-start.2
  0.0 0.0 copy-start.3
  0.0 0.0 copy-start.4
  0.0 0.0 copy-start.5
  0.0 0.8 collective-permute-start
  0.8 2.5 %take.1 = (f32[512,256]{1,0:T(8,128)S(1)}, f32[512,256]{1,0:T(8,128)S(1)}, f32[512,512]{1,0:T(8,128)S(1)}) custom-call(f32[512,1024]{1,0:T(8,128)} %bitcast.23), custom_call_target="tpu_custom_call" | custom-call | tf_op jit(solution)/shard_map/take/pallas_call | solution.py:169
  3.3 0.1 collective-permute-start.1
  3.4 3.0 %collective-permute-done.1 = f32[512,512]{1,0:T(8,128)} collective-permute-done((f32[512,512]{1,0:T(8,128)S(1)}, f32[512,512]{1,0:T(8,128)}, u32[]{:S(2)}, u32[]{:S(2)}) %collective-permute-start.1) | collective-permute-done | bytes 1048608 | tf_op jit(solution)/shard_map/ppermute | solution.py:338
  6.4 1.9 %collective-permute-start.2 = (f32[512,512]{1,0:T(8,128)}, f32[512,512]{1,0:T(8,128)S(1)}, u32[]{:S(2)}, u32[]{:S(2)}) collective-permute-start(f32[512,512]{1,0:T(8,128)} %collective-permute-done.1), channel_id=1, source_target_pairs={{24,8},{0,16},{40,24},{16,32},{56,40},{32,48},{72,56},{48,64},{88,... | collective-permute-start | bytes 3145736 | tf_op jit(solution)/shard_map/ppermute | solution.py:343
  8.3 1.5 %collective-permute-start.5 = (f32[512,256]{1,0:T(8,128)S(1)}, f32[512,256]{1,0:T(8,128)}, u32[]{:S(2)}, u32[]{:S(2)}) collective-permute-start(f32[512,256]{1,0:T(8,128)S(1)} %get-tuple-element.15), channel_id=1, source_target_pairs={{56,0},{64,120},{57,1},{65,121},{58,2},{66,122},{59,3},{67,123},{6... | collective-permute-start | bytes 1572872 | tf_op jit(solution)/shard_map/ppermute | solution.py:340
  9.8 2.9 %collective-permute-start.9 = (f32[512,256]{1,0:T(8,128)S(1)}, f32[512,256]{1,0:T(8,128)S(1)}, u32[]{:S(2)}, u32[]{:S(2)}) collective-permute-start(f32[512,256]{1,0:T(8,128)S(1)} %get-tuple-element.18), channel_id=1, source_target_pairs={{16,8},{8,16},{32,24},{24,32},{48,40},{40,48},{64,56},{56,64},{80,... | collective-permute-start | bytes 1572872 | tf_op jit(solution)/shard_map/ppermute | solution.py:339
  12.7 2.7 %collective-permute-start.4 = (f32[512,256]{1,0:T(8,128)S(1)}, f32[512,256]{1,0:T(8,128)}, u32[]{:S(2)}, u32[]{:S(2)}) collective-permute-start(f32[512,256]{1,0:T(8,128)S(1)} %get-tuple-element.15), channel_id=1, source_target_pairs={{16,8},{8,16},{32,24},{24,32},{48,40},{40,48},{80,72},{72,80},{96,... | collective-permute-start | bytes 1572872 | tf_op jit(solution)/shard_map/ppermute | solution.py:342
  15.4 0.0 collective-permute-done.5
  15.4 1.5 %collective-permute-start.6 = (f32[512,256]{1,0:T(8,128)}, f32[512,256]{1,0:T(8,128)}, u32[]{:S(2)}, u32[]{:S(2)}) collective-permute-start(f32[512,256]{1,0:T(8,128)} %collective-permute-done.5), channel_id=1, source_target_pairs={{0,64},{120,56},{1,65},{121,57},{2,66},{122,58},{3,67},{123,59},{4... | collective-permute-start | bytes 1572872 | tf_op jit(solution)/shard_map/ppermute | solution.py:341
  16.8 0.0 copy-done
  16.8 0.0 copy-done.1
  16.8 0.0 copy-done.2
  16.9 0.0 copy-done.3
  16.9 0.0 copy-done.4
  16.9 0.0 copy-done.5
  16.9 2.0 %row_bands.1 = (bf16[2,256,1280]{2,1,0:T(8,128)(2,1)S(1)}, bf16[2,256,1280]{2,1,0:T(8,128)(2,1)S(1)}) custom-call(s32[1]{0:T(128)} %bitcast.place, s32[64,128]{1,0:T(8,128)S(1)} %bitcast.10, s32[64,128]{1,0:T(8,128)S(1)} %bitcast.12, s32[64,128]{1,0:T(8,128)S(1)} %bitcast.14, f32[64,128]{1,0:T(8,128)S(1)} %bitcast.16, f32[64,128]{1,0:T(8,128)S(1)} %bitcast.18, ...), custom_call_target="tpu_custom_call" | custom-call | tf_op jit(solution)/shard_map/row_bands/pallas_call | solution.py:125
  18.8 0.0 collective-permute-done.refs_1_
  18.8 11.2 %collective-permute-done.2.refs_2_ = f32[512,512]{1,0:T(8,128)S(1)} collective-permute-done((f32[512,512]{1,0:T(8,128)}, f32[512,512]{1,0:T(8,128)S(1)}, u32[]{:S(2)}, u32[]{:S(2)}) %collective-permute-start.2) | collective-permute-done | bytes 1048608 | tf_op jit(solution)/shard_map/ppermute | solution.py:343
  30.1 0.0 copy-start.6
  30.1 1.0 %copy-done.6 = f32[512,512]{1,0:T(8,128)} copy-done((f32[512,512]{1,0:T(8,128)}, f32[512,512]{1,0:T(8,128)S(1)}, u32[]{:S(2)}) %copy-start.6) | copy-done | bytes 1048600
  31.0 2.6 %rows.6.refs_4_ = f32[512,256]{1,0:T(8,128)S(1)} custom-call(s32[1]{0:T(128)} %bitcast.place, f32[512,1024]{1,0:T(8,128)} %bitcast.24, f32[512,1024]{1,0:T(8,128)} %collective-permute-done.refs_1_, f32[512,512]{1,0:T(8,128)} %copy-done.6, bf16[2,256,1280]{2,1,0:T(8,128)(2,1)S(1)} %get-tuple-element.13.refs_3_.refs_4_, ...), custom_call_target="tpu_custom_call" | custom-call | tf_op jit(solution)/shard_map/rows/pallas_call | solution.py:217
  33.6 3.9 %collective-permute-start.8 = (f32[512,256]{1,0:T(8,128)S(1)}, f32[512,256]{1,0:T(8,128)S(1)}, u32[]{:S(2)}, u32[]{:S(2)}) collective-permute-start(f32[512,256]{1,0:T(8,128)S(1)} %rows.6.refs_4_), channel_id=1, source_target_pairs={{0,1},{1,2},{2,3},{3,4},{4,5},{5,6},{6,7},{8,9},{9,10},{10,11},{11... | collective-permute-start | bytes 1572872 | tf_op jit(solution)/shard_map/ppermute | solution.py:353
  37.6 0.0 collective-permute-done.9.refs_2_
  37.6 0.0 copy-start.7
  37.6 0.8 copy-done.7
  38.4 2.6 %rows.7.refs_1_ = f32[512,256]{1,0:T(8,128)S(1)} custom-call(s32[1]{0:T(128)} %bitcast.place, f32[512,1024]{1,0:T(8,128)} %bitcast.25, f32[512,1024]{1,0:T(8,128)} %collective-permute-done.refs_1_, f32[512,256]{1,0:T(8,128)} %copy-done.7, bf16[2,256,1280]{2,1,0:T(8,128)(2,1)S(1)} %get-tuple-element.13.refs_3_.refs_4_, ...), custom_call_target="tpu_custom_call" | custom-call | tf_op jit(solution)/shard_map/rows/pallas_call | solution.py:217
  41.0 3.8 %collective-permute-start.10 = (f32[512,256]{1,0:T(8,128)S(1)}, f32[512,256]{1,0:T(8,128)S(1)}, u32[]{:S(2)}, u32[]{:S(2)}) collective-permute-start(f32[512,256]{1,0:T(8,128)S(1)} %rows.7.refs_1_), channel_id=1, source_target_pairs={{1,0},{2,1},{3,2},{4,3},{5,4},{6,5},{7,6},{9,8},{10,9},{11,10},{12... | collective-permute-start | bytes 1572872 | tf_op jit(solution)/shard_map/ppermute | solution.py:353
  44.8 0.0 collective-permute-done.4.refs_2_
  44.8 0.0 collective-permute-done.6.refs_3_
  44.8 2.8 %rows.5.refs_2_ = f32[512,256]{1,0:T(8,128)S(1)} custom-call(s32[1]{0:T(128)} %bitcast.place, f32[512,1024]{1,0:T(8,128)} %bitcast.26, f32[512,1024]{1,0:T(8,128)} %collective-permute-done.refs_1_, f32[512,256]{1,0:T(8,128)} %collective-permute-done.4.refs_2_, f32[512,256]{1,0:T(8,128)} %collective-permute-done.6.refs_3_, ...), custom_call_target="tpu_custom_call" | custom-call | tf_op jit(solution)/shard_map/rows/pallas_call | solution.py:217
  47.6 3.0 %collective-permute-start.7 = (f32[512,256]{1,0:T(8,128)S(1)}, f32[512,256]{1,0:T(8,128)}, u32[]{:S(2)}, u32[]{:S(2)}) collective-permute-start(f32[512,256]{1,0:T(8,128)S(1)} %rows.5.refs_2_), channel_id=1, source_target_pairs={{1,0},{2,1},{3,2},{4,3},{5,4},{6,5},{7,6},{9,8},{10,9},{11,10},{12... | collective-permute-start | bytes 1572872 | tf_op jit(solution)/shard_map/ppermute | solution.py:353
  50.6 2.6 %rows.4.refs_3_ = f32[512,256]{1,0:T(8,128)S(1)} custom-call(s32[1]{0:T(128)} %bitcast.place, f32[512,1024]{1,0:T(8,128)} %bitcast.27, f32[512,1024]{1,0:T(8,128)} %collective-permute-done.refs_1_, f32[512,512]{1,0:T(8,128)} %copy-done.6, bf16[2,256,1280]{2,1,0:T(8,128)(2,1)S(1)} %get-tuple-element.13.refs_3_.refs_4_, ...), custom_call_target="tpu_custom_call" | custom-call | tf_op jit(solution)/shard_map/rows/pallas_call | solution.py:217
  53.3 3.8 %collective-permute-start.3 = (f32[512,256]{1,0:T(8,128)S(1)}, f32[512,256]{1,0:T(8,128)}, u32[]{:S(2)}, u32[]{:S(2)}) collective-permute-start(f32[512,256]{1,0:T(8,128)S(1)} %rows.4.refs_3_), channel_id=1, source_target_pairs={{0,1},{1,2},{2,3},{3,4},{4,5},{5,6},{6,7},{8,9},{9,10},{10,11},{11... | collective-permute-start | bytes 1572872 | tf_op jit(solution)/shard_map/ppermute | solution.py:353
  57.1 3.1 %col_bands.1 = (bf16[4,1280,256]{2,1,0:T(8,128)(2,1)S(1)}, bf16[4,1280,256]{2,1,0:T(8,128)(2,1)S(1)}) custom-call(s32[1]{0:T(128)} %bitcast.8.place, s32[64,128]{1,0:T(8,128)S(1)} %bitcast.11, s32[64,128]{1,0:T(8,128)S(1)} %bitcast.13, s32[64,128]{1,0:T(8,128)S(1)} %bitcast.15, f32[64,128]{1,0:T(8,128)S(1)} %bitcast.17, f32[64,128]{1,0:T(8,128)S(1)} %bitcast.19, ...), custom_call_target="tpu_custom_call" | custom-call | tf_op jit(solution)/shard_map/col_bands/pallas_call | solution.py:125
  60.1 8.9 %collective-permute-done.8.refs_0_ = f32[512,256]{1,0:T(8,128)S(1)} collective-permute-done((f32[512,256]{1,0:T(8,128)S(1)}, f32[512,256]{1,0:T(8,128)S(1)}, u32[]{:S(2)}, u32[]{:S(2)}) %collective-permute-start.8) | collective-permute-done | bytes 524320 | tf_op jit(solution)/shard_map/ppermute | solution.py:353
  69.0 5.3 %collective-permute-done.10.refs_5_ = f32[512,256]{1,0:T(8,128)S(1)} collective-permute-done((f32[512,256]{1,0:T(8,128)S(1)}, f32[512,256]{1,0:T(8,128)S(1)}, u32[]{:S(2)}, u32[]{:S(2)}) %collective-permute-start.10) | collective-permute-done | bytes 524320 | tf_op jit(solution)/shard_map/ppermute | solution.py:353
  74.3 5.1 %cols.1.part = f32[512,1024]{1,0:T(8,128)} custom-call(f32[512,256]{1,0:T(8,128)S(1)} %collective-permute-done.8.refs_0_, f32[512,256]{1,0:T(8,128)S(1)} %rows.7.refs_1_, f32[512,256]{1,0:T(8,128)S(1)} %rows.5.refs_2_, f32[512,256]{1,0:T(8,128)S(1)} %rows.4.refs_3_, f32[512,256]{1,0:T(8,128)S(1)} %rows.6.refs_4_, ...), custom_call_target="tpu_custom_call" | custom-call | tf_op jit(solution)/shard_map/cols/pallas_call | solution.py:254
  79.4 6.2 %collective-permute-done.7.east = f32[512,256]{1,0:T(8,128)} collective-permute-done((f32[512,256]{1,0:T(8,128)S(1)}, f32[512,256]{1,0:T(8,128)}, u32[]{:S(2)}, u32[]{:S(2)}) %collective-permute-start.7) | collective-permute-done | bytes 524320 | tf_op jit(solution)/shard_map/ppermute | solution.py:353
  85.6 0.0 collective-permute-done.3.west
  85.6 3.8 %tail.1 = f32[512,1024]{1,0:T(8,128)} custom-call(f32[512,256]{1,0:T(8,128)} %collective-permute-done.3.west, f32[512,256]{1,0:T(8,128)} %collective-permute-done.7.east, bf16[4,1280,256]{2,1,0:T(8,128)(2,1)S(1)} %get-tuple-element.16.refs_6_.band_high, bf16[4,1280,256]{2,1,0:T(8,128)(2,1)S(1)} %get-tuple-element.17.refs_7_.band_low, ...), custom_call_target="tpu_custom_call", output_to_operand_aliasing={{}: (4, {})} | custom-call | tf_op jit(solution)/shard_map/tail/pallas_call | solution.py:293
Async XLA Ops:
  0.0 16.8 %copy-start = (s32[1,1,8192]{2,1,0:T(1,128)S(1)}, s32[1,1,8192]{2,1,0:T(1,128)}, u32[]{:S(2)}) copy-start(s32[1,1,8192]{2,1,0:T(1,128)} %param.8) | copy-start | bytes 98308
  0.0 16.8 %copy-start.1 = (s32[1,1,8192]{2,1,0:T(1,128)S(1)}, s32[1,1,8192]{2,1,0:T(1,128)}, u32[]{:S(2)}) copy-start(s32[1,1,8192]{2,1,0:T(1,128)} %param.9) | copy-start | bytes 98308
  0.0 16.8 %copy-start.2 = (s32[1,1,8192]{2,1,0:T(1,128)S(1)}, s32[1,1,8192]{2,1,0:T(1,128)}, u32[]{:S(2)}) copy-start(s32[1,1,8192]{2,1,0:T(1,128)} %param.10) | copy-start | bytes 98308
  0.0 16.8 %copy-start.3 = (f32[1,1,8192]{2,1,0:T(1,128)S(1)}, f32[1,1,8192]{2,1,0:T(1,128)}, u32[]{:S(2)}) copy-start(f32[1,1,8192]{2,1,0:T(1,128)} %param.11) | copy-start | bytes 98308
  0.0 16.8 %copy-start.4 = (f32[1,8192]{1,0:T(1,128)S(1)}, f32[1,8192]{1,0:T(1,128)}, u32[]{:S(2)}) copy-start(f32[1,8192]{1,0:T(1,128)} %param.12) | copy-start | bytes 98308
  0.0 16.8 %copy-start.5 = (f32[1,8192]{1,0:T(1,128)S(1)}, f32[1,8192]{1,0:T(1,128)}, u32[]{:S(2)}) copy-start(f32[1,8192]{1,0:T(1,128)} %param.13) | copy-start | bytes 98308
  0.0 18.8 %collective-permute-start = (f32[512,1024]{1,0:T(8,128)}, f32[512,1024]{1,0:T(8,128)}, u32[]{:S(2)}, u32[]{:S(2)}) collective-permute-start(f32[512,1024]{1,0:T(8,128)} %bitcast.22), channel_id=1, source_target_pairs={{0,8},{8,0},{16,24},{24,16},{32,40},{40,32},{48,56},{56,48},{64,72... | collective-permute-start | bytes 6291464 | tf_op jit(solution)/shard_map/ppermute | solution.py:336
  3.3 3.1 %collective-permute-start.1 = (f32[512,512]{1,0:T(8,128)S(1)}, f32[512,512]{1,0:T(8,128)}, u32[]{:S(2)}, u32[]{:S(2)}) collective-permute-start(f32[512,512]{1,0:T(8,128)S(1)} %get-tuple-element.12), channel_id=1, source_target_pairs={{0,8},{8,0},{16,24},{24,16},{32,40},{40,32},{48,56},{56,48},{64,72... | collective-permute-start | bytes 3145736 | tf_op jit(solution)/shard_map/ppermute | solution.py:338
  6.4 23.6 %collective-permute-start.2 = (f32[512,512]{1,0:T(8,128)}, f32[512,512]{1,0:T(8,128)S(1)}, u32[]{:S(2)}, u32[]{:S(2)}) collective-permute-start(f32[512,512]{1,0:T(8,128)} %collective-permute-done.1), channel_id=1, source_target_pairs={{24,8},{0,16},{40,24},{16,32},{56,40},{32,48},{72,56},{48,64},{88,... | collective-permute-start | bytes 3145736 | tf_op jit(solution)/shard_map/ppermute | solution.py:343
  8.3 7.0 %collective-permute-start.5 = (f32[512,256]{1,0:T(8,128)S(1)}, f32[512,256]{1,0:T(8,128)}, u32[]{:S(2)}, u32[]{:S(2)}) collective-permute-start(f32[512,256]{1,0:T(8,128)S(1)} %get-tuple-element.15), channel_id=1, source_target_pairs={{56,0},{64,120},{57,1},{65,121},{58,2},{66,122},{59,3},{67,123},{6... | collective-permute-start | bytes 1572872 | tf_op jit(solution)/shard_map/ppermute | solution.py:340
  9.8 27.8 %collective-permute-start.9 = (f32[512,256]{1,0:T(8,128)S(1)}, f32[512,256]{1,0:T(8,128)S(1)}, u32[]{:S(2)}, u32[]{:S(2)}) collective-permute-start(f32[512,256]{1,0:T(8,128)S(1)} %get-tuple-element.18), channel_id=1, source_target_pairs={{16,8},{8,16},{32,24},{24,32},{48,40},{40,48},{64,56},{56,64},{80,... | collective-permute-start | bytes 1572872 | tf_op jit(solution)/shard_map/ppermute | solution.py:339
  12.7 32.1 %collective-permute-start.4 = (f32[512,256]{1,0:T(8,128)S(1)}, f32[512,256]{1,0:T(8,128)}, u32[]{:S(2)}, u32[]{:S(2)}) collective-permute-start(f32[512,256]{1,0:T(8,128)S(1)} %get-tuple-element.15), channel_id=1, source_target_pairs={{16,8},{8,16},{32,24},{24,32},{48,40},{40,48},{80,72},{72,80},{96,... | collective-permute-start | bytes 1572872 | tf_op jit(solution)/shard_map/ppermute | solution.py:342
  15.4 29.4 %collective-permute-start.6 = (f32[512,256]{1,0:T(8,128)}, f32[512,256]{1,0:T(8,128)}, u32[]{:S(2)}, u32[]{:S(2)}) collective-permute-start(f32[512,256]{1,0:T(8,128)} %collective-permute-done.5), channel_id=1, source_target_pairs={{0,64},{120,56},{1,65},{121,57},{2,66},{122,58},{3,67},{123,59},{4... | collective-permute-start | bytes 1572872 | tf_op jit(solution)/shard_map/ppermute | solution.py:341
  30.1 1.0 %copy-start.6 = (f32[512,512]{1,0:T(8,128)}, f32[512,512]{1,0:T(8,128)S(1)}, u32[]{:S(2)}) copy-start(f32[512,512]{1,0:T(8,128)S(1)} %collective-permute-done.2.refs_2_) | copy-start | bytes 3145732
  33.6 35.4 %collective-permute-start.8 = (f32[512,256]{1,0:T(8,128)S(1)}, f32[512,256]{1,0:T(8,128)S(1)}, u32[]{:S(2)}, u32[]{:S(2)}) collective-permute-start(f32[512,256]{1,0:T(8,128)S(1)} %rows.6.refs_4_), channel_id=1, source_target_pairs={{0,1},{1,2},{2,3},{3,4},{4,5},{5,6},{6,7},{8,9},{9,10},{10,11},{11... | collective-permute-start | bytes 1572872 | tf_op jit(solution)/shard_map/ppermute | solution.py:353
  37.6 0.8 copy-start.7
  41.0 33.3 %collective-permute-start.10 = (f32[512,256]{1,0:T(8,128)S(1)}, f32[512,256]{1,0:T(8,128)S(1)}, u32[]{:S(2)}, u32[]{:S(2)}) collective-permute-start(f32[512,256]{1,0:T(8,128)S(1)} %rows.7.refs_1_), channel_id=1, source_target_pairs={{1,0},{2,1},{3,2},{4,3},{5,4},{6,5},{7,6},{9,8},{10,9},{11,10},{12... | collective-permute-start | bytes 1572872 | tf_op jit(solution)/shard_map/ppermute | solution.py:353
  47.6 38.0 %collective-permute-start.7 = (f32[512,256]{1,0:T(8,128)S(1)}, f32[512,256]{1,0:T(8,128)}, u32[]{:S(2)}, u32[]{:S(2)}) collective-permute-start(f32[512,256]{1,0:T(8,128)S(1)} %rows.5.refs_2_), channel_id=1, source_target_pairs={{1,0},{2,1},{3,2},{4,3},{5,4},{6,5},{7,6},{9,8},{10,9},{11,10},{12... | collective-permute-start | bytes 1572872 | tf_op jit(solution)/shard_map/ppermute | solution.py:353
  53.3 32.4 %collective-permute-start.3 = (f32[512,256]{1,0:T(8,128)S(1)}, f32[512,256]{1,0:T(8,128)}, u32[]{:S(2)}, u32[]{:S(2)}) collective-permute-start(f32[512,256]{1,0:T(8,128)S(1)} %rows.4.refs_3_), channel_id=1, source_target_pairs={{0,1},{1,2},{2,3},{3,4},{4,5},{5,6},{6,7},{8,9},{9,10},{10,11},{11... | collective-permute-start | bytes 1572872 | tf_op jit(solution)/shard_map/ppermute | solution.py:353

commit v17 on v16

--- a/solution.py
+++ b/solution.py
@@ -237,7 +237,7 @@
         low[:, at : at + ref.shape[1]] = l
         at += ref.shape[1]
     for pair in range(out.shape[1] // PAIR):
-        begin = (pair - 1) * PAIR
+        begin = (pair - 2) * PAIR
         skip = max(0, -begin)
         stop = min(at, begin + SPAN)
         ext = slice(begin + skip, stop)
@@ -262,9 +262,8 @@
     )(*args)
 
 
-def tail_kernel(west, east, band_high, band_low, part, out, landed, sems):
-    last = band_high.shape[0] - 1
-    jobs = ((east, last, slice(SPAN - east.shape[1], SPAN)), (west, 0, slice(0, west.shape[1])))
+def tail_kernel(jobs, *refs):
+    *sides, band_high, band_low, part, out, landed, sems = refs
     here = [pl.ds(pair * PAIR, PAIR) for _, pair, _ in jobs]
     arrive = [
         pltpu.make_async_copy(part.at[:, cols], landed.at[i], sems.at[0, i])
@@ -276,9 +275,10 @@
     ]
     for copy in arrive:
         copy.start()
-    for i, (side, pair, rows) in enumerate(jobs):
-        h, l = split(side[...])
-        value = dot3(h, l, band_high[pair, rows], band_low[pair, rows])
+    pieces = [split(side[...]) for side in sides]
+    for i, (side, pair, at) in enumerate(jobs):
+        rows = slice(at, at + PAIR)
+        value = dot3(*pieces[side], band_high[pair, rows], band_low[pair, rows])
         arrive[i].wait()
         landed[i] = landed[i] + value
         leave[i].start()
@@ -286,19 +286,20 @@
         copy.wait()
 
 
-def apply_tail(west, east, bands, part):
+def apply_tail(sides, bands, part, jobs):
     rows, width = part.shape
-    args = [held(a) for a in (west, east, *bands)]
+    args = [held(a) for a in (*sides, *bands)]
     hbm = pl.BlockSpec(memory_space=pltpu.HBM)
     return pl.pallas_call(
-        tail_kernel,
+        functools.partial(tail_kernel, jobs),
         out_shape=jax.ShapeDtypeStruct((rows, width), jnp.float32),
-        in_specs=[VMEM_SPEC] * 4 + [hbm],
+        in_specs=[VMEM_SPEC] * len(args) + [hbm],
         out_specs=hbm,
         scratch_shapes=[
-            pltpu.VMEM((2, rows, PAIR), jnp.float32), pltpu.SemaphoreType.DMA((2, 2)),
+            pltpu.VMEM((len(jobs), rows, PAIR), jnp.float32),
+            pltpu.SemaphoreType.DMA((2, len(jobs))),
         ],
-        input_output_aliases={4: 0},
+        input_output_aliases={len(args): 0},
         compiler_params=pltpu.CompilerParams(vmem_limit_bytes=16 << 20),
         name="tail",
     )(*args, in_hbm(part))
@@ -334,7 +335,9 @@
 
     starts = (0, width - PAIR, PAIR, width - 2 * PAIR)
     chip = lax.ppermute(block, "row", chip_pairs)
-    own0, own1, own2 = take_columns(block, [(0, PAIR), (PAIR, 2 * PAIR), (2 * PAIR, width)])
+    own0, own1, own2 = take_columns(
+        block, [(0, PAIR), (PAIR, 2 * PAIR), (2 * PAIR, width)]
+    )
     copy2 = lax.ppermute(own2, "row", chip_pairs)
     across0 = lax.ppermute(own0, "row", cross_pairs)
     ends = lax.ppermute(own1, "row", [(middle - 1, 0), (middle, last)])
@@ -352,12 +355,18 @@
         pairs = forward(col_count) if k % 2 else backward(col_count)
         side.append(lax.ppermute(half[k], "col", pairs))
     col_bands = build_bands(lat_col, fields, width // PAIR, False)
-    parts = [side[1], half[0], half[2], half[3], half[1], side[0]]
+    parts = [half[0], half[2], half[3], half[1]]
     part = apply_cols(parts, col_bands, width)
-    return apply_tail(side[3], side[2], col_bands, part)[None]
+    end = width // PAIR - 1
+    first = [(0, end - 1, SPAN - PAIR), (0, end, SPAN - 2 * PAIR), (1, 0, PAIR), (1, 1, 0)]
+    second = [(0, end, SPAN - PAIR), (1, 0, 0)]
+    part = apply_tail(side[:2], col_bands, part, first)
+    return apply_tail(side[2:], col_bands, part, second)[None]
 
 
 def solution(mesh):
     in_specs = (P(None, "row", "col"), P(), P(), P(), P(), P(), P())
     out_specs = P(None, "row", "col")
-    return jax.shard_map(body, mesh=mesh, in_specs=in_specs, out_specs=out_specs, check_vma=False)
+    return jax.shard_map(
+        body, mesh=mesh, in_specs=in_specs, out_specs=out_specs, check_vma=False
+    )

time: 89.8 us -> 92.3 us (1.028)
  the two profiles are of different devices: /device:TPU:77 before, /device:TPU:88 now
where the time goes in v17:
time: 92.3 us; the launch traced here: 91.7 us
  waiting for transfers between devices  33.4 us (36%)
  Pallas kernels  31.1 us (34%)
  starting transfers between devices  26 us (28%)
  local copies, waits for them, and re-layouts  0.99 us (1%)
    ppermute x4, waiting for transfers between devices, body(): side.append(lax.ppermute(half[k], 'col', pairs))  20.4 us
    ppermute x4, starting transfers between devices, body(): side.append(lax.ppermute(half[k], 'col', pairs))  13.4 us
    ppermute x1, waiting for transfers between devices, body(): across2 = lax.ppermute(copy2, 'row', copy_pairs)  10.8 us
    pallas_call x4, Pallas kernels, apply_rows(): pl.pallas_call(functools.partial(rows_kernel, starts), out_shape=pltpu.VM...  10.7 us
    pallas_call x2, Pallas kernels, apply_tail(): pl.pallas_call(functools.partial(tail_kernel, jobs), out_shape=jax.ShapeD...  8.44 us
    pallas_call x2, Pallas kernels, build_bands(): pl.pallas_call(functools.partial(band_kernel, transposed), out_shape=(ban...  5.05 us
    pallas_call x1, Pallas kernels, apply_cols(): pl.pallas_call(cols_kernel, out_shape=jax.ShapeDtypeStruct((rows, width),...  4.33 us
    ppermute x1, starting transfers between devices, body(): across1 = lax.ppermute(own1, 'row', other_pairs)  3.64 us
  transfers between devices with their start and end apart: 11, of which 3 were waited for; matrix products, arithmetic and copies ran while one was open for 0% of the time, Pallas kernels for 27%

profile of v17, /device:TPU:88, one launch (start us, length us, event | category | flops | bytes accessed | tf_op | source)
XLA Modules:
  0.0 91.7 jit_solution(10163981864512046313)
XLA Ops:
  0.0 0.0 copy-start.5
  0.0 0.0 copy-start.4
  0.0 0.0 copy-start.3
  0.0 0.0 copy-start.2
  0.0 0.0 copy-start.1
  0.0 0.0 copy-start
  0.0 2.6 %take.1 = (f32[512,256]{1,0:T(8,128)S(1)}, f32[512,256]{1,0:T(8,128)S(1)}, f32[512,512]{1,0:T(8,128)S(1)}) custom-call(f32[512,1024]{1,0:T(8,128)} %bitcast.22), custom_call_target="tpu_custom_call" | custom-call | tf_op jit(solution)/shard_map/take/pallas_call | solution.py:169
  2.6 0.1 collective-permute-start.5
  2.7 0.5 collective-permute-start
  3.2 2.1 %collective-permute-done.5 = f32[512,512]{1,0:T(8,128)S(1)} collective-permute-done((f32[512,512]{1,0:T(8,128)S(1)}, f32[512,512]{1,0:T(8,128)S(1)}, u32[]{:S(2)}, u32[]{:S(2)}) %collective-permute-start.5) | collective-permute-done | bytes 1048608 | tf_op jit(solution)/shard_map/ppermute | solution.py:341
  5.4 3.5 %collective-permute-start.6 = (f32[512,512]{1,0:T(8,128)S(1)}, f32[512,512]{1,0:T(8,128)S(1)}, u32[]{:S(2)}, u32[]{:S(2)}) collective-permute-start(f32[512,512]{1,0:T(8,128)S(1)} %collective-permute-done.5), channel_id=1, source_target_pairs={{24,8},{0,16},{40,24},{16,32},{56,40},{32,48},{72,56},{48,64},{88,... | collective-permute-start | bytes 3145736 | tf_op jit(solution)/shard_map/ppermute | solution.py:346
  8.9 1.5 %collective-permute-start.2 = (f32[512,256]{1,0:T(8,128)S(1)}, f32[512,256]{1,0:T(8,128)}, u32[]{:S(2)}, u32[]{:S(2)}) collective-permute-start(f32[512,256]{1,0:T(8,128)S(1)} %get-tuple-element.12), channel_id=1, source_target_pairs={{56,0},{64,120},{57,1},{65,121},{58,2},{66,122},{59,3},{67,123},{6... | collective-permute-start | bytes 1572872 | tf_op jit(solution)/shard_map/ppermute | solution.py:343
  10.4 1.9 %collective-permute-start.8 = (f32[512,256]{1,0:T(8,128)S(1)}, f32[512,256]{1,0:T(8,128)}, u32[]{:S(2)}, u32[]{:S(2)}) collective-permute-start(f32[512,256]{1,0:T(8,128)S(1)} %get-tuple-element.18), channel_id=1, source_target_pairs={{16,8},{8,16},{32,24},{24,32},{48,40},{40,48},{64,56},{56,64},{80,... | collective-permute-start | bytes 1572872 | tf_op jit(solution)/shard_map/ppermute | solution.py:342
  12.3 3.6 %collective-permute-start.1 = (f32[512,256]{1,0:T(8,128)S(1)}, f32[512,256]{1,0:T(8,128)}, u32[]{:S(2)}, u32[]{:S(2)}) collective-permute-start(f32[512,256]{1,0:T(8,128)S(1)} %get-tuple-element.12), channel_id=1, source_target_pairs={{16,8},{8,16},{32,24},{24,32},{48,40},{40,48},{80,72},{72,80},{96,... | collective-permute-start | bytes 1572872 | tf_op jit(solution)/shard_map/ppermute | solution.py:345
  15.9 0.0 collective-permute-done.2
  16.0 1.5 %collective-permute-start.3 = (f32[512,256]{1,0:T(8,128)}, f32[512,256]{1,0:T(8,128)}, u32[]{:S(2)}, u32[]{:S(2)}) collective-permute-start(f32[512,256]{1,0:T(8,128)} %collective-permute-done.2), channel_id=1, source_target_pairs={{0,64},{120,56},{1,65},{121,57},{2,66},{122,58},{3,67},{123,59},{4... | collective-permute-start | bytes 1572872 | tf_op jit(solution)/shard_map/ppermute | solution.py:344
  17.4 0.0 copy-done.5
  17.4 0.0 copy-done.4
  17.4 0.0 copy-done.3
  17.4 0.0 copy-done.2
  17.4 0.0 copy-done.1
  17.4 0.0 copy-done
  17.4 2.0 %row_bands.1 = (bf16[2,256,1280]{2,1,0:T(8,128)(2,1)S(1)}, bf16[2,256,1280]{2,1,0:T(8,128)(2,1)S(1)}) custom-call(s32[1]{0:T(128)} %bitcast.place, s32[64,128]{1,0:T(8,128)S(1)} %bitcast.10, s32[64,128]{1,0:T(8,128)S(1)} %bitcast.12, s32[64,128]{1,0:T(8,128)S(1)} %bitcast.14, f32[64,128]{1,0:T(8,128)S(1)} %bitcast.16, f32[64,128]{1,0:T(8,128)S(1)} %bitcast.18, ...), custom_call_target="tpu_custom_call" | custom-call | tf_op jit(solution)/shard_map/row_bands/pallas_call | solution.py:125
  19.4 10.8 %collective-permute-done.6.refs_2_ = f32[512,512]{1,0:T(8,128)S(1)} collective-permute-done((f32[512,512]{1,0:T(8,128)S(1)}, f32[512,512]{1,0:T(8,128)S(1)}, u32[]{:S(2)}, u32[]{:S(2)}) %collective-permute-start.6) | collective-permute-done | bytes 1048608 | tf_op jit(solution)/shard_map/ppermute | solution.py:346
  30.3 0.0 copy-start.6
  30.3 0.0 collective-permute-done.refs_1_
  30.3 1.0 %copy-done.6 = f32[512,512]{1,0:T(8,128)} copy-done((f32[512,512]{1,0:T(8,128)}, f32[512,512]{1,0:T(8,128)S(1)}, u32[]{:S(2)}) %copy-start.6) | copy-done | bytes 1048600
  31.2 2.6 %rows.5.refs_2_ = f32[512,256]{1,0:T(8,128)S(1)} custom-call(s32[1]{0:T(128)} %bitcast.place, f32[512,1024]{1,0:T(8,128)} %bitcast.24, f32[512,1024]{1,0:T(8,128)} %collective-permute-done.refs_1_, f32[512,512]{1,0:T(8,128)} %copy-done.6, bf16[2,256,1280]{2,1,0:T(8,128)(2,1)S(1)} %get-tuple-element.13.refs_4_.refs_3_, ...), custom_call_target="tpu_custom_call" | custom-call | tf_op jit(solution)/shard_map/rows/pallas_call | solution.py:217
  33.9 4.1 %collective-permute-start.7 = (f32[512,256]{1,0:T(8,128)S(1)}, f32[512,256]{1,0:T(8,128)S(1)}, u32[]{:S(2)}, u32[]{:S(2)}) collective-permute-start(f32[512,256]{1,0:T(8,128)S(1)} %rows.5.refs_2_), channel_id=1, source_target_pairs={{0,1},{1,2},{2,3},{3,4},{4,5},{5,6},{6,7},{8,9},{9,10},{10,11},{11... | collective-permute-start | bytes 1572872 | tf_op jit(solution)/shard_map/ppermute | solution.py:356
  37.9 2.6 %rows.7.refs_3_ = f32[512,256]{1,0:T(8,128)S(1)} custom-call(s32[1]{0:T(128)} %bitcast.place, f32[512,1024]{1,0:T(8,128)} %bitcast.25, f32[512,1024]{1,0:T(8,128)} %collective-permute-done.refs_1_, f32[512,512]{1,0:T(8,128)} %copy-done.6, bf16[2,256,1280]{2,1,0:T(8,128)(2,1)S(1)} %get-tuple-element.13.refs_4_.refs_3_, ...), custom_call_target="tpu_custom_call" | custom-call | tf_op jit(solution)/shard_map/rows/pallas_call | solution.py:217
  40.6 4.2 %collective-permute-start.10 = (f32[512,256]{1,0:T(8,128)S(1)}, f32[512,256]{1,0:T(8,128)S(1)}, u32[]{:S(2)}, u32[]{:S(2)}) collective-permute-start(f32[512,256]{1,0:T(8,128)S(1)} %rows.7.refs_3_), channel_id=1, source_target_pairs={{0,1},{1,2},{2,3},{3,4},{4,5},{5,6},{6,7},{8,9},{9,10},{10,11},{11... | collective-permute-start | bytes 1572872 | tf_op jit(solution)/shard_map/ppermute | solution.py:356
  44.8 0.0 collective-permute-done.8.refs_2_
  44.8 2.6 %rows.6.refs_0_ = f32[512,256]{1,0:T(8,128)S(1)} custom-call(s32[1]{0:T(128)} %bitcast.place, f32[512,1024]{1,0:T(8,128)} %bitcast.26, f32[512,1024]{1,0:T(8,128)} %collective-permute-done.refs_1_, f32[512,256]{1,0:T(8,128)} %collective-permute-done.8.refs_2_, bf16[2,256,1280]{2,1,0:T(8,128)(2,1)S(1)} %get-tuple-element.13.refs_4_.refs_3_, ...), custom_call_target="tpu_custom_call" | custom-call | tf_op jit(solution)/shard_map/rows/pallas_call | solution.py:217
  47.4 3.2 %collective-permute-start.9 = (f32[512,256]{1,0:T(8,128)S(1)}, f32[512,256]{1,0:T(8,128)}, u32[]{:S(2)}, u32[]{:S(2)}) collective-permute-start(f32[512,256]{1,0:T(8,128)S(1)} %rows.6.refs_0_), channel_id=1, source_target_pairs={{1,0},{2,1},{3,2},{4,3},{5,4},{6,5},{7,6},{9,8},{10,9},{11,10},{12... | collective-permute-start | bytes 1572872 | tf_op jit(solution)/shard_map/ppermute | solution.py:356
  50.6 0.0 collective-permute-done.1.refs_2_
  50.6 0.0 collective-permute-done.3.refs_3_
  50.6 2.8 %rows.4.refs_1_ = f32[512,256]{1,0:T(8,128)S(1)} custom-call(s32[1]{0:T(128)} %bitcast.place, f32[512,1024]{1,0:T(8,128)} %bitcast.27, f32[512,1024]{1,0:T(8,128)} %collective-permute-done.refs_1_, f32[512,256]{1,0:T(8,128)} %collective-permute-done.1.refs_2_, f32[512,256]{1,0:T(8,128)} %collective-permute-done.3.refs_3_, ...), custom_call_target="tpu_custom_call" | custom-call | tf_op jit(solution)/shard_map/rows/pallas_call | solution.py:217
  53.5 1.9 %collective-permute-start.4 = (f32[512,256]{1,0:T(8,128)S(1)}, f32[512,256]{1,0:T(8,128)}, u32[]{:S(2)}, u32[]{:S(2)}) collective-permute-start(f32[512,256]{1,0:T(8,128)S(1)} %rows.4.refs_1_), channel_id=1, source_target_pairs={{1,0},{2,1},{3,2},{4,3},{5,4},{6,5},{7,6},{9,8},{10,9},{11,10},{12... | collective-permute-start | bytes 1572872 | tf_op jit(solution)/shard_map/ppermute | solution.py:356
  55.4 3.1 %col_bands.1 = (bf16[4,1280,256]{2,1,0:T(8,128)(2,1)S(1)}, bf16[4,1280,256]{2,1,0:T(8,128)(2,1)S(1)}) custom-call(s32[1]{0:T(128)} %bitcast.8.place, s32[64,128]{1,0:T(8,128)S(1)} %bitcast.11, s32[64,128]{1,0:T(8,128)S(1)} %bitcast.13, s32[64,128]{1,0:T(8,128)S(1)} %bitcast.15, f32[64,128]{1,0:T(8,128)S(1)} %bitcast.17, f32[64,128]{1,0:T(8,128)S(1)} %bitcast.19, ...), custom_call_target="tpu_custom_call" | custom-call | tf_op jit(solution)/shard_map/col_bands/pallas_call | solution.py:125
  58.5 4.3 %cols.1.refs_4_ = f32[512,1024]{1,0:T(8,128)} custom-call(f32[512,256]{1,0:T(8,128)S(1)} %rows.6.refs_0_, f32[512,256]{1,0:T(8,128)S(1)} %rows.4.refs_1_, f32[512,256]{1,0:T(8,128)S(1)} %rows.5.refs_2_, f32[512,256]{1,0:T(8,128)S(1)} %rows.7.refs_3_, bf16[4,1280,256]{2,1,0:T(8,128)(2,1)S(1)} %get-tuple-element.16.refs_4_.refs_2_, ...), custom_call_target="tpu_custom_call" | custom-call | tf_op jit(solution)/shard_map/cols/pallas_call | solution.py:254
  62.8 20.4 %collective-permute-done.10.refs_1_ = f32[512,256]{1,0:T(8,128)S(1)} collective-permute-done((f32[512,256]{1,0:T(8,128)S(1)}, f32[512,256]{1,0:T(8,128)S(1)}, u32[]{:S(2)}, u32[]{:S(2)}) %collective-permute-start.10) | collective-permute-done | bytes 524320 | tf_op jit(solution)/shard_map/ppermute | solution.py:356
  83.2 0.0 collective-permute-done.9.refs_0_
  83.2 4.8 %tail.2.refs_4_ = f32[512,1024]{1,0:T(8,128)} custom-call(f32[512,256]{1,0:T(8,128)} %collective-permute-done.9.refs_0_, f32[512,256]{1,0:T(8,128)S(1)} %collective-permute-done.10.refs_1_, bf16[4,1280,256]{2,1,0:T(8,128)(2,1)S(1)} %get-tuple-element.16.refs_4_.refs_2_, ...), custom_call_target="tpu_custom_call", output_to_operand_aliasing={{}: (4, {})} | custom-call | tf_op jit(solution)/shard_map/tail/pallas_call | solution.py:293
  88.1 0.0 collective-permute-done.7.refs_1_
  88.1 0.0 collective-permute-done.4.refs_0_
  88.1 3.6 %tail.3 = f32[512,1024]{1,0:T(8,128)} custom-call(f32[512,256]{1,0:T(8,128)} %collective-permute-done.4.refs_0_, f32[512,256]{1,0:T(8,128)S(1)} %collective-permute-done.7.refs_1_, bf16[4,1280,256]{2,1,0:T(8,128)(2,1)S(1)} %get-tuple-element.16.refs_4_.refs_2_, ...), custom_call_target="tpu_custom_call", output_to_operand_aliasing={{}: (4, {})} | custom-call | tf_op jit(solution)/shard_map/tail/pallas_call | solution.py:293
Async XLA Ops:
  0.0 17.4 %copy-start.5 = (f32[1,8192]{1,0:T(1,128)S(1)}, f32[1,8192]{1,0:T(1,128)}, u32[]{:S(2)}) copy-start(f32[1,8192]{1,0:T(1,128)} %param.13) | copy-start | bytes 98308
  0.0 17.4 %copy-start.4 = (f32[1,8192]{1,0:T(1,128)S(1)}, f32[1,8192]{1,0:T(1,128)}, u32[]{:S(2)}) copy-start(f32[1,8192]{1,0:T(1,128)} %param.12) | copy-start | bytes 98308
  0.0 17.4 %copy-start.3 = (f32[1,1,8192]{2,1,0:T(1,128)S(1)}, f32[1,1,8192]{2,1,0:T(1,128)}, u32[]{:S(2)}) copy-start(f32[1,1,8192]{2,1,0:T(1,128)} %param.11) | copy-start | bytes 98308
  0.0 17.4 %copy-start.2 = (s32[1,1,8192]{2,1,0:T(1,128)S(1)}, s32[1,1,8192]{2,1,0:T(1,128)}, u32[]{:S(2)}) copy-start(s32[1,1,8192]{2,1,0:T(1,128)} %param.10) | copy-start | bytes 98308
  0.0 17.4 %copy-start.1 = (s32[1,1,8192]{2,1,0:T(1,128)S(1)}, s32[1,1,8192]{2,1,0:T(1,128)}, u32[]{:S(2)}) copy-start(s32[1,1,8192]{2,1,0:T(1,128)} %param.9) | copy-start | bytes 98308
  0.0 17.4 %copy-start = (s32[1,1,8192]{2,1,0:T(1,128)S(1)}, s32[1,1,8192]{2,1,0:T(1,128)}, u32[]{:S(2)}) copy-start(s32[1,1,8192]{2,1,0:T(1,128)} %param.8) | copy-start | bytes 98308
  2.6 2.7 %collective-permute-start.5 = (f32[512,512]{1,0:T(8,128)S(1)}, f32[512,512]{1,0:T(8,128)S(1)}, u32[]{:S(2)}, u32[]{:S(2)}) collective-permute-start(f32[512,512]{1,0:T(8,128)S(1)} %get-tuple-element.15), channel_id=1, source_target_pairs={{0,8},{8,0},{16,24},{24,16},{32,40},{40,32},{48,56},{56,48},{64,72... | collective-permute-start | bytes 3145736 | tf_op jit(solution)/shard_map/ppermute | solution.py:341
  2.7 27.5 %collective-permute-start = (f32[512,1024]{1,0:T(8,128)}, f32[512,1024]{1,0:T(8,128)}, u32[]{:S(2)}, u32[]{:S(2)}) collective-permute-start(f32[512,1024]{1,0:T(8,128)} %bitcast.23), channel_id=1, source_target_pairs={{0,8},{8,0},{16,24},{24,16},{32,40},{40,32},{48,56},{56,48},{64,72... | collective-permute-start | bytes 6291464 | tf_op jit(solution)/shard_map/ppermute | solution.py:337
  5.4 24.9 %collective-permute-start.6 = (f32[512,512]{1,0:T(8,128)S(1)}, f32[512,512]{1,0:T(8,128)S(1)}, u32[]{:S(2)}, u32[]{:S(2)}) collective-permute-start(f32[512,512]{1,0:T(8,128)S(1)} %collective-permute-done.5), channel_id=1, source_target_pairs={{24,8},{0,16},{40,24},{16,32},{56,40},{32,48},{72,56},{48,64},{88,... | collective-permute-start | bytes 3145736 | tf_op jit(solution)/shard_map/ppermute | solution.py:346
  8.9 7.0 %collective-permute-start.2 = (f32[512,256]{1,0:T(8,128)S(1)}, f32[512,256]{1,0:T(8,128)}, u32[]{:S(2)}, u32[]{:S(2)}) collective-permute-start(f32[512,256]{1,0:T(8,128)S(1)} %get-tuple-element.12), channel_id=1, source_target_pairs={{56,0},{64,120},{57,1},{65,121},{58,2},{66,122},{59,3},{67,123},{6... | collective-permute-start | bytes 1572872 | tf_op jit(solution)/shard_map/ppermute | solution.py:343
  10.4 34.4 %collective-permute-start.8 = (f32[512,256]{1,0:T(8,128)S(1)}, f32[512,256]{1,0:T(8,128)}, u32[]{:S(2)}, u32[]{:S(2)}) collective-permute-start(f32[512,256]{1,0:T(8,128)S(1)} %get-tuple-element.18), channel_id=1, source_target_pairs={{16,8},{8,16},{32,24},{24,32},{48,40},{40,48},{64,56},{56,64},{80,... | collective-permute-start | bytes 1572872 | tf_op jit(solution)/shard_map/ppermute | solution.py:342
  12.3 38.3 %collective-permute-start.1 = (f32[512,256]{1,0:T(8,128)S(1)}, f32[512,256]{1,0:T(8,128)}, u32[]{:S(2)}, u32[]{:S(2)}) collective-permute-start(f32[512,256]{1,0:T(8,128)S(1)} %get-tuple-element.12), channel_id=1, source_target_pairs={{16,8},{8,16},{32,24},{24,32},{48,40},{40,48},{80,72},{72,80},{96,... | collective-permute-start | bytes 1572872 | tf_op jit(solution)/shard_map/ppermute | solution.py:345
  16.0 34.7 %collective-permute-start.3 = (f32[512,256]{1,0:T(8,128)}, f32[512,256]{1,0:T(8,128)}, u32[]{:S(2)}, u32[]{:S(2)}) collective-permute-start(f32[512,256]{1,0:T(8,128)} %collective-permute-done.2), channel_id=1, source_target_pairs={{0,64},{120,56},{1,65},{121,57},{2,66},{122,58},{3,67},{123,59},{4... | collective-permute-start | bytes 1572872 | tf_op jit(solution)/shard_map/ppermute | solution.py:344
  30.3 1.0 %copy-start.6 = (f32[512,512]{1,0:T(8,128)}, f32[512,512]{1,0:T(8,128)S(1)}, u32[]{:S(2)}) copy-start(f32[512,512]{1,0:T(8,128)S(1)} %collective-permute-done.6.refs_2_) | copy-start | bytes 3145732
  33.9 54.2 %collective-permute-start.7 = (f32[512,256]{1,0:T(8,128)S(1)}, f32[512,256]{1,0:T(8,128)S(1)}, u32[]{:S(2)}, u32[]{:S(2)}) collective-permute-start(f32[512,256]{1,0:T(8,128)S(1)} %rows.5.refs_2_), channel_id=1, source_target_pairs={{0,1},{1,2},{2,3},{3,4},{4,5},{5,6},{6,7},{8,9},{9,10},{10,11},{11... | collective-permute-start | bytes 1572872 | tf_op jit(solution)/shard_map/ppermute | solution.py:356
  40.6 42.7 %collective-permute-start.10 = (f32[512,256]{1,0:T(8,128)S(1)}, f32[512,256]{1,0:T(8,128)S(1)}, u32[]{:S(2)}, u32[]{:S(2)}) collective-permute-start(f32[512,256]{1,0:T(8,128)S(1)} %rows.7.refs_3_), channel_id=1, source_target_pairs={{0,1},{1,2},{2,3},{3,4},{4,5},{5,6},{6,7},{8,9},{9,10},{10,11},{11... | collective-permute-start | bytes 1572872 | tf_op jit(solution)/shard_map/ppermute | solution.py:356
  47.4 35.8 %collective-permute-start.9 = (f32[512,256]{1,0:T(8,128)S(1)}, f32[512,256]{1,0:T(8,128)}, u32[]{:S(2)}, u32[]{:S(2)}) collective-permute-start(f32[512,256]{1,0:T(8,128)S(1)} %rows.6.refs_0_), channel_id=1, source_target_pairs={{1,0},{2,1},{3,2},{4,3},{5,4},{6,5},{7,6},{9,8},{10,9},{11,10},{12... | collective-permute-start | bytes 1572872 | tf_op jit(solution)/shard_map/ppermute | solution.py:356
  53.5 34.6 %collective-permute-start.4 = (f32[512,256]{1,0:T(8,128)S(1)}, f32[512,256]{1,0:T(8,128)}, u32[]{:S(2)}, u32[]{:S(2)}) collective-permute-start(f32[512,256]{1,0:T(8,128)S(1)} %rows.4.refs_1_), channel_id=1, source_target_pairs={{1,0},{2,1},{3,2},{4,3},{5,4},{6,5},{7,6},{9,8},{10,9},{11,10},{12... | collective-permute-start | bytes 1572872 | tf_op jit(solution)/shard_map/ppermute | solution.py:356

commit v18 on v15

--- a/solution.py
+++ b/solution.py
@@ -161,7 +161,7 @@
         leave.wait()
 
 
-def take_columns(source, ranges):
+def take_columns(source, space, ranges):
     rows = source.shape[0]
     starts = [start for start, _ in ranges]
     shapes = [(rows, stop - start) for start, stop in ranges]
@@ -169,13 +169,13 @@
     return pl.pallas_call(
         functools.partial(take_kernel, starts),
         out_shape=tuple(jax.ShapeDtypeStruct(shape, jnp.float32) for shape in shapes),
-        in_specs=[hbm],
+        in_specs=[pl.BlockSpec(memory_space=space)],
         out_specs=(hbm,) * len(ranges),
         scratch_shapes=[pltpu.VMEM(shape, jnp.float32) for shape in shapes]
         + [pltpu.SemaphoreType.DMA((2, len(ranges), 4))],
         compiler_params=pltpu.CompilerParams(vmem_limit_bytes=8 << 20),
         name="take",
-    )(in_hbm(source))
+    )(source)
 
 
 def rows_kernel(starts, place, *refs):
@@ -218,13 +218,14 @@
         functools.partial(rows_kernel, starts),
         out_shape=pltpu.VMEM((rows, width), jnp.float32),
         in_specs=[pl.BlockSpec(memory_space=pltpu.SMEM)]
-        + [pl.BlockSpec(memory_space=pltpu.HBM)] * len(sources)
+        + [pl.BlockSpec(memory_space=pltpu.HBM)]
+        + [pl.BlockSpec(memory_space=pl.ANY)] * (len(sources) - 1)
         + [VMEM_SPEC] * 2,
         out_specs=VMEM_SPEC,
         scratch_shapes=[ext, ext, landed, pltpu.SemaphoreType.DMA((len(sources),))],
         compiler_params=pltpu.CompilerParams(vmem_limit_bytes=16 << 20),
         name="rows",
-    )(place, *(in_hbm(a) for a in sources), *(held(a) for a in bands))
+    )(place, in_hbm(sources[0]), *sources[1:], *(held(a) for a in bands))
 
 
 def cols_kernel(*refs):
@@ -324,10 +325,8 @@
 
     starts = (0, width - PAIR, PAIR, width - 2 * PAIR)
     chip = lax.ppermute(block, "row", chip_pairs)
-    own0, own1, own2 = take_columns(
-        block, [(0, PAIR), (PAIR, 2 * PAIR), (2 * PAIR, width)]
-    )
-    copy2 = lax.ppermute(own2, "row", chip_pairs)
+    own0, own1 = take_columns(in_hbm(block), pltpu.HBM, [(0, PAIR), (PAIR, 2 * PAIR)])
+    (copy2,) = take_columns(chip, pl.ANY, [(2 * PAIR, width)])
     across0 = lax.ppermute(own0, "row", cross_pairs)
     ends = lax.ppermute(own1, "row", [(middle - 1, 0), (middle, last)])
     relay = lax.ppermute(ends, "row", [(0, middle), (last, middle - 1)])

time: 89 us -> 87.4 us (0.982)
  the two profiles are of different devices: /device:TPU:77 before, /device:TPU:115 now
where the time goes in v18:
time: 87.4 us; the launch traced here: 86.9 us
  Pallas kernels  31.3 us (36%)
  starting transfers between devices  29.3 us (34%)
  waiting for transfers between devices  26.1 us (30%)
    ppermute x4, waiting for transfers between devices, body(): side.append(lax.ppermute(half[k], 'col', pairs))  15.8 us
    ppermute x4, starting transfers between devices, body(): side.append(lax.ppermute(half[k], 'col', pairs))  15.4 us
    pallas_call x4, Pallas kernels, apply_rows(): pl.pallas_call(functools.partial(rows_kernel, starts), out_shape=pltpu.VM...  13.2 us
    pallas_call x1, Pallas kernels, apply_cols(): pl.pallas_call(cols_kernel, out_shape=jax.ShapeDtypeStruct((rows, width),...  6.97 us
    ppermute x1, waiting for transfers between devices, body(): across0 = lax.ppermute(own0, 'row', cross_pairs)  6.26 us
    pallas_call x2, Pallas kernels, build_bands(): pl.pallas_call(functools.partial(band_kernel, transposed), out_shape=(ban...  5.05 us
    ppermute x1, starting transfers between devices, body(): across0 = lax.ppermute(own0, 'row', cross_pairs)  4.6 us
    ppermute x1, waiting for transfers between devices, body(): chip = lax.ppermute(block, 'row', chip_pairs)  4 us
  transfers between devices with their start and end apart: 10, of which 4 were waited for; matrix products, arithmetic and copies ran while one was open for 0% of the time, Pallas kernels for 31%

profile of v18, /device:TPU:115, one launch (start us, length us, event | category | flops | bytes accessed | tf_op | source)
XLA Modules:
  0.0 86.9 jit_solution(11009908121520564797)
XLA Ops:
  0.0 0.0 copy-start
  0.0 0.0 copy-start.1
  0.0 0.0 copy-start.2
  0.0 0.0 copy-start.3
  0.0 0.0 copy-start.4
  0.0 0.0 copy-start.5
  0.0 0.8 collective-permute-start
  0.8 4.0 %collective-permute-done.source.refs_1_ = f32[512,1024]{1,0:T(8,128)S(1)} collective-permute-done((f32[512,1024]{1,0:T(8,128)}, f32[512,1024]{1,0:T(8,128)S(1)}, u32[]{:S(2)}, u32[]{:S(2)}) %collective-permute-start) | collective-permute-done | bytes 2097184 | tf_op jit(solution)/shard_map/ppermute | solution.py:327
  4.8 1.1 %take.2 = f32[512,512]{1,0:T(8,128)} custom-call(f32[512,1024]{1,0:T(8,128)S(1)} %collective-permute-done.source.refs_1_), custom_call_target="tpu_custom_call" | custom-call | tf_op jit(solution)/shard_map/take/pallas_call | solution.py:169
  5.9 2.0 %collective-permute-start.1 = (f32[512,512]{1,0:T(8,128)}, f32[512,512]{1,0:T(8,128)S(1)}, u32[]{:S(2)}, u32[]{:S(2)}) collective-permute-start(f32[512,512]{1,0:T(8,128)} %take.2), channel_id=1, source_target_pairs={{24,8},{0,16},{40,24},{16,32},{56,40},{32,48},{72,56},{48,64},{88,... | collective-permute-start | bytes 3145736 | tf_op jit(solution)/shard_map/ppermute | solution.py:334
  7.9 2.1 %take.3 = (f32[512,256]{1,0:T(8,128)}, f32[512,256]{1,0:T(8,128)}) custom-call(f32[512,1024]{1,0:T(8,128)} %bitcast.23), custom_call_target="tpu_custom_call" | custom-call | tf_op jit(solution)/shard_map/take/pallas_call | solution.py:169
  10.1 3.8 %collective-permute-start.4 = (f32[512,256]{1,0:T(8,128)}, f32[512,256]{1,0:T(8,128)}, u32[]{:S(2)}, u32[]{:S(2)}) collective-permute-start(f32[512,256]{1,0:T(8,128)} %get-tuple-element.13), channel_id=1, source_target_pairs={{56,0},{64,120},{57,1},{65,121},{58,2},{66,122},{59,3},{67,123},{6... | collective-permute-start | bytes 1572872 | tf_op jit(solution)/shard_map/ppermute | solution.py:331
  13.8 4.6 %collective-permute-start.8 = (f32[512,256]{1,0:T(8,128)}, f32[512,256]{1,0:T(8,128)}, u32[]{:S(2)}, u32[]{:S(2)}) collective-permute-start(f32[512,256]{1,0:T(8,128)} %get-tuple-element.16), channel_id=1, source_target_pairs={{16,8},{8,16},{32,24},{24,32},{48,40},{40,48},{64,56},{56,64},{80,... | collective-permute-start | bytes 1572872 | tf_op jit(solution)/shard_map/ppermute | solution.py:330
  18.4 1.5 %collective-permute-start.3 = (f32[512,256]{1,0:T(8,128)}, f32[512,256]{1,0:T(8,128)}, u32[]{:S(2)}, u32[]{:S(2)}) collective-permute-start(f32[512,256]{1,0:T(8,128)} %get-tuple-element.13), channel_id=1, source_target_pairs={{16,8},{8,16},{32,24},{24,32},{48,40},{40,48},{80,72},{72,80},{96,... | collective-permute-start | bytes 1572872 | tf_op jit(solution)/shard_map/ppermute | solution.py:333
  19.9 0.0 collective-permute-done.4
  19.9 1.3 %collective-permute-start.5 = (f32[512,256]{1,0:T(8,128)}, f32[512,256]{1,0:T(8,128)}, u32[]{:S(2)}, u32[]{:S(2)}) collective-permute-start(f32[512,256]{1,0:T(8,128)} %collective-permute-done.4), channel_id=1, source_target_pairs={{0,64},{120,56},{1,65},{121,57},{2,66},{122,58},{3,67},{123,59},{4... | collective-permute-start | bytes 1572872 | tf_op jit(solution)/shard_map/ppermute | solution.py:332
  21.2 0.0 copy-done
  21.2 0.0 copy-done.1
  21.2 0.0 copy-done.2
  21.3 0.0 copy-done.3
  21.3 0.0 copy-done.4
  21.3 0.0 copy-done.5
  21.3 1.9 %row_bands.1 = (bf16[2,256,1280]{2,1,0:T(8,128)(2,1)S(1)}, bf16[2,256,1280]{2,1,0:T(8,128)(2,1)S(1)}) custom-call(s32[1]{0:T(128)} %bitcast.place, s32[64,128]{1,0:T(8,128)S(1)} %bitcast.10, s32[64,128]{1,0:T(8,128)S(1)} %bitcast.12, s32[64,128]{1,0:T(8,128)S(1)} %bitcast.14, f32[64,128]{1,0:T(8,128)S(1)} %bitcast.16, f32[64,128]{1,0:T(8,128)S(1)} %bitcast.18, ...), custom_call_target="tpu_custom_call" | custom-call | tf_op jit(solution)/shard_map/row_bands/pallas_call | solution.py:125
  23.2 6.3 %collective-permute-done.8.refs_2_ = f32[512,256]{1,0:T(8,128)} collective-permute-done((f32[512,256]{1,0:T(8,128)}, f32[512,256]{1,0:T(8,128)}, u32[]{:S(2)}, u32[]{:S(2)}) %collective-permute-start.8) | collective-permute-done | bytes 524320 | tf_op jit(solution)/shard_map/ppermute | solution.py:330
  29.5 3.3 %rows.7.refs_1_ = f32[512,256]{1,0:T(8,128)} custom-call(s32[1]{0:T(128)} %bitcast.place, f32[512,1024]{1,0:T(8,128)} %bitcast.24, f32[512,1024]{1,0:T(8,128)S(1)} %collective-permute-done.source.refs_1_, f32[512,256]{1,0:T(8,128)} %collective-permute-done.8.refs_2_, bf16[2,256,1280]{2,1,0:T(8,128)(2,1)S(1)} %get-tuple-element.11.refs_3_.refs_4_, ...), custom_call_target="tpu_custom_call" | custom-call | tf_op jit(solution)/shard_map/rows/pallas_call | solution.py:217
  32.8 2.0 %collective-permute-start.9 = (f32[512,256]{1,0:T(8,128)}, f32[512,256]{1,0:T(8,128)}, u32[]{:S(2)}, u32[]{:S(2)}) collective-permute-start(f32[512,256]{1,0:T(8,128)} %rows.7.refs_1_), channel_id=1, source_target_pairs={{1,0},{2,1},{3,2},{4,3},{5,4},{6,5},{7,6},{9,8},{10,9},{11,10},{12... | collective-permute-start | bytes 1572872 | tf_op jit(solution)/shard_map/ppermute | solution.py:344
  34.7 0.0 collective-permute-done.1.refs_2_
  34.8 3.2 %rows.6.refs_4_ = f32[512,256]{1,0:T(8,128)} custom-call(s32[1]{0:T(128)} %bitcast.place, f32[512,1024]{1,0:T(8,128)} %bitcast.25, f32[512,1024]{1,0:T(8,128)S(1)} %collective-permute-done.source.refs_1_, f32[512,512]{1,0:T(8,128)S(1)} %collective-permute-done.1.refs_2_, bf16[2,256,1280]{2,1,0:T(8,128)(2,1)S(1)} %get-tuple-element.11.refs_3_.refs_4_, ...), custom_call_target="tpu_custom_call" | custom-call | tf_op jit(solution)/shard_map/rows/pallas_call | solution.py:217
  38.0 5.7 %collective-permute-start.7 = (f32[512,256]{1,0:T(8,128)}, f32[512,256]{1,0:T(8,128)}, u32[]{:S(2)}, u32[]{:S(2)}) collective-permute-start(f32[512,256]{1,0:T(8,128)} %rows.6.refs_4_), channel_id=1, source_target_pairs={{0,1},{1,2},{2,3},{3,4},{4,5},{5,6},{6,7},{8,9},{9,10},{10,11},{11... | collective-permute-start | bytes 1572872 | tf_op jit(solution)/shard_map/ppermute | solution.py:344
  43.7 0.0 collective-permute-done.3.refs_2_
  43.7 0.0 collective-permute-done.5.refs_3_
  43.7 3.5 %rows.5.refs_2_ = f32[512,256]{1,0:T(8,128)} custom-call(s32[1]{0:T(128)} %bitcast.place, f32[512,1024]{1,0:T(8,128)} %bitcast.26, f32[512,1024]{1,0:T(8,128)S(1)} %collective-permute-done.source.refs_1_, f32[512,256]{1,0:T(8,128)} %collective-permute-done.3.refs_2_, f32[512,256]{1,0:T(8,128)} %collective-permute-done.5.refs_3_, ...), custom_call_target="tpu_custom_call" | custom-call | tf_op jit(solution)/shard_map/rows/pallas_call | solution.py:217
  47.2 1.9 %collective-permute-start.6 = (f32[512,256]{1,0:T(8,128)}, f32[512,256]{1,0:T(8,128)}, u32[]{:S(2)}, u32[]{:S(2)}) collective-permute-start(f32[512,256]{1,0:T(8,128)} %rows.5.refs_2_), channel_id=1, source_target_pairs={{1,0},{2,1},{3,2},{4,3},{5,4},{6,5},{7,6},{9,8},{10,9},{11,10},{12... | collective-permute-start | bytes 1572872 | tf_op jit(solution)/shard_map/ppermute | solution.py:344
  49.2 3.2 %rows.4.refs_3_ = f32[512,256]{1,0:T(8,128)} custom-call(s32[1]{0:T(128)} %bitcast.place, f32[512,1024]{1,0:T(8,128)} %bitcast.27, f32[512,1024]{1,0:T(8,128)S(1)} %collective-permute-done.source.refs_1_, f32[512,512]{1,0:T(8,128)S(1)} %collective-permute-done.1.refs_2_, bf16[2,256,1280]{2,1,0:T(8,128)(2,1)S(1)} %get-tuple-element.11.refs_3_.refs_4_, ...), custom_call_target="tpu_custom_call" | custom-call | tf_op jit(solution)/shard_map/rows/pallas_call | solution.py:217
  52.4 5.8 %collective-permute-start.2 = (f32[512,256]{1,0:T(8,128)}, f32[512,256]{1,0:T(8,128)S(1)}, u32[]{:S(2)}, u32[]{:S(2)}) collective-permute-start(f32[512,256]{1,0:T(8,128)} %rows.4.refs_3_), channel_id=1, source_target_pairs={{0,1},{1,2},{2,3},{3,4},{4,5},{5,6},{6,7},{8,9},{9,10},{10,11},{11... | collective-permute-start | bytes 1572872 | tf_op jit(solution)/shard_map/ppermute | solution.py:344
  58.2 3.1 %col_bands.1 = (bf16[4,1280,256]{2,1,0:T(8,128)(2,1)S(1)}, bf16[4,1280,256]{2,1,0:T(8,128)(2,1)S(1)}) custom-call(s32[1]{0:T(128)} %bitcast.8.place, s32[64,128]{1,0:T(8,128)S(1)} %bitcast.11, s32[64,128]{1,0:T(8,128)S(1)} %bitcast.13, s32[64,128]{1,0:T(8,128)S(1)} %bitcast.15, f32[64,128]{1,0:T(8,128)S(1)} %bitcast.17, f32[64,128]{1,0:T(8,128)S(1)} %bitcast.19, ...), custom_call_target="tpu_custom_call" | custom-call | tf_op jit(solution)/shard_map/col_bands/pallas_call | solution.py:125
  61.3 0.0 collective-permute-done.9.refs_5_
  61.3 11.7 %collective-permute-done.7.refs_0_ = f32[512,256]{1,0:T(8,128)} collective-permute-done((f32[512,256]{1,0:T(8,128)}, f32[512,256]{1,0:T(8,128)}, u32[]{:S(2)}, u32[]{:S(2)}) %collective-permute-start.7) | collective-permute-done | bytes 524320 | tf_op jit(solution)/shard_map/ppermute | solution.py:344
  73.0 7.0 %cols.1.part = f32[512,1024]{1,0:T(8,128)} custom-call(f32[512,256]{1,0:T(8,128)} %collective-permute-done.7.refs_0_, f32[512,256]{1,0:T(8,128)} %rows.7.refs_1_, f32[512,256]{1,0:T(8,128)} %rows.5.refs_2_, f32[512,256]{1,0:T(8,128)} %rows.4.refs_3_, f32[512,256]{1,0:T(8,128)} %rows.6.refs_4_, f32[512,256]{1,0:T(8,128)} %collective-permute-done.9.refs_5_, ...), custom_call_target="tpu_custom_call" | custom-call | tf_op jit(solution)/shard_map/cols/pallas_call | solution.py:255
  80.0 0.0 collective-permute-done.6.east
  80.0 4.2 %collective-permute-done.2.west = f32[512,256]{1,0:T(8,128)S(1)} collective-permute-done((f32[512,256]{1,0:T(8,128)}, f32[512,256]{1,0:T(8,128)S(1)}, u32[]{:S(2)}, u32[]{:S(2)}) %collective-permute-start.2) | collective-permute-done | bytes 524320 | tf_op jit(solution)/shard_map/ppermute | solution.py:344
  84.1 2.8 %tail.1 = f32[512,1024]{1,0:T(8,128)} custom-call(f32[512,256]{1,0:T(8,128)S(1)} %collective-permute-done.2.west, f32[512,256]{1,0:T(8,128)} %collective-permute-done.6.east, bf16[4,1280,256]{2,1,0:T(8,128)(2,1)S(1)} %get-tuple-element.14.refs_6_.band_high, ...), custom_call_target="tpu_custom_call", output_to_operand_aliasing={{}: (4, {})} | custom-call | tf_op jit(solution)/shard_map/tail/pallas_call | solution.py:286
Async XLA Ops:
  0.0 21.2 %copy-start = (s32[1,1,8192]{2,1,0:T(1,128)S(1)}, s32[1,1,8192]{2,1,0:T(1,128)}, u32[]{:S(2)}) copy-start(s32[1,1,8192]{2,1,0:T(1,128)} %param.8) | copy-start | bytes 98308
  0.0 21.2 %copy-start.1 = (s32[1,1,8192]{2,1,0:T(1,128)S(1)}, s32[1,1,8192]{2,1,0:T(1,128)}, u32[]{:S(2)}) copy-start(s32[1,1,8192]{2,1,0:T(1,128)} %param.9) | copy-start | bytes 98308
  0.0 21.2 %copy-start.2 = (s32[1,1,8192]{2,1,0:T(1,128)S(1)}, s32[1,1,8192]{2,1,0:T(1,128)}, u32[]{:S(2)}) copy-start(s32[1,1,8192]{2,1,0:T(1,128)} %param.10) | copy-start | bytes 98308
  0.0 21.2 %copy-start.3 = (f32[1,1,8192]{2,1,0:T(1,128)S(1)}, f32[1,1,8192]{2,1,0:T(1,128)}, u32[]{:S(2)}) copy-start(f32[1,1,8192]{2,1,0:T(1,128)} %param.11) | copy-start | bytes 98308
  0.0 21.2 %copy-start.4 = (f32[1,8192]{1,0:T(1,128)S(1)}, f32[1,8192]{1,0:T(1,128)}, u32[]{:S(2)}) copy-start(f32[1,8192]{1,0:T(1,128)} %param.12) | copy-start | bytes 98308
  0.0 21.2 %copy-start.5 = (f32[1,8192]{1,0:T(1,128)S(1)}, f32[1,8192]{1,0:T(1,128)}, u32[]{:S(2)}) copy-start(f32[1,8192]{1,0:T(1,128)} %param.13) | copy-start | bytes 98308
  0.0 4.8 %collective-permute-start = (f32[512,1024]{1,0:T(8,128)}, f32[512,1024]{1,0:T(8,128)S(1)}, u32[]{:S(2)}, u32[]{:S(2)}) collective-permute-start(f32[512,1024]{1,0:T(8,128)} %bitcast.22), channel_id=1, source_target_pairs={{0,8},{8,0},{16,24},{24,16},{32,40},{40,32},{48,56},{56,48},{64,72... | collective-permute-start | bytes 6291464 | tf_op jit(solution)/shard_map/ppermute | solution.py:327
  5.9 28.8 %collective-permute-start.1 = (f32[512,512]{1,0:T(8,128)}, f32[512,512]{1,0:T(8,128)S(1)}, u32[]{:S(2)}, u32[]{:S(2)}) collective-permute-start(f32[512,512]{1,0:T(8,128)} %take.2), channel_id=1, source_target_pairs={{24,8},{0,16},{40,24},{16,32},{56,40},{32,48},{72,56},{48,64},{88,... | collective-permute-start | bytes 3145736 | tf_op jit(solution)/shard_map/ppermute | solution.py:334
  10.1 9.9 %collective-permute-start.4 = (f32[512,256]{1,0:T(8,128)}, f32[512,256]{1,0:T(8,128)}, u32[]{:S(2)}, u32[]{:S(2)}) collective-permute-start(f32[512,256]{1,0:T(8,128)} %get-tuple-element.13), channel_id=1, source_target_pairs={{56,0},{64,120},{57,1},{65,121},{58,2},{66,122},{59,3},{67,123},{6... | collective-permute-start | bytes 1572872 | tf_op jit(solution)/shard_map/ppermute | solution.py:331
  13.8 15.7 %collective-permute-start.8 = (f32[512,256]{1,0:T(8,128)}, f32[512,256]{1,0:T(8,128)}, u32[]{:S(2)}, u32[]{:S(2)}) collective-permute-start(f32[512,256]{1,0:T(8,128)} %get-tuple-element.16), channel_id=1, source_target_pairs={{16,8},{8,16},{32,24},{24,32},{48,40},{40,48},{64,56},{56,64},{80,... | collective-permute-start | bytes 1572872 | tf_op jit(solution)/shard_map/ppermute | solution.py:330
  18.4 25.3 %collective-permute-start.3 = (f32[512,256]{1,0:T(8,128)}, f32[512,256]{1,0:T(8,128)}, u32[]{:S(2)}, u32[]{:S(2)}) collective-permute-start(f32[512,256]{1,0:T(8,128)} %get-tuple-element.13), channel_id=1, source_target_pairs={{16,8},{8,16},{32,24},{24,32},{48,40},{40,48},{80,72},{72,80},{96,... | collective-permute-start | bytes 1572872 | tf_op jit(solution)/shard_map/ppermute | solution.py:333
  19.9 23.8 %collective-permute-start.5 = (f32[512,256]{1,0:T(8,128)}, f32[512,256]{1,0:T(8,128)}, u32[]{:S(2)}, u32[]{:S(2)}) collective-permute-start(f32[512,256]{1,0:T(8,128)} %collective-permute-done.4), channel_id=1, source_target_pairs={{0,64},{120,56},{1,65},{121,57},{2,66},{122,58},{3,67},{123,59},{4... | collective-permute-start | bytes 1572872 | tf_op jit(solution)/shard_map/ppermute | solution.py:332
  32.8 28.5 %collective-permute-start.9 = (f32[512,256]{1,0:T(8,128)}, f32[512,256]{1,0:T(8,128)}, u32[]{:S(2)}, u32[]{:S(2)}) collective-permute-start(f32[512,256]{1,0:T(8,128)} %rows.7.refs_1_), channel_id=1, source_target_pairs={{1,0},{2,1},{3,2},{4,3},{5,4},{6,5},{7,6},{9,8},{10,9},{11,10},{12... | collective-permute-start | bytes 1572872 | tf_op jit(solution)/shard_map/ppermute | solution.py:344
  38.0 35.0 %collective-permute-start.7 = (f32[512,256]{1,0:T(8,128)}, f32[512,256]{1,0:T(8,128)}, u32[]{:S(2)}, u32[]{:S(2)}) collective-permute-start(f32[512,256]{1,0:T(8,128)} %rows.6.refs_4_), channel_id=1, source_target_pairs={{0,1},{1,2},{2,3},{3,4},{4,5},{5,6},{6,7},{8,9},{9,10},{10,11},{11... | collective-permute-start | bytes 1572872 | tf_op jit(solution)/shard_map/ppermute | solution.py:344
  47.2 32.7 %collective-permute-start.6 = (f32[512,256]{1,0:T(8,128)}, f32[512,256]{1,0:T(8,128)}, u32[]{:S(2)}, u32[]{:S(2)}) collective-permute-start(f32[512,256]{1,0:T(8,128)} %rows.5.refs_2_), channel_id=1, source_target_pairs={{1,0},{2,1},{3,2},{4,3},{5,4},{6,5},{7,6},{9,8},{10,9},{11,10},{12... | collective-permute-start | bytes 1572872 | tf_op jit(solution)/shard_map/ppermute | solution.py:344
  52.4 31.7 %collective-permute-start.2 = (f32[512,256]{1,0:T(8,128)}, f32[512,256]{1,0:T(8,128)S(1)}, u32[]{:S(2)}, u32[]{:S(2)}) collective-permute-start(f32[512,256]{1,0:T(8,128)} %rows.4.refs_3_), channel_id=1, source_target_pairs={{0,1},{1,2},{2,3},{3,4},{4,5},{5,6},{6,7},{8,9},{9,10},{10,11},{11... | collective-permute-start | bytes 1572872 | tf_op jit(solution)/shard_map/ppermute | solution.py:344
